TPU v7x, 32 devices: a whole 2x2x4 slice. The times are simulated.
32 devices in a mesh: rep: 4 (over z), fsdp: 8 (over y, x, core).
Axes of the slice: x: 2, y: 2, z: 4, core: 2. Of those that a mesh axis runs over, the one named last changes fastest.
Arguments:
- tokens: bfloat16 [4096, 2048], P(('rep', 'fsdp')), may hold values from -6 to 6
- cotangent: bfloat16 [4096, 2048], P(('rep', 'fsdp')), may hold values from -6 to 6
- doc_lengths: int32 [4, 8], replicated, may hold values from 1 to 513, as said below
- norm1_gain: bfloat16 [2048], P('fsdp'), may hold values from 0.5 to 1.5
- w_query: bfloat16 [2048, 2048], P('fsdp'), may hold values from -0.125 to 0.125
- w_key: bfloat16 [2048, 256], P('fsdp'), may hold values from -0.125 to 0.125
- w_value: bfloat16 [2048, 256], P('fsdp'), may hold values from -0.125 to 0.125
- w_out: bfloat16 [2048, 2048], P('fsdp'), may hold values from -0.5 to 0.5
- norm2_gain: bfloat16 [2048], P('fsdp'), may hold values from 0.5 to 1.5
- w_gate: bfloat16 [2048, 5632], P('fsdp'), may hold values from -0.125 to 0.125
- w_up: bfloat16 [2048, 5632], P('fsdp'), may hold values from -0.125 to 0.125
- w_down: bfloat16 [5632, 2048], P('fsdp'), may hold values from -0.078125 to 0.078125
Outputs:
- output: bfloat16 [4096, 2048], P(('rep', 'fsdp'))
- grad_input: bfloat16 [4096, 2048], P(('rep', 'fsdp'))
- grad_norm1: float32 [2048], P('fsdp')
- grad_query: float32 [2048, 2048], P('fsdp')
- grad_key: float32 [2048, 256], P('fsdp')
- grad_value: float32 [2048, 256], P('fsdp')
- grad_out_proj: float32 [2048, 2048], P('fsdp')
- grad_norm2: float32 [2048], P('fsdp')
- grad_gate: float32 [2048, 5632], P('fsdp')
- grad_up: float32 [2048, 5632], P('fsdp')
- grad_down: float32 [5632, 2048], P('fsdp')
Inputs may be any that keep to these rules, and one draw needn't show every extreme that they name: `doc_lengths`: row s lists in order the lengths of the documents packed into sequence s, and as its last entry the length of the tail padding, at most 128; each row sums to 1024, and in each row exactly one document has 513 tokens.
All inputs are finite; a program needn't handle non-finite values.
Results may differ from a plain program's by a relative error of at most 0.022.
Values may be sent and summed in bfloat16 or wider, within the bound.
No kernel may reach another device: no remote copies, remote signals or barrier semaphores. Data moves between devices by JAX's collectives and lax.ppermute only.
A program may use at most 384 MiB of HBM per device.

v0:
```python
import math

import jax
import jax.numpy as jnp
from jax import lax
from jax.sharding import PartitionSpec as P

D = 2048
H = 32
KVH = 4
HD = 64
FF = 5632
DOCS = 8


NORM_EPS = 1e-05
ROPE_BASE = 10000.0
MASK_FILL = -1e30


def angle_tables(positions, head_dim):
    fractions = jnp.arange(0, head_dim, 2, dtype=jnp.float32) / head_dim
    inverse = jnp.exp(-math.log(ROPE_BASE) * fractions)
    angles = positions[:, None] * inverse[None, :]
    angles = jnp.concatenate([angles, angles], axis=-1)
    return (jnp.cos(angles)[:, None, :], jnp.sin(angles)[:, None, :])


def rotate(vectors, cos_table, sin_table):
    half_dim = vectors.shape[-1] // 2
    turned = jnp.concatenate([-vectors[..., half_dim:], vectors[..., :half_dim]], axis=-1)
    return vectors * cos_table + turned * sin_table


def rotate_back(gradients, cos_table, sin_table):
    half_dim = gradients.shape[-1] // 2
    moved = gradients * sin_table
    turned = jnp.concatenate([moved[..., half_dim:], -moved[..., :half_dim]], axis=-1)
    return gradients * cos_table + turned


def masks_for(lengths, offset, tok_count, seq_len):
    bounds = jnp.cumsum(lengths, dtype=jnp.int32)
    key_pos = jnp.arange(seq_len, dtype=jnp.int32)
    key_seg = jnp.sum(
        (bounds[None, :] <= key_pos[:, None]).astype(jnp.int32), axis=1, dtype=jnp.int32
    )
    key_valid = key_seg < DOCS - 1
    query_pos = offset + jnp.arange(tok_count, dtype=jnp.int32)
    query_seg = lax.dynamic_slice_in_dim(key_seg, offset, tok_count)
    query_valid = lax.dynamic_slice_in_dim(key_valid, offset, tok_count)
    allowed = (key_pos[None, :] <= query_pos[:, None]) & (query_seg[:, None] == key_seg[None, :])
    allowed = allowed & query_valid[:, None] & key_valid[None, :] | (
        key_pos[None, :] == query_pos[:, None]
    )
    return (allowed, query_valid, query_pos)


def masked_scores(query_grp, key_grp, allowed):
    score_scale = 1.0 / math.sqrt(query_grp.shape[-1])
    scores = (
        jnp.einsum("tgd,sd->tgs", query_grp, key_grp, preferred_element_type=jnp.float32)
        * score_scale
    )
    return jnp.where(allowed[:, None, :], scores, MASK_FILL)


def attend_forward(query_grp, key_grp, value_grp, allowed):
    scores = masked_scores(query_grp, key_grp, allowed)
    highest = jnp.max(scores, axis=-1, keepdims=True)
    weights = jnp.exp(scores - highest)
    totals = jnp.sum(weights, axis=-1, keepdims=True)
    prob_low = (weights / totals).astype(jnp.bfloat16)
    mixed = jnp.einsum("tgs,sd->tgd", prob_low, value_grp, preferred_element_type=jnp.float32)
    logsum = highest[..., 0] + jnp.log(totals[..., 0])
    return (mixed, logsum)


def attend_backward(query_grp, key_grp, value_grp, allowed, logsum, grad_mixed):
    score_scale = 1.0 / math.sqrt(query_grp.shape[-1])
    scores = masked_scores(query_grp, key_grp, allowed)
    probs_f32 = jnp.exp(scores - logsum[..., None])
    grad_probs = jnp.einsum(
        "tgd,sd->tgs", grad_mixed, value_grp, preferred_element_type=jnp.float32
    )
    inner_sum = jnp.sum(probs_f32 * grad_probs, axis=-1, keepdims=True)
    grad_scores = (probs_f32 * (grad_probs - inner_sum)).astype(jnp.bfloat16)
    grad_query = (
        jnp.einsum("tgs,sd->tgd", grad_scores, key_grp, preferred_element_type=jnp.float32)
        * score_scale
    )
    grad_key = (
        jnp.einsum("tgs,tgd->sd", grad_scores, query_grp, preferred_element_type=jnp.float32)
        * score_scale
    )
    grad_value = jnp.einsum(
        "tgs,tgd->sd",
        probs_f32.astype(jnp.bfloat16),
        grad_mixed,
        preferred_element_type=jnp.float32,
    )
    return (grad_query, grad_key, grad_value)


def norm_parts(vectors):
    scale_inv = lax.rsqrt(jnp.mean(vectors * vectors, axis=-1, keepdims=True) + NORM_EPS)
    return (scale_inv, vectors * scale_inv)


def norm_back(grad_hidden, normed, scale_inv, gain):
    grad_normed = grad_hidden * gain
    return scale_inv * (
        grad_normed - normed * jnp.mean(grad_normed * normed, axis=-1, keepdims=True)
    )


def local(
    tokens,
    cotangent,
    doc_lengths,
    norm1_gain,
    w_query,
    w_key,
    w_value,
    w_out,
    norm2_gain,
    w_gate,
    w_up,
    w_down,
):
    tok_rows = tokens.shape[0]
    group_size = lax.axis_size("fsdp")
    seq_len = tok_rows * group_size
    member = lax.axis_index("fsdp")
    replica = lax.axis_index("rep")
    offset = member * tok_rows
    lengths = lax.dynamic_index_in_dim(doc_lengths, replica, 0, keepdims=False)
    allowed, query_valid, query_pos = masks_for(lengths, offset, tok_rows, seq_len)
    valid_col = query_valid.astype(jnp.float32)[:, None]
    cos_table, sin_table = angle_tables(query_pos.astype(jnp.float32), HD)
    heads_per = H // KVH
    kv_width = KVH * HD
    gain_one, full_query, full_key, full_value, full_out = (
        lax.all_gather(norm1_gain, "fsdp", axis=0, tiled=True),
        lax.all_gather(w_query, "fsdp", axis=0, tiled=True),
        lax.all_gather(w_key, "fsdp", axis=0, tiled=True),
        lax.all_gather(w_value, "fsdp", axis=0, tiled=True),
        lax.all_gather(w_out, "fsdp", axis=0, tiled=True),
    )
    inputs = tokens.astype(jnp.float32)
    scale_one, normed_one = norm_parts(inputs)
    hidden_one = (normed_one * gain_one.astype(jnp.float32)).astype(jnp.bfloat16)
    queries = jnp.dot(hidden_one, full_query, preferred_element_type=jnp.float32).reshape(
        tok_rows, H, HD
    )
    key_proj = jnp.dot(hidden_one, full_key, preferred_element_type=jnp.float32).reshape(
        tok_rows, KVH, HD
    )
    value_low = jnp.dot(hidden_one, full_value, preferred_element_type=jnp.float32).astype(
        jnp.bfloat16
    )
    query_low = rotate(queries, cos_table, sin_table).astype(jnp.bfloat16)
    key_low = (
        rotate(key_proj, cos_table, sin_table).astype(jnp.bfloat16).reshape(tok_rows, kv_width)
    )
    kv_local = jnp.concatenate([key_low, value_low], axis=1)
    kv_seq = lax.all_gather(kv_local, "fsdp", axis=0, tiled=True)
    key_seq = kv_seq[:, :kv_width].reshape(seq_len, KVH, HD).transpose(1, 0, 2)
    value_seq = kv_seq[:, kv_width:].reshape(seq_len, KVH, HD).transpose(1, 0, 2)
    query_grp = query_low.reshape(tok_rows, KVH, heads_per, HD).transpose(1, 0, 2, 3)

    def forward_entry(packed):
        return attend_forward(packed[0], packed[1], packed[2], allowed)

    mixed, logsum = lax.map(forward_entry, (query_grp, key_seq, value_seq))
    attn_low = (mixed.transpose(1, 0, 2, 3).reshape(tok_rows, H * HD) * valid_col).astype(
        jnp.bfloat16
    )
    resid_one = inputs + jnp.dot(attn_low, full_out, preferred_element_type=jnp.float32)
    gain_two, full_gate, full_up, full_down = (
        lax.all_gather(norm2_gain, "fsdp", axis=0, tiled=True),
        lax.all_gather(w_gate, "fsdp", axis=0, tiled=True),
        lax.all_gather(w_up, "fsdp", axis=0, tiled=True),
        lax.all_gather(w_down, "fsdp", axis=0, tiled=True),
    )
    scale_two, normed_two = norm_parts(resid_one)
    hidden_two = (normed_two * gain_two.astype(jnp.float32)).astype(jnp.bfloat16)
    gate_pre = jnp.dot(hidden_two, full_gate, preferred_element_type=jnp.float32)
    up_pre = jnp.dot(hidden_two, full_up, preferred_element_type=jnp.float32)
    sigmoid_gate = jax.nn.sigmoid(gate_pre)
    silu_gate = gate_pre * sigmoid_gate
    inner_low = (silu_gate * up_pre).astype(jnp.bfloat16)
    result = (resid_one + jnp.dot(inner_low, full_down, preferred_element_type=jnp.float32)).astype(
        jnp.bfloat16
    )
    gain_one, full_query, full_key, full_value, full_out = (
        lax.all_gather(norm1_gain, "fsdp", axis=0, tiled=True),
        lax.all_gather(w_query, "fsdp", axis=0, tiled=True),
        lax.all_gather(w_key, "fsdp", axis=0, tiled=True),
        lax.all_gather(w_value, "fsdp", axis=0, tiled=True),
        lax.all_gather(w_out, "fsdp", axis=0, tiled=True),
    )
    gain_two, full_gate, full_up, full_down = (
        lax.all_gather(norm2_gain, "fsdp", axis=0, tiled=True),
        lax.all_gather(w_gate, "fsdp", axis=0, tiled=True),
        lax.all_gather(w_up, "fsdp", axis=0, tiled=True),
        lax.all_gather(w_down, "fsdp", axis=0, tiled=True),
    )
    grad_res = cotangent.astype(jnp.float32)
    grad_inner = jnp.einsum("td,fd->tf", cotangent, full_down, preferred_element_type=jnp.float32)
    grad_gate_low = (
        grad_inner * up_pre * sigmoid_gate * (1.0 + gate_pre * (1.0 - sigmoid_gate))
    ).astype(jnp.bfloat16)
    grad_up_low = (grad_inner * silu_gate).astype(jnp.bfloat16)
    grad_hidden_two = jnp.einsum(
        "tf,df->td", grad_gate_low, full_gate, preferred_element_type=jnp.float32
    )
    grad_hidden_two = grad_hidden_two + jnp.einsum(
        "tf,df->td", grad_up_low, full_up, preferred_element_type=jnp.float32
    )
    gain_two_local = jnp.sum(grad_hidden_two * normed_two, axis=0)
    grad_resid = grad_res + norm_back(
        grad_hidden_two, normed_two, scale_two, gain_two.astype(jnp.float32)
    )
    grad_attn_low = grad_resid.astype(jnp.bfloat16)
    grad_mix_low = jnp.einsum(
        "td,ed->te", grad_attn_low, full_out, preferred_element_type=jnp.float32
    ).astype(jnp.bfloat16)
    grad_mix_low = grad_mix_low * query_valid.astype(jnp.bfloat16)[:, None]
    grad_mix_grp = grad_mix_low.reshape(tok_rows, KVH, heads_per, HD).transpose(1, 0, 2, 3)

    def backward_entry(packed):
        return attend_backward(packed[0], packed[1], packed[2], allowed, packed[3], packed[4])

    grad_query_grp, grad_key_seq, grad_value_seq = lax.map(
        backward_entry, (query_grp, key_seq, value_seq, logsum, grad_mix_grp)
    )
    grad_queries = grad_query_grp.transpose(1, 0, 2, 3).reshape(tok_rows, H, HD)
    grad_query_low = (
        rotate_back(grad_queries, cos_table, sin_table)
        .reshape(tok_rows, H * HD)
        .astype(jnp.bfloat16)
    )
    kv_full = jnp.concatenate(
        [
            grad_key_seq.transpose(1, 0, 2).reshape(seq_len, kv_width),
            grad_value_seq.transpose(1, 0, 2).reshape(seq_len, kv_width),
        ],
        axis=1,
    )
    kv_grad = lax.psum_scatter(
        kv_full.astype(jnp.bfloat16), "fsdp", scatter_dimension=0, tiled=True
    ).astype(jnp.float32)
    grad_key_low = rotate_back(
        kv_grad[:, :kv_width].reshape(tok_rows, KVH, HD), cos_table, sin_table
    )
    grad_key_low = grad_key_low.reshape(tok_rows, kv_width).astype(jnp.bfloat16)
    grad_value_low = kv_grad[:, kv_width:].astype(jnp.bfloat16)
    grad_hidden_one = jnp.einsum(
        "te,de->td", grad_query_low, full_query, preferred_element_type=jnp.float32
    )
    grad_hidden_one = grad_hidden_one + jnp.einsum(
        "te,de->td", grad_key_low, full_key, preferred_element_type=jnp.float32
    )
    grad_hidden_one = grad_hidden_one + jnp.einsum(
        "te,de->td", grad_value_low, full_value, preferred_element_type=jnp.float32
    )
    gain_one_local = jnp.sum(grad_hidden_one * normed_one, axis=0)
    grad_inputs = (
        grad_resid + norm_back(grad_hidden_one, normed_one, scale_one, gain_one.astype(jnp.float32))
    ).astype(jnp.bfloat16)
    grad_qkv_cols = jnp.concatenate([grad_query_low, grad_key_low, grad_value_low], axis=1)
    grad_gate_up_cols = jnp.concatenate([grad_gate_low, grad_up_low], axis=1)
    gain_one_part, gain_two_part = (
        lax.psum_scatter(gain_one_local, "fsdp", scatter_dimension=0, tiled=True),
        lax.psum_scatter(gain_two_local, "fsdp", scatter_dimension=0, tiled=True),
    )
    part_qkv = lax.psum_scatter(
        jnp.einsum(
            "tc,tk->ck", hidden_one, grad_qkv_cols, preferred_element_type=jnp.float32
        ).astype(jnp.bfloat16),
        "fsdp",
        scatter_dimension=0,
        tiled=True,
    )
    part_out = lax.psum_scatter(
        jnp.einsum("tc,tk->ck", attn_low, grad_attn_low, preferred_element_type=jnp.float32).astype(
            jnp.bfloat16
        ),
        "fsdp",
        scatter_dimension=0,
        tiled=True,
    )
    part_gate_up = lax.psum_scatter(
        jnp.einsum(
            "tc,tk->ck", hidden_two, grad_gate_up_cols, preferred_element_type=jnp.float32
        ).astype(jnp.bfloat16),
        "fsdp",
        scatter_dimension=0,
        tiled=True,
    )
    part_down = lax.psum_scatter(
        jnp.einsum("tc,tk->ck", inner_low, cotangent, preferred_element_type=jnp.float32).astype(
            jnp.bfloat16
        ),
        "fsdp",
        scatter_dimension=0,
        tiled=True,
    )
    summed = (
        lax.psum(gain_one_part.astype(jnp.bfloat16), "rep").astype(jnp.float32),
        lax.psum(part_qkv, "rep").astype(jnp.float32),
        lax.psum(part_out, "rep").astype(jnp.float32),
        lax.psum(gain_two_part.astype(jnp.bfloat16), "rep").astype(jnp.float32),
        lax.psum(part_gate_up, "rep").astype(jnp.float32),
        lax.psum(part_down, "rep").astype(jnp.float32),
    )
    grad_norm_one, grad_qkv, grad_out_part, grad_norm_two, grad_gate_up, grad_down_part = summed
    grad_query_part = grad_qkv[:, :D]
    grad_key_part = grad_qkv[:, D : D + kv_width]
    grad_value_part = grad_qkv[:, D + kv_width :]
    grad_gate_part = grad_gate_up[:, :FF]
    grad_up_part = grad_gate_up[:, FF:]
    return (
        result,
        grad_inputs,
        grad_norm_one,
        grad_query_part,
        grad_key_part,
        grad_value_part,
        grad_out_part,
        grad_norm_two,
        grad_gate_part,
        grad_up_part,
        grad_down_part,
    )


def solution(mesh):
    placed = (
        P(("rep", "fsdp"), None),
        P(("rep", "fsdp"), None),
        P(),
        P("fsdp"),
        P("fsdp", None),
        P("fsdp", None),
        P("fsdp", None),
        P("fsdp", None),
        P("fsdp"),
        P("fsdp", None),
        P("fsdp", None),
        P("fsdp", None),
    )
    return jax.shard_map(
        local,
        mesh=mesh,
        in_specs=placed,
        out_specs=(
            P(("rep", "fsdp"), None),
            P(("rep", "fsdp"), None),
            P("fsdp"),
            P("fsdp", None),
            P("fsdp", None),
            P("fsdp", None),
            P("fsdp", None),
            P("fsdp"),
            P("fsdp", None),
            P("fsdp", None),
            P("fsdp", None),
        ),
        check_vma=False,
    )
```

profile of v0, /device:TPU:0, one launch (start us, length us, event | category | flops | bytes accessed | tf_op | source)
XLA Modules:
  0.0 1672.1 jit_solution(14276761914154948728)
XLA Ops:
  9.4 10.3 all-gather
  21.3 14.8 all-gather.13.cloned.1.call-done
  36.2 1.7 fusion.106
  38.2 23.4 %all-gather.15.cloned.1.call-done = bf16[2048,256]{1,0:T(8,128)(2,1)} async-done(((bf16[256,256]{1,0:T(8,128)(2,1)}), bf16[2048,256]{1,0:T(8,128)(2,1)}) %all-gather.15.cloned.1.call-update) | async-done | bytes 1048592 | tf_op jit(solution)/shard_map/all_gather | solution.py:147
  61.6 1.6 convolution_convert_fusion.5
  67.7 8.8 all-gather.1
  76.5 11.1 all-gather.17.cloned.1.call-done
  89.3 54.5 %all-gather.11.cloned.1.call-done = bf16[2048,2048]{1,0:T(8,128)(2,1)} async-done(((bf16[256,2048]{1,0:T(8,128)(2,1)}), bf16[2048,2048]{1,0:T(8,128)(2,1)}) %all-gather.11.cloned.1.call-update) | async-done | bytes 8388624 | tf_op jit(solution)/shard_map/all_gather | solution.py:145
  143.7 6.9 fusion.108
  151.1 15.0 while.28
  153.9 1.3 fusion.172
  167.1 1.7 fusion.88
  168.8 31.1 %all-gather.19.cloned.1.call-done = bf16[2048,2048]{1,0:T(8,128)(2,1)} async-done(((bf16[256,2048]{1,0:T(8,128)(2,1)}), bf16[2048,2048]{1,0:T(8,128)(2,1)}) %all-gather.19.cloned.1.call-update) | async-done | bytes 8388624 | tf_op jit(solution)/shard_map/all_gather | solution.py:148
  199.9 4.8 multiply_reduce_fusion.3
  204.8 113.3 %all-gather.21.cloned.1.call-done = bf16[2048,5632]{1,0:T(8,128)(2,1)} async-done(((bf16[256,5632]{1,0:T(8,128)(2,1)}), bf16[2048,5632]{1,0:T(8,128)(2,1)}) %all-gather.21.cloned.1.call-update) | async-done | bytes 23068688 | tf_op jit(solution)/shard_map/all_gather | solution.py:182
  318.1 12.3 fusion.117
  330.4 106.1 %all-gather.23.cloned.1.call-done = bf16[2048,5632]{1,0:T(8,128)(2,1)} async-done(((bf16[256,5632]{1,0:T(8,128)(2,1)}), bf16[2048,5632]{1,0:T(8,128)(2,1)}) %all-gather.23.cloned.1.call-update) | async-done | bytes 23068688 | tf_op jit(solution)/shard_map/all_gather | solution.py:183
  436.5 12.3 fusion.118
  448.8 106.1 %all-gather.25.cloned.1.call-done = bf16[5632,2048]{1,0:T(8,128)(2,1)} async-done(((bf16[704,2048]{1,0:T(8,128)(2,1)}), bf16[5632,2048]{1,0:T(8,128)(2,1)}) %all-gather.25.cloned.1.call-update) | async-done | bytes 23068688 | tf_op jit(solution)/shard_map/all_gather | solution.py:184
  554.9 14.9 multiply_convert_fusion.1
  569.8 12.3 fusion.119
  582.1 13.2 multiply_reduce_fusion.1
  595.3 1.7 multiply_add_fusion
  597.0 7.1 fusion.71
  604.1 2.0 copy.58
  607.3 42.6 %while.29 = (s32[]{:T(128)}, f32[4,128,8,64]{1,3,2,0:T(8,128)}, bf16[4,1024,64]{1,2,0:T(8,128)(2,1)}, bf16[4,1024,64]{1,2,0:T(8,128)(2,1)}, bf16[4,128,8,64]{1,3...) while((s32[]{:T(128)}, f32[4,128,8,64]{1,3,2,0:T(8,128)}, ...), condition=%wide.region_11.12_spmd.clone, body=%wide.region_9.11_spmd.clone.sunk | while | flops 687864832 | bytes 44211620 | solution.py:235
  607.5 1.7 fusion.181
  609.5 2.4 multiply_reduce_fusion.5
  613.2 1.5 fusion.183
  614.7 1.4 fusion.184
  618.1 1.7 fusion.181
  620.1 2.4 multiply_reduce_fusion.5
  623.8 1.5 fusion.183
  625.3 1.4 fusion.184
  628.7 1.7 fusion.181
  630.7 2.4 multiply_reduce_fusion.5
  634.4 1.5 fusion.183
  635.9 1.4 fusion.184
  639.3 1.7 fusion.181
  641.3 2.4 multiply_reduce_fusion.5
  645.0 1.5 fusion.183
  646.5 1.4 fusion.184
  649.9 2.3 pad_maximum_fusion.1
  652.2 2.3 copy.60
  654.6 5.6 convolution_convert_fusion.3
  661.0 1.4 bitcast_multiply_fusion
  662.7 27.9 %reduce-scatter.16.cloned.1.call-done = bf16[128,512]{1,0:T(8,128)(2,1)} async-done(((bf16[1024,512]{1,0:T(8,128)(2,1)}), bf16[128,512]{1,0:T(8,128)(2,1)}) %reduce-scatter.16.cloned.1.call-update) | async-done | bytes 131088
  691.9 6.6 convolution_convert_fusion.2
  699.7 14.1 convolution_convert_fusion.1
  714.8 20.3 %convolution_convert_fusion = bf16[2048,11264]{1,0:T(8,128)(2,1)} fusion(bf16[128,2048]{1,0:T(8,128)(2,1)S(1)} %copy-done.9, bf16[128,5632]{1,0:T(8,128)(2,1)} %get-tuple-element.242, bf16[128,5632]{1,0:T(8,128)(2,1)} %get-tuple-element.243), kind=kOutput, calls=%fused_computation.73 | convolution fusion | flops 5934415872 | bytes 49545216 | tf_op jit(solution)/shard_map/tc,tk->ck/dot_general | solution.py:295
  735.5 29.7 %reduce-scatter.12.cloned.1.call-done = bf16[256,2048]{1,0:T(8,128)(2,1)} async-done(((bf16[2048,2048]{1,0:T(8,128)(2,1)}), bf16[256,2048]{1,0:T(8,128)(2,1)}) %reduce-scatter.12.cloned.1.call-update) | async-done | bytes 1048592 | tf_op jit(solution)/shard_map/reduce_scatter | solution.py:286
  765.3 85.5 %reduce-scatter.10.cloned.1.call-done = bf16[256,2560]{1,0:T(8,128)(2,1)} async-done(((bf16[2048,2560]{1,0:T(8,128)(2,1)}), bf16[256,2560]{1,0:T(8,128)(2,1)}) %reduce-scatter.10.cloned.1.call-update) | async-done | bytes 1310736 | tf_op jit(solution)/shard_map/reduce_scatter | solution.py:278
  850.8 149.8 %reduce-scatter.14.cloned.1.call-done = bf16[704,2048]{1,0:T(8,128)(2,1)} async-done(((bf16[5632,2048]{1,0:T(8,128)(2,1)}), bf16[704,2048]{1,0:T(8,128)(2,1)}) %reduce-scatter.14.cloned.1.call-update) | async-done | bytes 2883600 | tf_op jit(solution)/shard_map/reduce_scatter | solution.py:302
  1000.6 268.4 %reduce-scatter.18.cloned.1.call-done = bf16[256,11264]{1,0:T(8,128)(2,1)} async-done(((bf16[2048,11264]{1,0:T(8,128)(2,1)}), bf16[256,11264]{1,0:T(8,128)(2,1)}) %reduce-scatter.18.cloned.1.call-update) | async-done | bytes 5767184
  1270.9 6.4 fusion.120
  1277.4 12.0 fusion.70
  1290.6 25.4 %all-reduce.3 = (bf16[2048]{0:T(1024)(128)(2,1)S(1)}, bf16[2048]{0:T(1024)(128)(2,1)S(1)}) all-reduce(f32[2048]{0:T(1024)S(1)} %get-tuple-element.174, f32[2048]{0:T(1024)S(1)} %get-tuple-element.172), channel_id=3, replica_groups=mesh['rep'=4,'fsdp'=8] {'fsdp'}, use_global_device_ids=true, to_apply=%region_15.16.clone | all-reduce | flops 4096 | bytes 24576
  1316.1 12.4 all-reduce.4
  1330.9 318.6 %all-reduce.8.cloned.1.call-done = (bf16[256,2560]{1,0:T(8,128)(2,1)}, bf16[256,2048]{1,0:T(8,128)(2,1)}, bf16[256,11264]{1,0:T(8,128)(2,1)}, bf16[704,2048]{1,0:T(8,128)(2,1)}) async-done(((bf16[256,2560]{1,0:T(8,128)(2,1)}, bf16[256,2048]{1,0:T(8,128)(2,1)}, bf16[256,11264]{1,0:T(8,128)(2,1)}, bf16[704,2048]{1,0:T(8,128)(2,1)}), (bf16[256,2560]{1,0:T(8,128)(2,1)}, bf16[256,2048]{1,0:T(8,128)(2,1)}, ...) | async-done | bytes 11010064 | tf_op jit(solution)/shard_map/psum | solution.py:312
  1649.5 2.9 slice.85
  1652.4 1.9 fusion.112
  1654.3 1.6 convert_element_type.153
  1655.8 5.9 fusion.111
  1661.8 3.3 convert_element_type.159
  (226 shorter events, 49.6 us)
Async XLA Ops:
  7.2 60.0 %copy-start = (s32[4,8]{1,0:T(4,128)S(1)}, s32[4,8]{1,0:T(4,128)}, u32[]{:S(2)}) copy-start(s32[4,8]{1,0:T(4,128)} %param.18) | copy-start | bytes 388
  7.2 54.4 %copy-start.3 = (bf16[128,2048]{1,0:T(8,128)(2,1)S(1)}, bf16[128,2048]{1,0:T(8,128)(2,1)}, u32[]{:S(2)}) copy-start(bf16[128,2048]{1,0:T(8,128)(2,1)} %param.16) | copy-start | bytes 1572868
  7.2 28.9 %all-gather.13.cloned.1.call-start = ((), (), s32[]{:S(2)}) async-start(), calls=%async_computation.6 | async-start | bytes 1179648 | tf_op jit(solution)/shard_map/all_gather | solution.py:146
  7.9 53.6 %all-gather.15.cloned.1.call-start = ((), (), s32[]{:S(2)}) async-start(), calls=%async_computation.7 | async-start | bytes 1179648 | tf_op jit(solution)/shard_map/all_gather | solution.py:147
  8.7 78.9 %all-gather.17.cloned.1.call-start = ((), (), s32[]{:S(2)}) async-start(), calls=%async_computation.8 | async-start | bytes 1179648 | tf_op jit(solution)/shard_map/all_gather | solution.py:167
  19.8 124.0 %copy-start.31 = (f32[8,1,256]{2,1,0:T(1,128)}, f32[8,1,256]{2,1,0:T(1,128)S(1)}, u32[]{:S(2)}) copy-start(f32[8,1,256]{2,1,0:T(1,128)S(1)} %convert_element_type.160) | copy-start | bytes 24580
  19.9 130.7 %copy-start.23 = (f32[128,64]{0,1:T(8,128)}, f32[128,64]{0,1:T(8,128)S(1)}, u32[]{:S(2)}) copy-start(f32[128,64]{0,1:T(8,128)S(1)} %get-tuple-element.260) | copy-start | bytes 98308
  20.0 130.7 %copy-start.25 = (f32[128,64]{0,1:T(8,128)}, f32[128,64]{0,1:T(8,128)S(1)}, u32[]{:S(2)}) copy-start(f32[128,64]{0,1:T(8,128)S(1)} %get-tuple-element.259) | copy-start | bytes 98308
  21.3 122.4 %copy-start.34 = (f32[128]{0:T(128)}, f32[128]{0:T(128)S(1)}, u32[]{:S(2)}) copy-start(f32[128]{0:T(128)S(1)} %add_rsqrt_fusion.1) | copy-start | bytes 1540
  63.8 79.9 %all-gather.11.cloned.1.call-start = ((), (), s32[]{:S(2)}) async-start(), calls=%async_computation.5 | async-start | bytes 9437184 | tf_op jit(solution)/shard_map/all_gather | solution.py:145
  64.4 135.5 %all-gather.19.cloned.1.call-start = ((), (), s32[]{:S(2)}) async-start(), calls=%async_computation.9 | async-start | bytes 9437184 | tf_op jit(solution)/shard_map/all_gather | solution.py:148
  65.0 2.6 copy-start.36
  65.0 253.1 %all-gather.21.cloned.1.call-start = ((), (), s32[]{:S(2)}) async-start(), calls=%async_computation.10 | async-start | bytes 25952256 | tf_op jit(solution)/shard_map/all_gather | solution.py:182
  65.6 370.9 %all-gather.23.cloned.1.call-start = ((), (), s32[]{:S(2)}) async-start(), calls=%async_computation.11 | async-start | bytes 25952256 | tf_op jit(solution)/shard_map/all_gather | solution.py:183
  66.3 488.5 %all-gather.25.cloned.1.call-start = ((), (), s32[]{:S(2)}) async-start(), calls=%async_computation.12 | async-start | bytes 25952256 | tf_op jit(solution)/shard_map/all_gather | solution.py:184
  67.1 623.6 %reduce-scatter.16.cloned.1.call-start = ((), (), s32[]{:S(2)}) async-start(), calls=%async_computation.16 | async-start | bytes 1179648
  166.1 1.0 copy-start.14
  167.1 1.7 copy-start.4
  167.1 1.7 copy-start.16
  168.8 35.9 %copy-start.6 = (bf16[128,2048]{0,1:T(8,128)(2,1)}, bf16[128,2048]{0,1:T(8,128)(2,1)S(1)}, u32[]{:S(2)}) copy-start(bf16[128,2048]{0,1:T(8,128)(2,1)S(1)} %fusion.88) | copy-start | bytes 1572868
  204.8 231.7 %copy-start.8 = (bf16[128,2048]{1,0:T(8,128)(2,1)}, bf16[128,2048]{1,0:T(8,128)(2,1)S(1)}, u32[]{:S(2)}) copy-start(bf16[128,2048]{1,0:T(8,128)(2,1)S(1)} %multiply_convert_fusion.4) | copy-start | bytes 1572868
  330.4 224.4 %copy-start.18 = (bf16[128,2048]{1,0:T(8,128)(2,1)S(1)}, bf16[128,2048]{1,0:T(8,128)(2,1)}, u32[]{:S(2)}) copy-start(bf16[128,2048]{1,0:T(8,128)(2,1)} %param.17) | copy-start | bytes 1572868
  569.8 12.3 copy-start.5
  607.5 2.0 copy-start.17
  611.9 2.8 copy-start.27
  613.2 2.9 copy-start.29
  616.1 1.2 copy-start.28
  617.3 0.8 copy-start.30
  618.1 2.0 copy-start.17
  622.5 2.8 copy-start.27
  623.8 2.9 copy-start.29
  626.7 1.2 copy-start.28
  628.7 2.0 copy-start.17
  633.1 2.8 copy-start.27
  634.4 2.9 copy-start.29
  637.3 1.2 copy-start.28
  638.5 0.8 copy-start.30
  639.3 2.0 copy-start.17
  643.7 2.8 copy-start.27
  645.0 2.9 copy-start.29
  647.9 1.2 copy-start.28
  649.1 0.8 copy-start.30
  649.9 4.7 copy-start.7
  654.5 110.8 %reduce-scatter.12.cloned.1.call-start = ((), (), s32[]{:S(2)}) async-start(), calls=%async_computation.14 | async-start | bytes 9437184 | tf_op jit(solution)/shard_map/reduce_scatter | solution.py:286
  660.2 2.4 copy-start.26
  660.2 190.5 %reduce-scatter.10.cloned.1.call-start = ((), (), s32[]{:S(2)}) async-start(), calls=%async_computation.13 | async-start | bytes 11796480 | tf_op jit(solution)/shard_map/reduce_scatter | solution.py:278
  660.3 2.3 copy-start.10
  662.4 29.5 %copy-start.32 = (f32[8,1,256]{2,1,0:T(1,128)S(1)}, f32[8,1,256]{2,1,0:T(1,128)}, u32[]{:S(2)}) copy-start(f32[8,1,256]{2,1,0:T(1,128)} %copy-done.31) | copy-start | bytes 24580
  662.4 29.5 %copy-start.35 = (f32[128]{0:T(128)S(1)}, f32[128]{0:T(128)}, u32[]{:S(2)}) copy-start(f32[128]{0:T(128)} %copy-done.34) | copy-start | bytes 1540
  662.7 35.8 %copy-start.12 = (bf16[128,2048]{0,1:T(8,128)(2,1)}, bf16[128,2048]{0,1:T(8,128)(2,1)S(1)}, u32[]{:S(2)}) copy-start(bf16[128,2048]{0,1:T(8,128)(2,1)S(1)} %fusion.87) | copy-start | bytes 1572868
  698.5 1.2 copy-start.19
  698.5 302.1 %reduce-scatter.14.cloned.1.call-start = ((), (), s32[]{:S(2)}) async-start(), calls=%async_computation.15 | async-start | bytes 25952256 | tf_op jit(solution)/shard_map/reduce_scatter | solution.py:302
  713.8 1.0 copy-start.9
  713.8 555.2 %reduce-scatter.18.cloned.1.call-start = ((), (), s32[]{:S(2)}) async-start(), calls=%async_computation.17 | async-start | bytes 51904512
  735.2 914.2 %all-reduce.8.cloned.1.call-start = ((), (), s32[]{:S(2)}) async-start(), calls=%async_computation.18 | async-start | bytes 22020096 | tf_op jit(solution)/shard_map/psum | solution.py:312
  1269.0 1.9 copy-start.13
  1270.9 6.5 copy-start.11
  1277.4 12.1 copy-start.20
  1277.4 12.5 copy-start.22
  1277.4 12.5 copy-start.33
  1649.5 4.8 copy-start.21
  1649.5 6.4 copy-start.2
  1655.8 5.9 copy-start.15
  1661.8 3.3 copy-start.1
  (3 other events, 2.2 us)
Sparse Core Ops, SparseCore 0:
  9.9 26.1 all-gather.12
  38.0 23.4 all-gather.14
  64.0 23.4 all-gather.16
  89.3 54.3 all-gather.10
  145.5 54.3 all-gather.18
  201.6 116.4 all-gather.20
  320.0 116.4 all-gather.22
  438.4 116.4 all-gather.24
  654.6 36.0 reduce-scatter.15
  694.0 71.2 reduce-scatter.11
  769.2 81.5 reduce-scatter.9
  854.7 145.8 reduce-scatter.13
  1004.7 264.2 reduce-scatter.17
  1271.8 377.6 all-reduce.7
where the time goes:
time: 1680 us; the launch traced here: 1670 us
  waiting for transfers between devices  1340 us (80%)
  matrix products  195 us (12%)
  blocking collectives  57 us (3%)
  other arithmetic  29.4 us (2%)
  local copies, waits for them, and re-layouts  28.5 us (2%)
    psum x1, waiting for transfers between devices, local(): lax.psum(part_qkv, 'rep').astype(jnp.float32)  319 us
    unnamed x16, waiting for transfers between devices  301 us
    reduce_scatter x1, waiting for transfers between devices, local(): lax.psum_scatter(jnp.einsum('tc,tk->ck', inner_low, cotangent, preferred_...  150 us
    all_gather x1, waiting for transfers between devices, local(): lax.all_gather(w_gate, 'fsdp', axis=0, tiled=True)  113 us
    all_gather x1, waiting for transfers between devices, local(): lax.all_gather(w_up, 'fsdp', axis=0, tiled=True)  106 us
    all_gather x1, waiting for transfers between devices, local(): lax.all_gather(w_down, 'fsdp', axis=0, tiled=True)  106 us
    reduce_scatter x1, waiting for transfers between devices, local(): lax.psum_scatter(jnp.einsum('tc,tk->ck', hidden_one, grad_qkv_cols, prefe...  85.5 us
    all_gather x1, waiting for transfers between devices, local(): lax.all_gather(w_query, 'fsdp', axis=0, tiled=True)  54.5 us
  transfers between devices with their start and end apart: 14, of which 14 were waited for; matrix products, arithmetic and copies ran while one was open for 8% of the time, Pallas kernels for 0%

commit v1 on v0

v1 whole, which is shorter than its diff:
```python
import math

import jax
import jax.numpy as jnp
from jax import lax
from jax.experimental import pallas as pl
from jax.experimental.pallas import tpu as pltpu
from jax.sharding import PartitionSpec as P

H = 32
KVH = 4
HD = 64
DOCS = 8

NORM_EPS = 1e-05
ROPE_BASE = 10000.0
MASK_FILL = -1e30
F32 = jnp.float32
BF16 = jnp.bfloat16


def dot(a, b):
    return jnp.dot(a, b, preferred_element_type=F32)


def dot_nt(a, b):
    return lax.dot_general(a, b, (((1,), (1,)), ((), ())), preferred_element_type=F32)


def dot_tn(a, b):
    return lax.dot_general(a, b, (((0,), (0,)), ((), ())), preferred_element_type=F32)


def angle_tables(positions):
    fractions = jnp.arange(0, HD, 2, dtype=F32) / HD
    inverse = jnp.exp(-math.log(ROPE_BASE) * fractions)
    angles = positions[:, None] * inverse[None, :]
    angles = jnp.concatenate([angles, angles], axis=-1)
    return jnp.cos(angles)[:, None, :], jnp.sin(angles)[:, None, :]


def rotate(v, cos_table, sin_table):
    half = HD // 2
    turned = jnp.concatenate([-v[..., half:], v[..., :half]], axis=-1)
    return v * cos_table + turned * sin_table


def rotate_back(v, cos_table, sin_table):
    half = HD // 2
    moved = v * sin_table
    turned = jnp.concatenate([moved[..., half:], -moved[..., :half]], axis=-1)
    return v * cos_table + turned


def norm_parts(v):
    inv = lax.rsqrt(jnp.mean(v * v, axis=-1, keepdims=True) + NORM_EPS)
    return inv, v * inv


def norm_back(grad_hidden, normed, inv, gain):
    e = grad_hidden * gain
    return inv * (e - normed * jnp.mean(e * normed, axis=-1, keepdims=True))


def pick_columns(array, chip, count):
    rows, cols = array.shape
    width = cols // count
    if width % 128:
        split = array.reshape(rows, count, width).transpose(1, 0, 2)
        return jnp.stack(
            [lax.dynamic_index_in_dim(split, chip ^ k, 0, keepdims=False) for k in range(count)]
        )

    def body(c_ref, in_ref, out_ref):
        out_ref[0] = in_ref[...]

    return pl.pallas_call(
        body,
        grid_spec=pltpu.PrefetchScalarGridSpec(
            num_scalar_prefetch=1,
            grid=(count,),
            in_specs=[pl.BlockSpec((rows, width), lambda k, c: (0, c[0] ^ k))],
            out_specs=pl.BlockSpec((1, rows, width), lambda k, c: (k, 0, 0)),
        ),
        out_shape=jax.ShapeDtypeStruct((count, rows, width), array.dtype),
        name="pick_columns",
    )(chip.reshape(1), array)


def place(blocks, order, axis, dtype):
    rows, cols = blocks[0].shape
    count = len(blocks)
    if axis == 1 and cols % 128:
        full = jnp.zeros((count, rows, cols), dtype)
        for k in range(count):
            full = lax.dynamic_update_slice(full, blocks[k].astype(dtype)[None], (order[k], 0, 0))
        return full.transpose(1, 0, 2).reshape(rows, count * cols)

    def body(o_ref, *refs):
        out_ref = refs[-1]
        for k in range(count):

            @pl.when(pl.program_id(0) == k)
            def _():
                out_ref[...] = refs[k][...].astype(dtype)

    if axis == 0:
        shape, spec = (count * rows, cols), pl.BlockSpec((rows, cols), lambda k, o: (o[k], 0))
    else:
        shape, spec = (rows, count * cols), pl.BlockSpec((rows, cols), lambda k, o: (0, o[k]))
    return pl.pallas_call(
        body,
        grid_spec=pltpu.PrefetchScalarGridSpec(
            num_scalar_prefetch=1,
            grid=(count,),
            in_specs=[pl.BlockSpec((rows, cols), lambda k, o: (0, 0))] * count,
            out_specs=spec,
        ),
        out_shape=jax.ShapeDtypeStruct(shape, dtype),
        name="place",
    )(order, *blocks)


def local(
    tokens,
    cotangent,
    doc_lengths,
    norm1_gain,
    w_query,
    w_key,
    w_value,
    w_out,
    norm2_gain,
    w_gate,
    w_up,
    w_down,
):
    rows, model = tokens.shape
    group = lax.axis_size("fsdp")
    reps = lax.axis_size("rep")
    chips = group // 2
    dev = lax.axis_index("fsdp")
    rep = lax.axis_index("rep")
    chip, core = dev // 2, dev % 2
    seq_len = rows * group
    own = rows * chips
    wrows = w_query.shape[0]
    ff = w_gate.shape[1]
    heads = H // chips
    kv_share = chips // KVH
    qw = heads * HD

    def hop(v, k):
        return lax.ppermute(v, "fsdp", [(i, i ^ (2 * k)) for i in range(group)])

    def swap(v):
        return lax.ppermute(v, "fsdp", [(i, i ^ 1) for i in range(group)])

    def by_core(mine, other, axis):
        return jnp.where(
            core == 0,
            jnp.concatenate([mine, other], axis=axis),
            jnp.concatenate([other, mine], axis=axis),
        )

    def gather_chips(v):
        return [v] + [hop(v, k) for k in range(1, chips)]

    def scatter_chips(partial):
        parts = partial.astype(BF16).reshape(chips, rows, model)
        total = parts[0].astype(F32)
        for k in range(1, chips):
            total = total + hop(parts[k], k).astype(F32)
        return total

    half = reps // 2

    def chain(v):
        acc = v
        for s in range(half - 1):
            got = lax.ppermute(acc, "rep", [(s, s + 1), (reps - 1 - s, reps - 2 - s)])
            acc = acc + got
        got = lax.ppermute(acc, "rep", [(half - 1, half), (half, half - 1)])
        tot = lax.optimization_barrier(acc + got)
        for s in reversed(range(half - 1)):
            got = lax.ppermute(tot, "rep", [(s + 1, s), (reps - 2 - s, reps - 1 - s)])
            tot = jnp.where((rep == s) | (rep == reps - 1 - s), got, tot)
        return tot

    chip_order = jnp.stack([chip ^ k for k in range(chips)]).astype(jnp.int32)

    gains = jnp.stack([norm1_gain, norm2_gain])
    gain_blocks = gather_chips(gains)
    gain_blocks = [(g, swap(g)) for g in gain_blocks]
    gain_full = jnp.zeros((group, 2, wrows), BF16)
    for k in range(chips):
        mine, other = gain_blocks[k]
        gain_full = lax.dynamic_update_slice(gain_full, mine[None], ((chip ^ k) * 2 + core, 0, 0))
        gain_full = lax.dynamic_update_slice(
            gain_full, other[None], ((chip ^ k) * 2 + 1 - core, 0, 0)
        )
    gain_full = gain_full.astype(F32).transpose(1, 0, 2).reshape(2, model)
    gain_one, gain_two = gain_full[0], gain_full[1]

    row_order = jnp.concatenate([chip_order * 2 + core, chip_order * 2 + 1 - core])

    def columns_of_chip(blocks):
        got = [blocks[0]] + [hop(blocks[k], k) for k in range(1, chips)]
        return place(got + [swap(b) for b in got], row_order, 0, BF16)

    x_blocks = gather_chips(tokens)
    q_blocks = pick_columns(w_query, chip, chips)
    kv_cols = jnp.stack([w_key.reshape(wrows, KVH, HD), w_value.reshape(wrows, KVH, HD)], axis=2)
    kv_cols = kv_cols.transpose(1, 0, 2, 3).reshape(KVH, wrows, 2 * HD)
    qkv_blocks = [
        jnp.concatenate(
            [
                q_blocks[k],
                lax.dynamic_index_in_dim(kv_cols, (chip ^ k) // kv_share, 0, keepdims=False),
            ],
            axis=1,
        )
        for k in range(chips)
    ]
    w_qkv = columns_of_chip(qkv_blocks)
    w_out_c = by_core(w_out, swap(w_out), 0)
    w_gate_c = columns_of_chip(pick_columns(w_gate, chip, chips))
    w_up_c = columns_of_chip(pick_columns(w_up, chip, chips))
    w_down_c = by_core(w_down, swap(w_down), 0)
    cot_rows = jnp.concatenate(gather_chips(cotangent), axis=0)

    lengths = lax.dynamic_index_in_dim(doc_lengths, rep, 0, keepdims=False)
    bounds = jnp.cumsum(lengths, dtype=jnp.int32)
    starts = chip_order * (2 * rows)
    within = jnp.arange(rows, dtype=jnp.int32)
    own_pos = (starts[:, None] + core * rows + within[None, :]).reshape(own)
    other_pos = (starts[:, None] + (1 - core) * rows + within[None, :]).reshape(own)
    key_pos = jnp.concatenate([own_pos, other_pos])

    def segment(pos):
        return jnp.sum((bounds[None, :] <= pos[:, None]).astype(jnp.int32), axis=1)

    q_seg, k_seg = segment(own_pos), segment(key_pos)
    q_valid, k_valid = q_seg < DOCS - 1, k_seg < DOCS - 1
    allowed = (key_pos[None, :] <= own_pos[:, None]) & (q_seg[:, None] == k_seg[None, :])
    allowed = allowed & q_valid[:, None] & k_valid[None, :] | (key_pos[None, :] == own_pos[:, None])
    valid_col = q_valid.astype(F32)[:, None]
    cos_table, sin_table = angle_tables(own_pos.astype(F32))

    x_rows = jnp.concatenate(x_blocks, axis=0).astype(F32)
    _, normed_rows = norm_parts(x_rows)
    hidden_one = (normed_rows * gain_one).astype(BF16)
    qkv = dot(hidden_one, w_qkv)
    scale = 1.0 / math.sqrt(HD)
    q_low = rotate(qkv[:, :qw].reshape(own, heads, HD), cos_table, sin_table).astype(BF16)
    k_low = rotate(qkv[:, qw : qw + HD].reshape(own, 1, HD), cos_table, sin_table)
    kv_low = jnp.concatenate([k_low.astype(BF16)[:, 0], qkv[:, qw + HD :].astype(BF16)], axis=1)
    kv_all = jnp.concatenate([kv_low, swap(kv_low)], axis=0)
    k_all, v_all = kv_all[:, :HD], kv_all[:, HD:]
    q_heads = q_low.transpose(1, 0, 2)

    def scores():
        s = jnp.einsum("htd,sd->hts", q_heads, k_all, preferred_element_type=F32) * scale
        return jnp.where(allowed[None], s, MASK_FILL)

    s = scores()
    highest = jnp.max(s, axis=-1, keepdims=True)
    weights = jnp.exp(s - highest)
    totals = jnp.sum(weights, axis=-1, keepdims=True)
    prob = (weights / totals).astype(BF16)
    logsum = highest + jnp.log(totals)
    mixed = jnp.einsum("hts,sd->htd", prob, v_all, preferred_element_type=F32)
    attn = (mixed.transpose(1, 0, 2).reshape(own, qw) * valid_col).astype(BF16)
    inputs = tokens.astype(F32)
    resid = inputs + scatter_chips(dot(attn, w_out_c))

    inv_two, normed_two = norm_parts(resid)
    hidden_two = jnp.concatenate(
        gather_chips((normed_two * gain_two).astype(BF16)), axis=0
    )
    gate = dot(hidden_two, w_gate_c)
    up = dot(hidden_two, w_up_c)
    sig = jax.nn.sigmoid(gate)
    silu = gate * sig
    inner = (silu * up).astype(BF16)
    result = (resid + scatter_chips(dot(inner, w_down_c))).astype(BF16)
    grad_inner = dot_nt(cot_rows, w_down_c)
    grad_gate = (grad_inner * up * sig * (1.0 + gate * (1.0 - sig))).astype(BF16)
    grad_up = (grad_inner * silu).astype(BF16)

    def pair_sum(partial, size):
        p = partial.astype(BF16)
        mine = lax.dynamic_index_in_dim(p, core, 0, keepdims=False)
        other = lax.dynamic_index_in_dim(p, 1 - core, 0, keepdims=False)
        return (mine.astype(F32) + swap(other).astype(F32)).astype(BF16)

    def rows_to_owner(partial):
        width = partial.shape[1]
        p = partial.astype(BF16).reshape(chips, 2, wrows, width).transpose(1, 0, 2, 3)
        p = pair_sum(p, width)
        sent = [lax.dynamic_index_in_dim(p, chip ^ k, 0, keepdims=False) for k in range(chips)]
        return [sent[0]] + [hop(sent[k], k) for k in range(1, chips)]

    down_rows = w_down.shape[0]
    down_part = pair_sum(
        dot_tn(inner, cot_rows).reshape(2, down_rows, model), down_rows
    )
    cuts = 4
    grad_down = jnp.concatenate(
        [chain(v) for v in jnp.split(down_part, cuts, axis=0)], axis=0
    ).astype(F32)

    gate_blocks = rows_to_owner(dot_tn(hidden_two, grad_gate))
    up_blocks = rows_to_owner(dot_tn(hidden_two, grad_up))
    grad_gate_out = place([chain(b) for b in gate_blocks], chip_order, 1, F32)
    grad_up_out = place([chain(b) for b in up_blocks], chip_order, 1, F32)

    grad_hidden_two = scatter_chips(dot_nt(grad_gate, w_gate_c) + dot_nt(grad_up, w_up_c))
    gain_two_local = jnp.sum(grad_hidden_two * normed_two, axis=0)
    grad_resid = cotangent.astype(F32) + norm_back(grad_hidden_two, normed_two, inv_two, gain_two)

    da = jnp.concatenate(gather_chips(grad_resid.astype(BF16)), axis=0)
    dob = dot_nt(da, w_out_c).astype(BF16) * q_valid.astype(BF16)[:, None]
    out_part = pair_sum(dot_tn(attn, da).reshape(2, wrows, model), wrows)
    grad_out = chain(out_part).astype(F32)
    dob_heads = dob.reshape(own, heads, HD).transpose(1, 0, 2)
    probs = jnp.exp(scores() - logsum)
    dp = jnp.einsum("htd,sd->hts", dob_heads, v_all, preferred_element_type=F32)
    inner_sum = jnp.sum(probs * dp, axis=-1, keepdims=True)
    ds = (probs * (dp - inner_sum)).astype(BF16)
    dq = jnp.einsum("hts,sd->htd", ds, k_all, preferred_element_type=F32) * scale
    dk = jnp.einsum("hts,htd->sd", ds, q_heads, preferred_element_type=F32) * scale
    dv = jnp.einsum("hts,htd->sd", probs.astype(BF16), dob_heads, preferred_element_type=F32)
    dkv = jnp.concatenate([dk, dv], axis=1)
    dkv = dkv[:own] + swap(dkv[own:].astype(BF16)).astype(F32)
    dq = rotate_back(dq.transpose(1, 0, 2), cos_table, sin_table).reshape(own, qw)
    dk = rotate_back(dkv[:, None, :HD], cos_table, sin_table)[:, 0]
    dqkv = jnp.concatenate([dq, dk, dkv[:, HD:]], axis=1).astype(BF16)
    grad_hidden_one = scatter_chips(dot_nt(dqkv, w_qkv))
    inv_one, normed_one = norm_parts(inputs)
    gain_one_local = jnp.sum(grad_hidden_one * normed_one, axis=0)
    grad_inputs = (
        grad_resid + norm_back(grad_hidden_one, normed_one, inv_one, gain_one)
    ).astype(BF16)
    qkv_blocks = [chain(b) for b in rows_to_owner(dot_tn(hidden_one, dqkv))]
    grad_query = place([b[:, :qw] for b in qkv_blocks], chip_order, 1, F32)
    kv_blocks = jnp.stack([b[:, qw:].astype(F32) for b in qkv_blocks])
    kv_abs = jnp.concatenate(
        [
            lax.dynamic_index_in_dim(kv_blocks, chip ^ a, 0, keepdims=True)
            for a in range(chips)
        ],
        axis=0,
    )
    kv_abs = kv_abs.reshape(KVH, kv_share, wrows, 2, HD).sum(axis=1)
    grad_key = kv_abs[:, :, 0].transpose(1, 0, 2).reshape(wrows, KVH * HD)
    grad_value = kv_abs[:, :, 1].transpose(1, 0, 2).reshape(wrows, KVH * HD)

    norms = jnp.stack([gain_one_local, gain_two_local])
    norms = norms.reshape(2, chips, 2, wrows).transpose(2, 1, 0, 3)
    mine = lax.dynamic_index_in_dim(norms, core, 0, keepdims=False)
    other = lax.dynamic_index_in_dim(norms, 1 - core, 0, keepdims=False)
    mine = mine + swap(other)
    total = lax.dynamic_index_in_dim(mine, chip, 0, keepdims=False)
    for k in range(1, chips):
        total = total + hop(lax.dynamic_index_in_dim(mine, chip ^ k, 0, keepdims=False), k)
    total = chain(total)
    return (
        result,
        grad_inputs,
        total[0],
        grad_query,
        grad_key,
        grad_value,
        grad_out,
        total[1],
        grad_gate_out,
        grad_up_out,
        grad_down,
    )


def solution(mesh):
    placed = (
        P(("rep", "fsdp"), None),
        P(("rep", "fsdp"), None),
        P(),
        P("fsdp"),
        P("fsdp", None),
        P("fsdp", None),
        P("fsdp", None),
        P("fsdp", None),
        P("fsdp"),
        P("fsdp", None),
        P("fsdp", None),
        P("fsdp", None),
    )
    return jax.shard_map(
        local,
        mesh=mesh,
        in_specs=placed,
        out_specs=(
            P(("rep", "fsdp"), None),
            P(("rep", "fsdp"), None),
            P("fsdp"),
            P("fsdp", None),
            P("fsdp", None),
            P("fsdp", None),
            P("fsdp", None),
            P("fsdp"),
            P("fsdp", None),
            P("fsdp", None),
            P("fsdp", None),
        ),
        check_vma=False,
    )
```

time: 1680 us -> 887 us (0.53)
  waiting for transfers between devices: 1340 us -> 411 us
  starting transfers between devices: 0.85 us -> 193 us
  matrix products: 195 us -> 98.3 us
  blocking collectives: 57 us -> 0 us
  Pallas kernels: 0 us -> 46.4 us
  other arithmetic: 29.4 us -> 74.4 us
  local copies, waits for them, and re-layouts: 28.5 us -> 49.2 us
    all_gather x8 -> x0, waiting for transfers between devices: 460 us -> none  [the longest x1 113 us: local(): lax.all_gather(w_gate, 'fsdp', axis=0, tiled=True)]
    ppermute x0 -> x128, waiting for transfers between devices: none -> 411 us  [the longest x48 188 us: hop(): return lax.ppermute(v, 'fsdp', [(i, i ^ 2 * k) for i in range(group)])]
    psum x1 -> x0, waiting for transfers between devices: 319 us -> none  [local(): lax.psum(part_qkv, 'rep').astype(jnp.float32)]
    unnamed x16 -> x0, waiting for transfers between devices: 301 us -> none
    reduce_scatter x3 -> x0, waiting for transfers between devices: 265 us -> none  [the longest x1 150 us: local(): lax.psum_scatter(jnp.einsum('tc,tk->ck', inner_low, cotangent, preferred_...]
    ppermute x0 -> x128, starting transfers between devices: none -> 193 us  [the longest x18 92.9 us: chain(): got = lax.ppermute(acc, 'rep', [(s, s + 1), (reps - 1 - s, reps - 2 - s)])]
    dot_general x46 -> x21, matrix products: 195 us -> 98.3 us  [the longest x5 26.8 us: dot(): return jnp.dot(a, b, preferred_element_type=F32)]
    pallas_call x0 -> x9, Pallas kernels: none -> 46.4 us  [the longest x6 34.8 us: place(): pl.pallas_call(body, grid_spec=pltpu.PrefetchScalarGridSpec(num_scalar_pr...]
  transfers between devices with their start and end apart: 14 -> 128, of which waited for: 14 -> 45; matrix products, arithmetic and copies ran while one was open for 8% -> 22% of each run, Pallas kernels for 0% -> 5%
where the time goes in v1:
time: 887 us; the launch traced here: 876 us
  waiting for transfers between devices  411 us (46%)
  starting transfers between devices  193 us (22%)
  matrix products  98.3 us (11%)
  other arithmetic  74.4 us (8%)
  local copies, waits for them, and re-layouts  49.2 us (6%)
  Pallas kernels  46.4 us (5%)
    ppermute x48, waiting for transfers between devices, hop(): return lax.ppermute(v, 'fsdp', [(i, i ^ 2 * k) for i in range(group)])  188 us
    ppermute x18, waiting for transfers between devices, chain(): got = lax.ppermute(tot, 'rep', [(s + 1, s), (reps - 2 - s, reps - 1 - s)])  158 us
    ppermute x18, starting transfers between devices, chain(): got = lax.ppermute(acc, 'rep', [(s, s + 1), (reps - 1 - s, reps - 2 - s)])  92.9 us
    ppermute x18, waiting for transfers between devices, chain(): got = lax.ppermute(acc, 'rep', [(s, s + 1), (reps - 1 - s, reps - 2 - s)])  64.1 us
    ppermute x48, starting transfers between devices, hop(): return lax.ppermute(v, 'fsdp', [(i, i ^ 2 * k) for i in range(group)])  59.7 us
    pallas_call x6, Pallas kernels, place(): pl.pallas_call(body, grid_spec=pltpu.PrefetchScalarGridSpec(num_scalar_pr...  34.8 us
    dot_general x5, matrix products, dot(): return jnp.dot(a, b, preferred_element_type=F32)  26.8 us
    ppermute x18, starting transfers between devices, chain(): got = lax.ppermute(tot, 'rep', [(s + 1, s), (reps - 2 - s, reps - 1 - s)])  23.6 us
  transfers between devices with their start and end apart: 128, of which 45 were waited for; matrix products, arithmetic and copies ran while one was open for 22% of the time, Pallas kernels for 5%

profile of v1, /device:TPU:0, one launch (start us, length us, event | category | flops | bytes accessed | tf_op | source)
XLA Modules:
  0.0 876.4 jit_solution(4297769791766369334)
XLA Ops:
  17.8 4.1 pick_columns.5
  25.3 4.1 pick_columns.4
  42.9 16.3 %collective-permute-done.10.refs_1_ = bf16[256,640]{1,0:T(8,128)(2,1)S(1)} collective-permute-done((bf16[256,640]{1,0:T(8,128)(2,1)}, bf16[256,640]{1,0:T(8,128)(2,1)S(1)}, u32[]{:S(2)}, u32[]{:S(2)}) %collective-permute-start.10) | collective-permute-done | bytes 327712 | tf_op jit(solution)/shard_map/ppermute | solution.py:154
  60.9 8.8 %collective-permute-done.12.refs_3_ = bf16[256,640]{1,0:T(8,128)(2,1)S(1)} collective-permute-done((bf16[256,640]{1,0:T(8,128)(2,1)}, bf16[256,640]{1,0:T(8,128)(2,1)S(1)}, u32[]{:S(2)}, u32[]{:S(2)}) %collective-permute-start.12) | collective-permute-done | bytes 327712 | tf_op jit(solution)/shard_map/ppermute | solution.py:154
  75.2 5.6 place.6
  95.0 3.9 fusion
  105.9 4.6 collective-permute-done.32.refs_1_
  111.0 21.7 %collective-permute-done.33.refs_2_ = bf16[256,1408]{1,0:T(8,128)(2,1)S(1)} collective-permute-done((bf16[256,1408]{1,0:T(8,128)(2,1)S(1)}, bf16[256,1408]{1,0:T(8,128)(2,1)S(1)}, u32[]{:S(2)}, u32[]{:S(2)}) %collective-permute-start.33) | collective-permute-done | bytes 720928 | tf_op jit(solution)/shard_map/ppermute | solution.py:154
  143.0 33.8 %collective-permute-done.26.refs_2_ = bf16[256,1408]{1,0:T(8,128)(2,1)S(1)} collective-permute-done((bf16[256,1408]{1,0:T(8,128)(2,1)S(1)}, bf16[256,1408]{1,0:T(8,128)(2,1)S(1)}, u32[]{:S(2)}, u32[]{:S(2)}) %collective-permute-start.26) | collective-permute-done | bytes 720928 | tf_op jit(solution)/shard_map/ppermute | solution.py:154
  201.0 7.3 place.8
  208.3 7.4 place.7
  215.8 5.5 collective-permute-done.23
  221.3 7.6 fusion.65
  228.9 8.5 fusion.35
  237.4 7.1 multiply_convert_fusion.2
  255.5 5.6 convolution_convert_fusion.7
  264.3 5.4 convolution_convert_fusion.2
  273.2 5.9 collective-permute-done.47
  279.6 10.7 %collective-permute-done.42 = bf16[128,2048]{1,0:T(8,128)(2,1)S(1)} collective-permute-done((bf16[128,2048]{1,0:T(8,128)(2,1)S(1)}, bf16[128,2048]{1,0:T(8,128)(2,1)S(1)}, u32[]{:S(2)}, u32[]{:S(2)}) %collective-permute-start.42) | collective-permute-done | bytes 524320 | tf_op jit(solution)/shard_map/ppermute | solution.py:154
  290.3 10.2 %collective-permute-done.41 = bf16[128,2048]{1,0:T(8,128)(2,1)S(1)} collective-permute-done((bf16[128,2048]{1,0:T(8,128)(2,1)S(1)}, bf16[128,2048]{1,0:T(8,128)(2,1)S(1)}, u32[]{:S(2)}, u32[]{:S(2)}) %collective-permute-start.41) | collective-permute-done | bytes 524320 | tf_op jit(solution)/shard_map/ppermute | solution.py:154
  307.1 5.3 convolution_convert_fusion.1
  315.8 3.8 collective-permute-done.51
  319.5 10.3 %collective-permute-done.50 = bf16[128,2048]{1,0:T(8,128)(2,1)S(1)} collective-permute-done((bf16[128,2048]{1,0:T(8,128)(2,1)}, bf16[128,2048]{1,0:T(8,128)(2,1)S(1)}, u32[]{:S(2)}, u32[]{:S(2)}) %collective-permute-start.50) | collective-permute-done | bytes 524320 | tf_op jit(solution)/shard_map/ppermute | solution.py:154
  330.6 4.9 fusion.19
  335.5 12.9 %multiply_reduce_fusion = (f32[8,512]{1,0:T(8,128)S(1)}, f32[8,512,1024]{2,1,0:T(8,128)}) fusion(f32[8,512,1024]{2,1,0:T(8,128)} %copy-done.2, f32[8,512]{1,0:T(8,128)S(1)} %copy-done.75, bf16[8,512,64]{1,2,0:T(8,128)(2,1)} %bitcast.264, bf16[1024,128]{0,1:T(8,128)(2,1)S(1)} %copy-done.24), kind=kOutput, calls=%fused_computation.1 | convolution fusion | flops 549449728 | bytes 34242560 | tf_op jit(solution)/shard_map/htd,sd->hts/dot_general | solution.py:328
  348.5 3.9 fusion.21
  352.3 7.9 multiply_convert_fusion
  376.4 8.5 collective-permute-done.55
  384.9 10.8 %collective-permute-done.54 = bf16[128,2048]{1,0:T(8,128)(2,1)S(1)} collective-permute-done((bf16[128,2048]{1,0:T(8,128)(2,1)S(1)}, bf16[128,2048]{1,0:T(8,128)(2,1)S(1)}, u32[]{:S(2)}, u32[]{:S(2)}) %collective-permute-start.54) | collective-permute-done | bytes 524320 | tf_op jit(solution)/shard_map/ppermute | solution.py:154
  406.0 3.9 collective-permute-start.60
  409.9 4.8 convolution_convert_fusion
  427.0 4.9 collective-permute-done.64
  443.0 7.2 collective-permute-start.68
  454.4 4.6 collective-permute-start.72
  461.4 4.4 collective-permute-start.76
  468.4 4.4 collective-permute-start.84
  479.9 4.6 collective-permute-done.66
  487.6 18.6 %collective-permute-start.100 = (bf16[256,1408]{1,0:T(8,128)(2,1)S(1)}, bf16[256,1408]{1,0:T(8,128)(2,1)S(1)}, u32[]{:S(2)}, u32[]{:S(2)}) collective-permute-start(bf16[256,1408]{1,0:T(8,128)(2,1)S(1)} %get-tuple-element.72), channel_id=1, source_target_pairs={{0,8},{24,16},{1,9},{25,17},{2,10},{26,18},{3,11},{27,19},{4,12},{... | collective-permute-start | bytes 2162696 | tf_op jit(solution)/shard_map/ppermute | solution.py:181
  508.7 11.3 %collective-permute-done.91 = bf16[256,1408]{1,0:T(8,128)(2,1)S(1)} collective-permute-done((bf16[256,1408]{1,0:T(8,128)(2,1)S(1)}, bf16[256,1408]{1,0:T(8,128)(2,1)S(1)}, u32[]{:S(2)}, u32[]{:S(2)}) %collective-permute-start.91) | collective-permute-done | bytes 720928 | tf_op jit(solution)/shard_map/ppermute | solution.py:154
  521.7 3.9 collective-permute-start.116
  530.8 16.1 %collective-permute-done.107 = bf16[256,1408]{1,0:T(8,128)(2,1)} collective-permute-done((bf16[256,1408]{1,0:T(8,128)(2,1)S(1)}, bf16[256,1408]{1,0:T(8,128)(2,1)}, u32[]{:S(2)}, u32[]{:S(2)}) %collective-permute-start.107) | collective-permute-done | bytes 720928 | tf_op jit(solution)/shard_map/ppermute | solution.py:154
  546.9 4.6 collective-permute-start.125
  558.3 14.7 %collective-permute-done.122 = bf16[176,2048]{1,0:T(8,128)(2,1)S(1)} collective-permute-done((bf16[176,2048]{1,0:T(8,128)(2,1)S(1)}, bf16[176,2048]{1,0:T(8,128)(2,1)S(1)}, u32[]{:S(2)}, u32[]{:S(2)}) %collective-permute-start.122) | collective-permute-done | bytes 720928 | tf_op jit(solution)/shard_map/ppermute | solution.py:181
  574.3 7.0 collective-permute-done.125
  582.1 7.7 collective-permute-start.88
  595.4 10.9 %collective-permute-done.88 = bf16[256,1408]{1,0:T(8,128)(2,1)S(1)} collective-permute-done((bf16[256,1408]{1,0:T(8,128)(2,1)S(1)}, bf16[256,1408]{1,0:T(8,128)(2,1)S(1)}, u32[]{:S(2)}, u32[]{:S(2)}) %collective-permute-start.88) | collective-permute-done | bytes 720928 | tf_op jit(solution)/shard_map/ppermute | solution.py:181
  607.0 13.7 %collective-permute-done.92 = bf16[256,1408]{1,0:T(8,128)(2,1)S(1)} collective-permute-done((bf16[256,1408]{1,0:T(8,128)(2,1)S(1)}, bf16[256,1408]{1,0:T(8,128)(2,1)S(1)}, u32[]{:S(2)}, u32[]{:S(2)}) %collective-permute-start.92) | collective-permute-done | bytes 720928 | tf_op jit(solution)/shard_map/ppermute | solution.py:181
  621.5 7.1 collective-permute-done.96
  630.4 7.2 collective-permute-start.104
  639.8 14.1 %collective-permute-start.112 = (bf16[256,1408]{1,0:T(8,128)(2,1)}, bf16[256,1408]{1,0:T(8,128)(2,1)}, u32[]{:S(2)}, u32[]{:S(2)}) collective-permute-start(bf16[256,1408]{1,0:T(8,128)(2,1)} %collective-permute-done.111), channel_id=1, source_target_pairs={{0,8},{24,16},{1,9},{25,17},{2,10},{26,18},{3,11},{27,19},{4,12},{... | collective-permute-start | bytes 2162696 | tf_op jit(solution)/shard_map/ppermute | solution.py:181
  664.0 3.9 place.9
  685.7 12.1 %collective-permute-done.102 = bf16[256,1408]{1,0:T(8,128)(2,1)} collective-permute-done((bf16[256,1408]{1,0:T(8,128)(2,1)S(1)}, bf16[256,1408]{1,0:T(8,128)(2,1)}, u32[]{:S(2)}, u32[]{:S(2)}) %collective-permute-start.102) | collective-permute-done | bytes 720928 | tf_op jit(solution)/shard_map/ppermute | solution.py:186
  701.1 34.4 %collective-permute-done.127 = bf16[176,2048]{1,0:T(8,128)(2,1)S(1)} collective-permute-done((bf16[176,2048]{1,0:T(8,128)(2,1)S(1)}, bf16[176,2048]{1,0:T(8,128)(2,1)S(1)}, u32[]{:S(2)}, u32[]{:S(2)}) %collective-permute-start.127) | collective-permute-done | bytes 720928 | tf_op jit(solution)/shard_map/ppermute | solution.py:186
  736.9 14.1 %collective-permute-done.124 = bf16[176,2048]{1,0:T(8,128)(2,1)S(1)} collective-permute-done((bf16[176,2048]{1,0:T(8,128)(2,1)S(1)}, bf16[176,2048]{1,0:T(8,128)(2,1)S(1)}, u32[]{:S(2)}, u32[]{:S(2)}) %collective-permute-start.124) | collective-permute-done | bytes 720928 | tf_op jit(solution)/shard_map/ppermute | solution.py:186
  752.3 14.1 %collective-permute-done.121 = bf16[176,2048]{1,0:T(8,128)(2,1)S(1)} collective-permute-done((bf16[176,2048]{1,0:T(8,128)(2,1)S(1)}, bf16[176,2048]{1,0:T(8,128)(2,1)S(1)}, u32[]{:S(2)}, u32[]{:S(2)}) %collective-permute-start.121) | collective-permute-done | bytes 720928 | tf_op jit(solution)/shard_map/ppermute | solution.py:186
  768.9 8.0 collective-permute-done.118
  789.4 14.0 %collective-permute-done.90 = bf16[256,1408]{1,0:T(8,128)(2,1)S(1)} collective-permute-done((bf16[256,1408]{1,0:T(8,128)(2,1)S(1)}, bf16[256,1408]{1,0:T(8,128)(2,1)S(1)}, u32[]{:S(2)}, u32[]{:S(2)}) %collective-permute-start.90) | collective-permute-done | bytes 720928 | tf_op jit(solution)/shard_map/ppermute | solution.py:186
  805.7 13.2 %collective-permute-done.94 = bf16[256,1408]{1,0:T(8,128)(2,1)S(1)} collective-permute-done((bf16[256,1408]{1,0:T(8,128)(2,1)S(1)}, bf16[256,1408]{1,0:T(8,128)(2,1)S(1)}, u32[]{:S(2)}, u32[]{:S(2)}) %collective-permute-start.94) | collective-permute-done | bytes 720928 | tf_op jit(solution)/shard_map/ppermute | solution.py:186
  819.9 14.5 %collective-permute-done.98 = bf16[256,1408]{1,0:T(8,128)(2,1)S(1)} collective-permute-done((bf16[256,1408]{1,0:T(8,128)(2,1)S(1)}, bf16[256,1408]{1,0:T(8,128)(2,1)S(1)}, u32[]{:S(2)}, u32[]{:S(2)}) %collective-permute-start.98) | collective-permute-done | bytes 720928 | tf_op jit(solution)/shard_map/ppermute | solution.py:186
  835.4 14.5 %collective-permute-done.106 = bf16[256,1408]{1,0:T(8,128)(2,1)S(1)} collective-permute-done((bf16[256,1408]{1,0:T(8,128)(2,1)S(1)}, bf16[256,1408]{1,0:T(8,128)(2,1)S(1)}, u32[]{:S(2)}, u32[]{:S(2)}) %collective-permute-start.106) | collective-permute-done | bytes 720928 | tf_op jit(solution)/shard_map/ppermute | solution.py:186
  850.8 5.3 place.10
  856.1 6.1 collective-permute-done.110
  863.2 6.7 collective-permute-done.114
  870.9 5.3 place.11
  (621 shorter events, 278.5 us)
Async XLA Ops:
  2.0 35.2 %collective-permute-start.3 = (bf16[2,256]{1,0:T(2,128)(2,1)S(1)}, bf16[2,256]{1,0:T(2,128)(2,1)S(1)}, u32[]{:S(2)}, u32[]{:S(2)}) collective-permute-start(bf16[2,256]{1,0:T(2,128)(2,1)S(1)} %get-tuple-element.57), channel_id=1, source_target_pairs={{0,1},{1,0},{2,3},{3,2},{4,5},{5,4},{6,7},{7,6},{8,9},{9,8},{10,11... | collective-permute-start | bytes 3080 | tf_op jit(solution)/shard_map/ppermute | solution.py:157
  2.6 35.2 %collective-permute-start.4 = (bf16[2,256]{1,0:T(2,128)(2,1)S(1)}, bf16[2,256]{1,0:T(2,128)(2,1)S(1)}, u32[]{:S(2)}, u32[]{:S(2)}) collective-permute-start(bf16[2,256]{1,0:T(2,128)(2,1)S(1)} %get-tuple-element.57), channel_id=1, source_target_pairs={{0,2},{1,3},{2,0},{3,1},{4,6},{5,7},{6,4},{7,5},{8,10},{9,11},{10,... | collective-permute-start | bytes 3080 | tf_op jit(solution)/shard_map/ppermute | solution.py:154
  5.1 32.7 %collective-permute-start.6 = (bf16[2,256]{1,0:T(2,128)(2,1)S(1)}, bf16[2,256]{1,0:T(2,128)(2,1)S(1)}, u32[]{:S(2)}, u32[]{:S(2)}) collective-permute-start(bf16[2,256]{1,0:T(2,128)(2,1)S(1)} %get-tuple-element.57), channel_id=1, source_target_pairs={{0,4},{1,5},{2,6},{3,7},{4,0},{5,1},{6,2},{7,3},{8,12},{9,13},{10,... | collective-permute-start | bytes 3080 | tf_op jit(solution)/shard_map/ppermute | solution.py:154
  6.6 32.5 %collective-permute-start.8 = (bf16[2,256]{1,0:T(2,128)(2,1)S(1)}, bf16[2,256]{1,0:T(2,128)(2,1)S(1)}, u32[]{:S(2)}, u32[]{:S(2)}) collective-permute-start(bf16[2,256]{1,0:T(2,128)(2,1)S(1)} %get-tuple-element.57), channel_id=1, source_target_pairs={{0,6},{1,7},{2,4},{3,5},{4,2},{5,3},{6,0},{7,1},{8,14},{9,15},{10,... | collective-permute-start | bytes 3080 | tf_op jit(solution)/shard_map/ppermute | solution.py:154
  6.7 63.4 %collective-permute-start.2 = (bf16[128,2048]{1,0:T(8,128)(2,1)}, bf16[128,2048]{1,0:T(8,128)(2,1)S(1)}, u32[]{:S(2)}, u32[]{:S(2)}) collective-permute-start(bf16[128,2048]{1,0:T(8,128)(2,1)} %param.12), channel_id=1, source_target_pairs={{0,6},{1,7},{2,4},{3,5},{4,2},{5,3},{6,0},{7,1},{8,14},{9,15},{10,... | collective-permute-start | bytes 1572872 | tf_op jit(solution)/shard_map/ppermute | solution.py:154
  37.2 32.8 %collective-permute-start.1 = (bf16[128,2048]{1,0:T(8,128)(2,1)S(1)}, bf16[128,2048]{1,0:T(8,128)(2,1)S(1)}, u32[]{:S(2)}, u32[]{:S(2)}) collective-permute-start(bf16[128,2048]{1,0:T(8,128)(2,1)S(1)} %copy-done.3), channel_id=1, source_target_pairs={{0,4},{1,5},{2,6},{3,7},{4,0},{5,1},{6,2},{7,3},{8,12},{9,13},{10,... | collective-permute-start | bytes 1572872 | tf_op jit(solution)/shard_map/ppermute | solution.py:154
  37.8 32.7 %collective-permute-start = (bf16[128,2048]{1,0:T(8,128)(2,1)S(1)}, bf16[128,2048]{1,0:T(8,128)(2,1)S(1)}, u32[]{:S(2)}, u32[]{:S(2)}) collective-permute-start(bf16[128,2048]{1,0:T(8,128)(2,1)S(1)} %copy-done.3), channel_id=1, source_target_pairs={{0,2},{1,3},{2,0},{3,1},{4,6},{5,7},{6,4},{7,5},{8,10},{9,11},{10,... | collective-permute-start | bytes 1572872 | tf_op jit(solution)/shard_map/ppermute | solution.py:154
  69.7 29.3 %collective-permute-start.43 = (bf16[128,2048]{1,0:T(8,128)(2,1)}, bf16[128,2048]{1,0:T(8,128)(2,1)}, u32[]{:S(2)}, u32[]{:S(2)}) collective-permute-start(bf16[128,2048]{1,0:T(8,128)(2,1)} %param.13), channel_id=1, source_target_pairs={{0,2},{1,3},{2,0},{3,1},{4,6},{5,7},{6,4},{7,5},{8,10},{9,11},{10,... | collective-permute-start | bytes 1572872 | tf_op jit(solution)/shard_map/ppermute | solution.py:154
  71.2 29.5 %collective-permute-start.44 = (bf16[128,2048]{1,0:T(8,128)(2,1)}, bf16[128,2048]{1,0:T(8,128)(2,1)}, u32[]{:S(2)}, u32[]{:S(2)}) collective-permute-start(bf16[128,2048]{1,0:T(8,128)(2,1)} %param.13), channel_id=1, source_target_pairs={{0,4},{1,5},{2,6},{3,7},{4,0},{5,1},{6,2},{7,3},{8,12},{9,13},{10,... | collective-permute-start | bytes 1572872 | tf_op jit(solution)/shard_map/ppermute | solution.py:154
  72.9 29.1 %collective-permute-start.45 = (bf16[128,2048]{1,0:T(8,128)(2,1)}, bf16[128,2048]{1,0:T(8,128)(2,1)}, u32[]{:S(2)}, u32[]{:S(2)}) collective-permute-start(bf16[128,2048]{1,0:T(8,128)(2,1)} %param.13), channel_id=1, source_target_pairs={{0,6},{1,7},{2,4},{3,5},{4,2},{5,3},{6,0},{7,1},{8,14},{9,15},{10,... | collective-permute-start | bytes 1572872 | tf_op jit(solution)/shard_map/ppermute | solution.py:154
  74.4 59.9 %collective-permute-start.18 = (bf16[256,2048]{1,0:T(8,128)(2,1)}, bf16[256,2048]{1,0:T(8,128)(2,1)}, u32[]{:S(2)}, u32[]{:S(2)}) collective-permute-start(bf16[256,2048]{1,0:T(8,128)(2,1)} %param.19), channel_id=1, source_target_pairs={{0,1},{1,0},{2,3},{3,2},{4,5},{5,4},{6,7},{7,6},{8,9},{9,8},{10,11... | collective-permute-start | bytes 3145736 | tf_op jit(solution)/shard_map/ppermute | solution.py:157
  99.0 33.8 %collective-permute-start.33 = (bf16[256,1408]{1,0:T(8,128)(2,1)S(1)}, bf16[256,1408]{1,0:T(8,128)(2,1)S(1)}, u32[]{:S(2)}, u32[]{:S(2)}) collective-permute-start(bf16[256,1408]{1,0:T(8,128)(2,1)S(1)} %copy-done.52), channel_id=1, source_target_pairs={{0,4},{1,5},{2,6},{3,7},{4,0},{5,1},{6,2},{7,3},{8,12},{9,13},{10,... | collective-permute-start | bytes 2162696 | tf_op jit(solution)/shard_map/ppermute | solution.py:154
  100.7 38.0 %collective-permute-start.34 = (bf16[256,1408]{1,0:T(8,128)(2,1)S(1)}, bf16[256,1408]{1,0:T(8,128)(2,1)S(1)}, u32[]{:S(2)}, u32[]{:S(2)}) collective-permute-start(bf16[256,1408]{1,0:T(8,128)(2,1)S(1)} %copy-done.51), channel_id=1, source_target_pairs={{0,6},{1,7},{2,4},{3,5},{4,2},{5,3},{6,0},{7,1},{8,14},{9,15},{10,... | collective-permute-start | bytes 2162696 | tf_op jit(solution)/shard_map/ppermute | solution.py:154
  102.1 36.7 %collective-permute-start.35 = (bf16[256,1408]{1,0:T(8,128)(2,1)S(1)}, bf16[256,1408]{1,0:T(8,128)(2,1)S(1)}, u32[]{:S(2)}, u32[]{:S(2)}) collective-permute-start(bf16[256,1408]{1,0:T(8,128)(2,1)S(1)} %copy-done.16), channel_id=1, source_target_pairs={{0,1},{1,0},{2,3},{3,2},{4,5},{5,4},{6,7},{7,6},{8,9},{9,8},{10,11... | collective-permute-start | bytes 2162696 | tf_op jit(solution)/shard_map/ppermute | solution.py:157
  110.5 30.9 %collective-permute-start.25 = (bf16[256,1408]{1,0:T(8,128)(2,1)S(1)}, bf16[256,1408]{1,0:T(8,128)(2,1)S(1)}, u32[]{:S(2)}, u32[]{:S(2)}) collective-permute-start(bf16[256,1408]{1,0:T(8,128)(2,1)S(1)} %copy-done.50), channel_id=1, source_target_pairs={{0,2},{1,3},{2,0},{3,1},{4,6},{5,7},{6,4},{7,5},{8,10},{9,11},{10,... | collective-permute-start | bytes 2162696 | tf_op jit(solution)/shard_map/ppermute | solution.py:154
  132.7 44.1 %collective-permute-start.26 = (bf16[256,1408]{1,0:T(8,128)(2,1)S(1)}, bf16[256,1408]{1,0:T(8,128)(2,1)S(1)}, u32[]{:S(2)}, u32[]{:S(2)}) collective-permute-start(bf16[256,1408]{1,0:T(8,128)(2,1)S(1)} %copy-done.49), channel_id=1, source_target_pairs={{0,4},{1,5},{2,6},{3,7},{4,0},{5,1},{6,2},{7,3},{8,12},{9,13},{10,... | collective-permute-start | bytes 2162696 | tf_op jit(solution)/shard_map/ppermute | solution.py:154
  134.4 44.1 %collective-permute-start.27 = (bf16[256,1408]{1,0:T(8,128)(2,1)S(1)}, bf16[256,1408]{1,0:T(8,128)(2,1)}, u32[]{:S(2)}, u32[]{:S(2)}) collective-permute-start(bf16[256,1408]{1,0:T(8,128)(2,1)S(1)} %copy-done.48), channel_id=1, source_target_pairs={{0,6},{1,7},{2,4},{3,5},{4,2},{5,3},{6,0},{7,1},{8,14},{9,15},{10,... | collective-permute-start | bytes 2162696 | tf_op jit(solution)/shard_map/ppermute | solution.py:154
  138.7 43.2 %collective-permute-start.28 = (bf16[256,1408]{1,0:T(8,128)(2,1)S(1)}, bf16[256,1408]{1,0:T(8,128)(2,1)}, u32[]{:S(2)}, u32[]{:S(2)}) collective-permute-start(bf16[256,1408]{1,0:T(8,128)(2,1)S(1)} %get-tuple-element.80.refs_0_), channel_id=1, source_target_pairs={{0,1},{1,0},{2,3},{3,2},{4,5},{5,4},{6,7},{7,6},{8,9},{9,8},{10,11... | collective-permute-start | bytes 2162696 | tf_op jit(solution)/shard_map/ppermute | solution.py:157
  138.8 45.0 %collective-permute-start.36 = (bf16[256,1408]{1,0:T(8,128)(2,1)S(1)}, bf16[256,1408]{1,0:T(8,128)(2,1)}, u32[]{:S(2)}, u32[]{:S(2)}) collective-permute-start(bf16[256,1408]{1,0:T(8,128)(2,1)S(1)} %collective-permute-done.32.refs_1_), channel_id=1, source_target_pairs={{0,1},{1,0},{2,3},{3,2},{4,5},{5,4},{6,7},{7,6},{8,9},{9,8},{10,11... | collective-permute-start | bytes 2162696 | tf_op jit(solution)/shard_map/ppermute | solution.py:157
  141.5 44.7 %collective-permute-start.21 = (bf16[128,2048]{1,0:T(8,128)(2,1)}, bf16[128,2048]{1,0:T(8,128)(2,1)}, u32[]{:S(2)}, u32[]{:S(2)}) collective-permute-start(bf16[128,2048]{1,0:T(8,128)(2,1)} %get-tuple-element.95), channel_id=1, source_target_pairs={{0,6},{1,7},{2,4},{3,5},{4,2},{5,3},{6,0},{7,1},{8,14},{9,15},{10,... | collective-permute-start | bytes 1572872 | tf_op jit(solution)/shard_map/ppermute | solution.py:154
  181.9 46.9 %collective-permute-start.39 = (bf16[704,2048]{1,0:T(8,128)(2,1)}, bf16[704,2048]{1,0:T(8,128)(2,1)}, u32[]{:S(2)}, u32[]{:S(2)}) collective-permute-start(bf16[704,2048]{1,0:T(8,128)(2,1)} %param.23), channel_id=1, source_target_pairs={{0,1},{1,0},{2,3},{3,2},{4,5},{5,4},{6,7},{7,6},{8,9},{9,8},{10,11... | collective-permute-start | bytes 8650760 | tf_op jit(solution)/shard_map/ppermute | solution.py:157
  261.3 28.9 %collective-permute-start.42 = (bf16[128,2048]{1,0:T(8,128)(2,1)S(1)}, bf16[128,2048]{1,0:T(8,128)(2,1)S(1)}, u32[]{:S(2)}, u32[]{:S(2)}) collective-permute-start(bf16[128,2048]{1,0:T(8,128)(2,1)S(1)} %get-tuple-element.92), channel_id=1, source_target_pairs={{0,6},{1,7},{2,4},{3,5},{4,2},{5,3},{6,0},{7,1},{8,14},{9,15},{10,... | collective-permute-start | bytes 1572872 | tf_op jit(solution)/shard_map/ppermute | solution.py:154
  263.0 37.5 %collective-permute-start.41 = (bf16[128,2048]{1,0:T(8,128)(2,1)S(1)}, bf16[128,2048]{1,0:T(8,128)(2,1)S(1)}, u32[]{:S(2)}, u32[]{:S(2)}) collective-permute-start(bf16[128,2048]{1,0:T(8,128)(2,1)S(1)} %get-tuple-element.93), channel_id=1, source_target_pairs={{0,4},{1,5},{2,6},{3,7},{4,0},{5,1},{6,2},{7,3},{8,12},{9,13},{10,... | collective-permute-start | bytes 1572872 | tf_op jit(solution)/shard_map/ppermute | solution.py:154
  269.8 30.7 %collective-permute-start.40 = (bf16[128,2048]{1,0:T(8,128)(2,1)S(1)}, bf16[128,2048]{1,0:T(8,128)(2,1)S(1)}, u32[]{:S(2)}, u32[]{:S(2)}) collective-permute-start(bf16[128,2048]{1,0:T(8,128)(2,1)S(1)} %get-tuple-element.91), channel_id=1, source_target_pairs={{0,2},{1,3},{2,0},{3,1},{4,6},{5,7},{6,4},{7,5},{8,10},{9,11},{10,... | collective-permute-start | bytes 1572872 | tf_op jit(solution)/shard_map/ppermute | solution.py:154
  279.1 154.2 %collective-permute-start.83 = (bf16[4,256,1408]{2,1,0:T(8,128)(2,1)}, bf16[4,256,1408]{2,1,0:T(8,128)(2,1)}, u32[]{:S(2)}, u32[]{:S(2)}) collective-permute-start(bf16[4,256,1408]{2,1,0:T(8,128)(2,1)} %dynamic-slice_bitcast_fusion.2), channel_id=1, source_target_pairs={{0,1},{1,0},{2,3},{3,2},{4,5},{5,4},{6,7},{7,6},{8,9},{9,8},{10,11... | collective-permute-start | bytes 8650760 | tf_op jit(solution)/shard_map/ppermute | solution.py:157
  315.7 127.2 %collective-permute-start.99 = (bf16[4,256,1408]{2,1,0:T(8,128)(2,1)}, bf16[4,256,1408]{2,1,0:T(8,128)(2,1)}, u32[]{:S(2)}, u32[]{:S(2)}) collective-permute-start(bf16[4,256,1408]{2,1,0:T(8,128)(2,1)} %dynamic-slice_bitcast_fusion.1), channel_id=1, source_target_pairs={{0,1},{1,0},{2,3},{3,2},{4,5},{5,4},{6,7},{7,6},{8,9},{9,8},{10,11... | collective-permute-start | bytes 8650760 | tf_op jit(solution)/shard_map/ppermute | solution.py:157
  418.1 56.2 %collective-permute-start.115 = (bf16[704,2048]{1,0:T(8,128)(2,1)}, bf16[704,2048]{1,0:T(8,128)(2,1)}, u32[]{:S(2)}, u32[]{:S(2)}) collective-permute-start(bf16[704,2048]{1,0:T(8,128)(2,1)} %dynamic-slice_bitcast_fusion), channel_id=1, source_target_pairs={{0,1},{1,0},{2,3},{3,2},{4,5},{5,4},{6,7},{7,6},{8,9},{9,8},{10,11... | collective-permute-start | bytes 8650760 | tf_op jit(solution)/shard_map/ppermute | solution.py:157
  425.6 50.0 %collective-permute-start.80 = (bf16[256,2048]{1,0:T(8,128)(2,1)S(1)}, bf16[256,2048]{1,0:T(8,128)(2,1)S(1)}, u32[]{:S(2)}, u32[]{:S(2)}) collective-permute-start(bf16[256,2048]{1,0:T(8,128)(2,1)S(1)} %fusion.14), channel_id=1, source_target_pairs={{0,8},{24,16},{1,9},{25,17},{2,10},{26,18},{3,11},{27,19},{4,12},{... | collective-permute-start | bytes 3145736 | tf_op jit(solution)/shard_map/ppermute | solution.py:181
  468.4 37.9 %collective-permute-start.84 = (bf16[256,1408]{1,0:T(8,128)(2,1)S(1)}, bf16[256,1408]{1,0:T(8,128)(2,1)S(1)}, u32[]{:S(2)}, u32[]{:S(2)}) collective-permute-start(bf16[256,1408]{1,0:T(8,128)(2,1)S(1)} %get-tuple-element.76), channel_id=1, source_target_pairs={{0,8},{24,16},{1,9},{25,17},{2,10},{26,18},{3,11},{27,19},{4,12},{... | collective-permute-start | bytes 2162696 | tf_op jit(solution)/shard_map/ppermute | solution.py:181
  472.9 34.0 %collective-permute-start.87 = (bf16[256,1408]{1,0:T(8,128)(2,1)S(1)}, bf16[256,1408]{1,0:T(8,128)(2,1)S(1)}, u32[]{:S(2)}, u32[]{:S(2)}) collective-permute-start(bf16[256,1408]{1,0:T(8,128)(2,1)S(1)} %get-tuple-element.75), channel_id=1, source_target_pairs={{0,2},{1,3},{2,0},{3,1},{4,6},{5,7},{6,4},{7,5},{8,10},{9,11},{10,... | collective-permute-start | bytes 2162696 | tf_op jit(solution)/shard_map/ppermute | solution.py:154
  484.5 35.5 %collective-permute-start.91 = (bf16[256,1408]{1,0:T(8,128)(2,1)S(1)}, bf16[256,1408]{1,0:T(8,128)(2,1)S(1)}, u32[]{:S(2)}, u32[]{:S(2)}) collective-permute-start(bf16[256,1408]{1,0:T(8,128)(2,1)S(1)} %get-tuple-element.74), channel_id=1, source_target_pairs={{0,4},{1,5},{2,6},{3,7},{4,0},{5,1},{6,2},{7,3},{8,12},{9,13},{10,... | collective-permute-start | bytes 2162696 | tf_op jit(solution)/shard_map/ppermute | solution.py:154
  485.3 36.5 %collective-permute-start.95 = (bf16[256,1408]{1,0:T(8,128)(2,1)S(1)}, bf16[256,1408]{1,0:T(8,128)(2,1)S(1)}, u32[]{:S(2)}, u32[]{:S(2)}) collective-permute-start(bf16[256,1408]{1,0:T(8,128)(2,1)S(1)} %get-tuple-element.73), channel_id=1, source_target_pairs={{0,6},{1,7},{2,4},{3,5},{4,2},{5,3},{6,0},{7,1},{8,14},{9,15},{10,... | collective-permute-start | bytes 2162696 | tf_op jit(solution)/shard_map/ppermute | solution.py:154
  487.6 40.5 %collective-permute-start.100 = (bf16[256,1408]{1,0:T(8,128)(2,1)S(1)}, bf16[256,1408]{1,0:T(8,128)(2,1)S(1)}, u32[]{:S(2)}, u32[]{:S(2)}) collective-permute-start(bf16[256,1408]{1,0:T(8,128)(2,1)S(1)} %get-tuple-element.72), channel_id=1, source_target_pairs={{0,8},{24,16},{1,9},{25,17},{2,10},{26,18},{3,11},{27,19},{4,12},{... | collective-permute-start | bytes 2162696 | tf_op jit(solution)/shard_map/ppermute | solution.py:181
  506.9 39.9 %collective-permute-start.107 = (bf16[256,1408]{1,0:T(8,128)(2,1)S(1)}, bf16[256,1408]{1,0:T(8,128)(2,1)}, u32[]{:S(2)}, u32[]{:S(2)}) collective-permute-start(bf16[256,1408]{1,0:T(8,128)(2,1)S(1)} %get-tuple-element.70), channel_id=1, source_target_pairs={{0,4},{1,5},{2,6},{3,7},{4,0},{5,1},{6,2},{7,3},{8,12},{9,13},{10,... | collective-permute-start | bytes 2162696 | tf_op jit(solution)/shard_map/ppermute | solution.py:154
  520.0 32.6 %collective-permute-start.111 = (bf16[256,1408]{1,0:T(8,128)(2,1)S(1)}, bf16[256,1408]{1,0:T(8,128)(2,1)}, u32[]{:S(2)}, u32[]{:S(2)}) collective-permute-start(bf16[256,1408]{1,0:T(8,128)(2,1)S(1)} %get-tuple-element.69), channel_id=1, source_target_pairs={{0,6},{1,7},{2,4},{3,5},{4,2},{5,3},{6,0},{7,1},{8,14},{9,15},{10,... | collective-permute-start | bytes 2162696 | tf_op jit(solution)/shard_map/ppermute | solution.py:154
  521.7 32.2 %collective-permute-start.116 = (bf16[176,2048]{1,0:T(8,128)(2,1)S(1)}, bf16[176,2048]{1,0:T(8,128)(2,1)S(1)}, u32[]{:S(2)}, u32[]{:S(2)}) collective-permute-start(bf16[176,2048]{1,0:T(8,128)(2,1)S(1)} %get-tuple-element.65), channel_id=1, source_target_pairs={{0,8},{24,16},{1,9},{25,17},{2,10},{26,18},{3,11},{27,19},{4,12},{... | collective-permute-start | bytes 2162696 | tf_op jit(solution)/shard_map/ppermute | solution.py:181
  528.1 29.5 %collective-permute-start.119 = (bf16[176,2048]{1,0:T(8,128)(2,1)S(1)}, bf16[176,2048]{1,0:T(8,128)(2,1)S(1)}, u32[]{:S(2)}, u32[]{:S(2)}) collective-permute-start(bf16[176,2048]{1,0:T(8,128)(2,1)S(1)} %get-tuple-element.68), channel_id=1, source_target_pairs={{0,8},{24,16},{1,9},{25,17},{2,10},{26,18},{3,11},{27,19},{4,12},{... | collective-permute-start | bytes 2162696 | tf_op jit(solution)/shard_map/ppermute | solution.py:181
  529.4 43.6 %collective-permute-start.122 = (bf16[176,2048]{1,0:T(8,128)(2,1)S(1)}, bf16[176,2048]{1,0:T(8,128)(2,1)S(1)}, u32[]{:S(2)}, u32[]{:S(2)}) collective-permute-start(bf16[176,2048]{1,0:T(8,128)(2,1)S(1)} %get-tuple-element.67), channel_id=1, source_target_pairs={{0,8},{24,16},{1,9},{25,17},{2,10},{26,18},{3,11},{27,19},{4,12},{... | collective-permute-start | bytes 2162696 | tf_op jit(solution)/shard_map/ppermute | solution.py:181
  546.9 34.5 %collective-permute-start.125 = (bf16[176,2048]{1,0:T(8,128)(2,1)S(1)}, bf16[176,2048]{1,0:T(8,128)(2,1)S(1)}, u32[]{:S(2)}, u32[]{:S(2)}) collective-permute-start(bf16[176,2048]{1,0:T(8,128)(2,1)S(1)} %get-tuple-element.66), channel_id=1, source_target_pairs={{0,8},{24,16},{1,9},{25,17},{2,10},{26,18},{3,11},{27,19},{4,12},{... | collective-permute-start | bytes 2162696 | tf_op jit(solution)/shard_map/ppermute | solution.py:181
  552.6 29.4 %collective-permute-start.70 = (bf16[256,640]{1,0:T(8,128)(2,1)S(1)}, bf16[256,640]{1,0:T(8,128)(2,1)S(1)}, u32[]{:S(2)}, u32[]{:S(2)}) collective-permute-start(bf16[256,640]{1,0:T(8,128)(2,1)S(1)} %add.514), channel_id=1, source_target_pairs={{8,0},{16,24},{9,1},{17,25},{10,2},{18,26},{11,3},{19,27},{12,4},{... | collective-permute-start | bytes 983048 | tf_op jit(solution)/shard_map/ppermute | solution.py:186
  553.9 35.8 %collective-permute-start.78 = (bf16[256,640]{1,0:T(8,128)(2,1)S(1)}, bf16[256,640]{1,0:T(8,128)(2,1)S(1)}, u32[]{:S(2)}, u32[]{:S(2)}) collective-permute-start(bf16[256,640]{1,0:T(8,128)(2,1)S(1)} %add.518), channel_id=1, source_target_pairs={{8,0},{16,24},{9,1},{17,25},{10,2},{18,26},{11,3},{19,27},{12,4},{... | collective-permute-start | bytes 983048 | tf_op jit(solution)/shard_map/ppermute | solution.py:186
  557.6 36.3 %collective-permute-start.81 = (bf16[256,2048]{1,0:T(8,128)(2,1)S(1)}, bf16[256,2048]{1,0:T(8,128)(2,1)S(1)}, u32[]{:S(2)}, u32[]{:S(2)}) collective-permute-start(bf16[256,2048]{1,0:T(8,128)(2,1)S(1)} %add.520), channel_id=1, source_target_pairs={{8,16},{16,8},{9,17},{17,9},{10,18},{18,10},{11,19},{19,11},{12,20... | collective-permute-start | bytes 3145736 | tf_op jit(solution)/shard_map/ppermute | solution.py:183
  589.8 30.9 %collective-permute-start.92 = (bf16[256,1408]{1,0:T(8,128)(2,1)S(1)}, bf16[256,1408]{1,0:T(8,128)(2,1)S(1)}, u32[]{:S(2)}, u32[]{:S(2)}) collective-permute-start(bf16[256,1408]{1,0:T(8,128)(2,1)S(1)} %collective-permute-done.91), channel_id=1, source_target_pairs={{0,8},{24,16},{1,9},{25,17},{2,10},{26,18},{3,11},{27,19},{4,12},{... | collective-permute-start | bytes 2162696 | tf_op jit(solution)/shard_map/ppermute | solution.py:181
  592.5 36.1 %collective-permute-start.96 = (bf16[256,1408]{1,0:T(8,128)(2,1)S(1)}, bf16[256,1408]{1,0:T(8,128)(2,1)S(1)}, u32[]{:S(2)}, u32[]{:S(2)}) collective-permute-start(bf16[256,1408]{1,0:T(8,128)(2,1)S(1)} %collective-permute-done.95), channel_id=1, source_target_pairs={{0,8},{24,16},{1,9},{25,17},{2,10},{26,18},{3,11},{27,19},{4,12},{... | collective-permute-start | bytes 2162696 | tf_op jit(solution)/shard_map/ppermute | solution.py:181
  593.9 36.5 %collective-permute-start.101 = (bf16[256,1408]{1,0:T(8,128)(2,1)S(1)}, bf16[256,1408]{1,0:T(8,128)(2,1)S(1)}, u32[]{:S(2)}, u32[]{:S(2)}) collective-permute-start(bf16[256,1408]{1,0:T(8,128)(2,1)S(1)} %add.532), channel_id=1, source_target_pairs={{8,16},{16,8},{9,17},{17,9},{10,18},{18,10},{11,19},{19,11},{12,20... | collective-permute-start | bytes 2162696 | tf_op jit(solution)/shard_map/ppermute | solution.py:183
  594.6 43.0 %collective-permute-start.126 = (bf16[176,2048]{1,0:T(8,128)(2,1)S(1)}, bf16[176,2048]{1,0:T(8,128)(2,1)S(1)}, u32[]{:S(2)}, u32[]{:S(2)}) collective-permute-start(bf16[176,2048]{1,0:T(8,128)(2,1)S(1)} %get-tuple-element.64), channel_id=1, source_target_pairs={{8,16},{16,8},{9,17},{17,9},{10,18},{18,10},{11,19},{19,11},{12,20... | collective-permute-start | bytes 2162696 | tf_op jit(solution)/shard_map/ppermute | solution.py:183
  606.3 33.5 %collective-permute-start.123 = (bf16[176,2048]{1,0:T(8,128)(2,1)S(1)}, bf16[176,2048]{1,0:T(8,128)(2,1)S(1)}, u32[]{:S(2)}, u32[]{:S(2)}) collective-permute-start(bf16[176,2048]{1,0:T(8,128)(2,1)S(1)} %get-tuple-element.63), channel_id=1, source_target_pairs={{8,16},{16,8},{9,17},{17,9},{10,18},{18,10},{11,19},{19,11},{12,20... | collective-permute-start | bytes 2162696 | tf_op jit(solution)/shard_map/ppermute | solution.py:183
  620.7 33.3 %collective-permute-start.120 = (bf16[176,2048]{1,0:T(8,128)(2,1)S(1)}, bf16[176,2048]{1,0:T(8,128)(2,1)S(1)}, u32[]{:S(2)}, u32[]{:S(2)}) collective-permute-start(bf16[176,2048]{1,0:T(8,128)(2,1)S(1)} %get-tuple-element.62), channel_id=1, source_target_pairs={{8,16},{16,8},{9,17},{17,9},{10,18},{18,10},{11,19},{19,11},{12,20... | collective-permute-start | bytes 2162696 | tf_op jit(solution)/shard_map/ppermute | solution.py:183
  628.6 31.3 %collective-permute-start.117 = (bf16[176,2048]{1,0:T(8,128)(2,1)}, bf16[176,2048]{1,0:T(8,128)(2,1)}, u32[]{:S(2)}, u32[]{:S(2)}) collective-permute-start(bf16[176,2048]{1,0:T(8,128)(2,1)} %get-tuple-element.61), channel_id=1, source_target_pairs={{8,16},{16,8},{9,17},{17,9},{10,18},{18,10},{11,19},{19,11},{12,20... | collective-permute-start | bytes 2162696 | tf_op jit(solution)/shard_map/ppermute | solution.py:183
  630.4 43.2 %collective-permute-start.104 = (bf16[256,1408]{1,0:T(8,128)(2,1)}, bf16[256,1408]{1,0:T(8,128)(2,1)}, u32[]{:S(2)}, u32[]{:S(2)}) collective-permute-start(bf16[256,1408]{1,0:T(8,128)(2,1)} %collective-permute-done.103), channel_id=1, source_target_pairs={{0,8},{24,16},{1,9},{25,17},{2,10},{26,18},{3,11},{27,19},{4,12},{... | collective-permute-start | bytes 2162696 | tf_op jit(solution)/shard_map/ppermute | solution.py:181
  637.6 38.8 %collective-permute-start.108 = (bf16[256,1408]{1,0:T(8,128)(2,1)}, bf16[256,1408]{1,0:T(8,128)(2,1)}, u32[]{:S(2)}, u32[]{:S(2)}) collective-permute-start(bf16[256,1408]{1,0:T(8,128)(2,1)} %collective-permute-done.107), channel_id=1, source_target_pairs={{0,8},{24,16},{1,9},{25,17},{2,10},{26,18},{3,11},{27,19},{4,12},{... | collective-permute-start | bytes 2162696 | tf_op jit(solution)/shard_map/ppermute | solution.py:181
  639.8 38.8 %collective-permute-start.112 = (bf16[256,1408]{1,0:T(8,128)(2,1)}, bf16[256,1408]{1,0:T(8,128)(2,1)}, u32[]{:S(2)}, u32[]{:S(2)}) collective-permute-start(bf16[256,1408]{1,0:T(8,128)(2,1)} %collective-permute-done.111), channel_id=1, source_target_pairs={{0,8},{24,16},{1,9},{25,17},{2,10},{26,18},{3,11},{27,19},{4,12},{... | collective-permute-start | bytes 2162696 | tf_op jit(solution)/shard_map/ppermute | solution.py:181
  659.9 37.8 %collective-permute-start.102 = (bf16[256,1408]{1,0:T(8,128)(2,1)S(1)}, bf16[256,1408]{1,0:T(8,128)(2,1)}, u32[]{:S(2)}, u32[]{:S(2)}) collective-permute-start(bf16[256,1408]{1,0:T(8,128)(2,1)S(1)} %add.533), channel_id=1, source_target_pairs={{8,0},{16,24},{9,1},{17,25},{10,2},{18,26},{11,3},{19,27},{12,4},{... | collective-permute-start | bytes 2162696 | tf_op jit(solution)/shard_map/ppermute | solution.py:186
  673.6 113.1 %collective-permute-start.82 = (bf16[256,2048]{1,0:T(8,128)(2,1)S(1)}, bf16[256,2048]{1,0:T(8,128)(2,1)S(1)}, u32[]{:S(2)}, u32[]{:S(2)}) collective-permute-start(bf16[256,2048]{1,0:T(8,128)(2,1)S(1)} %add.521), channel_id=1, source_target_pairs={{8,0},{16,24},{9,1},{17,25},{10,2},{18,26},{11,3},{19,27},{12,4},{... | collective-permute-start | bytes 3145736 | tf_op jit(solution)/shard_map/ppermute | solution.py:186
  676.4 90.8 %collective-permute-start.89 = (bf16[256,1408]{1,0:T(8,128)(2,1)S(1)}, bf16[256,1408]{1,0:T(8,128)(2,1)S(1)}, u32[]{:S(2)}, u32[]{:S(2)}) collective-permute-start(bf16[256,1408]{1,0:T(8,128)(2,1)S(1)} %add.525), channel_id=1, source_target_pairs={{8,16},{16,8},{9,17},{17,9},{10,18},{18,10},{11,19},{19,11},{12,20... | collective-permute-start | bytes 2162696 | tf_op jit(solution)/shard_map/ppermute | solution.py:183
  678.6 89.5 %collective-permute-start.93 = (bf16[256,1408]{1,0:T(8,128)(2,1)S(1)}, bf16[256,1408]{1,0:T(8,128)(2,1)S(1)}, u32[]{:S(2)}, u32[]{:S(2)}) collective-permute-start(bf16[256,1408]{1,0:T(8,128)(2,1)S(1)} %add.527), channel_id=1, source_target_pairs={{8,16},{16,8},{9,17},{17,9},{10,18},{18,10},{11,19},{19,11},{12,20... | collective-permute-start | bytes 2162696 | tf_op jit(solution)/shard_map/ppermute | solution.py:183
  682.3 53.3 %collective-permute-start.127 = (bf16[176,2048]{1,0:T(8,128)(2,1)S(1)}, bf16[176,2048]{1,0:T(8,128)(2,1)S(1)}, u32[]{:S(2)}, u32[]{:S(2)}) collective-permute-start(bf16[176,2048]{1,0:T(8,128)(2,1)S(1)} %add.548), channel_id=1, source_target_pairs={{8,0},{16,24},{9,1},{17,25},{10,2},{18,26},{11,3},{19,27},{12,4},{... | collective-permute-start | bytes 2162696 | tf_op jit(solution)/shard_map/ppermute | solution.py:186
  697.7 53.3 %collective-permute-start.124 = (bf16[176,2048]{1,0:T(8,128)(2,1)S(1)}, bf16[176,2048]{1,0:T(8,128)(2,1)S(1)}, u32[]{:S(2)}, u32[]{:S(2)}) collective-permute-start(bf16[176,2048]{1,0:T(8,128)(2,1)S(1)} %add.546), channel_id=1, source_target_pairs={{8,0},{16,24},{9,1},{17,25},{10,2},{18,26},{11,3},{19,27},{12,4},{... | collective-permute-start | bytes 2162696 | tf_op jit(solution)/shard_map/ppermute | solution.py:186
  735.5 30.9 %collective-permute-start.121 = (bf16[176,2048]{1,0:T(8,128)(2,1)S(1)}, bf16[176,2048]{1,0:T(8,128)(2,1)S(1)}, u32[]{:S(2)}, u32[]{:S(2)}) collective-permute-start(bf16[176,2048]{1,0:T(8,128)(2,1)S(1)} %add.544), channel_id=1, source_target_pairs={{8,0},{16,24},{9,1},{17,25},{10,2},{18,26},{11,3},{19,27},{12,4},{... | collective-permute-start | bytes 2162696 | tf_op jit(solution)/shard_map/ppermute | solution.py:186
  782.2 36.7 %collective-permute-start.94 = (bf16[256,1408]{1,0:T(8,128)(2,1)S(1)}, bf16[256,1408]{1,0:T(8,128)(2,1)S(1)}, u32[]{:S(2)}, u32[]{:S(2)}) collective-permute-start(bf16[256,1408]{1,0:T(8,128)(2,1)S(1)} %add.528), channel_id=1, source_target_pairs={{8,0},{16,24},{9,1},{17,25},{10,2},{18,26},{11,3},{19,27},{12,4},{... | collective-permute-start | bytes 2162696 | tf_op jit(solution)/shard_map/ppermute | solution.py:186
  783.7 50.7 %collective-permute-start.98 = (bf16[256,1408]{1,0:T(8,128)(2,1)S(1)}, bf16[256,1408]{1,0:T(8,128)(2,1)S(1)}, u32[]{:S(2)}, u32[]{:S(2)}) collective-permute-start(bf16[256,1408]{1,0:T(8,128)(2,1)S(1)} %add.530), channel_id=1, source_target_pairs={{8,0},{16,24},{9,1},{17,25},{10,2},{18,26},{11,3},{19,27},{12,4},{... | collective-permute-start | bytes 2162696 | tf_op jit(solution)/shard_map/ppermute | solution.py:186
  785.2 64.6 %collective-permute-start.106 = (bf16[256,1408]{1,0:T(8,128)(2,1)S(1)}, bf16[256,1408]{1,0:T(8,128)(2,1)S(1)}, u32[]{:S(2)}, u32[]{:S(2)}) collective-permute-start(bf16[256,1408]{1,0:T(8,128)(2,1)S(1)} %add.535), channel_id=1, source_target_pairs={{8,0},{16,24},{9,1},{17,25},{10,2},{18,26},{11,3},{19,27},{12,4},{... | collective-permute-start | bytes 2162696 | tf_op jit(solution)/shard_map/ppermute | solution.py:186
  786.7 75.5 %collective-permute-start.110 = (bf16[256,1408]{1,0:T(8,128)(2,1)S(1)}, bf16[256,1408]{1,0:T(8,128)(2,1)S(1)}, u32[]{:S(2)}, u32[]{:S(2)}) collective-permute-start(bf16[256,1408]{1,0:T(8,128)(2,1)S(1)} %add.537), channel_id=1, source_target_pairs={{8,0},{16,24},{9,1},{17,25},{10,2},{18,26},{11,3},{19,27},{12,4},{... | collective-permute-start | bytes 2162696 | tf_op jit(solution)/shard_map/ppermute | solution.py:186
  803.5 66.5 %collective-permute-start.114 = (bf16[256,1408]{1,0:T(8,128)(2,1)S(1)}, bf16[256,1408]{1,0:T(8,128)(2,1)S(1)}, u32[]{:S(2)}, u32[]{:S(2)}) collective-permute-start(bf16[256,1408]{1,0:T(8,128)(2,1)S(1)} %add.539), channel_id=1, source_target_pairs={{8,0},{16,24},{9,1},{17,25},{10,2},{18,26},{11,3},{19,27},{12,4},{... | collective-permute-start | bytes 2162696 | tf_op jit(solution)/shard_map/ppermute | solution.py:186
  (170 other events, 2620.7 us)

commit v2 on v1

v2 whole, which is shorter than its diff:
```python
import math

import jax
import jax.numpy as jnp
from jax import lax
from jax.experimental import pallas as pl
from jax.experimental.pallas import tpu as pltpu
from jax.sharding import PartitionSpec as P

H = 32
KVH = 4
HD = 64
DOCS = 8

NORM_EPS = 1e-05
ROPE_BASE = 10000.0
MASK_FILL = -1e30
F32 = jnp.float32
BF16 = jnp.bfloat16


def dot(a, b):
    return jnp.dot(a, b, preferred_element_type=F32)


def dot_nt(a, b):
    return lax.dot_general(a, b, (((1,), (1,)), ((), ())), preferred_element_type=F32)


def dot_tn(a, b):
    return lax.dot_general(a, b, (((0,), (0,)), ((), ())), preferred_element_type=F32)


def tiny():
    return pl.CostEstimate(flops=1024, bytes_accessed=1024, transcendentals=0)


def whole():
    return pl.BlockSpec(memory_space=pltpu.VMEM)


def turned(v):
    low = lax.broadcasted_iota(jnp.int32, v.shape, 1) % HD < HD // 2
    return jnp.where(low, pltpu.roll(v, 128 - HD // 2, 1), pltpu.roll(v, HD // 2, 1))


def scalars():
    return pl.BlockSpec(memory_space=pltpu.SMEM)


def pick_qkv(w_query, w_key, w_value, gain, chips):
    rows, cols = w_query.shape
    qw, share = cols // chips, chips // KVH

    def body(g_ref, q_ref, k_ref, v_ref, out_ref):
        gain = g_ref[...]
        out_ref[0, :, :qw] = (q_ref[...].astype(F32) * gain).astype(BF16)
        for n in range(KVH):

            @pl.when(pl.program_id(0) // share == n)
            def _():
                at = slice(n * HD, (n + 1) * HD)
                kv = jnp.concatenate([k_ref[:, at], v_ref[:, at]], axis=1)
                out_ref[0, :, qw:] = (kv.astype(F32) * gain).astype(BF16)

    small = pl.BlockSpec((rows, KVH * HD), lambda k: (0, 0))
    return pl.pallas_call(
        body,
        grid=(chips,),
        in_specs=[
            pl.BlockSpec((rows, 1), lambda k: (0, 0)),
            pl.BlockSpec((rows, qw), lambda k: (0, k)),
            small,
            small,
        ],
        out_specs=pl.BlockSpec((1, rows, qw + 2 * HD), lambda k: (k, 0, 0)),
        out_shape=jax.ShapeDtypeStruct((chips, rows, qw + 2 * HD), BF16),
        cost_estimate=tiny(),
        name="pick_qkv",
    )(gain, w_query, w_key, w_value)


def pick_half(w_gate, w_up, gain, ids, count):
    rows, cols = w_gate.shape
    width, part = cols // count, rows // 2
    if width % 128:
        out = []
        for w in (w_gate, w_up):
            v = lax.dynamic_slice_in_dim((w.astype(F32) * gain).astype(BF16), ids[2] * part, part)
            out.append(v.reshape(part, count, width).transpose(1, 0, 2))
        return out

    def body(s_ref, n_ref, a_ref, b_ref, c_ref, d_ref):
        c_ref[0] = (a_ref[...].astype(F32) * n_ref[...]).astype(BF16)
        d_ref[0] = (b_ref[...].astype(F32) * n_ref[...]).astype(BF16)

    return pl.pallas_call(
        body,
        grid_spec=pltpu.PrefetchScalarGridSpec(
            num_scalar_prefetch=1,
            grid=(count,),
            in_specs=[pl.BlockSpec((part, 1), lambda k, s: (s[2], 0))]
            + [pl.BlockSpec((part, width), lambda k, s: (s[2], k))] * 2,
            out_specs=[pl.BlockSpec((1, part, width), lambda k, s: (k, 0, 0))] * 2,
        ),
        out_shape=[jax.ShapeDtypeStruct((count, part, width), BF16)] * 2,
        cost_estimate=tiny(),
        name="pick_half",
    )(ids, gain, w_gate, w_up)


def join_cores(ids, near, far):
    rows, cols = near.shape

    def body(s_ref, a_ref, b_ref, out_ref):
        @pl.when(pl.program_id(0) == 0)
        def _():
            out_ref[...] = a_ref[...]

        @pl.when(pl.program_id(0) == 1)
        def _():
            out_ref[...] = b_ref[...]

    return pl.pallas_call(
        body,
        grid_spec=pltpu.PrefetchScalarGridSpec(
            num_scalar_prefetch=1,
            grid=(2,),
            in_specs=[pl.BlockSpec((rows, cols), lambda f, s: (0, 0))] * 2,
            out_specs=pl.BlockSpec((rows, cols), lambda f, s: (s[1] ^ f, 0)),
        ),
        out_shape=jax.ShapeDtypeStruct((2 * rows, cols), near.dtype),
        cost_estimate=tiny(),
        name="join_cores",
    )(ids, near, far)


def qkv_kernel(ids, x_blocks, near, far, cos_table, sin_table):
    rows, model = x_blocks[0].shape
    chips = len(x_blocks)
    own = rows * chips
    wrows, width = near.shape[1:]
    qw = width - 2 * HD

    def body(c_ref, cos_ref, sin_ref, n_ref, f_ref, *refs):
        x_refs, (z_ref, q_ref, kv_ref, w_ref) = refs[:chips], refs[chips:]
        chip, core = c_ref[0], c_ref[1]
        for k in range(chips):
            at = pl.multiple_of((2 * k + core) * wrows, wrows)
            w_ref[pl.ds(at, wrows), :] = n_ref[k]
            at = pl.multiple_of((2 * k + 1 - core) * wrows, wrows)
            w_ref[pl.ds(at, wrows), :] = f_ref[k]
            x = x_refs[k][...].astype(F32)
            inv = lax.rsqrt(jnp.mean(x * x, axis=-1, keepdims=True) + NORM_EPS)
            at = pl.multiple_of((chip ^ k) * rows, rows)
            z_ref[pl.ds(at, rows), :] = (x * inv).astype(BF16)
        total = dot(z_ref[...], w_ref[...])
        cos, sin = cos_ref[...], sin_ref[...]
        for j in range(qw // 128):
            v = total[:, j * 128 : (j + 1) * 128]
            q_ref[:, j * 128 : (j + 1) * 128] = (v * cos + turned(v) * sin).astype(BF16)
        v = total[:, qw:]
        key = lax.broadcasted_iota(jnp.int32, v.shape, 1) < HD
        kv_ref[...] = jnp.where(key, v * cos + turned(v) * sin, v).astype(BF16)

    return pl.pallas_call(
        body,
        in_specs=[scalars()] + [whole()] * (4 + chips),
        out_specs=[whole()] * 4,
        out_shape=[
            jax.ShapeDtypeStruct((own, model), BF16),
            jax.ShapeDtypeStruct((own, qw), BF16),
            jax.ShapeDtypeStruct((own, 2 * HD), BF16),
            jax.ShapeDtypeStruct((2 * chips * wrows, width), BF16),
        ],
        cost_estimate=tiny(),
        name="qkv_forward",
    )(ids, cos_table, sin_table, near, far, *x_blocks)


def attention_mask(s_ref, l_ref, rows, own):
    core, rep, block = s_ref[1], s_ref[4], pl.program_id(0)

    def coded(pos):
        bound, code = 0, jnp.zeros(pos.shape, jnp.int32)
        for n in range(DOCS):
            bound = bound + l_ref[rep, n]
            code = code + jnp.where(pos >= bound, 1, 0)
        return jnp.where(code < DOCS - 1, code, 1000 + pos)

    q_pos = (2 * block + core) * rows + lax.broadcasted_iota(jnp.int32, (rows, 1), 0)
    index = lax.broadcasted_iota(jnp.int32, (1, 2 * own), 1)
    side = jnp.where(index < own, core, 1 - core)
    index = jnp.where(index < own, index, index - own)
    k_pos = (2 * (index // rows) + side) * rows + index % rows
    q_code = coded(q_pos)
    allowed = (coded(k_pos) == q_code) & (k_pos <= q_pos)
    return jnp.where(allowed, 0.0, MASK_FILL), jnp.where(q_code < DOCS, 1.0, 0.0)


def attention_forward(ids, lengths, q, kv_own, kv_other, rows):
    own, qw = q.shape
    heads = qw // HD
    scale = 1.0 / math.sqrt(HD)

    def body(s_ref, d_ref, q_ref, a_ref, b_ref, o_ref, l_ref):
        bias, valid = attention_mask(s_ref, d_ref, rows, own)
        lane = lax.broadcasted_iota(jnp.int32, (rows, 128), 1)
        k_a, v_a = a_ref[:, :HD], a_ref[:, HD:]
        k_b, v_b = b_ref[:, :HD], b_ref[:, HD:]
        sums = jnp.zeros((rows, 128), F32)
        pair = []
        for h in range(heads):
            qh = q_ref[:, h * HD : (h + 1) * HD] * jnp.asarray(scale, BF16)
            s = jnp.concatenate([dot_nt(qh, k_a), dot_nt(qh, k_b)], axis=1) + bias
            top = jnp.max(s, axis=-1, keepdims=True)
            p = jnp.exp(s - top)
            tot = jnp.sum(p, axis=-1, keepdims=True)
            p = (p * (1.0 / tot)).astype(BF16)
            mixed = dot(p[:, :own], v_a) + dot(p[:, own:], v_b)
            pair.append((mixed * valid).astype(BF16))
            sums = jnp.where(lane == h, top + jnp.log(tot), sums)
            if h % 2:
                o_ref[:, (h - 1) * HD : (h + 1) * HD] = jnp.concatenate(pair, axis=1)
                pair = []
        l_ref[...] = sums

    return pl.pallas_call(
        body,
        grid=(own // rows,),
        in_specs=[
            scalars(),
            scalars(),
            pl.BlockSpec((rows, qw), lambda i: (i, 0)),
            pl.BlockSpec((own, 2 * HD), lambda i: (0, 0)),
            pl.BlockSpec((own, 2 * HD), lambda i: (0, 0)),
        ],
        out_specs=[
            pl.BlockSpec((rows, qw), lambda i: (i, 0)),
            pl.BlockSpec((rows, 128), lambda i: (i, 0)),
        ],
        out_shape=[
            jax.ShapeDtypeStruct((own, qw), BF16),
            jax.ShapeDtypeStruct((own, 128), F32),
        ],
        cost_estimate=tiny(),
        name="attention_forward",
    )(ids, lengths, q, kv_own, kv_other)


def attention_backward(
    ids, lengths, q, kv_own, kv_other, sums, d_out, cos_table, sin_table, rows
):
    own, qw = q.shape
    heads = qw // HD
    scale = 1.0 / math.sqrt(HD)
    seq_len = 2 * own

    def body(
        s_ref, n_ref, q_ref, a_ref, b_ref, l_ref, d_ref, cos_ref, sin_ref, dq_ref, dkv_ref,
    ):
        @pl.when(pl.program_id(0) == 0)
        def _():
            dkv_ref[...] = jnp.zeros_like(dkv_ref)

        bias, valid = attention_mask(s_ref, n_ref, rows, own)
        valid = valid.astype(BF16)
        k_a, v_a = a_ref[:, :HD], a_ref[:, HD:]
        k_b, v_b = b_ref[:, :HD], b_ref[:, HD:]
        cos, sin = cos_ref[...], sin_ref[...]
        pair = []
        dk = jnp.zeros((seq_len, HD), F32)
        dv = jnp.zeros((seq_len, HD), F32)
        for h in range(heads):
            qh = q_ref[:, h * HD : (h + 1) * HD] * jnp.asarray(scale, BF16)
            dh = d_ref[:, h * HD : (h + 1) * HD] * valid
            s = jnp.concatenate([dot_nt(qh, k_a), dot_nt(qh, k_b)], axis=1) + bias
            p = jnp.exp(s - l_ref[:, h : h + 1])
            dp = jnp.concatenate([dot_nt(dh, v_a), dot_nt(dh, v_b)], axis=1)
            inner = jnp.sum(p * dp, axis=-1, keepdims=True)
            ds = (p * (dp - inner)).astype(BF16)
            dq = (dot(ds[:, :own], k_a) + dot(ds[:, own:], k_b)) * scale
            dk = dk + dot_tn(ds, qh)
            dv = dv + dot_tn(p.astype(BF16), dh)
            pair.append(dq)
            if h % 2:
                v = jnp.concatenate(pair, axis=1)
                dq_ref[:, (h - 1) * HD : (h + 1) * HD] = (v * cos - turned(v) * sin).astype(BF16)
                pair = []
        dkv_ref[...] += jnp.concatenate([dk, dv], axis=1)

    return pl.pallas_call(
        body,
        grid=(own // rows,),
        in_specs=[
            scalars(),
            scalars(),
            pl.BlockSpec((rows, qw), lambda i: (i, 0)),
            pl.BlockSpec((own, 2 * HD), lambda i: (0, 0)),
            pl.BlockSpec((own, 2 * HD), lambda i: (0, 0)),
            pl.BlockSpec((rows, 128), lambda i: (i, 0)),
            pl.BlockSpec((rows, qw), lambda i: (i, 0)),
            pl.BlockSpec((rows, 128), lambda i: (i, 0)),
            pl.BlockSpec((rows, 128), lambda i: (i, 0)),
        ],
        out_specs=[
            pl.BlockSpec((rows, qw), lambda i: (i, 0)),
            pl.BlockSpec((seq_len, 2 * HD), lambda i: (0, 0)),
        ],
        out_shape=[
            jax.ShapeDtypeStruct((own, qw), BF16),
            jax.ShapeDtypeStruct((seq_len, 2 * HD), F32),
        ],
        cost_estimate=tiny(),
        name="attention_backward",
    )(ids, lengths, q, kv_own, kv_other, sums, d_out, cos_table, sin_table)


def out_proj(ids, attn, near, far, chips):
    own, depth = attn.shape
    wrows, model = near.shape
    rows = own // chips

    def body(c_ref, a_ref, n_ref, f_ref, *outs):
        chip, core, w_ref = c_ref[0], c_ref[1], outs[-1]
        w_ref[pl.ds(pl.multiple_of(core * wrows, wrows), wrows), :] = n_ref[...]
        w_ref[pl.ds(pl.multiple_of((1 - core) * wrows, wrows), wrows), :] = f_ref[...]
        for k in range(chips):
            at = pl.multiple_of((chip ^ k) * rows, rows)
            outs[k][...] = dot(a_ref[pl.ds(at, rows), :], w_ref[...]).astype(BF16)

    return pl.pallas_call(
        body,
        in_specs=[scalars()] + [whole()] * 3,
        out_specs=[whole()] * (chips + 1),
        out_shape=[jax.ShapeDtypeStruct((rows, model), BF16)] * chips
        + [jax.ShapeDtypeStruct((depth, model), BF16)],
        cost_estimate=tiny(),
        name="out_proj",
    )(ids, attn, near, far)


def residual_norm(tokens, parts):
    rows, model = tokens.shape

    def body(x_ref, *refs):
        y_ref, z_ref = refs[-2:]
        y = x_ref[...].astype(F32)
        for p in refs[:-2]:
            y = y + p[...].astype(F32)
        y_ref[...] = y
        inv = lax.rsqrt(jnp.mean(y * y, axis=-1, keepdims=True) + NORM_EPS)
        z_ref[...] = (y * inv).astype(BF16)

    return pl.pallas_call(
        body,
        in_specs=[whole()] * (1 + len(parts)),
        out_specs=[whole()] * 2,
        out_shape=[
            jax.ShapeDtypeStruct((rows, model), F32),
            jax.ShapeDtypeStruct((rows, model), BF16),
        ],
        cost_estimate=tiny(),
        name="residual_norm",
    )(tokens, *parts)


def residual_norm_back(base, parts, y, copies):
    rows, model = y.shape
    count = parts.shape[0] // rows

    def body(b_ref, y_ref, p_ref, f_ref, l_ref, n_ref):
        e = p_ref[:rows, :].astype(F32)
        for i in range(1, count):
            e = e + p_ref[i * rows : (i + 1) * rows, :].astype(F32)
        v = y_ref[...].astype(F32)
        inv = lax.rsqrt(jnp.mean(v * v, axis=-1, keepdims=True) + NORM_EPS)
        z = v * inv
        ez = e * z
        n_ref[...] = jnp.sum(ez, axis=0, keepdims=True)
        out = b_ref[...].astype(F32) + inv * (e - z * jnp.mean(ez, axis=-1, keepdims=True))
        f_ref[...] = out
        for i in range(copies):
            l_ref[i * rows : (i + 1) * rows, :] = out.astype(BF16)

    return pl.pallas_call(
        body,
        in_specs=[whole()] * 3,
        out_specs=[whole()] * 3,
        out_shape=[
            jax.ShapeDtypeStruct((rows, model), F32),
            jax.ShapeDtypeStruct((copies * rows, model), BF16),
            jax.ShapeDtypeStruct((1, model), F32),
        ],
        cost_estimate=tiny(),
        name="residual_norm_back",
    )(base, y, parts)


def feed_forward(ids, z_blocks, cot, weights, w_down):
    rows, model = z_blocks[0].shape
    chips = len(z_blocks)
    part, width = weights[0][0].shape[1:]
    own, tile = rows * chips, 256

    def body(s_ref, *refs):
        z_refs, c_ref, w_refs = refs[:chips], refs[chips], refs[chips + 1 : chips + 9]
        d_ref, m_ref, dg_ref, du_ref, z_ref, g_ref, u_ref = refs[chips + 9 :]
        chip, core, half = s_ref[0], s_ref[1], s_ref[2]

        @pl.when(pl.program_id(0) == 0)
        def _():
            for k in range(chips):
                at = pl.multiple_of((chip ^ k) * rows, rows)
                z_ref[pl.ds(at, rows), :] = z_refs[k][...]

        for w, out in ((w_refs[:4], g_ref), (w_refs[4:], u_ref)):
            for i in range(4):
                side = core if i < 2 else 1 - core
                piece = half if i % 2 == 0 else 1 - half
                for j in range(chips):
                    at = pl.multiple_of((2 * (2 * j + side) + piece) * part, part)
                    out[pl.ds(at, part), :] = w[i][j]
        gate = dot(z_ref[...], g_ref[...])
        up = dot(z_ref[...], u_ref[...])
        sig = 1.0 / (1.0 + jnp.exp(-gate))
        silu = gate * sig
        m_ref[...] = (silu * up).astype(BF16)
        dm = dot_nt(c_ref[...], d_ref[...])
        dg_ref[...] = (dm * up * sig * (1.0 + gate * (1.0 - sig))).astype(BF16)
        du_ref[...] = (dm * silu).astype(BF16)

    joined = pl.BlockSpec((own, model), lambda n, s: (0, 0))
    out_tile = pl.BlockSpec((own, tile), lambda n, s: (0, n))
    return pl.pallas_call(
        body,
        grid_spec=pltpu.PrefetchScalarGridSpec(
            num_scalar_prefetch=1,
            grid=(pl.cdiv(width, tile),),
            in_specs=[pl.BlockSpec((rows, model), lambda n, s: (0, 0))] * chips
            + [joined]
            + [pl.BlockSpec((chips, part, tile), lambda n, s: (0, 0, n))] * 8
            + [pl.BlockSpec((tile, model), lambda n, s: (n, 0))],
            out_specs=[out_tile] * 3
            + [joined]
            + [pl.BlockSpec((model, tile), lambda n, s: (0, n))] * 2,
        ),
        out_shape=[jax.ShapeDtypeStruct((own, width), BF16)] * 3
        + [jax.ShapeDtypeStruct((own, model), BF16)]
        + [jax.ShapeDtypeStruct((model, width), BF16)] * 2,
        cost_estimate=tiny(),
        name="feed_forward",
    )(ids, *z_blocks, cot, *weights[0], *weights[1], w_down)


def strips(value, ref, lead=()):
    rows, width = value.shape
    for t in range(pl.cdiv(width, 128)):
        v = value[:, t * 128 : (t + 1) * 128]
        if v.shape[1] < 128:
            v = jnp.concatenate([v, jnp.zeros((rows, 128 - v.shape[1]), v.dtype)], axis=1)
        ref[(*lead, slice(t * rows, (t + 1) * rows), slice(None))] = v


def weight_grad(ids, left, right, chips):
    own, model = left.shape
    width = right.shape[1]
    rows = model // (2 * chips)
    long = pl.cdiv(width, 128) * rows
    group = min(4, chips)
    turns = chips // group

    def body(c_ref, l_ref, r_ref, near_ref, far_ref):
        step = pl.program_id(0)
        near = step >= turns
        side = jnp.where(near, c_ref[1], 1 - c_ref[1])
        first = jnp.where(near, step - turns, step) * group
        blocks = []
        for j in range(group):
            at = pl.multiple_of((2 * (first + j) + side) * rows, rows)
            blocks.append(l_ref[:, pl.ds(at, rows)])
        out = dot_tn(jnp.concatenate(blocks, axis=1), r_ref[...]).astype(BF16)

        @pl.when(near)
        def _():
            for j in range(group):
                strips(out[j * rows : (j + 1) * rows], near_ref, (j,))

        @pl.when(step < turns)
        def _():
            for j in range(group):
                strips(out[j * rows : (j + 1) * rows], far_ref, (j,))

    return pl.pallas_call(
        body,
        grid_spec=pltpu.PrefetchScalarGridSpec(
            num_scalar_prefetch=1,
            grid=(2 * turns,),
            in_specs=[
                pl.BlockSpec((own, model), lambda t, c: (0, 0)),
                pl.BlockSpec((own, width), lambda t, c: (0, 0)),
            ],
            out_specs=[
                pl.BlockSpec((group, long, 128), lambda t, c: (jnp.maximum(t - turns, 0), 0, 0)),
                pl.BlockSpec((group, long, 128), lambda t, c: (jnp.minimum(t, turns - 1), 0, 0)),
            ],
        ),
        out_shape=[jax.ShapeDtypeStruct((chips, long, 128), BF16)] * 2,
        cost_estimate=tiny(),
        name="weight_grad",
    )(ids, left, right)


def row_grad(ids, left, right, cuts):
    own, depth = left.shape
    model = right.shape[1]
    rows, width = depth // 2, model // cuts
    long = width // 128 * rows

    def body(c_ref, l_ref, r_ref, near_ref, far_ref, full_ref):
        core = c_ref[1]
        full_ref[...] = dot_tn(l_ref[...], r_ref[...])
        near = full_ref[pl.ds(pl.multiple_of(core * rows, 8), rows), :]
        far = full_ref[pl.ds(pl.multiple_of((1 - core) * rows, 8), rows), :]
        strips(near.astype(BF16), near_ref, (0,))
        strips(far.astype(BF16), far_ref, (0,))

    out = pl.BlockSpec((1, long, 128), lambda n, c: (n, 0, 0))
    return pl.pallas_call(
        body,
        grid_spec=pltpu.PrefetchScalarGridSpec(
            num_scalar_prefetch=1,
            grid=(cuts,),
            in_specs=[
                pl.BlockSpec((own, depth), lambda n, c: (0, 0)),
                pl.BlockSpec((own, width), lambda n, c: (0, n)),
            ],
            out_specs=[out] * 2,
            scratch_shapes=[pltpu.VMEM((depth, width), F32)],
        ),
        out_shape=[jax.ShapeDtypeStruct((cuts, long, 128), BF16)] * 2,
        cost_estimate=tiny(),
        name="row_grad",
    )(ids, left, right)


def beside(blocks, rows, width, scale=None):
    count = len(blocks)
    tiles = pl.cdiv(width, 128)
    if scale is None:
        scale = jnp.ones((rows, 1), F32)
    if width % 128:
        full = [b.reshape(tiles, rows, 128).transpose(1, 0, 2).reshape(rows, -1) for b in blocks]
        return jnp.concatenate([f[:, :width] for f in full], axis=1).astype(F32) * scale

    def body(s_ref, *refs):
        scale, out_ref = s_ref[...], refs[-1]
        for k in range(count):

            @pl.when(pl.program_id(0) == k)
            def _():
                for t in range(tiles):
                    v = refs[k][t * rows : (t + 1) * rows, :].astype(F32)
                    out_ref[:, t * 128 : (t + 1) * 128] = v * scale

    return pl.pallas_call(
        body,
        grid=(count,),
        in_specs=[pl.BlockSpec((rows, 1), lambda k: (0, 0))]
        + [pl.BlockSpec((tiles * rows, 128), lambda k: (0, 0))] * count,
        out_specs=pl.BlockSpec((rows, width), lambda k: (0, k)),
        out_shape=jax.ShapeDtypeStruct((rows, count * width), F32),
        cost_estimate=tiny(),
        name="beside",
    )(scale, *blocks)


def chain_step(ids, own, outer, sent, inner, total, coming):
    def size(v):
        return 0 if v is None else v.shape[0]

    ins = [own, outer, sent, inner, total, coming]
    have = [v is not None for v in ins]
    sizes = [size(own), size(sent), max(size(sent), size(coming)), size(total)]
    wanted = [have[0], have[2], have[2] and have[5], have[4]]

    def body(s_ref, *refs):
        refs = list(refs)
        o_ref, x_ref, i_ref, y_ref, t_ref, c_ref = [refs.pop(0) if h else None for h in have]
        s_out, t_out, a_out, f_out = [refs.pop(0) if w else None for w in wanted]
        ends = s_ref[3] == 1
        if s_out is not None:
            s_out[...] = (o_ref[...].astype(F32) + x_ref[: size(own)].astype(F32)).astype(BF16)
        if t_out is not None:
            t_out[...] = (i_ref[...].astype(F32) + y_ref[...].astype(F32)).astype(BF16)
        if f_out is not None:
            f_out[...] = jnp.where(ends, x_ref[: size(total)], t_ref[...])
        if a_out is not None:

            @pl.when(ends)
            def _():
                a_out[: size(coming)] = c_ref[...]

            @pl.when(jnp.logical_not(ends))
            def _():
                a_out[: size(sent)] = t_out[...]

    outs = pl.pallas_call(
        body,
        in_specs=[scalars()] + [whole()] * sum(have),
        out_specs=[whole()] * sum(wanted),
        out_shape=[jax.ShapeDtypeStruct((n, 128), BF16) for n, w in zip(sizes, wanted) if w],
        cost_estimate=tiny(),
        name="chain_step",
    )(ids, *[v for v in ins if v is not None])
    outs = list(outs)
    return [outs.pop(0) if w else None for w in wanted]


def local(
    tokens,
    cotangent,
    doc_lengths,
    norm1_gain,
    w_query,
    w_key,
    w_value,
    w_out,
    norm2_gain,
    w_gate,
    w_up,
    w_down,
):
    rows, model = tokens.shape
    group = lax.axis_size("fsdp")
    reps = lax.axis_size("rep")
    chips = group // 2
    dev = lax.axis_index("fsdp").astype(jnp.int32)
    rep = lax.axis_index("rep").astype(jnp.int32)
    chip, core, half = dev >> 1, dev & 1, rep & 1
    ends = jnp.where((rep == 0) | (rep == reps - 1), 1, 0).astype(jnp.int32)
    ids = jnp.stack([chip, core, half, ends, rep])
    seq_len = rows * group
    own = rows * chips
    wrows = w_query.shape[0]
    width = w_gate.shape[1] // chips
    kv_share = chips // KVH
    qw = H // chips * HD
    tie = lax.optimization_barrier
    sides = [[2 * k + c for k in range(chips)] for c in range(2)]

    def exchange(v):
        return lax.all_to_all(v, "fsdp", 0, 0, axis_index_groups=sides, tiled=True)

    def hop(v, k):
        return lax.ppermute(v, "fsdp", [(i, i ^ (2 * k)) for i in range(group)])

    def hops(blocks):
        return [blocks[0]] + [hop(blocks[k], k) for k in range(1, chips)]

    def swap(v):
        return lax.ppermute(v, "fsdp", [(i, i ^ 1) for i in range(group)])

    def trade(v):
        return lax.ppermute(v, "rep", [(i, i ^ 1) for i in range(reps)])

    def copies(v):
        return jnp.broadcast_to(v[None], (chips,) + v.shape).reshape(chips * v.shape[0], -1)

    sums_of = {}
    outer_pairs = [(0, 1), (1, 0), (2, 3), (3, 2)]

    class Line:
        def __init__(self):
            self.own = self.sent = self.total = self.outer = self.inner = None

        def busy(self):
            return any(v is not None for v in (self.own, self.sent, self.total))

    lines = [Line(), Line()]
    turn = [0]

    def visit(*carry, new=None):
        if reps != 4:
            if new is not None:
                sums_of[new[0]] = lax.psum(new[1], "rep")
            return carry if len(carry) != 1 else carry[0]
        line = lines[turn[0] % 2]
        turn[0] += 1
        extra = [line.outer, line.inner, None if new is None else new[1]]
        tied = tie(tuple(carry) + tuple(v for v in extra if v is not None))
        carry, tied = tied[: len(carry)], list(tied[len(carry) :])
        outer, inner, coming = [None if v is None else tied.pop(0) for v in extra]
        value = lambda pair: None if pair is None else pair[1]
        if outer is None:
            ahead = coming
        else:
            own_sum, middle, ahead, final = chain_step(
                ids, value(line.own), outer, value(line.sent), inner, value(line.total), coming
            )
            if final is not None:
                sums_of[line.total[0]] = final
            line.total = None if middle is None else (line.sent[0], middle)
            line.sent = None if own_sum is None else (line.own[0], own_sum)
            if ahead is None:
                ahead = coming if coming is not None else middle
        line.own = None if coming is None else (new[0], coming)
        line.outer = None if ahead is None else lax.ppermute(ahead, "rep", outer_pairs)
        line.inner = (
            None if line.sent is None else lax.ppermute(line.sent[1], "rep", [(1, 2), (2, 1)])
        )
        return carry if len(carry) != 1 else carry[0]

    starts = 2 * rows * jnp.arange(chips, dtype=jnp.int32) + core * rows
    own_pos = (starts[:, None] + jnp.arange(rows, dtype=jnp.int32)[None, :]).reshape(own)
    lane = jnp.arange(128)
    inverse = jnp.exp(-math.log(ROPE_BASE) / (HD // 2) * (lane % (HD // 2)).astype(F32))
    angles = own_pos.astype(F32)[:, None] * inverse[None, :]
    cos_table = jnp.cos(angles)
    sin_table = jnp.sin(angles) * jnp.where(lane % HD < HD // 2, -1.0, 1.0)[None, :]

    gain_one = norm1_gain.astype(F32)[:, None]
    gain_two = norm2_gain.astype(F32)[:, None]
    x_blocks = hops([tokens] * chips)
    qkv_near = exchange(pick_qkv(w_query, w_key, w_value, gain_one, chips))
    gate_part, up_part = pick_half(w_gate, w_up, gain_two, ids, chips)
    w_out_far = swap(w_out)
    w_down_c = join_cores(ids, w_down, swap(w_down))
    *x_blocks, qkv_near, cos_table, sin_table, gate_part, up_part, w_out_far, w_down_c = tie(
        (*x_blocks, qkv_near, cos_table, sin_table, gate_part, up_part, w_out_far, w_down_c)
    )
    gate_near = exchange(gate_part)
    normed_one, queries, kv_near, w_qkv = qkv_kernel(
        ids, x_blocks, qkv_near, swap(qkv_near), cos_table, sin_table
    )
    queries, gate_near, up_part, cot = tie((queries, gate_near, up_part, cotangent))
    up_near = exchange(up_part)
    gate_traded = trade(gate_near)
    kv_far = swap(kv_near)
    attn, sums = attention_forward(ids, doc_lengths, queries, kv_near, kv_far, rows)
    attn, up_near = tie((attn, up_near))
    up_traded = trade(up_near)
    *mixed, w_out_c = out_proj(ids, attn, w_out, w_out_far, chips)
    *mixed, cot = tie((*mixed, cot))
    parts = hops(mixed)
    cot_rows = exchange(copies(cot))
    *parts, gate_traded = tie((*parts, gate_traded))
    resid, normed = residual_norm(tokens, parts)
    z_blocks = hops([normed] * chips)
    weights = [
        [near, far, swap(near), swap(far)]
        for near, far in ((gate_near, gate_traded), (up_near, up_traded))
    ]
    inner, grad_gate, grad_up, normed_two, w_gate_c, w_up_c = feed_forward(
        ids, z_blocks, cot_rows, weights, w_down_c
    )

    down_near, down_far = row_grad(ids, inner, cot_rows, 4)
    down_far = swap(down_far)
    grad_gate, grad_up, down_near = tie((grad_gate, grad_up, down_near))
    back = (dot_nt(grad_gate, w_gate_c) + dot_nt(grad_up, w_up_c)).astype(BF16)
    back, down_near, down_far, grad_gate = tie((back, down_near, down_far, grad_gate))
    parts = exchange(back)
    down = [down_near[k] + down_far[k] for k in range(4)]
    grad_gate = visit(grad_gate, new=("down0", down[0]))
    gate_near, gate_far = weight_grad(ids, normed_two, grad_gate, chips)
    gate_near, gate_far, grad_up = visit(gate_near, gate_far, grad_up, new=("down1", down[1]))
    gate_far = swap(gate_far)
    up_near, up_far = weight_grad(ids, normed_two, grad_up, chips)
    up_near, up_far, parts = visit(up_near, up_far, parts, new=("down2", down[2]))
    gate_part = exchange(gate_near + gate_far)
    up_far = swap(up_far)
    grad_resid, da, gain_two_local = residual_norm_back(cotangent, parts, resid, chips)
    da, inner = visit(da, inner, new=("down3", down[3]))
    out = dot(inner, w_down_c).astype(BF16)
    up_part = up_near + up_far
    out, up_part, gate_part = visit(out, up_part, gate_part, new=None)
    da = exchange(da)
    da, up_part = visit(da, up_part, new=("gate0", gate_part[0]))
    up_part = exchange(up_part)
    dob = dot_nt(da, w_out_c).astype(BF16)
    out_near, out_far = row_grad(ids, attn, da, 2)
    dob, out_near, out_far = visit(dob, out_near, out_far, new=("gate1", gate_part[1]))
    out_far = swap(out_far)
    dq, dkv = attention_backward(
        ids, doc_lengths, queries, kv_near, kv_far, sums, dob, cos_table, sin_table, rows
    )
    dq, dkv = visit(dq, dkv, new=("gate2", gate_part[2]))
    dkv = dkv[:own] + swap(dkv[own:].astype(BF16)).astype(F32)
    half_turn = jnp.concatenate([dkv[:, HD // 2 : HD], dkv[:, : HD // 2]], axis=1)
    dk = dkv[:, :HD] * cos_table[:, :HD] - half_turn * sin_table[:, :HD]
    dqkv = jnp.concatenate([dq, dk.astype(BF16), dkv[:, HD:].astype(BF16)], axis=1)
    back = dot_nt(dqkv, w_qkv).astype(BF16)
    dqkv, back, up_part = visit(dqkv, back, up_part, new=("gate3", gate_part[3]))
    parts = exchange(back)
    qkv_near, qkv_far = weight_grad(ids, normed_one, dqkv, chips)
    qkv_near, qkv_far = visit(qkv_near, qkv_far, new=("up0", up_part[0]))
    qkv_part = qkv_near + swap(qkv_far)
    qkv_part, parts = visit(qkv_part, parts, new=("up1", up_part[1]))
    qkv_part = exchange(qkv_part)
    _, grad_inputs, gain_one_local = residual_norm_back(grad_resid, parts, tokens, 1)
    gain_one_local = visit(gain_one_local, new=("up2", up_part[2]))
    norms = jnp.concatenate([gain_one_local, gain_two_local], axis=0)
    norms = norms.reshape(2, chips, 2, wrows).transpose(2, 1, 0, 3)
    mine = lax.dynamic_index_in_dim(norms, core, 0, keepdims=False)
    other = lax.dynamic_index_in_dim(norms, 1 - core, 0, keepdims=False)
    norms = mine + swap(other)
    out_part = out_near + out_far
    norms, qkv_part, out_part = visit(norms, qkv_part, out_part, new=("up3", up_part[3]))
    parts = exchange(out).reshape(chips, rows, model)
    visit(new=("out0", out_part[0]))
    parts = visit(parts, new=("out1", out_part[1]))
    norms = jnp.sum(exchange(norms), axis=0)
    result = (resid + jnp.sum(parts.astype(F32), axis=0)).astype(BF16)
    qkv_part = qkv_part.reshape(2, chips // 2 * qkv_part.shape[1], 128)
    visit(new=("qkv0", qkv_part[0]))
    norms = visit(norms, new=("qkv1", qkv_part[1]))
    if reps == 4:
        norms = norms + lax.ppermute(norms, "rep", [(0, 1), (3, 2)])
        norms = norms + lax.ppermute(norms, "rep", [(1, 2), (2, 1)])
        norms = jnp.where(ends == 1, lax.ppermute(norms, "rep", [(1, 0), (2, 3)]), norms)
    else:
        norms = lax.psum(norms, "rep")
        for k in range(4, chips):
            visit(new=(f"gate{k}", gate_part[k]))
            visit(new=(f"up{k}", up_part[k]))
    while any(line.busy() for line in lines):
        visit()

    def summed(name, count):
        return [sums_of[f"{name}{k}"] for k in range(count)]

    qkv = jnp.concatenate(summed("qkv", 2)).reshape(chips, -1, 128)
    grad_query = beside([b[: qw // 128 * wrows] for b in qkv], wrows, qw, gain_one)
    kv = qkv[:, qw // 128 * wrows :].astype(F32).reshape(KVH, kv_share, wrows, 2, HD).sum(axis=1)
    kv = kv * gain_one[None, :, :, None]
    grad_key = kv[:, :, 0].transpose(1, 0, 2).reshape(wrows, KVH * HD)
    grad_value = kv[:, :, 1].transpose(1, 0, 2).reshape(wrows, KVH * HD)
    return (
        result,
        grad_inputs,
        norms[0] / gain_one[:, 0],
        grad_query,
        grad_key,
        grad_value,
        beside(summed("out", 2), wrows, model // 2),
        norms[1] / gain_two[:, 0],
        beside(summed("gate", chips), wrows, width, gain_two),
        beside(summed("up", chips), wrows, width, gain_two),
        beside(summed("down", 4), w_down.shape[0], model // 4),
    )


def solution(mesh):
    placed = (
        P(("rep", "fsdp"), None),
        P(("rep", "fsdp"), None),
        P(),
        P("fsdp"),
        P("fsdp", None),
        P("fsdp", None),
        P("fsdp", None),
        P("fsdp", None),
        P("fsdp"),
        P("fsdp", None),
        P("fsdp", None),
        P("fsdp", None),
    )
    return jax.shard_map(
        local,
        mesh=mesh,
        in_specs=placed,
        out_specs=(
            P(("rep", "fsdp"), None),
            P(("rep", "fsdp"), None),
            P("fsdp"),
            P("fsdp", None),
            P("fsdp", None),
            P("fsdp", None),
            P("fsdp", None),
            P("fsdp"),
            P("fsdp", None),
            P("fsdp", None),
            P("fsdp", None),
        ),
        check_vma=False,
    )
```

time: 887 us -> 677 us (0.76)
  waiting for transfers between devices: 411 us -> 185 us
  Pallas kernels: 46.4 us -> 230 us
  matrix products: 98.3 us -> 25.6 us
  other arithmetic: 74.4 us -> 25.1 us
  local copies, waits for them, and re-layouts: 49.2 us -> 25.5 us
  starting transfers between devices: 193 us -> 174 us
    pallas_call x9 -> x42, Pallas kernels: 46.4 us -> 230 us  [the longest x21 74.3 us: chain_step(): pl.pallas_call(body, in_specs=[scalars()] + [whole()] * sum(have), out_sp...]
    ppermute x54 -> x42, waiting for transfers between devices: 222 us -> 75 us  [the longest x21 60 us: visit(): lax.ppermute(ahead, 'rep', outer_pairs)]
    ppermute x48 -> x9, waiting for transfers between devices: 188 us -> 71 us  [hop(): return lax.ppermute(v, 'fsdp', [(i, i ^ 2 * k) for i in range(group)])]
    all_to_all x0 -> x12, starting transfers between devices: none -> 49.7 us  [exchange(): return lax.all_to_all(v, 'fsdp', 0, 0, axis_index_groups=sides, tiled=True)]
    dot_general x11 -> x0, matrix products: 49 us -> none  [the longest x5 21.6 us: dot_tn(): lax.dot_general(a, b, (((0,), (0,)), ((), ())), preferred_element_type=F32)]
    ppermute x48 -> x9, starting transfers between devices: 59.7 us -> 14.1 us  [hop(): return lax.ppermute(v, 'fsdp', [(i, i ^ 2 * k) for i in range(group)])]
    all_to_all x0 -> x12, waiting for transfers between devices: none -> 37.1 us  [exchange(): return lax.all_to_all(v, 'fsdp', 0, 0, axis_index_groups=sides, tiled=True)]
    convert_element_type x15 -> x5, other arithmetic: 31.8 us -> 1.79 us  [the longest x1 0.91 us: local(): result = (resid + jnp.sum(parts.astype(F32), axis=0)).astype(BF16)]
  transfers between devices with their start and end apart: 128 -> 78, of which waited for: 45 -> 24; matrix products, arithmetic and copies ran while one was open for 22% -> 9% of each run, Pallas kernels for 5% -> 28%
where the time goes in v2:
time: 677 us; the launch traced here: 666 us
  Pallas kernels  230 us (34%)
  waiting for transfers between devices  185 us (27%)
  starting transfers between devices  174 us (26%)
  matrix products  25.6 us (4%)
  local copies, waits for them, and re-layouts  25.5 us (4%)
  other arithmetic  25.1 us (4%)
    ppermute x21, starting transfers between devices, visit(): lax.ppermute(ahead, 'rep', outer_pairs)  75.3 us
    pallas_call x21, Pallas kernels, chain_step(): pl.pallas_call(body, in_specs=[scalars()] + [whole()] * sum(have), out_sp...  74.3 us
    ppermute x9, waiting for transfers between devices, hop(): return lax.ppermute(v, 'fsdp', [(i, i ^ 2 * k) for i in range(group)])  71 us
    ppermute x21, waiting for transfers between devices, visit(): lax.ppermute(ahead, 'rep', outer_pairs)  60 us
    all_to_all x12, starting transfers between devices, exchange(): return lax.all_to_all(v, 'fsdp', 0, 0, axis_index_groups=sides, tiled=True)  49.7 us
    all_to_all x12, waiting for transfers between devices, exchange(): return lax.all_to_all(v, 'fsdp', 0, 0, axis_index_groups=sides, tiled=True)  37.1 us
    pallas_call x3, Pallas kernels, weight_grad(): pl.pallas_call(body, grid_spec=pltpu.PrefetchScalarGridSpec(num_scalar_pr...  25.7 us
    ppermute x16, starting transfers between devices, visit(): lax.ppermute(line.sent[1], 'rep', [(1, 2), (2, 1)])  24.2 us
  transfers between devices with their start and end apart: 78, of which 24 were waited for; matrix products, arithmetic and copies ran while one was open for 9% of the time, Pallas kernels for 28%

profile of v2, /device:TPU:0, one launch (start us, length us, event | category | flops | bytes accessed | tf_op | source)
XLA Modules:
  0.0 666.4 jit_solution(9398547336315116888)
XLA Ops:
  2.7 4.0 pick_qkv.1
  6.7 5.1 all-to-all-start
  16.8 4.9 pick_half.1
  23.6 6.1 join_cores.1.refs_13_
  29.7 11.2 %collective-permute-done.refs_1_ = bf16[128,2048]{1,0:T(8,128)(2,1)S(1)} collective-permute-done((bf16[128,2048]{1,0:T(8,128)(2,1)S(1)}, bf16[128,2048]{1,0:T(8,128)(2,1)S(1)}, u32[]{:S(2)}, u32[]{:S(2)}) %collective-permute-start) | collective-permute-done | bytes 524320 | tf_op jit(solution)/shard_map/ppermute | solution.py:656
  40.9 11.1 %collective-permute-done.2.refs_3_ = bf16[128,2048]{1,0:T(8,128)(2,1)} collective-permute-done((bf16[128,2048]{1,0:T(8,128)(2,1)S(1)}, bf16[128,2048]{1,0:T(8,128)(2,1)}, u32[]{:S(2)}, u32[]{:S(2)}) %collective-permute-start.2) | collective-permute-done | bytes 524320 | tf_op jit(solution)/shard_map/ppermute | solution.py:656
  56.6 6.5 qkv_forward.1
  63.1 11.3 %all-to-all-done.1.refs_5_ = bf16[4,128,1408]{2,1,0:T(8,128)(2,1)S(1)} async-done(((bf16[4,128,1408]{2,1,0:T(8,128)(2,1)}), bf16[4,128,1408]{2,1,0:T(8,128)(2,1)S(1)}, u32[]{:S(2)}, u32[]{:S(2)}) %all-to-all-start.1) | async-done | bytes 1441824 | tf_op jit(solution)/shard_map/all_to_all | solution.py:653
  74.4 4.3 all-to-all-start.2
  82.0 17.0 %attention_forward.1 = (bf16[512,512]{1,0:T(8,128)(2,1)}, f32[512,128]{1,0:T(8,128)}) custom-call(s32[5]{0:T(128)} %stack.23.s_ref.c_ref, s32[4,8]{1,0:T(4,128)} %n_ref.3, bf16[512,512]{1,0:T(8,128)(2,1)} %get-tuple-element.233.q_ref, bf16[512,128]{1,0:T(8,128)(2,1)} %get-tuple-element.234.a_ref, bf16[512,128]{1,0:T(8,128)(2,1)} %collective-permute-done.6.b_ref), custom_call_target="tpu_custom_call" | custom-call | flops 1024 | bytes 1024 | tf_op jit(solution)/shard_map/attention_forward/pallas_call | solution.py:228
  99.4 4.6 out_proj.1
  107.4 5.9 collective-permute-done.10.refs_6_
  121.7 21.6 %collective-permute-done.8.refs_2_ = bf16[128,2048]{1,0:T(8,128)(2,1)} collective-permute-done((bf16[128,2048]{1,0:T(8,128)(2,1)}, bf16[128,2048]{1,0:T(8,128)(2,1)}, u32[]{:S(2)}, u32[]{:S(2)}) %collective-permute-start.8) | collective-permute-done | bytes 524320 | tf_op jit(solution)/shard_map/ppermute | solution.py:656
  148.8 15.0 %collective-permute-done.11.refs_1_ = bf16[128,2048]{1,0:T(8,128)(2,1)S(1)} collective-permute-done((bf16[128,2048]{1,0:T(8,128)(2,1)}, bf16[128,2048]{1,0:T(8,128)(2,1)S(1)}, u32[]{:S(2)}, u32[]{:S(2)}) %collective-permute-start.11) | collective-permute-done | bytes 524320 | tf_op jit(solution)/shard_map/ppermute | solution.py:656
  166.5 12.1 %collective-permute-done.13.refs_3_ = bf16[128,2048]{1,0:T(8,128)(2,1)S(1)} collective-permute-done((bf16[128,2048]{1,0:T(8,128)(2,1)}, bf16[128,2048]{1,0:T(8,128)(2,1)S(1)}, u32[]{:S(2)}, u32[]{:S(2)}) %collective-permute-start.13) | collective-permute-done | bytes 524320 | tf_op jit(solution)/shard_map/ppermute | solution.py:656
  180.0 19.5 %feed_forward.1 = (bf16[512,1408]{1,0:T(8,128)(2,1)}, bf16[512,1408]{1,0:T(8,128)(2,1)}, bf16[512,1408]{1,0:T(8,128)(2,1)}, bf16[512,2048]{1,0:T(8,128)(2,1)}, b...) custom-call(s32[5]{0:T(128)} %stack.23.s_ref.c_ref, bf16[128,2048]{1,0:T(8,128)(2,1)} %get-tuple-element.254.refs_0_, ...), custom_call_target="tpu_custom_call" | custom-call | flops 1024 | bytes 1024 | tf_op jit(solution)/shard_map/feed_forward/pallas_call | solution.py:435
  199.5 8.2 %row_grad.2 = (bf16[4,2816,128]{2,1,0:T(8,128)(2,1)}, bf16[4,2816,128]{2,1,0:T(8,128)(2,1)}) custom-call(s32[5]{0:T(128)} %stack.23.s_ref.c_ref, bf16[512,1408]{1,0:T(8,128)(2,1)} %get-tuple-element.284.l_ref, bf16[512,2048]{1,0:T(8,128)(2,1)} %bitcast.84), custom_call_target="tpu_custom_call" | custom-call | flops 1024 | bytes 1024 | tf_op jit(solution)/shard_map/row_grad/pallas_call | solution.py:529
  207.8 5.6 fusion.13
  213.5 4.6 add_convert_fusion
  219.7 9.6 %weight_grad.3 = (bf16[4,2816,128]{2,1,0:T(8,128)(2,1)}, bf16[4,2816,128]{2,1,0:T(8,128)(2,1)}) custom-call(s32[5]{0:T(128)} %stack.23.s_ref.c_ref, bf16[512,2048]{1,0:T(8,128)(2,1)} %get-tuple-element.259.l_ref, bf16[512,1408]{1,0:T(8,128)(2,1)} %get-tuple-element.273.r_ref), custom_call_target="tpu_custom_call" | custom-call | flops 1024 | bytes 1024 | tf_op jit(solution)/shard_map/weight_grad/pallas_call | solution.py:494
  229.8 3.9 all-to-all-start.4
  235.4 5.0 add.126
  240.4 18.4 %all-to-all-done.4 = bf16[4,128,2048]{2,1,0:T(8,128)(2,1)S(1)} async-done(((bf16[4,128,2048]{2,1,0:T(8,128)(2,1)}), bf16[4,128,2048]{2,1,0:T(8,128)(2,1)S(1)}, u32[]{:S(2)}, u32[]{:S(2)}) %all-to-all-start.4) | async-done | bytes 2097184 | tf_op jit(solution)/shard_map/all_to_all | solution.py:653
  260.1 4.1 all-to-all-start.5
  264.2 9.6 %weight_grad.4 = (bf16[4,2816,128]{2,1,0:T(8,128)(2,1)}, bf16[4,2816,128]{2,1,0:T(8,128)(2,1)}) custom-call(s32[5]{0:T(128)} %stack.23.s_ref.c_ref, bf16[512,2048]{1,0:T(8,128)(2,1)} %get-tuple-element.259.l_ref, bf16[512,1408]{1,0:T(8,128)(2,1)} %get-tuple-element.276.r_ref), custom_call_target="tpu_custom_call" | custom-call | flops 1024 | bytes 1024 | tf_op jit(solution)/shard_map/weight_grad/pallas_call | solution.py:494
  275.5 4.5 residual_norm_back.2
  280.0 12.6 %collective-permute-done.21.refs_1_ = bf16[2816,128]{1,0:T(8,128)(2,1)} collective-permute-done((bf16[2816,128]{1,0:T(8,128)(2,1)}, bf16[2816,128]{1,0:T(8,128)(2,1)}, u32[]{:S(2)}, u32[]{:S(2)}) %collective-permute-start.21) | collective-permute-done | bytes 720928 | tf_op jit(solution)/shard_map/ppermute | solution.py:708
  292.6 4.3 all-to-all-done.5
  296.9 4.5 all-to-all-start.7
  315.1 7.9 %convolution_convert_fusion.1 = bf16[512,2048]{1,0:T(8,128)(2,1)} fusion(bf16[512,1408]{1,0:T(8,128)(2,1)} %get-tuple-element.284.l_ref, bf16[1408,2048]{1,0:T(8,128)(2,1)} %join_cores.1.refs_13_), kind=kOutput, calls=%fused_computation.3 | convolution fusion | flops 2953838592 | bytes 9306112 | tf_op jit(solution)/shard_map/dot_general | solution.py:23
  323.0 4.1 add.125
  328.7 5.5 collective-permute-done.26.refs_1_
  341.1 7.3 %collective-permute-start.28 = (bf16[2816,128]{1,0:T(8,128)(2,1)}, bf16[2816,128]{1,0:T(8,128)(2,1)}, u32[]{:S(2)}, u32[]{:S(2)}) collective-permute-start(bf16[2816,128]{1,0:T(8,128)(2,1)} %get-tuple-element.305.refs_3_), channel_id=1, source_target_pairs={{0,8},{8,0},{16,24},{24,16},{1,9},{9,1},{17,25},{25,17},{2,10},{10... | collective-permute-start | bytes 2162696 | tf_op jit(solution)/shard_map/ppermute | solution.py:708
  357.5 4.7 row_grad.3
  362.1 4.3 convolution_convert_fusion.2.d_ref
  366.4 21.8 %attention_backward.1 = (bf16[512,512]{1,0:T(8,128)(2,1)}, f32[1024,128]{1,0:T(8,128)}) custom-call(s32[5]{0:T(128)} %stack.23.s_ref.c_ref, s32[4,8]{1,0:T(4,128)} %n_ref.3, bf16[512,512]{1,0:T(8,128)(2,1)} %get-tuple-element.233.q_ref, bf16[512,128]{1,0:T(8,128)(2,1)} %get-tuple-element.234.a_ref, bf16[512,128]{1,0:T(8,128)(2,1)} %collective-permute-done.6.b_ref, ...), custom_call_target="tpu_custom_call" | custom-call | flops 1024 | bytes 1024 | tf_op jit(solution)/shard_map/attention_backward/pallas_call | solution.py:292
  396.9 4.4 chain_step.26
  409.2 5.0 collective-permute-done.33.refs_1_
  414.2 4.5 all-to-all-start.9
  420.3 6.5 weight_grad.5
  438.8 9.3 %collective-permute-done.37.refs_1_ = bf16[2816,128]{1,0:T(8,128)(2,1)S(1)} collective-permute-done((bf16[2816,128]{1,0:T(8,128)(2,1)S(1)}, bf16[2816,128]{1,0:T(8,128)(2,1)S(1)}, u32[]{:S(2)}, u32[]{:S(2)}) %collective-permute-start.37) | collective-permute-done | bytes 720928 | tf_op jit(solution)/shard_map/ppermute | solution.py:708
  448.0 4.4 all-to-all-start.10
  452.5 4.3 chain_step.28
  456.8 7.2 %collective-permute-start.39 = (bf16[2816,128]{1,0:T(8,128)(2,1)}, bf16[2816,128]{1,0:T(8,128)(2,1)}, u32[]{:S(2)}, u32[]{:S(2)}) collective-permute-start(bf16[2816,128]{1,0:T(8,128)(2,1)} %get-tuple-element.348), channel_id=1, source_target_pairs={{0,8},{8,0},{16,24},{24,16},{1,9},{9,1},{17,25},{25,17},{2,10},{10... | collective-permute-start | bytes 2162696 | tf_op jit(solution)/shard_map/ppermute | solution.py:708
  476.1 6.8 %collective-permute-start.43 = (bf16[2816,128]{1,0:T(8,128)(2,1)}, bf16[2816,128]{1,0:T(8,128)(2,1)}, u32[]{:S(2)}, u32[]{:S(2)}) collective-permute-start(bf16[2816,128]{1,0:T(8,128)(2,1)} %get-tuple-element.357), channel_id=1, source_target_pairs={{0,8},{8,0},{16,24},{24,16},{1,9},{9,1},{17,25},{25,17},{2,10},{10... | collective-permute-start | bytes 2162696 | tf_op jit(solution)/shard_map/ppermute | solution.py:708
  484.4 4.0 residual_norm_back.3
  492.1 4.3 chain_step.32
  500.9 4.4 chain_step.30
  510.9 5.2 collective-permute-done.52.refs_1_
  516.0 4.3 chain_step.33
  525.7 5.8 collective-permute-done.45.refs_1_
  531.5 4.3 chain_step.31
  541.2 4.2 all-to-all-start.11
  546.9 4.2 chain_step.34
  555.0 7.4 %collective-permute-done.47.refs_1_ = bf16[2816,128]{1,0:T(8,128)(2,1)} collective-permute-done((bf16[2816,128]{1,0:T(8,128)(2,1)}, bf16[2816,128]{1,0:T(8,128)(2,1)}, u32[]{:S(2)}, u32[]{:S(2)}) %collective-permute-start.47) | collective-permute-done | bytes 720928 | tf_op jit(solution)/shard_map/ppermute | solution.py:708
  562.4 4.2 chain_step.38
  572.9 4.8 collective-permute-start.49
  578.5 4.9 beside.9
  583.4 8.9 %collective-permute-done.49 = f32[2,256]{1,0:T(2,128)S(1)} collective-permute-done((f32[2,256]{1,0:T(2,128)S(1)}, f32[2,256]{1,0:T(2,128)S(1)}, u32[]{:S(2)}, u32[]{:S(2)}) %collective-permute-start.49) | collective-permute-done | bytes 2080 | tf_op jit(solution)/shard_map/ppermute | solution.py:819
  596.8 4.0 collective-permute-start.58
  612.0 4.8 beside.7
  620.6 3.9 collective-permute-start.60
  628.1 8.1 %collective-permute-start.65 = (bf16[2560,128]{1,0:T(8,128)(2,1)}, bf16[2560,128]{1,0:T(8,128)(2,1)S(1)}, u32[]{:S(2)}, u32[]{:S(2)}) collective-permute-start(bf16[2560,128]{1,0:T(8,128)(2,1)} %get-tuple-element.416.refs_1_), channel_id=1, source_target_pairs={{0,8},{8,0},{16,24},{24,16},{1,9},{9,1},{17,25},{25,17},{2,10},{10... | collective-permute-start | bytes 1966088 | tf_op jit(solution)/shard_map/ppermute | solution.py:708
  639.9 5.1 beside.8
  (257 shorter events, 204.7 us)
Async XLA Ops:
  0.6 23.0 %collective-permute-start.4 = (bf16[704,2048]{1,0:T(8,128)(2,1)}, bf16[704,2048]{1,0:T(8,128)(2,1)}, u32[]{:S(2)}, u32[]{:S(2)}) collective-permute-start(bf16[704,2048]{1,0:T(8,128)(2,1)} %a_ref.3), channel_id=1, source_target_pairs={{0,1},{1,0},{2,3},{3,2},{4,5},{5,4},{6,7},{7,6},{8,9},{9,8},{10,11... | collective-permute-start | bytes 8650760 | tf_op jit(solution)/shard_map/ppermute | solution.py:662
  1.2 50.9 %collective-permute-start.3 = (bf16[256,2048]{1,0:T(8,128)(2,1)}, bf16[256,2048]{1,0:T(8,128)(2,1)S(1)}, u32[]{:S(2)}, u32[]{:S(2)}) collective-permute-start(bf16[256,2048]{1,0:T(8,128)(2,1)} %n_ref.2), channel_id=1, source_target_pairs={{0,1},{1,0},{2,3},{3,2},{4,5},{5,4},{6,7},{7,6},{8,9},{9,8},{10,11... | collective-permute-start | bytes 3145736 | tf_op jit(solution)/shard_map/ppermute | solution.py:662
  6.7 45.3 %all-to-all-start = ((bf16[4,256,640]{2,1,0:T(8,128)(2,1)}), bf16[4,256,640]{2,1,0:T(8,128)(2,1)S(1)}, u32[]{:S(2)}, u32[]{:S(2)}) async-start(bf16[4,256,640]{2,1,0:T(8,128)(2,1)} %pick_qkv.1), calls=%async_computation | async-start | bytes 2621440 | tf_op jit(solution)/shard_map/all_to_all | solution.py:653
  11.8 29.1 %collective-permute-start = (bf16[128,2048]{1,0:T(8,128)(2,1)S(1)}, bf16[128,2048]{1,0:T(8,128)(2,1)S(1)}, u32[]{:S(2)}, u32[]{:S(2)}) collective-permute-start(bf16[128,2048]{1,0:T(8,128)(2,1)S(1)} %copy-done.6), channel_id=1, source_target_pairs={{0,2},{1,3},{2,0},{3,1},{4,6},{5,7},{6,4},{7,5},{8,10},{9,11},{10,... | collective-permute-start | bytes 1572872 | tf_op jit(solution)/shard_map/ppermute | solution.py:656
  13.9 27.0 %collective-permute-start.1 = (bf16[128,2048]{1,0:T(8,128)(2,1)S(1)}, bf16[128,2048]{1,0:T(8,128)(2,1)}, u32[]{:S(2)}, u32[]{:S(2)}) collective-permute-start(bf16[128,2048]{1,0:T(8,128)(2,1)S(1)} %copy-done.6), channel_id=1, source_target_pairs={{0,4},{1,5},{2,6},{3,7},{4,0},{5,1},{6,2},{7,3},{8,12},{9,13},{10,... | collective-permute-start | bytes 1572872 | tf_op jit(solution)/shard_map/ppermute | solution.py:656
  15.3 36.7 %collective-permute-start.2 = (bf16[128,2048]{1,0:T(8,128)(2,1)S(1)}, bf16[128,2048]{1,0:T(8,128)(2,1)}, u32[]{:S(2)}, u32[]{:S(2)}) collective-permute-start(bf16[128,2048]{1,0:T(8,128)(2,1)S(1)} %copy-done.6), channel_id=1, source_target_pairs={{0,6},{1,7},{2,4},{3,5},{4,2},{5,3},{6,0},{7,1},{8,14},{9,15},{10,... | collective-permute-start | bytes 1572872 | tf_op jit(solution)/shard_map/ppermute | solution.py:656
  53.0 21.4 %all-to-all-start.1 = ((bf16[4,128,1408]{2,1,0:T(8,128)(2,1)}), bf16[4,128,1408]{2,1,0:T(8,128)(2,1)S(1)}, u32[]{:S(2)}, u32[]{:S(2)}) async-start(bf16[4,128,1408]{2,1,0:T(8,128)(2,1)} %get-tuple-element.231), calls=%async_computation.1 | async-start | bytes 2883584 | tf_op jit(solution)/shard_map/all_to_all | solution.py:653
  74.4 24.6 %all-to-all-start.2 = ((bf16[4,128,1408]{2,1,0:T(8,128)(2,1)}), bf16[4,128,1408]{2,1,0:T(8,128)(2,1)}, u32[]{:S(2)}, u32[]{:S(2)}) async-start(bf16[4,128,1408]{2,1,0:T(8,128)(2,1)} %get-tuple-element.236), calls=%async_computation.2 | async-start | bytes 2883584 | tf_op jit(solution)/shard_map/all_to_all | solution.py:653
  78.8 34.6 %collective-permute-start.10 = (bf16[4,128,1408]{2,1,0:T(8,128)(2,1)S(1)}, bf16[4,128,1408]{2,1,0:T(8,128)(2,1)S(1)}, u32[]{:S(2)}, u32[]{:S(2)}) collective-permute-start(bf16[4,128,1408]{2,1,0:T(8,128)(2,1)S(1)} %all-to-all-done.1.refs_5_), channel_id=1, source_target_pairs={{0,8},{8,0},{16,24},{24,16},{1,9},{9,1},{17,25},{25,17},{2,10},{10... | collective-permute-start | bytes 4325384 | tf_op jit(solution)/shard_map/ppermute | solution.py:665
  99.0 44.3 %collective-permute-start.16 = (bf16[4,128,1408]{2,1,0:T(8,128)(2,1)}, bf16[4,128,1408]{2,1,0:T(8,128)(2,1)}, u32[]{:S(2)}, u32[]{:S(2)}) collective-permute-start(bf16[4,128,1408]{2,1,0:T(8,128)(2,1)} %all-to-all-done.2.refs_9_), channel_id=1, source_target_pairs={{0,8},{8,0},{16,24},{24,16},{1,9},{9,1},{17,25},{25,17},{2,10},{10... | collective-permute-start | bytes 4325384 | tf_op jit(solution)/shard_map/ppermute | solution.py:665
  99.4 47.8 %collective-permute-start.14 = (bf16[4,128,1408]{2,1,0:T(8,128)(2,1)S(1)}, bf16[4,128,1408]{2,1,0:T(8,128)(2,1)}, u32[]{:S(2)}, u32[]{:S(2)}) collective-permute-start(bf16[4,128,1408]{2,1,0:T(8,128)(2,1)S(1)} %all-to-all-done.1.refs_5_), channel_id=1, source_target_pairs={{0,1},{1,0},{2,3},{3,2},{4,5},{5,4},{6,7},{7,6},{8,9},{9,8},{10,11... | collective-permute-start | bytes 4325384 | tf_op jit(solution)/shard_map/ppermute | solution.py:662
  104.1 17.5 %collective-permute-start.7 = (bf16[128,2048]{1,0:T(8,128)(2,1)}, bf16[128,2048]{1,0:T(8,128)(2,1)}, u32[]{:S(2)}, u32[]{:S(2)}) collective-permute-start(bf16[128,2048]{1,0:T(8,128)(2,1)} %get-tuple-element.245), channel_id=1, source_target_pairs={{0,2},{1,3},{2,0},{3,1},{4,6},{5,7},{6,4},{7,5},{8,10},{9,11},{10,... | collective-permute-start | bytes 1572872 | tf_op jit(solution)/shard_map/ppermute | solution.py:656
  106.0 37.4 %collective-permute-start.8 = (bf16[128,2048]{1,0:T(8,128)(2,1)}, bf16[128,2048]{1,0:T(8,128)(2,1)}, u32[]{:S(2)}, u32[]{:S(2)}) collective-permute-start(bf16[128,2048]{1,0:T(8,128)(2,1)} %get-tuple-element.246), channel_id=1, source_target_pairs={{0,4},{1,5},{2,6},{3,7},{4,0},{5,1},{6,2},{7,3},{8,12},{9,13},{10,... | collective-permute-start | bytes 1572872 | tf_op jit(solution)/shard_map/ppermute | solution.py:656
  113.4 30.0 %collective-permute-start.9 = (bf16[128,2048]{1,0:T(8,128)(2,1)}, bf16[128,2048]{1,0:T(8,128)(2,1)}, u32[]{:S(2)}, u32[]{:S(2)}) collective-permute-start(bf16[128,2048]{1,0:T(8,128)(2,1)} %get-tuple-element.247), channel_id=1, source_target_pairs={{0,6},{1,7},{2,4},{3,5},{4,2},{5,3},{6,0},{7,1},{8,14},{9,15},{10,... | collective-permute-start | bytes 1572872 | tf_op jit(solution)/shard_map/ppermute | solution.py:656
  117.8 60.7 %all-to-all-start.3 = ((bf16[4,128,2048]{2,1,0:T(8,128)(2,1)}), bf16[4,128,2048]{2,1,0:T(8,128)(2,1)S(1)}, u32[]{:S(2)}, u32[]{:S(2)}) async-start(bf16[4,128,2048]{2,1,0:T(8,128)(2,1)} %broadcast_in_dim.35), calls=%async_computation.3 | async-start | bytes 4194304 | tf_op jit(solution)/shard_map/all_to_all | solution.py:653
  121.6 56.9 %collective-permute-start.17 = (bf16[4,128,1408]{2,1,0:T(8,128)(2,1)}, bf16[4,128,1408]{2,1,0:T(8,128)(2,1)}, u32[]{:S(2)}, u32[]{:S(2)}) collective-permute-start(bf16[4,128,1408]{2,1,0:T(8,128)(2,1)} %all-to-all-done.2.refs_9_), channel_id=1, source_target_pairs={{0,1},{1,0},{2,3},{3,2},{4,5},{5,4},{6,7},{7,6},{8,9},{9,8},{10,11... | collective-permute-start | bytes 4325384 | tf_op jit(solution)/shard_map/ppermute | solution.py:662
  143.3 35.2 %collective-permute-start.15 = (bf16[4,128,1408]{2,1,0:T(8,128)(2,1)}, bf16[4,128,1408]{2,1,0:T(8,128)(2,1)}, u32[]{:S(2)}, u32[]{:S(2)}) collective-permute-start(bf16[4,128,1408]{2,1,0:T(8,128)(2,1)} %copy-done.14), channel_id=1, source_target_pairs={{0,1},{1,0},{2,3},{3,2},{4,5},{5,4},{6,7},{7,6},{8,9},{9,8},{10,11... | collective-permute-start | bytes 4325384 | tf_op jit(solution)/shard_map/ppermute | solution.py:662
  143.3 35.2 %collective-permute-start.18 = (bf16[4,128,1408]{2,1,0:T(8,128)(2,1)}, bf16[4,128,1408]{2,1,0:T(8,128)(2,1)}, u32[]{:S(2)}, u32[]{:S(2)}) collective-permute-start(bf16[4,128,1408]{2,1,0:T(8,128)(2,1)} %collective-permute-done.16.refs_10_), channel_id=1, source_target_pairs={{0,1},{1,0},{2,3},{3,2},{4,5},{5,4},{6,7},{7,6},{8,9},{9,8},{10,11... | collective-permute-start | bytes 4325384 | tf_op jit(solution)/shard_map/ppermute | solution.py:662
  147.1 16.7 %collective-permute-start.11 = (bf16[128,2048]{1,0:T(8,128)(2,1)}, bf16[128,2048]{1,0:T(8,128)(2,1)S(1)}, u32[]{:S(2)}, u32[]{:S(2)}) collective-permute-start(bf16[128,2048]{1,0:T(8,128)(2,1)} %get-tuple-element.254.refs_0_), channel_id=1, source_target_pairs={{0,2},{1,3},{2,0},{3,1},{4,6},{5,7},{6,4},{7,5},{8,10},{9,11},{10,... | collective-permute-start | bytes 1572872 | tf_op jit(solution)/shard_map/ppermute | solution.py:656
  147.2 19.2 %collective-permute-start.12 = (bf16[128,2048]{1,0:T(8,128)(2,1)}, bf16[128,2048]{1,0:T(8,128)(2,1)S(1)}, u32[]{:S(2)}, u32[]{:S(2)}) collective-permute-start(bf16[128,2048]{1,0:T(8,128)(2,1)} %get-tuple-element.254.refs_0_), channel_id=1, source_target_pairs={{0,4},{1,5},{2,6},{3,7},{4,0},{5,1},{6,2},{7,3},{8,12},{9,13},{10,... | collective-permute-start | bytes 1572872 | tf_op jit(solution)/shard_map/ppermute | solution.py:656
  229.8 29.0 %all-to-all-start.4 = ((bf16[4,128,2048]{2,1,0:T(8,128)(2,1)}), bf16[4,128,2048]{2,1,0:T(8,128)(2,1)S(1)}, u32[]{:S(2)}, u32[]{:S(2)}) async-start(bf16[4,128,2048]{2,1,0:T(8,128)(2,1)} %bitcast.93), calls=%async_computation.4 | async-start | bytes 4194304 | tf_op jit(solution)/shard_map/all_to_all | solution.py:653
  233.7 40.1 %collective-permute-start.20 = (bf16[2816,128]{1,0:T(8,128)(2,1)}, bf16[2816,128]{1,0:T(8,128)(2,1)}, u32[]{:S(2)}, u32[]{:S(2)}) collective-permute-start(bf16[2816,128]{1,0:T(8,128)(2,1)} %get-tuple-element.280.refs_0_), channel_id=1, source_target_pairs={{0,8},{8,0},{16,24},{24,16},{1,9},{9,1},{17,25},{25,17},{2,10},{10... | collective-permute-start | bytes 2162696 | tf_op jit(solution)/shard_map/ppermute | solution.py:708
  260.1 36.8 %all-to-all-start.5 = ((bf16[4,2816,128]{2,1,0:T(8,128)(2,1)}), bf16[4,2816,128]{2,1,0:T(8,128)(2,1)S(1)}, u32[]{:S(2)}, u32[]{:S(2)}) async-start(bf16[4,2816,128]{2,1,0:T(8,128)(2,1)} %add.126), calls=%async_computation.5 | async-start | bytes 5767168 | tf_op jit(solution)/shard_map/all_to_all | solution.py:653
  273.8 49.2 %collective-permute-start.22 = (bf16[4,2816,128]{2,1,0:T(8,128)(2,1)}, bf16[4,2816,128]{2,1,0:T(8,128)(2,1)}, u32[]{:S(2)}, u32[]{:S(2)}) collective-permute-start(bf16[4,2816,128]{2,1,0:T(8,128)(2,1)} %get-tuple-element.286), channel_id=1, source_target_pairs={{0,1},{1,0},{2,3},{3,2},{4,5},{5,4},{6,7},{7,6},{8,9},{9,8},{10,11... | collective-permute-start | bytes 8650760 | tf_op jit(solution)/shard_map/ppermute | solution.py:662
  273.8 18.9 %collective-permute-start.21 = (bf16[2816,128]{1,0:T(8,128)(2,1)}, bf16[2816,128]{1,0:T(8,128)(2,1)}, u32[]{:S(2)}, u32[]{:S(2)}) collective-permute-start(bf16[2816,128]{1,0:T(8,128)(2,1)} %get-tuple-element.283.refs_0_), channel_id=1, source_target_pairs={{0,8},{8,0},{16,24},{24,16},{1,9},{9,1},{17,25},{25,17},{2,10},{10... | collective-permute-start | bytes 2162696 | tf_op jit(solution)/shard_map/ppermute | solution.py:708
  296.9 37.4 %all-to-all-start.7 = ((bf16[4,128,2048]{2,1,0:T(8,128)(2,1)}), bf16[4,128,2048]{2,1,0:T(8,128)(2,1)}, u32[]{:S(2)}, u32[]{:S(2)}) async-start(bf16[4,128,2048]{2,1,0:T(8,128)(2,1)} %bitcast.91), calls=%async_computation.7 | async-start | bytes 4194304 | tf_op jit(solution)/shard_map/all_to_all | solution.py:653
  301.4 25.7 %collective-permute-start.24 = (bf16[2816,128]{1,0:T(8,128)(2,1)}, bf16[2816,128]{1,0:T(8,128)(2,1)}, u32[]{:S(2)}, u32[]{:S(2)}) collective-permute-start(bf16[2816,128]{1,0:T(8,128)(2,1)} %get-tuple-element.289.refs_2_.refs_0_), channel_id=1, source_target_pairs={{0,8},{8,0},{16,24},{24,16},{1,9},{9,1},{17,25},{25,17},{2,10},{10... | collective-permute-start | bytes 2162696 | tf_op jit(solution)/shard_map/ppermute | solution.py:708
  305.7 21.4 %collective-permute-start.25 = (bf16[2816,128]{1,0:T(8,128)(2,1)}, bf16[2816,128]{1,0:T(8,128)(2,1)}, u32[]{:S(2)}, u32[]{:S(2)}) collective-permute-start(bf16[2816,128]{1,0:T(8,128)(2,1)} %chain_step.21.refs_2_), channel_id=1, source_target_pairs={{8,16},{16,8},{9,17},{17,9},{10,18},{18,10},{11,19},{19,11},{12,20... | collective-permute-start | bytes 2162696 | tf_op jit(solution)/shard_map/ppermute | solution.py:710
  307.3 27.0 %collective-permute-start.26 = (bf16[2816,128]{1,0:T(8,128)(2,1)}, bf16[2816,128]{1,0:T(8,128)(2,1)}, u32[]{:S(2)}, u32[]{:S(2)}) collective-permute-start(bf16[2816,128]{1,0:T(8,128)(2,1)} %get-tuple-element.296.refs_2_.refs_0_), channel_id=1, source_target_pairs={{0,8},{8,0},{16,24},{24,16},{1,9},{9,1},{17,25},{25,17},{2,10},{10... | collective-permute-start | bytes 2162696 | tf_op jit(solution)/shard_map/ppermute | solution.py:708
  313.5 20.8 %collective-permute-start.27 = (bf16[2816,128]{1,0:T(8,128)(2,1)}, bf16[2816,128]{1,0:T(8,128)(2,1)}, u32[]{:S(2)}, u32[]{:S(2)}) collective-permute-start(bf16[2816,128]{1,0:T(8,128)(2,1)} %chain_step.22.refs_2_), channel_id=1, source_target_pairs={{8,16},{16,8},{9,17},{17,9},{10,18},{18,10},{11,19},{19,11},{12,20... | collective-permute-start | bytes 2162696 | tf_op jit(solution)/shard_map/ppermute | solution.py:710
  334.3 79.9 %all-to-all-start.8 = ((bf16[4,2816,128]{2,1,0:T(8,128)(2,1)}), bf16[4,2816,128]{2,1,0:T(8,128)(2,1)S(1)}, u32[]{:S(2)}, u32[]{:S(2)}) async-start(bf16[4,2816,128]{2,1,0:T(8,128)(2,1)} %add.125), calls=%async_computation.8 | async-start | bytes 5767168 | tf_op jit(solution)/shard_map/all_to_all | solution.py:653
  341.1 25.3 %collective-permute-start.28 = (bf16[2816,128]{1,0:T(8,128)(2,1)}, bf16[2816,128]{1,0:T(8,128)(2,1)}, u32[]{:S(2)}, u32[]{:S(2)}) collective-permute-start(bf16[2816,128]{1,0:T(8,128)(2,1)} %get-tuple-element.305.refs_3_), channel_id=1, source_target_pairs={{0,8},{8,0},{16,24},{24,16},{1,9},{9,1},{17,25},{25,17},{2,10},{10... | collective-permute-start | bytes 2162696 | tf_op jit(solution)/shard_map/ppermute | solution.py:708
  348.4 18.0 %collective-permute-start.29 = (bf16[2816,128]{1,0:T(8,128)(2,1)}, bf16[2816,128]{1,0:T(8,128)(2,1)}, u32[]{:S(2)}, u32[]{:S(2)}) collective-permute-start(bf16[2816,128]{1,0:T(8,128)(2,1)} %get-tuple-element.306.refs_1_), channel_id=1, source_target_pairs={{8,16},{16,8},{9,17},{17,9},{10,18},{18,10},{11,19},{19,11},{12,20... | collective-permute-start | bytes 2162696 | tf_op jit(solution)/shard_map/ppermute | solution.py:710
  353.7 34.6 %collective-permute-start.30 = (bf16[2816,128]{1,0:T(8,128)(2,1)}, bf16[2816,128]{1,0:T(8,128)(2,1)}, u32[]{:S(2)}, u32[]{:S(2)}) collective-permute-start(bf16[2816,128]{1,0:T(8,128)(2,1)} %get-tuple-element.313), channel_id=1, source_target_pairs={{0,8},{8,0},{16,24},{24,16},{1,9},{9,1},{17,25},{25,17},{2,10},{10... | collective-permute-start | bytes 2162696 | tf_op jit(solution)/shard_map/ppermute | solution.py:708
  355.8 32.5 %collective-permute-start.31 = (bf16[2816,128]{1,0:T(8,128)(2,1)}, bf16[2816,128]{1,0:T(8,128)(2,1)}, u32[]{:S(2)}, u32[]{:S(2)}) collective-permute-start(bf16[2816,128]{1,0:T(8,128)(2,1)} %get-tuple-element.314.refs_2_), channel_id=1, source_target_pairs={{8,16},{16,8},{9,17},{17,9},{10,18},{18,10},{11,19},{19,11},{12,20... | collective-permute-start | bytes 2162696 | tf_op jit(solution)/shard_map/ppermute | solution.py:710
  393.6 20.6 %collective-permute-start.33 = (bf16[2816,128]{1,0:T(8,128)(2,1)}, bf16[2816,128]{1,0:T(8,128)(2,1)}, u32[]{:S(2)}, u32[]{:S(2)}) collective-permute-start(bf16[2816,128]{1,0:T(8,128)(2,1)} %get-tuple-element.322), channel_id=1, source_target_pairs={{0,8},{8,0},{16,24},{24,16},{1,9},{9,1},{17,25},{25,17},{2,10},{10... | collective-permute-start | bytes 2162696 | tf_op jit(solution)/shard_map/ppermute | solution.py:708
  401.3 28.1 %collective-permute-start.34 = (bf16[2816,128]{1,0:T(8,128)(2,1)}, bf16[2816,128]{1,0:T(8,128)(2,1)}, u32[]{:S(2)}, u32[]{:S(2)}) collective-permute-start(bf16[2816,128]{1,0:T(8,128)(2,1)} %get-tuple-element.330), channel_id=1, source_target_pairs={{0,8},{8,0},{16,24},{24,16},{1,9},{9,1},{17,25},{25,17},{2,10},{10... | collective-permute-start | bytes 2162696 | tf_op jit(solution)/shard_map/ppermute | solution.py:708
  401.4 28.1 %collective-permute-start.35 = (bf16[2816,128]{1,0:T(8,128)(2,1)}, bf16[2816,128]{1,0:T(8,128)(2,1)}, u32[]{:S(2)}, u32[]{:S(2)}) collective-permute-start(bf16[2816,128]{1,0:T(8,128)(2,1)} %get-tuple-element.331.refs_2_), channel_id=1, source_target_pairs={{8,16},{16,8},{9,17},{17,9},{10,18},{18,10},{11,19},{19,11},{12,20... | collective-permute-start | bytes 2162696 | tf_op jit(solution)/shard_map/ppermute | solution.py:710
  414.2 33.8 %all-to-all-start.9 = ((bf16[4,128,2048]{2,1,0:T(8,128)(2,1)}), bf16[4,128,2048]{2,1,0:T(8,128)(2,1)}, u32[]{:S(2)}, u32[]{:S(2)}) async-start(bf16[4,128,2048]{2,1,0:T(8,128)(2,1)} %bitcast.92), calls=%async_computation.9 | async-start | bytes 4194304 | tf_op jit(solution)/shard_map/all_to_all | solution.py:653
  429.5 18.5 %collective-permute-start.37 = (bf16[2816,128]{1,0:T(8,128)(2,1)S(1)}, bf16[2816,128]{1,0:T(8,128)(2,1)S(1)}, u32[]{:S(2)}, u32[]{:S(2)}) collective-permute-start(bf16[2816,128]{1,0:T(8,128)(2,1)S(1)} %copy-done.2), channel_id=1, source_target_pairs={{0,8},{8,0},{16,24},{24,16},{1,9},{9,1},{17,25},{25,17},{2,10},{10... | collective-permute-start | bytes 2162696 | tf_op jit(solution)/shard_map/ppermute | solution.py:708
  448.0 20.7 %all-to-all-start.10 = ((bf16[4,1280,128]{2,1,0:T(8,128)(2,1)}), bf16[4,1280,128]{2,1,0:T(8,128)(2,1)S(1)}, u32[]{:S(2)}, u32[]{:S(2)}) async-start(bf16[4,1280,128]{2,1,0:T(8,128)(2,1)} %add.128), calls=%async_computation.10 | async-start | bytes 2621440 | tf_op jit(solution)/shard_map/all_to_all | solution.py:653
  456.8 31.6 %collective-permute-start.39 = (bf16[2816,128]{1,0:T(8,128)(2,1)}, bf16[2816,128]{1,0:T(8,128)(2,1)}, u32[]{:S(2)}, u32[]{:S(2)}) collective-permute-start(bf16[2816,128]{1,0:T(8,128)(2,1)} %get-tuple-element.348), channel_id=1, source_target_pairs={{0,8},{8,0},{16,24},{24,16},{1,9},{9,1},{17,25},{25,17},{2,10},{10... | collective-permute-start | bytes 2162696 | tf_op jit(solution)/shard_map/ppermute | solution.py:708
  464.0 24.5 %collective-permute-start.40 = (bf16[2816,128]{1,0:T(8,128)(2,1)}, bf16[2816,128]{1,0:T(8,128)(2,1)}, u32[]{:S(2)}, u32[]{:S(2)}) collective-permute-start(bf16[2816,128]{1,0:T(8,128)(2,1)} %get-tuple-element.349.refs_2_), channel_id=1, source_target_pairs={{8,16},{16,8},{9,17},{17,9},{10,18},{18,10},{11,19},{19,11},{12,20... | collective-permute-start | bytes 2162696 | tf_op jit(solution)/shard_map/ppermute | solution.py:710
  465.5 23.8 %collective-permute-start.42 = (bf16[2,2048,128]{2,1,0:T(8,128)(2,1)}, bf16[2,2048,128]{2,1,0:T(8,128)(2,1)}, u32[]{:S(2)}, u32[]{:S(2)}) collective-permute-start(bf16[2,2048,128]{2,1,0:T(8,128)(2,1)} %get-tuple-element.354), channel_id=1, source_target_pairs={{0,1},{1,0},{2,3},{3,2},{4,5},{5,4},{6,7},{7,6},{8,9},{9,8},{10,11... | collective-permute-start | bytes 3145736 | tf_op jit(solution)/shard_map/ppermute | solution.py:662
  468.7 57.0 %all-to-all-start.6 = ((bf16[4,128,2048]{2,1,0:T(8,128)(2,1)}), bf16[4,128,2048]{2,1,0:T(8,128)(2,1)S(1)}, u32[]{:S(2)}, u32[]{:S(2)}) async-start(bf16[4,128,2048]{2,1,0:T(8,128)(2,1)} %bitcast.90), calls=%async_computation.6 | async-start | bytes 4194304 | tf_op jit(solution)/shard_map/all_to_all | solution.py:653
  476.1 24.8 %collective-permute-start.43 = (bf16[2816,128]{1,0:T(8,128)(2,1)}, bf16[2816,128]{1,0:T(8,128)(2,1)}, u32[]{:S(2)}, u32[]{:S(2)}) collective-permute-start(bf16[2816,128]{1,0:T(8,128)(2,1)} %get-tuple-element.357), channel_id=1, source_target_pairs={{0,8},{8,0},{16,24},{24,16},{1,9},{9,1},{17,25},{25,17},{2,10},{10... | collective-permute-start | bytes 2162696 | tf_op jit(solution)/shard_map/ppermute | solution.py:708
  482.9 18.0 %collective-permute-start.44 = (bf16[2816,128]{1,0:T(8,128)(2,1)}, bf16[2816,128]{1,0:T(8,128)(2,1)}, u32[]{:S(2)}, u32[]{:S(2)}) collective-permute-start(bf16[2816,128]{1,0:T(8,128)(2,1)} %get-tuple-element.358.refs_2_), channel_id=1, source_target_pairs={{8,16},{16,8},{9,17},{17,9},{10,18},{18,10},{11,19},{19,11},{12,20... | collective-permute-start | bytes 2162696 | tf_op jit(solution)/shard_map/ppermute | solution.py:710
  496.5 19.6 %collective-permute-start.52 = (bf16[2816,128]{1,0:T(8,128)(2,1)}, bf16[2816,128]{1,0:T(8,128)(2,1)}, u32[]{:S(2)}, u32[]{:S(2)}) collective-permute-start(bf16[2816,128]{1,0:T(8,128)(2,1)} %get-tuple-element.381), channel_id=1, source_target_pairs={{0,8},{8,0},{16,24},{24,16},{1,9},{9,1},{17,25},{25,17},{2,10},{10... | collective-permute-start | bytes 2162696 | tf_op jit(solution)/shard_map/ppermute | solution.py:708
  498.7 17.3 %collective-permute-start.53 = (bf16[2816,128]{1,0:T(8,128)(2,1)}, bf16[2816,128]{1,0:T(8,128)(2,1)}, u32[]{:S(2)}, u32[]{:S(2)}) collective-permute-start(bf16[2816,128]{1,0:T(8,128)(2,1)} %get-tuple-element.382.refs_2_), channel_id=1, source_target_pairs={{8,16},{16,8},{9,17},{17,9},{10,18},{18,10},{11,19},{19,11},{12,20... | collective-permute-start | bytes 2162696 | tf_op jit(solution)/shard_map/ppermute | solution.py:710
  505.2 26.2 %collective-permute-start.45 = (bf16[2816,128]{1,0:T(8,128)(2,1)}, bf16[2816,128]{1,0:T(8,128)(2,1)}, u32[]{:S(2)}, u32[]{:S(2)}) collective-permute-start(bf16[2816,128]{1,0:T(8,128)(2,1)} %get-tuple-element.363), channel_id=1, source_target_pairs={{0,8},{8,0},{16,24},{24,16},{1,9},{9,1},{17,25},{25,17},{2,10},{10... | collective-permute-start | bytes 2162696 | tf_op jit(solution)/shard_map/ppermute | solution.py:708
  507.1 24.4 %collective-permute-start.46 = (bf16[2816,128]{1,0:T(8,128)(2,1)}, bf16[2816,128]{1,0:T(8,128)(2,1)}, u32[]{:S(2)}, u32[]{:S(2)}) collective-permute-start(bf16[2816,128]{1,0:T(8,128)(2,1)} %get-tuple-element.364.refs_2_), channel_id=1, source_target_pairs={{8,16},{16,8},{9,17},{17,9},{10,18},{18,10},{11,19},{19,11},{12,20... | collective-permute-start | bytes 2162696 | tf_op jit(solution)/shard_map/ppermute | solution.py:710
  520.3 26.6 %collective-permute-start.54 = (bf16[2816,128]{1,0:T(8,128)(2,1)}, bf16[2816,128]{1,0:T(8,128)(2,1)}, u32[]{:S(2)}, u32[]{:S(2)}) collective-permute-start(bf16[2816,128]{1,0:T(8,128)(2,1)} %get-tuple-element.387), channel_id=1, source_target_pairs={{0,8},{8,0},{16,24},{24,16},{1,9},{9,1},{17,25},{25,17},{2,10},{10... | collective-permute-start | bytes 2162696 | tf_op jit(solution)/shard_map/ppermute | solution.py:708
  524.1 22.8 %collective-permute-start.55 = (bf16[2816,128]{1,0:T(8,128)(2,1)}, bf16[2816,128]{1,0:T(8,128)(2,1)}, u32[]{:S(2)}, u32[]{:S(2)}) collective-permute-start(bf16[2816,128]{1,0:T(8,128)(2,1)} %get-tuple-element.388.refs_2_), channel_id=1, source_target_pairs={{8,16},{16,8},{9,17},{17,9},{10,18},{18,10},{11,19},{19,11},{12,20... | collective-permute-start | bytes 2162696 | tf_op jit(solution)/shard_map/ppermute | solution.py:710
  535.8 26.6 %collective-permute-start.47 = (bf16[2816,128]{1,0:T(8,128)(2,1)}, bf16[2816,128]{1,0:T(8,128)(2,1)}, u32[]{:S(2)}, u32[]{:S(2)}) collective-permute-start(bf16[2816,128]{1,0:T(8,128)(2,1)} %get-tuple-element.373), channel_id=1, source_target_pairs={{0,8},{8,0},{16,24},{24,16},{1,9},{9,1},{17,25},{25,17},{2,10},{10... | collective-permute-start | bytes 2162696 | tf_op jit(solution)/shard_map/ppermute | solution.py:708
  539.6 22.8 %collective-permute-start.48 = (bf16[2816,128]{1,0:T(8,128)(2,1)}, bf16[2816,128]{1,0:T(8,128)(2,1)}, u32[]{:S(2)}, u32[]{:S(2)}) collective-permute-start(bf16[2816,128]{1,0:T(8,128)(2,1)} %get-tuple-element.374.refs_2_), channel_id=1, source_target_pairs={{8,16},{16,8},{9,17},{17,9},{10,18},{18,10},{11,19},{19,11},{12,20... | collective-permute-start | bytes 2162696 | tf_op jit(solution)/shard_map/ppermute | solution.py:710
  551.1 42.3 %collective-permute-start.56 = (bf16[2816,128]{1,0:T(8,128)(2,1)}, bf16[2816,128]{1,0:T(8,128)(2,1)}, u32[]{:S(2)}, u32[]{:S(2)}) collective-permute-start(bf16[2816,128]{1,0:T(8,128)(2,1)} %get-tuple-element.393), channel_id=1, source_target_pairs={{0,8},{8,0},{16,24},{24,16},{1,9},{9,1},{17,25},{25,17},{2,10},{10... | collective-permute-start | bytes 2162696 | tf_op jit(solution)/shard_map/ppermute | solution.py:708
  566.5 36.3 %collective-permute-start.61 = (bf16[2816,128]{1,0:T(8,128)(2,1)}, bf16[2816,128]{1,0:T(8,128)(2,1)}, u32[]{:S(2)}, u32[]{:S(2)}) collective-permute-start(bf16[2816,128]{1,0:T(8,128)(2,1)} %get-tuple-element.407), channel_id=1, source_target_pairs={{0,8},{8,0},{16,24},{24,16},{1,9},{9,1},{17,25},{25,17},{2,10},{10... | collective-permute-start | bytes 2162696 | tf_op jit(solution)/shard_map/ppermute | solution.py:708
  570.0 23.4 %collective-permute-start.57 = (bf16[2048,128]{1,0:T(8,128)(2,1)}, bf16[2048,128]{1,0:T(8,128)(2,1)}, u32[]{:S(2)}, u32[]{:S(2)}) collective-permute-start(bf16[2048,128]{1,0:T(8,128)(2,1)} %get-tuple-element.394.refs_2_), channel_id=1, source_target_pairs={{8,16},{16,8},{9,17},{17,9},{10,18},{18,10},{11,19},{19,11},{12,20... | collective-permute-start | bytes 1572872 | tf_op jit(solution)/shard_map/ppermute | solution.py:710
  571.4 31.4 %collective-permute-start.62 = (bf16[2048,128]{1,0:T(8,128)(2,1)}, bf16[2048,128]{1,0:T(8,128)(2,1)}, u32[]{:S(2)}, u32[]{:S(2)}) collective-permute-start(bf16[2048,128]{1,0:T(8,128)(2,1)} %get-tuple-element.408.refs_2_), channel_id=1, source_target_pairs={{8,16},{16,8},{9,17},{17,9},{10,18},{18,10},{11,19},{19,11},{12,20... | collective-permute-start | bytes 1572872 | tf_op jit(solution)/shard_map/ppermute | solution.py:710
  572.9 19.4 %collective-permute-start.49 = (f32[2,256]{1,0:T(2,128)S(1)}, f32[2,256]{1,0:T(2,128)S(1)}, u32[]{:S(2)}, u32[]{:S(2)}) collective-permute-start(f32[2,256]{1,0:T(2,128)S(1)} %reduce_sum.27), channel_id=1, source_target_pairs={{0,8},{24,16},{1,9},{25,17},{2,10},{26,18},{3,11},{27,19},{4,12},{... | collective-permute-start | bytes 6152 | tf_op jit(solution)/shard_map/ppermute | solution.py:819
  596.8 20.0 %collective-permute-start.58 = (bf16[2048,128]{1,0:T(8,128)(2,1)}, bf16[2048,128]{1,0:T(8,128)(2,1)}, u32[]{:S(2)}, u32[]{:S(2)}) collective-permute-start(bf16[2048,128]{1,0:T(8,128)(2,1)} %get-tuple-element.398.refs_3_), channel_id=1, source_target_pairs={{0,8},{8,0},{16,24},{24,16},{1,9},{9,1},{17,25},{25,17},{2,10},{10... | collective-permute-start | bytes 1572872 | tf_op jit(solution)/shard_map/ppermute | solution.py:708
  606.2 19.0 %collective-permute-start.63 = (bf16[2048,128]{1,0:T(8,128)(2,1)}, bf16[2048,128]{1,0:T(8,128)(2,1)}, u32[]{:S(2)}, u32[]{:S(2)}) collective-permute-start(bf16[2048,128]{1,0:T(8,128)(2,1)} %get-tuple-element.412.refs_3_), channel_id=1, source_target_pairs={{0,8},{8,0},{16,24},{24,16},{1,9},{9,1},{17,25},{25,17},{2,10},{10... | collective-permute-start | bytes 1572872 | tf_op jit(solution)/shard_map/ppermute | solution.py:708
  620.6 19.4 %collective-permute-start.60 = (bf16[2560,128]{1,0:T(8,128)(2,1)}, bf16[2560,128]{1,0:T(8,128)(2,1)S(1)}, u32[]{:S(2)}, u32[]{:S(2)}) collective-permute-start(bf16[2560,128]{1,0:T(8,128)(2,1)} %get-tuple-element.402.refs_1_), channel_id=1, source_target_pairs={{0,8},{8,0},{16,24},{24,16},{1,9},{9,1},{17,25},{25,17},{2,10},{10... | collective-permute-start | bytes 1966088 | tf_op jit(solution)/shard_map/ppermute | solution.py:708
  628.1 23.8 %collective-permute-start.65 = (bf16[2560,128]{1,0:T(8,128)(2,1)}, bf16[2560,128]{1,0:T(8,128)(2,1)S(1)}, u32[]{:S(2)}, u32[]{:S(2)}) collective-permute-start(bf16[2560,128]{1,0:T(8,128)(2,1)} %get-tuple-element.416.refs_1_), channel_id=1, source_target_pairs={{0,8},{8,0},{16,24},{24,16},{1,9},{9,1},{17,25},{25,17},{2,10},{10... | collective-permute-start | bytes 1966088 | tf_op jit(solution)/shard_map/ppermute | solution.py:708
  (48 other events, 454.3 us)

commit v3 on v2

--- a/solution.py
+++ b/solution.py
@@ -15,6 +15,7 @@
 NORM_EPS = 1e-05
 ROPE_BASE = 10000.0
 MASK_FILL = -1e30
+TILE = 512
 F32 = jnp.float32
 BF16 = jnp.bfloat16
 
@@ -178,8 +179,8 @@
     )(ids, cos_table, sin_table, near, far, *x_blocks)
 
 
-def attention_mask(s_ref, l_ref, rows, own):
-    core, rep, block = s_ref[1], s_ref[4], pl.program_id(0)
+def attention_mask(s_ref, l_ref, rows, block):
+    core, rep, span = s_ref[1], s_ref[4], (block + 1) * rows
 
     def coded(pos):
         bound, code = 0, jnp.zeros(pos.shape, jnp.int32)
@@ -189,56 +190,58 @@
         return jnp.where(code < DOCS - 1, code, 1000 + pos)
 
     q_pos = (2 * block + core) * rows + lax.broadcasted_iota(jnp.int32, (rows, 1), 0)
-    index = lax.broadcasted_iota(jnp.int32, (1, 2 * own), 1)
-    side = jnp.where(index < own, core, 1 - core)
-    index = jnp.where(index < own, index, index - own)
+    index = lax.broadcasted_iota(jnp.int32, (1, 2 * span), 1)
+    side = jnp.where(index < span, core, 1 - core)
+    index = jnp.where(index < span, index, index - span)
     k_pos = (2 * (index // rows) + side) * rows + index % rows
     q_code = coded(q_pos)
     allowed = (coded(k_pos) == q_code) & (k_pos <= q_pos)
     return jnp.where(allowed, 0.0, MASK_FILL), jnp.where(q_code < DOCS, 1.0, 0.0)
 
 
-def attention_forward(ids, lengths, q, kv_own, kv_other, rows):
+def attention_forward(ids, lengths, q, kv_own, kv_other, rows, stack=4):
     own, qw = q.shape
+    scale = 1.0 / math.sqrt(HD)
     heads = qw // HD
-    scale = 1.0 / math.sqrt(HD)
+    stack = min(stack, heads)
 
     def body(s_ref, d_ref, q_ref, a_ref, b_ref, o_ref, l_ref):
-        bias, valid = attention_mask(s_ref, d_ref, rows, own)
-        lane = lax.broadcasted_iota(jnp.int32, (rows, 128), 1)
-        k_a, v_a = a_ref[:, :HD], a_ref[:, HD:]
-        k_b, v_b = b_ref[:, :HD], b_ref[:, HD:]
-        sums = jnp.zeros((rows, 128), F32)
-        pair = []
-        for h in range(heads):
-            qh = q_ref[:, h * HD : (h + 1) * HD] * jnp.asarray(scale, BF16)
-            s = jnp.concatenate([dot_nt(qh, k_a), dot_nt(qh, k_b)], axis=1) + bias
-            top = jnp.max(s, axis=-1, keepdims=True)
-            p = jnp.exp(s - top)
-            tot = jnp.sum(p, axis=-1, keepdims=True)
-            p = (p * (1.0 / tot)).astype(BF16)
-            mixed = dot(p[:, :own], v_a) + dot(p[:, own:], v_b)
-            pair.append((mixed * valid).astype(BF16))
-            sums = jnp.where(lane == h, top + jnp.log(tot), sums)
-            if h % 2:
-                o_ref[:, (h - 1) * HD : (h + 1) * HD] = jnp.concatenate(pair, axis=1)
-                pair = []
-        l_ref[...] = sums
-
+        for block in range(own // rows):
+
+            @pl.when(pl.program_id(0) == block)
+            def _(block=block):
+                span = (block + 1) * rows
+                bias, valid = attention_mask(s_ref, d_ref, rows, block)
+                lane = lax.broadcasted_iota(jnp.int32, (rows, 128), 1)
+                sums = jnp.zeros((rows, 128), F32)
+                keys = jnp.concatenate([a_ref[:span, :], b_ref[:span, :]], axis=0)
+                k, v = keys[:, :HD], keys[:, HD:]
+                for g in range(heads // stack):
+                    qs = [q_ref[:, h * HD : (h + 1) * HD] for h in range(g * stack, (g + 1) * stack)]
+                    qs = jnp.concatenate(qs, axis=0) * jnp.asarray(scale, BF16)
+                    s = dot_nt(qs, k).reshape(stack, rows, 2 * span) + bias[None]
+                    top = jnp.max(s, axis=-1, keepdims=True)
+                    p = jnp.exp(s - top)
+                    tot = jnp.sum(p, axis=-1, keepdims=True)
+                    p = (p * (1.0 / tot)).astype(BF16).reshape(stack * rows, 2 * span)
+                    o = dot(p, v).reshape(stack, rows, HD) * valid[None]
+                    o = o.astype(BF16)
+                    lse = top + jnp.log(tot)
+                    for t in range(stack):
+                        h = g * stack + t
+                        sums = jnp.where(lane == h, lse[t], sums)
+                        if t % 2:
+                            pair = jnp.concatenate([o[t - 1], o[t]], axis=1)
+                            o_ref[:, (h - 1) * HD : (h + 1) * HD] = pair
+                l_ref[...] = sums
+
+    blocked = lambda i: (i, 0)
+    fixed = pl.BlockSpec((own, 2 * HD), lambda i: (0, 0))
     return pl.pallas_call(
         body,
         grid=(own // rows,),
-        in_specs=[
-            scalars(),
-            scalars(),
-            pl.BlockSpec((rows, qw), lambda i: (i, 0)),
-            pl.BlockSpec((own, 2 * HD), lambda i: (0, 0)),
-            pl.BlockSpec((own, 2 * HD), lambda i: (0, 0)),
-        ],
-        out_specs=[
-            pl.BlockSpec((rows, qw), lambda i: (i, 0)),
-            pl.BlockSpec((rows, 128), lambda i: (i, 0)),
-        ],
+        in_specs=[scalars(), scalars(), pl.BlockSpec((rows, qw), blocked), fixed, fixed],
+        out_specs=[pl.BlockSpec((rows, qw), blocked), pl.BlockSpec((rows, 128), blocked)],
         out_shape=[
             jax.ShapeDtypeStruct((own, qw), BF16),
             jax.ShapeDtypeStruct((own, 128), F32),
@@ -249,12 +252,13 @@
 
 
 def attention_backward(
-    ids, lengths, q, kv_own, kv_other, sums, d_out, cos_table, sin_table, rows
+    ids, lengths, q, kv_own, kv_other, sums, d_out, cos_table, sin_table, rows, stack=2
 ):
     own, qw = q.shape
+    scale = 1.0 / math.sqrt(HD)
     heads = qw // HD
-    scale = 1.0 / math.sqrt(HD)
-    seq_len = 2 * own
+    stack = min(stack, heads)
+    blocks = own // rows
 
     def body(
         s_ref, n_ref, q_ref, a_ref, b_ref, l_ref, d_ref, cos_ref, sin_ref, dq_ref, dkv_ref,
@@ -263,57 +267,133 @@
         def _():
             dkv_ref[...] = jnp.zeros_like(dkv_ref)
 
-        bias, valid = attention_mask(s_ref, n_ref, rows, own)
-        valid = valid.astype(BF16)
-        k_a, v_a = a_ref[:, :HD], a_ref[:, HD:]
-        k_b, v_b = b_ref[:, :HD], b_ref[:, HD:]
-        cos, sin = cos_ref[...], sin_ref[...]
-        pair = []
-        dk = jnp.zeros((seq_len, HD), F32)
-        dv = jnp.zeros((seq_len, HD), F32)
-        for h in range(heads):
-            qh = q_ref[:, h * HD : (h + 1) * HD] * jnp.asarray(scale, BF16)
-            dh = d_ref[:, h * HD : (h + 1) * HD] * valid
-            s = jnp.concatenate([dot_nt(qh, k_a), dot_nt(qh, k_b)], axis=1) + bias
-            p = jnp.exp(s - l_ref[:, h : h + 1])
-            dp = jnp.concatenate([dot_nt(dh, v_a), dot_nt(dh, v_b)], axis=1)
-            inner = jnp.sum(p * dp, axis=-1, keepdims=True)
-            ds = (p * (dp - inner)).astype(BF16)
-            dq = (dot(ds[:, :own], k_a) + dot(ds[:, own:], k_b)) * scale
-            dk = dk + dot_tn(ds, qh)
-            dv = dv + dot_tn(p.astype(BF16), dh)
-            pair.append(dq)
-            if h % 2:
-                v = jnp.concatenate(pair, axis=1)
-                dq_ref[:, (h - 1) * HD : (h + 1) * HD] = (v * cos - turned(v) * sin).astype(BF16)
-                pair = []
-        dkv_ref[...] += jnp.concatenate([dk, dv], axis=1)
-
-    return pl.pallas_call(
-        body,
-        grid=(own // rows,),
-        in_specs=[
-            scalars(),
-            scalars(),
-            pl.BlockSpec((rows, qw), lambda i: (i, 0)),
-            pl.BlockSpec((own, 2 * HD), lambda i: (0, 0)),
-            pl.BlockSpec((own, 2 * HD), lambda i: (0, 0)),
-            pl.BlockSpec((rows, 128), lambda i: (i, 0)),
-            pl.BlockSpec((rows, qw), lambda i: (i, 0)),
-            pl.BlockSpec((rows, 128), lambda i: (i, 0)),
-            pl.BlockSpec((rows, 128), lambda i: (i, 0)),
-        ],
-        out_specs=[
-            pl.BlockSpec((rows, qw), lambda i: (i, 0)),
-            pl.BlockSpec((seq_len, 2 * HD), lambda i: (0, 0)),
-        ],
+        for block in range(blocks):
+
+            @pl.when(pl.program_id(0) == block)
+            def _(block=block):
+                span = (block + 1) * rows
+                bias, valid = attention_mask(s_ref, n_ref, rows, block)
+                valid = valid.astype(BF16)
+                cos, sin = cos_ref[...], sin_ref[...]
+                keys = jnp.concatenate([a_ref[:span, :], b_ref[:span, :]], axis=0)
+                k, v = keys[:, :HD], keys[:, HD:]
+                dk, dv = 0.0, 0.0
+                for g in range(heads // stack):
+                    part = range(g * stack, (g + 1) * stack)
+                    qs = [q_ref[:, h * HD : (h + 1) * HD] for h in part]
+                    qs = jnp.concatenate(qs, axis=0) * jnp.asarray(scale, BF16)
+                    ds = [d_ref[:, h * HD : (h + 1) * HD] * valid for h in part]
+                    ds = jnp.concatenate(ds, axis=0)
+                    lse = jnp.stack([l_ref[:, h : h + 1] for h in part])
+                    s = dot_nt(qs, k).reshape(stack, rows, 2 * span) + bias[None]
+                    p = jnp.exp(s - lse)
+                    dp = dot_nt(ds, v).reshape(stack, rows, 2 * span)
+                    inner = jnp.sum(p * dp, axis=-1, keepdims=True)
+                    grad = (p * (dp - inner)).astype(BF16).reshape(stack * rows, 2 * span)
+                    p = p.astype(BF16).reshape(stack * rows, 2 * span)
+                    dq = (dot(grad, k) * scale).reshape(stack, rows, HD)
+                    dk = dk + dot_tn(grad, qs)
+                    dv = dv + dot_tn(p, ds)
+                    for t in range(1, stack, 2):
+                        h = g * stack + t
+                        w = jnp.concatenate([dq[t - 1], dq[t]], axis=1)
+                        w = w * cos - turned(w) * sin
+                        dq_ref[:, (h - 1) * HD : (h + 1) * HD] = w.astype(BF16)
+                both = jnp.concatenate([dk, dv], axis=1)
+                dkv_ref[:span, :] += both[:span]
+                dkv_ref[own : own + span, :] += both[span:]
+
+    blocked = lambda i: (i, 0)
+    fixed = pl.BlockSpec((own, 2 * HD), lambda i: (0, 0))
+    table = pl.BlockSpec((rows, 128), blocked)
+    wide = pl.BlockSpec((rows, qw), blocked)
+    return pl.pallas_call(
+        body,
+        grid=(blocks,),
+        in_specs=[scalars(), scalars(), wide, fixed, fixed, table, wide, table, table],
+        out_specs=[wide, pl.BlockSpec((2 * own, 2 * HD), lambda i: (0, 0))],
         out_shape=[
             jax.ShapeDtypeStruct((own, qw), BF16),
-            jax.ShapeDtypeStruct((seq_len, 2 * HD), F32),
+            jax.ShapeDtypeStruct((2 * own, 2 * HD), F32),
         ],
         cost_estimate=tiny(),
         name="attention_backward",
     )(ids, lengths, q, kv_own, kv_other, sums, d_out, cos_table, sin_table)
+
+
+def feed_forward(ids, z_blocks, cot, weights, w_down):
+    rows, model = z_blocks[0].shape
+    chips = len(z_blocks)
+    part, width = weights[0][0].shape[1:]
+    own, tile = rows * chips, min(TILE, width)
+    turns = pl.cdiv(width, tile)
+
+    def body(s_ref, *refs):
+        z_refs, c_ref, w_refs = refs[:chips], refs[chips], refs[chips + 1 : chips + 9]
+        d_ref, m_ref, dg_ref, du_ref, z_ref, b_ref, w_ref, acc_ref = refs[chips + 9 :]
+        chip, core, half = s_ref[0], s_ref[1], s_ref[2]
+        turn = pl.program_id(0)
+
+        @pl.when(turn == 0)
+        def _():
+            for k in range(chips):
+                at = pl.multiple_of((chip ^ k) * rows, rows)
+                z_ref[pl.ds(at, rows), :] = z_refs[k][...]
+
+        def work(cols, first, last):
+            for m in range(2):
+                for i in range(4):
+                    side = core if i < 2 else 1 - core
+                    piece = half if i % 2 == 0 else 1 - half
+                    for j in range(chips):
+                        at = pl.multiple_of((2 * (2 * j + side) + piece) * part, part)
+                        w_ref[m, pl.ds(at, part), :cols] = w_refs[4 * m + i][j, :, :cols]
+            gate = dot(z_ref[...], w_ref[0, :, :cols])
+            up = dot(z_ref[...], w_ref[1, :, :cols])
+            dm = dot_nt(c_ref[...], d_ref[:cols, :])
+            sig = 1.0 / (1.0 + jnp.exp(-gate))
+            silu = gate * sig
+            m_ref[:, :cols] = (silu * up).astype(BF16)
+            dg = (dm * up * sig * (1.0 + gate * (1.0 - sig))).astype(BF16)
+            du = (dm * silu).astype(BF16)
+            dg_ref[:, :cols] = dg
+            du_ref[:, :cols] = du
+            back = dot_nt(dg, w_ref[0, :, :cols]) + dot_nt(du, w_ref[1, :, :cols])
+            if not first:
+                back = back + acc_ref[...]
+            if last:
+                b_ref[...] = back.astype(BF16)
+            else:
+                acc_ref[...] = back
+
+        for n in range(turns):
+
+            @pl.when(turn == n)
+            def _(n=n):
+                work(min(tile, width - n * tile), n == 0, n == turns - 1)
+
+    joined = pl.BlockSpec((own, model), lambda n, s: (0, 0))
+    out_tile = pl.BlockSpec((own, tile), lambda n, s: (0, n))
+    return pl.pallas_call(
+        body,
+        grid_spec=pltpu.PrefetchScalarGridSpec(
+            num_scalar_prefetch=1,
+            grid=(turns,),
+            in_specs=[pl.BlockSpec((rows, model), lambda n, s: (0, 0))] * chips
+            + [joined]
+            + [pl.BlockSpec((chips, part, tile), lambda n, s: (0, 0, n))] * 8
+            + [pl.BlockSpec((tile, model), lambda n, s: (n, 0))],
+            out_specs=[out_tile] * 3 + [joined] * 2,
+            scratch_shapes=[
+                pltpu.VMEM((2, model, tile), BF16),
+                pltpu.VMEM((own, model), F32),
+            ],
+        ),
+        out_shape=[jax.ShapeDtypeStruct((own, width), BF16)] * 3
+        + [jax.ShapeDtypeStruct((own, model), BF16)] * 2,
+        cost_estimate=tiny(),
+        name="feed_forward",
+    )(ids, *z_blocks, cot, *weights[0], *weights[1], w_down)
 
 
 def out_proj(ids, attn, near, far, chips):
@@ -397,62 +477,6 @@
     )(base, y, parts)
 
 
-def feed_forward(ids, z_blocks, cot, weights, w_down):
-    rows, model = z_blocks[0].shape
-    chips = len(z_blocks)
-    part, width = weights[0][0].shape[1:]
-    own, tile = rows * chips, 256
-
-    def body(s_ref, *refs):
-        z_refs, c_ref, w_refs = refs[:chips], refs[chips], refs[chips + 1 : chips + 9]
-        d_ref, m_ref, dg_ref, du_ref, z_ref, g_ref, u_ref = refs[chips + 9 :]
-        chip, core, half = s_ref[0], s_ref[1], s_ref[2]
-
-        @pl.when(pl.program_id(0) == 0)
-        def _():
-            for k in range(chips):
-                at = pl.multiple_of((chip ^ k) * rows, rows)
-                z_ref[pl.ds(at, rows), :] = z_refs[k][...]
-
-        for w, out in ((w_refs[:4], g_ref), (w_refs[4:], u_ref)):
-            for i in range(4):
-                side = core if i < 2 else 1 - core
-                piece = half if i % 2 == 0 else 1 - half
-                for j in range(chips):
-                    at = pl.multiple_of((2 * (2 * j + side) + piece) * part, part)
-                    out[pl.ds(at, part), :] = w[i][j]
-        gate = dot(z_ref[...], g_ref[...])
-        up = dot(z_ref[...], u_ref[...])
-        sig = 1.0 / (1.0 + jnp.exp(-gate))
-        silu = gate * sig
-        m_ref[...] = (silu * up).astype(BF16)
-        dm = dot_nt(c_ref[...], d_ref[...])
-        dg_ref[...] = (dm * up * sig * (1.0 + gate * (1.0 - sig))).astype(BF16)
-        du_ref[...] = (dm * silu).astype(BF16)
-
-    joined = pl.BlockSpec((own, model), lambda n, s: (0, 0))
-    out_tile = pl.BlockSpec((own, tile), lambda n, s: (0, n))
-    return pl.pallas_call(
-        body,
-        grid_spec=pltpu.PrefetchScalarGridSpec(
-            num_scalar_prefetch=1,
-            grid=(pl.cdiv(width, tile),),
-            in_specs=[pl.BlockSpec((rows, model), lambda n, s: (0, 0))] * chips
-            + [joined]
-            + [pl.BlockSpec((chips, part, tile), lambda n, s: (0, 0, n))] * 8
-            + [pl.BlockSpec((tile, model), lambda n, s: (n, 0))],
-            out_specs=[out_tile] * 3
-            + [joined]
-            + [pl.BlockSpec((model, tile), lambda n, s: (0, n))] * 2,
-        ),
-        out_shape=[jax.ShapeDtypeStruct((own, width), BF16)] * 3
-        + [jax.ShapeDtypeStruct((own, model), BF16)]
-        + [jax.ShapeDtypeStruct((model, width), BF16)] * 2,
-        cost_estimate=tiny(),
-        name="feed_forward",
-    )(ids, *z_blocks, cot, *weights[0], *weights[1], w_down)
-
-
 def strips(value, ref, lead=()):
     rows, width = value.shape
     for t in range(pl.cdiv(width, 128)):
@@ -544,77 +568,127 @@
     )(ids, left, right)
 
 
-def beside(blocks, rows, width, scale=None):
+def chain_step(ids, own, outer, sent, inner, coming):
+    def size(v):
+        return 0 if v is None else v[0].shape[1] if isinstance(v, tuple) else v.shape[0]
+
+    ins = [own, outer if own is not None else None, sent, inner, coming]
+    have = [v is not None for v in ins]
+    sizes = [size(own), max(size(sent), size(coming))]
+
+    def body(s_ref, *refs):
+        refs = list(refs)
+        o_ref, x_ref, i_ref, y_ref, c_ref = [refs.pop(0) if h else None for h in have]
+        s_out, a_out = [refs.pop(0) if n else None for n in sizes]
+        ends = s_ref[3] == 1
+
+        def each(count, work):
+            step = math.gcd(512, count)
+
+            def turn(n, carry):
+                work(pl.ds(pl.multiple_of(n * step, step), step))
+                return carry
+
+            lax.fori_loop(0, count // step, turn, 0)
+
+        if s_out is not None:
+
+            def add_own(at):
+                s_out[at, :] = o_ref[at, :] + x_ref[at, :]
+
+            each(size(own), add_own)
+        if c_ref is not None:
+
+            @pl.when(ends)
+            def _():
+                def copy(at):
+                    a_out[at, :] = c_ref[at, :]
+
+                each(size(coming), copy)
+
+        if i_ref is not None:
+
+            @pl.when(jnp.logical_not(ends))
+            def _():
+                def add_sent(at):
+                    a_out[at, :] = i_ref[at, :] + y_ref[at, :]
+
+                each(size(sent), add_sent)
+
+    def spec(v):
+        if not isinstance(v, tuple):
+            return pl.BlockSpec(v.shape, lambda i: (0, 0))
+        block = v[1]
+        return pl.BlockSpec((pl.Squeezed(), *v[0].shape[1:]), lambda i: (block, 0, 0))
+
+    outs = pl.pallas_call(
+        body,
+        grid=(1,),
+        in_specs=[scalars()] + [spec(v) for v in ins if v is not None],
+        out_specs=[pl.BlockSpec((n, 128), lambda i: (0, 0)) for n in sizes if n],
+        out_shape=[jax.ShapeDtypeStruct((n, 128), BF16) for n in sizes if n],
+        cost_estimate=tiny(),
+        name="chain_step",
+    )(ids, *[v[0] if isinstance(v, tuple) else v for v in ins if v is not None])
+    outs = list(outs)
+    return [outs.pop(0) if n else None for n in sizes]
+
+
+def beside(ids, blocks, rows, width, scale=None):
     count = len(blocks)
     tiles = pl.cdiv(width, 128)
+    long = tiles * rows
     if scale is None:
         scale = jnp.ones((rows, 1), F32)
     if width % 128:
-        full = [b.reshape(tiles, rows, 128).transpose(1, 0, 2).reshape(rows, -1) for b in blocks]
+        full = [
+            a[:long].reshape(tiles, rows, 128).transpose(1, 0, 2).reshape(rows, -1)
+            for a, b in blocks
+        ]
         return jnp.concatenate([f[:, :width] for f in full], axis=1).astype(F32) * scale
 
-    def body(s_ref, *refs):
+    def body(c_ref, s_ref, *refs):
         scale, out_ref = s_ref[...], refs[-1]
         for k in range(count):
-
-            @pl.when(pl.program_id(0) == k)
-            def _():
-                for t in range(tiles):
-                    v = refs[k][t * rows : (t + 1) * rows, :].astype(F32)
-                    out_ref[:, t * 128 : (t + 1) * 128] = v * scale
-
+            for end in (0, 1):
+
+                @pl.when((pl.program_id(0) == k) & (c_ref[3] == end))
+                def _(ref=refs[2 * k + end]):
+                    for t in range(tiles):
+                        v = ref[t * rows : (t + 1) * rows, :].astype(F32)
+                        out_ref[:, t * 128 : (t + 1) * 128] = v * scale
+
+    return pl.pallas_call(
+        body,
+        grid_spec=pltpu.PrefetchScalarGridSpec(
+            num_scalar_prefetch=1,
+            grid=(count,),
+            in_specs=[pl.BlockSpec((rows, 1), lambda k, c: (0, 0))]
+            + [pl.BlockSpec((long, 128), lambda k, c: (0, 0))] * (2 * count),
+            out_specs=pl.BlockSpec((rows, width), lambda k, c: (0, k)),
+        ),
+        out_shape=jax.ShapeDtypeStruct((rows, count * width), F32),
+        cost_estimate=tiny(),
+        name="beside",
+    )(ids, scale, *[v for pair in blocks for v in pair])
+
+
+def pair_sum(near, far):
+    count, rows, lanes = near.shape
+
+    def body(a_ref, b_ref, out_ref):
+        out_ref[...] = a_ref[...] + b_ref[...]
+
+    spec = pl.BlockSpec((1, rows, lanes), lambda k: (k, 0, 0))
     return pl.pallas_call(
         body,
         grid=(count,),
-        in_specs=[pl.BlockSpec((rows, 1), lambda k: (0, 0))]
-        + [pl.BlockSpec((tiles * rows, 128), lambda k: (0, 0))] * count,
-        out_specs=pl.BlockSpec((rows, width), lambda k: (0, k)),
-        out_shape=jax.ShapeDtypeStruct((rows, count * width), F32),
-        cost_estimate=tiny(),
-        name="beside",
-    )(scale, *blocks)
-
-
-def chain_step(ids, own, outer, sent, inner, total, coming):
-    def size(v):
-        return 0 if v is None else v.shape[0]
-
-    ins = [own, outer, sent, inner, total, coming]
-    have = [v is not None for v in ins]
-    sizes = [size(own), size(sent), max(size(sent), size(coming)), size(total)]
-    wanted = [have[0], have[2], have[2] and have[5], have[4]]
-
-    def body(s_ref, *refs):
-        refs = list(refs)
-        o_ref, x_ref, i_ref, y_ref, t_ref, c_ref = [refs.pop(0) if h else None for h in have]
-        s_out, t_out, a_out, f_out = [refs.pop(0) if w else None for w in wanted]
-        ends = s_ref[3] == 1
-        if s_out is not None:
-            s_out[...] = (o_ref[...].astype(F32) + x_ref[: size(own)].astype(F32)).astype(BF16)
-        if t_out is not None:
-            t_out[...] = (i_ref[...].astype(F32) + y_ref[...].astype(F32)).astype(BF16)
-        if f_out is not None:
-            f_out[...] = jnp.where(ends, x_ref[: size(total)], t_ref[...])
-        if a_out is not None:
-
-            @pl.when(ends)
-            def _():
-                a_out[: size(coming)] = c_ref[...]
-
-            @pl.when(jnp.logical_not(ends))
-            def _():
-                a_out[: size(sent)] = t_out[...]
-
-    outs = pl.pallas_call(
-        body,
-        in_specs=[scalars()] + [whole()] * sum(have),
-        out_specs=[whole()] * sum(wanted),
-        out_shape=[jax.ShapeDtypeStruct((n, 128), BF16) for n, w in zip(sizes, wanted) if w],
-        cost_estimate=tiny(),
-        name="chain_step",
-    )(ids, *[v for v in ins if v is not None])
-    outs = list(outs)
-    return [outs.pop(0) if w else None for w in wanted]
+        in_specs=[spec] * 2,
+        out_specs=spec,
+        out_shape=jax.ShapeDtypeStruct(near.shape, BF16),
+        cost_estimate=tiny(),
+        name="pair_sum",
+    )(near, far)
 
 
 def local(
@@ -683,7 +757,8 @@
     def visit(*carry, new=None):
         if reps != 4:
             if new is not None:
-                sums_of[new[0]] = lax.psum(new[1], "rep")
+                value = lax.psum(new[1][new[2]], "rep")
+                sums_of[f"{new[0]}{new[2]}"] = (value, value)
             return carry if len(carry) != 1 else carry[0]
         line = lines[turn[0] % 2]
         turn[0] += 1
@@ -691,20 +766,20 @@
         tied = tie(tuple(carry) + tuple(v for v in extra if v is not None))
         carry, tied = tied[: len(carry)], list(tied[len(carry) :])
         outer, inner, coming = [None if v is None else tied.pop(0) for v in extra]
+        coming = None if new is None else (coming, new[2])
         value = lambda pair: None if pair is None else pair[1]
+        if line.total is not None:
+            sums_of[line.total[0]] = (line.total[1], outer)
+        own_sum = ahead = None
         if outer is None:
-            ahead = coming
-        else:
-            own_sum, middle, ahead, final = chain_step(
-                ids, value(line.own), outer, value(line.sent), inner, value(line.total), coming
+            ahead = None if coming is None else coming[0][coming[1]]
+        elif line.own is not None or line.sent is not None or coming is not None:
+            own_sum, ahead = chain_step(
+                ids, value(line.own), outer, value(line.sent), inner, coming
             )
-            if final is not None:
-                sums_of[line.total[0]] = final
-            line.total = None if middle is None else (line.sent[0], middle)
-            line.sent = None if own_sum is None else (line.own[0], own_sum)
-            if ahead is None:
-                ahead = coming if coming is not None else middle
-        line.own = None if coming is None else (new[0], coming)
+        line.total = None if line.sent is None else (line.sent[0], ahead)
+        line.sent = None if line.own is None else (line.own[0], own_sum)
+        line.own = None if coming is None else (f"{new[0]}{new[2]}", coming)
         line.outer = None if ahead is None else lax.ppermute(ahead, "rep", outer_pairs)
         line.inner = (
             None if line.sent is None else lax.ppermute(line.sent[1], "rep", [(1, 2), (2, 1)])
@@ -726,8 +801,8 @@
     gate_part, up_part = pick_half(w_gate, w_up, gain_two, ids, chips)
     w_out_far = swap(w_out)
     w_down_c = join_cores(ids, w_down, swap(w_down))
-    *x_blocks, qkv_near, cos_table, sin_table, gate_part, up_part, w_out_far, w_down_c = tie(
-        (*x_blocks, qkv_near, cos_table, sin_table, gate_part, up_part, w_out_far, w_down_c)
+    *x_blocks, cos_table, sin_table, gate_part, up_part, w_out_far, w_down_c = tie(
+        (*x_blocks, cos_table, sin_table, gate_part, up_part, w_out_far, w_down_c)
     )
     gate_near = exchange(gate_part)
     normed_one, queries, kv_near, w_qkv = qkv_kernel(
@@ -751,88 +826,90 @@
         [near, far, swap(near), swap(far)]
         for near, far in ((gate_near, gate_traded), (up_near, up_traded))
     ]
-    inner, grad_gate, grad_up, normed_two, w_gate_c, w_up_c = feed_forward(
+    inner, grad_gate, grad_up, normed_two, back = feed_forward(
         ids, z_blocks, cot_rows, weights, w_down_c
     )
 
+    parts = exchange(back)
     down_near, down_far = row_grad(ids, inner, cot_rows, 4)
     down_far = swap(down_far)
-    grad_gate, grad_up, down_near = tie((grad_gate, grad_up, down_near))
-    back = (dot_nt(grad_gate, w_gate_c) + dot_nt(grad_up, w_up_c)).astype(BF16)
-    back, down_near, down_far, grad_gate = tie((back, down_near, down_far, grad_gate))
-    parts = exchange(back)
-    down = [down_near[k] + down_far[k] for k in range(4)]
-    grad_gate = visit(grad_gate, new=("down0", down[0]))
+    grad_gate, down_near = tie((grad_gate, down_near))
     gate_near, gate_far = weight_grad(ids, normed_two, grad_gate, chips)
-    gate_near, gate_far, grad_up = visit(gate_near, gate_far, grad_up, new=("down1", down[1]))
+    gate_near, gate_far, down_far, grad_up = tie((gate_near, gate_far, down_far, grad_up))
     gate_far = swap(gate_far)
+    down = pair_sum(down_near, down_far)
+    grad_up = visit(grad_up, new=("down", down, 0))
     up_near, up_far = weight_grad(ids, normed_two, grad_up, chips)
-    up_near, up_far, parts = visit(up_near, up_far, parts, new=("down2", down[2]))
-    gate_part = exchange(gate_near + gate_far)
+    up_near, up_far, parts = visit(up_near, up_far, parts, new=("down", down, 1))
+    gate_part = exchange(pair_sum(gate_near, gate_far))
     up_far = swap(up_far)
     grad_resid, da, gain_two_local = residual_norm_back(cotangent, parts, resid, chips)
-    da, inner = visit(da, inner, new=("down3", down[3]))
+    da, inner = visit(da, inner, new=("down", down, 2))
     out = dot(inner, w_down_c).astype(BF16)
-    up_part = up_near + up_far
-    out, up_part, gate_part = visit(out, up_part, gate_part, new=None)
+    up_part = pair_sum(up_near, up_far)
+    out, up_part, gate_part = visit(out, up_part, gate_part, new=("down", down, 3))
     da = exchange(da)
-    da, up_part = visit(da, up_part, new=("gate0", gate_part[0]))
+    da, up_part = visit(da, up_part, new=("gate", gate_part, 0))
     up_part = exchange(up_part)
     dob = dot_nt(da, w_out_c).astype(BF16)
     out_near, out_far = row_grad(ids, attn, da, 2)
-    dob, out_near, out_far = visit(dob, out_near, out_far, new=("gate1", gate_part[1]))
+    dob, out_near, out_far = visit(dob, out_near, out_far, new=("gate", gate_part, 1))
     out_far = swap(out_far)
     dq, dkv = attention_backward(
         ids, doc_lengths, queries, kv_near, kv_far, sums, dob, cos_table, sin_table, rows
     )
-    dq, dkv = visit(dq, dkv, new=("gate2", gate_part[2]))
+    dq, dkv = visit(dq, dkv, new=("gate", gate_part, 2))
     dkv = dkv[:own] + swap(dkv[own:].astype(BF16)).astype(F32)
     half_turn = jnp.concatenate([dkv[:, HD // 2 : HD], dkv[:, : HD // 2]], axis=1)
     dk = dkv[:, :HD] * cos_table[:, :HD] - half_turn * sin_table[:, :HD]
     dqkv = jnp.concatenate([dq, dk.astype(BF16), dkv[:, HD:].astype(BF16)], axis=1)
     back = dot_nt(dqkv, w_qkv).astype(BF16)
-    dqkv, back, up_part = visit(dqkv, back, up_part, new=("gate3", gate_part[3]))
+    dqkv, back, up_part = visit(dqkv, back, up_part, new=("gate", gate_part, 3))
     parts = exchange(back)
     qkv_near, qkv_far = weight_grad(ids, normed_one, dqkv, chips)
-    qkv_near, qkv_far = visit(qkv_near, qkv_far, new=("up0", up_part[0]))
-    qkv_part = qkv_near + swap(qkv_far)
-    qkv_part, parts = visit(qkv_part, parts, new=("up1", up_part[1]))
+    qkv_near, qkv_far = visit(qkv_near, qkv_far, new=("up", up_part, 0))
+    qkv_part = pair_sum(qkv_near, swap(qkv_far))
+    qkv_part, parts = visit(qkv_part, parts, new=("up", up_part, 1))
     qkv_part = exchange(qkv_part)
     _, grad_inputs, gain_one_local = residual_norm_back(grad_resid, parts, tokens, 1)
-    gain_one_local = visit(gain_one_local, new=("up2", up_part[2]))
+    gain_one_local = visit(gain_one_local, new=("up", up_part, 2))
     norms = jnp.concatenate([gain_one_local, gain_two_local], axis=0)
     norms = norms.reshape(2, chips, 2, wrows).transpose(2, 1, 0, 3)
     mine = lax.dynamic_index_in_dim(norms, core, 0, keepdims=False)
     other = lax.dynamic_index_in_dim(norms, 1 - core, 0, keepdims=False)
     norms = mine + swap(other)
-    out_part = out_near + out_far
-    norms, qkv_part, out_part = visit(norms, qkv_part, out_part, new=("up3", up_part[3]))
+    out_part = pair_sum(out_near, out_far)
+    norms, qkv_part, out_part = visit(norms, qkv_part, out_part, new=("up", up_part, 3))
     parts = exchange(out).reshape(chips, rows, model)
-    visit(new=("out0", out_part[0]))
-    parts = visit(parts, new=("out1", out_part[1]))
+    visit(new=("out", out_part, 0))
+    parts = visit(parts, new=("out", out_part, 1))
     norms = jnp.sum(exchange(norms), axis=0)
     result = (resid + jnp.sum(parts.astype(F32), axis=0)).astype(BF16)
-    qkv_part = qkv_part.reshape(2, chips // 2 * qkv_part.shape[1], 128)
-    visit(new=("qkv0", qkv_part[0]))
-    norms = visit(norms, new=("qkv1", qkv_part[1]))
+    visit(new=("qkv", qkv_part, 0))
+    norms = visit(norms, new=("qkv", qkv_part, 1))
+    for k in range(2, chips):
+        visit(new=("qkv", qkv_part, k))
+    if reps != 4:
+        for k in range(4, chips):
+            visit(new=("gate", gate_part, k))
+            visit(new=("up", up_part, k))
     if reps == 4:
         norms = norms + lax.ppermute(norms, "rep", [(0, 1), (3, 2)])
         norms = norms + lax.ppermute(norms, "rep", [(1, 2), (2, 1)])
         norms = jnp.where(ends == 1, lax.ppermute(norms, "rep", [(1, 0), (2, 3)]), norms)
     else:
         norms = lax.psum(norms, "rep")
-        for k in range(4, chips):
-            visit(new=(f"gate{k}", gate_part[k]))
-            visit(new=(f"up{k}", up_part[k]))
     while any(line.busy() for line in lines):
         visit()
 
     def summed(name, count):
         return [sums_of[f"{name}{k}"] for k in range(count)]
 
-    qkv = jnp.concatenate(summed("qkv", 2)).reshape(chips, -1, 128)
-    grad_query = beside([b[: qw // 128 * wrows] for b in qkv], wrows, qw, gain_one)
-    kv = qkv[:, qw // 128 * wrows :].astype(F32).reshape(KVH, kv_share, wrows, 2, HD).sum(axis=1)
+    qkv = summed("qkv", chips)
+    grad_query = beside(ids, qkv, wrows, qw, gain_one)
+    at = qw // 128 * wrows
+    kv = [jnp.where(ends == 1, b[at : at + wrows], a[at : at + wrows]) for a, b in qkv]
+    kv = jnp.stack(kv).astype(F32).reshape(KVH, kv_share, wrows, 2, HD).sum(axis=1)
     kv = kv * gain_one[None, :, :, None]
     grad_key = kv[:, :, 0].transpose(1, 0, 2).reshape(wrows, KVH * HD)
     grad_value = kv[:, :, 1].transpose(1, 0, 2).reshape(wrows, KVH * HD)
@@ -843,11 +920,11 @@
         grad_query,
         grad_key,
         grad_value,
-        beside(summed("out", 2), wrows, model // 2),
+        beside(ids, summed("out", 2), wrows, model // 2),
         norms[1] / gain_two[:, 0],
-        beside(summed("gate", chips), wrows, width, gain_two),
-        beside(summed("up", chips), wrows, width, gain_two),
-        beside(summed("down", 4), w_down.shape[0], model // 4),
+        beside(ids, summed("gate", chips), wrows, width, gain_two),
+        beside(ids, summed("up", chips), wrows, width, gain_two),
+        beside(ids, summed("down", 4), w_down.shape[0], model // 4),
     )
 
 

time: 677 us -> 658 us (0.972)
  starting transfers between devices: 174 us -> 147 us
  waiting for transfers between devices: 185 us -> 203 us
  other arithmetic: 25.1 us -> 9.8 us
  matrix products: 25.6 us -> 14.7 us
  blocking collectives: 0 us -> 8.63 us
    all_to_all x12 -> x11, waiting for transfers between devices: 37.1 us -> 58.8 us  [exchange(): return lax.all_to_all(v, 'fsdp', 0, 0, axis_index_groups=sides, tiled=True)]
    ppermute x21 -> x22, starting transfers between devices: 75.3 us -> 53.9 us  [visit(): lax.ppermute(ahead, 'rep', outer_pairs)]
    ppermute x21 -> x22, waiting for transfers between devices: 60 us -> 77.2 us  [visit(): lax.ppermute(ahead, 'rep', outer_pairs)]
    ppermute x9, waiting for transfers between devices: 71 us -> 54.4 us  [hop(): return lax.ppermute(v, 'fsdp', [(i, i ^ 2 * k) for i in range(group)])]
    add x5 -> x0, other arithmetic: 16.3 us -> none  [the longest x1 5.01 us: local(): gate_part = exchange(gate_near + gate_far)]
    unnamed x72 -> x97, local copies, waits for them, and re-layouts: 7.82 us -> 20.1 us
    dot_general x4 -> x2, matrix products: 17.7 us -> 7.45 us  [dot_nt(): lax.dot_general(a, b, (((1,), (1,)), ((), ())), preferred_element_type=F32)]
    ppermute x1, waiting for transfers between devices: 8.94 us -> 0.01 us  [local(): norms = norms + lax.ppermute(norms, 'rep', [(0, 1), (3, 2)])]
  transfers between devices with their start and end apart: 78 -> 80, of which waited for: 24 -> 25; matrix products, arithmetic and copies ran while one was open for 9% -> 5% of each run, Pallas kernels for 28% -> 30%
where the time goes in v3:
time: 658 us; the launch traced here: 650 us
  Pallas kernels  234 us (36%)
  waiting for transfers between devices  203 us (31%)
  starting transfers between devices  147 us (22%)
  local copies, waits for them, and re-layouts  30.9 us (5%)
  matrix products  14.7 us (2%)
  other arithmetic  9.8 us (1%)
  blocking collectives  8.63 us (1%)
    ppermute x22, waiting for transfers between devices, visit(): lax.ppermute(ahead, 'rep', outer_pairs)  77.2 us
    pallas_call x20, Pallas kernels, chain_step(): pl.pallas_call(body, grid=(1,), in_specs=[scalars()] + [spec(v) for v in...  59.4 us
    all_to_all x11, waiting for transfers between devices, exchange(): return lax.all_to_all(v, 'fsdp', 0, 0, axis_index_groups=sides, tiled=True)  58.8 us
    ppermute x9, waiting for transfers between devices, hop(): return lax.ppermute(v, 'fsdp', [(i, i ^ 2 * k) for i in range(group)])  54.4 us
    ppermute x22, starting transfers between devices, visit(): lax.ppermute(ahead, 'rep', outer_pairs)  53.9 us
    all_to_all x11, starting transfers between devices, exchange(): return lax.all_to_all(v, 'fsdp', 0, 0, axis_index_groups=sides, tiled=True)  45 us
    pallas_call x5, Pallas kernels, beside(): pl.pallas_call(body, grid_spec=pltpu.PrefetchScalarGridSpec(num_scalar_pr...  27.5 us
    pallas_call x1, Pallas kernels, feed_forward(): pl.pallas_call(body, grid_spec=pltpu.PrefetchScalarGridSpec(num_scalar_pr...  26.1 us
  transfers between devices with their start and end apart: 80, of which 25 were waited for; matrix products, arithmetic and copies ran while one was open for 5% of the time, Pallas kernels for 30%

profile of v3, /device:TPU:0, one launch (start us, length us, event | category | flops | bytes accessed | tf_op | source)
XLA Modules:
  0.0 650.0 jit_solution(15929774526765194399)
XLA Ops:
  2.6 4.1 pick_qkv.1
  6.7 4.7 all-to-all-start
  16.6 12.6 %all-to-all-done.n_ref = bf16[4,256,640]{2,1,0:T(8,128)(2,1)S(1)} async-done(((bf16[4,256,640]{2,1,0:T(8,128)(2,1)}), bf16[4,256,640]{2,1,0:T(8,128)(2,1)S(1)}, u32[]{:S(2)}, u32[]{:S(2)}) %all-to-all-start) | async-done | bytes 1310752 | tf_op jit(solution)/shard_map/all_to_all | solution.py:727
  31.1 4.9 pick_half.1
  36.0 6.1 join_cores.1.refs_13_
  42.1 9.9 %collective-permute-done.2.refs_3_ = bf16[128,2048]{1,0:T(8,128)(2,1)} collective-permute-done((bf16[128,2048]{1,0:T(8,128)(2,1)S(1)}, bf16[128,2048]{1,0:T(8,128)(2,1)}, u32[]{:S(2)}, u32[]{:S(2)}) %collective-permute-start.2) | collective-permute-done | bytes 524320 | tf_op jit(solution)/shard_map/ppermute | solution.py:730
  52.0 3.6 all-to-all-start.1
  55.6 6.5 qkv_forward.1
  62.1 11.1 %all-to-all-done.1.refs_5_ = bf16[4,128,1408]{2,1,0:T(8,128)(2,1)S(1)} async-done(((bf16[4,128,1408]{2,1,0:T(8,128)(2,1)}), bf16[4,128,1408]{2,1,0:T(8,128)(2,1)S(1)}, u32[]{:S(2)}, u32[]{:S(2)}) %all-to-all-start.1) | async-done | bytes 1441824 | tf_op jit(solution)/shard_map/all_to_all | solution.py:727
  73.2 4.6 all-to-all-start.2
  81.1 8.9 %attention_forward.1 = (bf16[512,512]{1,0:T(8,128)(2,1)}, f32[512,128]{1,0:T(8,128)}) custom-call(s32[5]{0:T(128)} %stack.38.s_ref.c_ref, s32[4,8]{1,0:T(4,128)} %n_ref.3, bf16[512,512]{1,0:T(8,128)(2,1)} %get-tuple-element.212.q_ref, bf16[512,128]{1,0:T(8,128)(2,1)} %get-tuple-element.213.a_ref, bf16[512,128]{1,0:T(8,128)(2,1)} %collective-permute-done.6.b_ref), custom_call_target="tpu_custom_call" | custom-call | flops 1024 | bytes 1024 | tf_op jit(solution)/shard_map/attention_forward/pallas_call | solution.py:240
  90.0 5.2 all-to-all-done.2.refs_9_
  96.9 4.6 out_proj.1
  103.5 8.9 %collective-permute-done.10.refs_6_ = bf16[4,128,1408]{2,1,0:T(8,128)(2,1)S(1)} collective-permute-done((bf16[4,128,1408]{2,1,0:T(8,128)(2,1)S(1)}, bf16[4,128,1408]{2,1,0:T(8,128)(2,1)S(1)}, u32[]{:S(2)}, u32[]{:S(2)}) %collective-permute-start.10) | collective-permute-done | bytes 1441824 | tf_op jit(solution)/shard_map/ppermute | solution.py:739
  116.9 3.6 all-to-all-start.3
  120.6 19.2 %collective-permute-done.8.refs_2_ = bf16[128,2048]{1,0:T(8,128)(2,1)} collective-permute-done((bf16[128,2048]{1,0:T(8,128)(2,1)}, bf16[128,2048]{1,0:T(8,128)(2,1)}, u32[]{:S(2)}, u32[]{:S(2)}) %collective-permute-start.8) | collective-permute-done | bytes 524320 | tf_op jit(solution)/shard_map/ppermute | solution.py:730
  147.8 13.2 %collective-permute-done.11.refs_1_ = bf16[128,2048]{1,0:T(8,128)(2,1)S(1)} collective-permute-done((bf16[128,2048]{1,0:T(8,128)(2,1)}, bf16[128,2048]{1,0:T(8,128)(2,1)S(1)}, u32[]{:S(2)}, u32[]{:S(2)}) %collective-permute-start.11) | collective-permute-done | bytes 524320 | tf_op jit(solution)/shard_map/ppermute | solution.py:730
  162.6 12.0 %collective-permute-done.13.refs_3_ = bf16[128,2048]{1,0:T(8,128)(2,1)S(1)} collective-permute-done((bf16[128,2048]{1,0:T(8,128)(2,1)}, bf16[128,2048]{1,0:T(8,128)(2,1)S(1)}, u32[]{:S(2)}, u32[]{:S(2)}) %collective-permute-start.13) | collective-permute-done | bytes 524320 | tf_op jit(solution)/shard_map/ppermute | solution.py:730
  176.0 26.1 %feed_forward.1 = (bf16[512,1408]{1,0:T(8,128)(2,1)}, bf16[512,1408]{1,0:T(8,128)(2,1)}, bf16[512,1408]{1,0:T(8,128)(2,1)}, bf16[512,2048]{1,0:T(8,128)(2,1)}, bf16[512,2048]{1,0:T(8,128)(2,1)}) custom-call(s32[5]{0:T(128)} %stack.38.s_ref.c_ref, bf16[128,2048]{1,0:T(8,128)(2,1)} %get-tuple-element.233.refs_0_, bf16[128,2048]{1,0:T(8,128)(2,1)} %copy-done.26, ...), custom_call_target="tpu_custom_call" | custom-call | flops 1024 | bytes 1024 | tf_op jit(solution)/shard_map/feed_forward/pallas_call | solution.py:377
  202.2 8.1 %row_grad.2 = (bf16[4,2816,128]{2,1,0:T(8,128)(2,1)}, bf16[4,2816,128]{2,1,0:T(8,128)(2,1)}) custom-call(s32[5]{0:T(128)} %stack.38.s_ref.c_ref, bf16[512,1408]{1,0:T(8,128)(2,1)} %get-tuple-element.257.l_ref, bf16[512,2048]{1,0:T(8,128)(2,1)} %bitcast.55), custom_call_target="tpu_custom_call" | custom-call | flops 1024 | bytes 1024 | tf_op jit(solution)/shard_map/row_grad/pallas_call | solution.py:553
  210.3 9.6 %weight_grad.3 = (bf16[4,2816,128]{2,1,0:T(8,128)(2,1)}, bf16[4,2816,128]{2,1,0:T(8,128)(2,1)}) custom-call(s32[5]{0:T(128)} %stack.38.s_ref.c_ref, bf16[512,2048]{1,0:T(8,128)(2,1)} %get-tuple-element.238.l_ref, bf16[512,1408]{1,0:T(8,128)(2,1)} %get-tuple-element.242.r_ref), custom_call_target="tpu_custom_call" | custom-call | flops 1024 | bytes 1024 | tf_op jit(solution)/shard_map/weight_grad/pallas_call | solution.py:518
  221.5 3.9 all-to-all-start.4
  225.7 4.9 pair_sum.7
  230.6 21.2 %all-to-all-done.4 = bf16[4,128,2048]{2,1,0:T(8,128)(2,1)S(1)} async-done(((bf16[4,128,2048]{2,1,0:T(8,128)(2,1)}), bf16[4,128,2048]{2,1,0:T(8,128)(2,1)S(1)}, u32[]{:S(2)}, u32[]{:S(2)}) %all-to-all-start.4) | async-done | bytes 2097184 | tf_op jit(solution)/shard_map/all_to_all | solution.py:727
  253.1 3.7 all-to-all-start.5
  256.8 4.9 pair_sum.5.refs_0_.refs_2_
  261.7 9.6 %weight_grad.4 = (bf16[4,2816,128]{2,1,0:T(8,128)(2,1)}, bf16[4,2816,128]{2,1,0:T(8,128)(2,1)}) custom-call(s32[5]{0:T(128)} %stack.38.s_ref.c_ref, bf16[512,2048]{1,0:T(8,128)(2,1)} %get-tuple-element.238.l_ref, bf16[512,1408]{1,0:T(8,128)(2,1)} %get-tuple-element.250.r_ref), custom_call_target="tpu_custom_call" | custom-call | flops 1024 | bytes 1024 | tf_op jit(solution)/shard_map/weight_grad/pallas_call | solution.py:518
  274.0 4.6 residual_norm_back.2
  278.5 13.7 %collective-permute-done.20.refs_1_ = bf16[2816,128]{1,0:T(8,128)(2,1)} collective-permute-done((bf16[2816,128]{1,0:T(8,128)(2,1)}, bf16[2816,128]{1,0:T(8,128)(2,1)}, u32[]{:S(2)}, u32[]{:S(2)}) %collective-permute-start.20) | collective-permute-done | bytes 720928 | tf_op jit(solution)/shard_map/ppermute | solution.py:783
  293.9 4.5 all-to-all-start.7
  306.0 7.3 %convolution_convert_fusion.1 = bf16[512,2048]{1,0:T(8,128)(2,1)} fusion(bf16[512,1408]{1,0:T(8,128)(2,1)S(1)} %copy-done.21, bf16[1408,2048]{1,0:T(8,128)(2,1)} %join_cores.1.refs_13_), kind=kOutput, calls=%fused_computation.2 | convolution fusion | flops 2953838592 | bytes 9306112 | tf_op jit(solution)/shard_map/dot_general | solution.py:24
  313.3 4.9 pair_sum.6
  318.6 14.3 %collective-permute-done.24.refs_1_ = bf16[2816,128]{1,0:T(8,128)(2,1)} collective-permute-done((bf16[2816,128]{1,0:T(8,128)(2,1)}, bf16[2816,128]{1,0:T(8,128)(2,1)}, u32[]{:S(2)}, u32[]{:S(2)}) %collective-permute-start.24) | collective-permute-done | bytes 720928 | tf_op jit(solution)/shard_map/ppermute | solution.py:783
  332.9 4.1 all-to-all-start.8
  345.4 3.8 collective-permute-start.28
  350.7 4.7 row_grad.3
  355.4 4.3 convolution_convert_fusion.2.d_ref
  359.7 15.3 %attention_backward.1 = (bf16[512,512]{1,0:T(8,128)(2,1)}, f32[1024,128]{1,0:T(8,128)}) custom-call(s32[5]{0:T(128)} %stack.38.s_ref.c_ref, s32[4,8]{1,0:T(4,128)} %n_ref.3, bf16[512,512]{1,0:T(8,128)(2,1)} %get-tuple-element.212.q_ref, bf16[512,128]{1,0:T(8,128)(2,1)} %get-tuple-element.213.a_ref, bf16[512,128]{1,0:T(8,128)(2,1)} %collective-permute-done.6.b_ref, ...), custom_call_target="tpu_custom_call" | custom-call | flops 1024 | bytes 1024 | tf_op jit(solution)/shard_map/attention_backward/pallas_call | solution.py:310
  380.1 3.7 collective-permute-start.31
  402.6 4.5 all-to-all-start.9
  407.1 6.3 weight_grad.5
  419.7 3.9 collective-permute-start.36
  425.4 3.8 pair_sum.8
  429.2 11.5 %collective-permute-done.36.refs_1_.refs_7_ = bf16[2816,128]{1,0:T(8,128)(2,1)S(1)} collective-permute-done((bf16[2816,128]{1,0:T(8,128)(2,1)}, bf16[2816,128]{1,0:T(8,128)(2,1)S(1)}, u32[]{:S(2)}, u32[]{:S(2)}) %collective-permute-start.36) | collective-permute-done | bytes 720928 | tf_op jit(solution)/shard_map/ppermute | solution.py:783
  441.5 4.2 all-to-all-start.10
  453.5 8.7 %all-to-all-done.10.refs_4_.refs_0_ = bf16[4,1280,128]{2,1,0:T(8,128)(2,1)S(1)} async-done(((bf16[4,1280,128]{2,1,0:T(8,128)(2,1)}), bf16[4,1280,128]{2,1,0:T(8,128)(2,1)S(1)}, u32[]{:S(2)}, u32[]{:S(2)}) %all-to-all-start.10) | async-done | bytes 1310752 | tf_op jit(solution)/shard_map/all_to_all | solution.py:727
  463.3 3.6 all-to-all-start.6
  466.9 3.4 chain_step.27
  474.6 4.0 residual_norm_back.3
  493.8 4.0 collective-permute-start.44
  499.4 6.4 collective-permute-done.51.refs_1_.refs_5_
  514.8 6.5 %collective-permute-done.44.refs_1_.refs_7_ = bf16[2816,128]{1,0:T(8,128)(2,1)} collective-permute-done((bf16[2816,128]{1,0:T(8,128)(2,1)}, bf16[2816,128]{1,0:T(8,128)(2,1)}, u32[]{:S(2)}, u32[]{:S(2)}) %collective-permute-start.44) | collective-permute-done | bytes 720928 | tf_op jit(solution)/shard_map/ppermute | solution.py:783
  524.6 4.1 collective-permute-start.46
  530.3 6.4 collective-permute-done.53.refs_1_
  545.3 8.6 %all_to_all.88 = f32[4,2,256]{2,1,0:T(2,128)S(1)} all-to-all(f32[4,2,256]{2,1,0:T(2,128)S(1)} %fusion.3), channel_id=1, replica_groups={{0,2,4,6},{1,3,5,7},{8,10,12,14},{9,11,13,15},{16,18,20,22},{17,19,21,2..., dimensions={0} | all-to-all | bytes 16384 | tf_op jit(solution)/shard_map/all_to_all | solution.py:727
  554.0 4.1 collective-permute-start.48
  558.9 6.6 %beside.9 = f32[704,2048]{1,0:T(8,128)} custom-call(s32[5]{0:T(128)} %stack.38.s_ref.c_ref, f32[704,1]{1,0:T(8,128)} %broadcast_in_dim.37.s_ref, bf16[2816,128]{1,0:T(8,128)(2,1)} %get-tuple-element.287.refs_0_, bf16[2816,128]{1,0:T(8,128)(2,1)} %collective-permute-done.28.refs_1_, bf16[2816,128]{1,0:T(8,128)(2,1)} %get-tuple-element.296.refs_2_, ...), custom_call_target="tpu_custom_call" | custom-call | flops 1024 | bytes 1024 | tf_op jit(solution)/shard_map/beside/pallas_call | solution.py:661
  574.8 5.8 collective-permute-start.57
  583.6 6.4 beside.7
  601.9 10.3 %collective-permute-done.59.refs_1_ = bf16[1280,128]{1,0:T(8,128)(2,1)S(1)} collective-permute-done((bf16[1280,128]{1,0:T(8,128)(2,1)}, bf16[1280,128]{1,0:T(8,128)(2,1)S(1)}, u32[]{:S(2)}, u32[]{:S(2)}) %collective-permute-start.59) | collective-permute-done | bytes 327712 | tf_op jit(solution)/shard_map/ppermute | solution.py:783
  622.2 6.4 beside.8
  632.2 3.5 collective-permute-start.68
  637.4 3.7 beside.6
  642.7 4.3 beside.5
  (286 shorter events, 186.6 us)
Async XLA Ops:
  0.6 28.6 %collective-permute-start.4 = (bf16[704,2048]{1,0:T(8,128)(2,1)}, bf16[704,2048]{1,0:T(8,128)(2,1)}, u32[]{:S(2)}, u32[]{:S(2)}) collective-permute-start(bf16[704,2048]{1,0:T(8,128)(2,1)} %a_ref.3), channel_id=1, source_target_pairs={{0,1},{1,0},{2,3},{3,2},{4,5},{5,4},{6,7},{7,6},{8,9},{9,8},{10,11... | collective-permute-start | bytes 8650760 | tf_op jit(solution)/shard_map/ppermute | solution.py:736
  6.7 22.5 %all-to-all-start = ((bf16[4,256,640]{2,1,0:T(8,128)(2,1)}), bf16[4,256,640]{2,1,0:T(8,128)(2,1)S(1)}, u32[]{:S(2)}, u32[]{:S(2)}) async-start(bf16[4,256,640]{2,1,0:T(8,128)(2,1)} %pick_qkv.1), calls=%async_computation | async-start | bytes 2621440 | tf_op jit(solution)/shard_map/all_to_all | solution.py:727
  11.4 40.6 %collective-permute-start.3 = (bf16[256,2048]{1,0:T(8,128)(2,1)S(1)}, bf16[256,2048]{1,0:T(8,128)(2,1)}, u32[]{:S(2)}, u32[]{:S(2)}) collective-permute-start(bf16[256,2048]{1,0:T(8,128)(2,1)S(1)} %copy-done.23), channel_id=1, source_target_pairs={{0,1},{1,0},{2,3},{3,2},{4,5},{5,4},{6,7},{7,6},{8,9},{9,8},{10,11... | collective-permute-start | bytes 3145736 | tf_op jit(solution)/shard_map/ppermute | solution.py:736
  11.6 30.4 %collective-permute-start = (bf16[128,2048]{1,0:T(8,128)(2,1)S(1)}, bf16[128,2048]{1,0:T(8,128)(2,1)S(1)}, u32[]{:S(2)}, u32[]{:S(2)}) collective-permute-start(bf16[128,2048]{1,0:T(8,128)(2,1)S(1)} %copy-done.7), channel_id=1, source_target_pairs={{0,2},{1,3},{2,0},{3,1},{4,6},{5,7},{6,4},{7,5},{8,10},{9,11},{10,... | collective-permute-start | bytes 1572872 | tf_op jit(solution)/shard_map/ppermute | solution.py:730
  13.5 28.5 %collective-permute-start.1 = (bf16[128,2048]{1,0:T(8,128)(2,1)S(1)}, bf16[128,2048]{1,0:T(8,128)(2,1)}, u32[]{:S(2)}, u32[]{:S(2)}) collective-permute-start(bf16[128,2048]{1,0:T(8,128)(2,1)S(1)} %copy-done.7), channel_id=1, source_target_pairs={{0,4},{1,5},{2,6},{3,7},{4,0},{5,1},{6,2},{7,3},{8,12},{9,13},{10,... | collective-permute-start | bytes 1572872 | tf_op jit(solution)/shard_map/ppermute | solution.py:730
  15.0 37.0 %collective-permute-start.2 = (bf16[128,2048]{1,0:T(8,128)(2,1)S(1)}, bf16[128,2048]{1,0:T(8,128)(2,1)}, u32[]{:S(2)}, u32[]{:S(2)}) collective-permute-start(bf16[128,2048]{1,0:T(8,128)(2,1)S(1)} %copy-done.7), channel_id=1, source_target_pairs={{0,6},{1,7},{2,4},{3,5},{4,2},{5,3},{6,0},{7,1},{8,14},{9,15},{10,... | collective-permute-start | bytes 1572872 | tf_op jit(solution)/shard_map/ppermute | solution.py:730
  29.2 26.3 %collective-permute-start.5 = (bf16[4,256,640]{2,1,0:T(8,128)(2,1)S(1)}, bf16[4,256,640]{2,1,0:T(8,128)(2,1)}, u32[]{:S(2)}, u32[]{:S(2)}) collective-permute-start(bf16[4,256,640]{2,1,0:T(8,128)(2,1)S(1)} %all-to-all-done.n_ref), channel_id=1, source_target_pairs={{0,1},{1,0},{2,3},{3,2},{4,5},{5,4},{6,7},{7,6},{8,9},{9,8},{10,11... | collective-permute-start | bytes 3932168 | tf_op jit(solution)/shard_map/ppermute | solution.py:736
  52.0 21.2 %all-to-all-start.1 = ((bf16[4,128,1408]{2,1,0:T(8,128)(2,1)}), bf16[4,128,1408]{2,1,0:T(8,128)(2,1)S(1)}, u32[]{:S(2)}, u32[]{:S(2)}) async-start(bf16[4,128,1408]{2,1,0:T(8,128)(2,1)} %get-tuple-element.210), calls=%async_computation.1 | async-start | bytes 2883584 | tf_op jit(solution)/shard_map/all_to_all | solution.py:727
  73.2 22.0 %all-to-all-start.2 = ((bf16[4,128,1408]{2,1,0:T(8,128)(2,1)}), bf16[4,128,1408]{2,1,0:T(8,128)(2,1)}, u32[]{:S(2)}, u32[]{:S(2)}) async-start(bf16[4,128,1408]{2,1,0:T(8,128)(2,1)} %get-tuple-element.215), calls=%async_computation.2 | async-start | bytes 2883584 | tf_op jit(solution)/shard_map/all_to_all | solution.py:727
  77.8 34.6 %collective-permute-start.10 = (bf16[4,128,1408]{2,1,0:T(8,128)(2,1)S(1)}, bf16[4,128,1408]{2,1,0:T(8,128)(2,1)S(1)}, u32[]{:S(2)}, u32[]{:S(2)}) collective-permute-start(bf16[4,128,1408]{2,1,0:T(8,128)(2,1)S(1)} %all-to-all-done.1.refs_5_), channel_id=1, source_target_pairs={{0,8},{8,0},{16,24},{24,16},{1,9},{9,1},{17,25},{25,17},{2,10},{10... | collective-permute-start | bytes 4325384 | tf_op jit(solution)/shard_map/ppermute | solution.py:739
  95.2 46.2 %collective-permute-start.16 = (bf16[4,128,1408]{2,1,0:T(8,128)(2,1)}, bf16[4,128,1408]{2,1,0:T(8,128)(2,1)}, u32[]{:S(2)}, u32[]{:S(2)}) collective-permute-start(bf16[4,128,1408]{2,1,0:T(8,128)(2,1)} %all-to-all-done.2.refs_9_), channel_id=1, source_target_pairs={{0,8},{8,0},{16,24},{24,16},{1,9},{9,1},{17,25},{25,17},{2,10},{10... | collective-permute-start | bytes 4325384 | tf_op jit(solution)/shard_map/ppermute | solution.py:739
  96.9 49.4 %collective-permute-start.14 = (bf16[4,128,1408]{2,1,0:T(8,128)(2,1)S(1)}, bf16[4,128,1408]{2,1,0:T(8,128)(2,1)}, u32[]{:S(2)}, u32[]{:S(2)}) collective-permute-start(bf16[4,128,1408]{2,1,0:T(8,128)(2,1)S(1)} %all-to-all-done.1.refs_5_), channel_id=1, source_target_pairs={{0,1},{1,0},{2,3},{3,2},{4,5},{5,4},{6,7},{7,6},{8,9},{9,8},{10,11... | collective-permute-start | bytes 4325384 | tf_op jit(solution)/shard_map/ppermute | solution.py:736
  101.5 19.0 %collective-permute-start.7 = (bf16[128,2048]{1,0:T(8,128)(2,1)}, bf16[128,2048]{1,0:T(8,128)(2,1)}, u32[]{:S(2)}, u32[]{:S(2)}) collective-permute-start(bf16[128,2048]{1,0:T(8,128)(2,1)} %get-tuple-element.224), channel_id=1, source_target_pairs={{0,2},{1,3},{2,0},{3,1},{4,6},{5,7},{6,4},{7,5},{8,10},{9,11},{10,... | collective-permute-start | bytes 1572872 | tf_op jit(solution)/shard_map/ppermute | solution.py:730
  103.0 36.9 %collective-permute-start.8 = (bf16[128,2048]{1,0:T(8,128)(2,1)}, bf16[128,2048]{1,0:T(8,128)(2,1)}, u32[]{:S(2)}, u32[]{:S(2)}) collective-permute-start(bf16[128,2048]{1,0:T(8,128)(2,1)} %get-tuple-element.225), channel_id=1, source_target_pairs={{0,4},{1,5},{2,6},{3,7},{4,0},{5,1},{6,2},{7,3},{8,12},{9,13},{10,... | collective-permute-start | bytes 1572872 | tf_op jit(solution)/shard_map/ppermute | solution.py:730
  112.4 27.4 %collective-permute-start.9 = (bf16[128,2048]{1,0:T(8,128)(2,1)}, bf16[128,2048]{1,0:T(8,128)(2,1)}, u32[]{:S(2)}, u32[]{:S(2)}) collective-permute-start(bf16[128,2048]{1,0:T(8,128)(2,1)} %get-tuple-element.226), channel_id=1, source_target_pairs={{0,6},{1,7},{2,4},{3,5},{4,2},{5,3},{6,0},{7,1},{8,14},{9,15},{10,... | collective-permute-start | bytes 1572872 | tf_op jit(solution)/shard_map/ppermute | solution.py:730
  116.9 57.6 %all-to-all-start.3 = ((bf16[4,128,2048]{2,1,0:T(8,128)(2,1)}), bf16[4,128,2048]{2,1,0:T(8,128)(2,1)S(1)}, u32[]{:S(2)}, u32[]{:S(2)}) async-start(bf16[4,128,2048]{2,1,0:T(8,128)(2,1)} %broadcast_in_dim.35), calls=%async_computation.3 | async-start | bytes 4194304 | tf_op jit(solution)/shard_map/all_to_all | solution.py:727
  120.6 54.0 %collective-permute-start.17 = (bf16[4,128,1408]{2,1,0:T(8,128)(2,1)}, bf16[4,128,1408]{2,1,0:T(8,128)(2,1)}, u32[]{:S(2)}, u32[]{:S(2)}) collective-permute-start(bf16[4,128,1408]{2,1,0:T(8,128)(2,1)} %all-to-all-done.2.refs_9_), channel_id=1, source_target_pairs={{0,1},{1,0},{2,3},{3,2},{4,5},{5,4},{6,7},{7,6},{8,9},{9,8},{10,11... | collective-permute-start | bytes 4325384 | tf_op jit(solution)/shard_map/ppermute | solution.py:736
  139.8 34.8 %collective-permute-start.15 = (bf16[4,128,1408]{2,1,0:T(8,128)(2,1)}, bf16[4,128,1408]{2,1,0:T(8,128)(2,1)}, u32[]{:S(2)}, u32[]{:S(2)}) collective-permute-start(bf16[4,128,1408]{2,1,0:T(8,128)(2,1)} %copy-done.20), channel_id=1, source_target_pairs={{0,1},{1,0},{2,3},{3,2},{4,5},{5,4},{6,7},{7,6},{8,9},{9,8},{10,11... | collective-permute-start | bytes 4325384 | tf_op jit(solution)/shard_map/ppermute | solution.py:736
  141.4 33.2 %collective-permute-start.18 = (bf16[4,128,1408]{2,1,0:T(8,128)(2,1)}, bf16[4,128,1408]{2,1,0:T(8,128)(2,1)}, u32[]{:S(2)}, u32[]{:S(2)}) collective-permute-start(bf16[4,128,1408]{2,1,0:T(8,128)(2,1)} %collective-permute-done.16.refs_10_), channel_id=1, source_target_pairs={{0,1},{1,0},{2,3},{3,2},{4,5},{5,4},{6,7},{7,6},{8,9},{9,8},{10,11... | collective-permute-start | bytes 4325384 | tf_op jit(solution)/shard_map/ppermute | solution.py:736
  144.6 16.4 %collective-permute-start.11 = (bf16[128,2048]{1,0:T(8,128)(2,1)}, bf16[128,2048]{1,0:T(8,128)(2,1)S(1)}, u32[]{:S(2)}, u32[]{:S(2)}) collective-permute-start(bf16[128,2048]{1,0:T(8,128)(2,1)} %get-tuple-element.233.refs_0_), channel_id=1, source_target_pairs={{0,2},{1,3},{2,0},{3,1},{4,6},{5,7},{6,4},{7,5},{8,10},{9,11},{10,... | collective-permute-start | bytes 1572872 | tf_op jit(solution)/shard_map/ppermute | solution.py:730
  146.4 16.2 %collective-permute-start.12 = (bf16[128,2048]{1,0:T(8,128)(2,1)}, bf16[128,2048]{1,0:T(8,128)(2,1)S(1)}, u32[]{:S(2)}, u32[]{:S(2)}) collective-permute-start(bf16[128,2048]{1,0:T(8,128)(2,1)} %get-tuple-element.233.refs_0_), channel_id=1, source_target_pairs={{0,4},{1,5},{2,6},{3,7},{4,0},{5,1},{6,2},{7,3},{8,12},{9,13},{10,... | collective-permute-start | bytes 1572872 | tf_op jit(solution)/shard_map/ppermute | solution.py:730
  221.5 30.3 %all-to-all-start.4 = ((bf16[4,128,2048]{2,1,0:T(8,128)(2,1)}), bf16[4,128,2048]{2,1,0:T(8,128)(2,1)S(1)}, u32[]{:S(2)}, u32[]{:S(2)}) async-start(bf16[4,128,2048]{2,1,0:T(8,128)(2,1)} %bitcast.60), calls=%async_computation.4 | async-start | bytes 4194304 | tf_op jit(solution)/shard_map/all_to_all | solution.py:727
  253.1 39.1 %all-to-all-start.5 = ((bf16[4,2816,128]{2,1,0:T(8,128)(2,1)}), bf16[4,2816,128]{2,1,0:T(8,128)(2,1)S(1)}, u32[]{:S(2)}, u32[]{:S(2)}) async-start(bf16[4,2816,128]{2,1,0:T(8,128)(2,1)} %pair_sum.7), calls=%async_computation.5 | async-start | bytes 5767168 | tf_op jit(solution)/shard_map/all_to_all | solution.py:727
  271.3 42.0 %collective-permute-start.21 = (bf16[4,2816,128]{2,1,0:T(8,128)(2,1)}, bf16[4,2816,128]{2,1,0:T(8,128)(2,1)}, u32[]{:S(2)}, u32[]{:S(2)}) collective-permute-start(bf16[4,2816,128]{2,1,0:T(8,128)(2,1)} %get-tuple-element.259), channel_id=1, source_target_pairs={{0,1},{1,0},{2,3},{3,2},{4,5},{5,4},{6,7},{7,6},{8,9},{9,8},{10,11... | collective-permute-start | bytes 8650760 | tf_op jit(solution)/shard_map/ppermute | solution.py:736
  273.4 18.9 %collective-permute-start.20 = (bf16[2816,128]{1,0:T(8,128)(2,1)}, bf16[2816,128]{1,0:T(8,128)(2,1)}, u32[]{:S(2)}, u32[]{:S(2)}) collective-permute-start(bf16[2816,128]{1,0:T(8,128)(2,1)} %slice_bitcast_fusion.1), channel_id=1, source_target_pairs={{0,8},{8,0},{16,24},{24,16},{1,9},{9,1},{17,25},{25,17},{2,10},{10... | collective-permute-start | bytes 2162696 | tf_op jit(solution)/shard_map/ppermute | solution.py:783
  293.9 39.0 %all-to-all-start.7 = ((bf16[4,128,2048]{2,1,0:T(8,128)(2,1)}), bf16[4,128,2048]{2,1,0:T(8,128)(2,1)}, u32[]{:S(2)}, u32[]{:S(2)}) async-start(bf16[4,128,2048]{2,1,0:T(8,128)(2,1)} %bitcast.59), calls=%async_computation.7 | async-start | bytes 4194304 | tf_op jit(solution)/shard_map/all_to_all | solution.py:727
  299.5 19.1 %collective-permute-start.23 = (bf16[2816,128]{1,0:T(8,128)(2,1)S(1)}, bf16[2816,128]{1,0:T(8,128)(2,1)S(1)}, u32[]{:S(2)}, u32[]{:S(2)}) collective-permute-start(bf16[2816,128]{1,0:T(8,128)(2,1)S(1)} %slice_bitcast_fusion), channel_id=1, source_target_pairs={{0,8},{8,0},{16,24},{24,16},{1,9},{9,1},{17,25},{25,17},{2,10},{10... | collective-permute-start | bytes 2162696 | tf_op jit(solution)/shard_map/ppermute | solution.py:783
  303.1 29.8 %collective-permute-start.24 = (bf16[2816,128]{1,0:T(8,128)(2,1)}, bf16[2816,128]{1,0:T(8,128)(2,1)}, u32[]{:S(2)}, u32[]{:S(2)}) collective-permute-start(bf16[2816,128]{1,0:T(8,128)(2,1)} %get-tuple-element.270), channel_id=1, source_target_pairs={{0,8},{8,0},{16,24},{24,16},{1,9},{9,1},{17,25},{25,17},{2,10},{10... | collective-permute-start | bytes 2162696 | tf_op jit(solution)/shard_map/ppermute | solution.py:783
  304.5 28.4 %collective-permute-start.25 = (bf16[2816,128]{1,0:T(8,128)(2,1)}, bf16[2816,128]{1,0:T(8,128)(2,1)}, u32[]{:S(2)}, u32[]{:S(2)}) collective-permute-start(bf16[2816,128]{1,0:T(8,128)(2,1)} %get-tuple-element.271.refs_2_), channel_id=1, source_target_pairs={{8,16},{16,8},{9,17},{17,9},{10,18},{18,10},{11,19},{19,11},{12,20... | collective-permute-start | bytes 2162696 | tf_op jit(solution)/shard_map/ppermute | solution.py:785
  332.9 68.2 %all-to-all-start.8 = ((bf16[4,2816,128]{2,1,0:T(8,128)(2,1)}), bf16[4,2816,128]{2,1,0:T(8,128)(2,1)S(1)}, u32[]{:S(2)}, u32[]{:S(2)}) async-start(bf16[4,2816,128]{2,1,0:T(8,128)(2,1)} %pair_sum.6), calls=%async_computation.8 | async-start | bytes 5767168 | tf_op jit(solution)/shard_map/all_to_all | solution.py:727
  340.0 19.7 %collective-permute-start.26 = (bf16[2816,128]{1,0:T(8,128)(2,1)}, bf16[2816,128]{1,0:T(8,128)(2,1)}, u32[]{:S(2)}, u32[]{:S(2)}) collective-permute-start(bf16[2816,128]{1,0:T(8,128)(2,1)} %get-tuple-element.279), channel_id=1, source_target_pairs={{0,8},{8,0},{16,24},{24,16},{1,9},{9,1},{17,25},{25,17},{2,10},{10... | collective-permute-start | bytes 2162696 | tf_op jit(solution)/shard_map/ppermute | solution.py:783
  340.5 19.2 %collective-permute-start.27 = (bf16[2816,128]{1,0:T(8,128)(2,1)}, bf16[2816,128]{1,0:T(8,128)(2,1)}, u32[]{:S(2)}, u32[]{:S(2)}) collective-permute-start(bf16[2816,128]{1,0:T(8,128)(2,1)} %get-tuple-element.280.refs_2_), channel_id=1, source_target_pairs={{8,16},{16,8},{9,17},{17,9},{10,18},{18,10},{11,19},{19,11},{12,20... | collective-permute-start | bytes 2162696 | tf_op jit(solution)/shard_map/ppermute | solution.py:785
  345.4 29.6 %collective-permute-start.28 = (bf16[2816,128]{1,0:T(8,128)(2,1)}, bf16[2816,128]{1,0:T(8,128)(2,1)}, u32[]{:S(2)}, u32[]{:S(2)}) collective-permute-start(bf16[2816,128]{1,0:T(8,128)(2,1)} %get-tuple-element.287.refs_0_), channel_id=1, source_target_pairs={{0,8},{8,0},{16,24},{24,16},{1,9},{9,1},{17,25},{25,17},{2,10},{10... | collective-permute-start | bytes 2162696 | tf_op jit(solution)/shard_map/ppermute | solution.py:783
  349.2 25.9 %collective-permute-start.29 = (bf16[2816,128]{1,0:T(8,128)(2,1)}, bf16[2816,128]{1,0:T(8,128)(2,1)}, u32[]{:S(2)}, u32[]{:S(2)}) collective-permute-start(bf16[2816,128]{1,0:T(8,128)(2,1)} %get-tuple-element.288.refs_2_), channel_id=1, source_target_pairs={{8,16},{16,8},{9,17},{17,9},{10,18},{18,10},{11,19},{19,11},{12,20... | collective-permute-start | bytes 2162696 | tf_op jit(solution)/shard_map/ppermute | solution.py:785
  376.7 16.4 %collective-permute-start.30 = (bf16[512,128]{1,0:T(8,128)(2,1)}, bf16[512,128]{1,0:T(8,128)(2,1)S(1)}, u32[]{:S(2)}, u32[]{:S(2)}) collective-permute-start(bf16[512,128]{1,0:T(8,128)(2,1)} %slice.124), channel_id=1, source_target_pairs={{0,1},{1,0},{2,3},{3,2},{4,5},{5,4},{6,7},{7,6},{8,9},{9,8},{10,11... | collective-permute-start | bytes 393224 | tf_op jit(solution)/shard_map/ppermute | solution.py:736
  380.1 21.0 %collective-permute-start.31 = (bf16[2816,128]{1,0:T(8,128)(2,1)}, bf16[2816,128]{1,0:T(8,128)(2,1)}, u32[]{:S(2)}, u32[]{:S(2)}) collective-permute-start(bf16[2816,128]{1,0:T(8,128)(2,1)} %get-tuple-element.296.refs_2_), channel_id=1, source_target_pairs={{0,8},{8,0},{16,24},{24,16},{1,9},{9,1},{17,25},{25,17},{2,10},{10... | collective-permute-start | bytes 2162696 | tf_op jit(solution)/shard_map/ppermute | solution.py:783
  383.8 17.3 %collective-permute-start.32 = (bf16[2816,128]{1,0:T(8,128)(2,1)}, bf16[2816,128]{1,0:T(8,128)(2,1)}, u32[]{:S(2)}, u32[]{:S(2)}) collective-permute-start(bf16[2816,128]{1,0:T(8,128)(2,1)} %get-tuple-element.297.refs_2_), channel_id=1, source_target_pairs={{8,16},{16,8},{9,17},{17,9},{10,18},{18,10},{11,19},{19,11},{12,20... | collective-permute-start | bytes 2162696 | tf_op jit(solution)/shard_map/ppermute | solution.py:785
  388.9 27.5 %collective-permute-start.33 = (bf16[2816,128]{1,0:T(8,128)(2,1)}, bf16[2816,128]{1,0:T(8,128)(2,1)}, u32[]{:S(2)}, u32[]{:S(2)}) collective-permute-start(bf16[2816,128]{1,0:T(8,128)(2,1)} %get-tuple-element.304.refs_4_), channel_id=1, source_target_pairs={{0,8},{8,0},{16,24},{24,16},{1,9},{9,1},{17,25},{25,17},{2,10},{10... | collective-permute-start | bytes 2162696 | tf_op jit(solution)/shard_map/ppermute | solution.py:783
  391.2 25.2 %collective-permute-start.34 = (bf16[2816,128]{1,0:T(8,128)(2,1)}, bf16[2816,128]{1,0:T(8,128)(2,1)}, u32[]{:S(2)}, u32[]{:S(2)}) collective-permute-start(bf16[2816,128]{1,0:T(8,128)(2,1)} %get-tuple-element.305.refs_2_), channel_id=1, source_target_pairs={{8,16},{16,8},{9,17},{17,9},{10,18},{18,10},{11,19},{19,11},{12,20... | collective-permute-start | bytes 2162696 | tf_op jit(solution)/shard_map/ppermute | solution.py:785
  402.6 38.0 %all-to-all-start.9 = ((bf16[4,128,2048]{2,1,0:T(8,128)(2,1)}), bf16[4,128,2048]{2,1,0:T(8,128)(2,1)}, u32[]{:S(2)}, u32[]{:S(2)}) async-start(bf16[4,128,2048]{2,1,0:T(8,128)(2,1)} %bitcast.58), calls=%async_computation.9 | async-start | bytes 4194304 | tf_op jit(solution)/shard_map/all_to_all | solution.py:727
  419.7 20.9 %collective-permute-start.36 = (bf16[2816,128]{1,0:T(8,128)(2,1)}, bf16[2816,128]{1,0:T(8,128)(2,1)S(1)}, u32[]{:S(2)}, u32[]{:S(2)}) collective-permute-start(bf16[2816,128]{1,0:T(8,128)(2,1)} %get-tuple-element.313.refs_6_), channel_id=1, source_target_pairs={{0,8},{8,0},{16,24},{24,16},{1,9},{9,1},{17,25},{25,17},{2,10},{10... | collective-permute-start | bytes 2162696 | tf_op jit(solution)/shard_map/ppermute | solution.py:783
  423.6 17.0 %collective-permute-start.37 = (bf16[2816,128]{1,0:T(8,128)(2,1)}, bf16[2816,128]{1,0:T(8,128)(2,1)S(1)}, u32[]{:S(2)}, u32[]{:S(2)}) collective-permute-start(bf16[2816,128]{1,0:T(8,128)(2,1)} %get-tuple-element.314.refs_2_), channel_id=1, source_target_pairs={{8,16},{16,8},{9,17},{17,9},{10,18},{18,10},{11,19},{19,11},{12,20... | collective-permute-start | bytes 2162696 | tf_op jit(solution)/shard_map/ppermute | solution.py:785
  441.5 20.7 %all-to-all-start.10 = ((bf16[4,1280,128]{2,1,0:T(8,128)(2,1)}), bf16[4,1280,128]{2,1,0:T(8,128)(2,1)S(1)}, u32[]{:S(2)}, u32[]{:S(2)}) async-start(bf16[4,1280,128]{2,1,0:T(8,128)(2,1)} %pair_sum.8), calls=%async_computation.10 | async-start | bytes 2621440 | tf_op jit(solution)/shard_map/all_to_all | solution.py:727
  449.1 29.5 %collective-permute-start.38 = (bf16[2816,128]{1,0:T(8,128)(2,1)}, bf16[2816,128]{1,0:T(8,128)(2,1)}, u32[]{:S(2)}, u32[]{:S(2)}) collective-permute-start(bf16[2816,128]{1,0:T(8,128)(2,1)} %get-tuple-element.322.refs_0_), channel_id=1, source_target_pairs={{0,8},{8,0},{16,24},{24,16},{1,9},{9,1},{17,25},{25,17},{2,10},{10... | collective-permute-start | bytes 2162696 | tf_op jit(solution)/shard_map/ppermute | solution.py:783
  452.0 26.6 %collective-permute-start.39 = (bf16[2816,128]{1,0:T(8,128)(2,1)}, bf16[2816,128]{1,0:T(8,128)(2,1)}, u32[]{:S(2)}, u32[]{:S(2)}) collective-permute-start(bf16[2816,128]{1,0:T(8,128)(2,1)} %get-tuple-element.323.refs_2_), channel_id=1, source_target_pairs={{8,16},{16,8},{9,17},{17,9},{10,18},{18,10},{11,19},{19,11},{12,20... | collective-permute-start | bytes 2162696 | tf_op jit(solution)/shard_map/ppermute | solution.py:785
  453.5 32.3 %collective-permute-start.41 = (bf16[2,2048,128]{2,1,0:T(8,128)(2,1)}, bf16[2,2048,128]{2,1,0:T(8,128)(2,1)}, u32[]{:S(2)}, u32[]{:S(2)}) collective-permute-start(bf16[2,2048,128]{2,1,0:T(8,128)(2,1)} %get-tuple-element.328), channel_id=1, source_target_pairs={{0,1},{1,0},{2,3},{3,2},{4,5},{5,4},{6,7},{7,6},{8,9},{9,8},{10,11... | collective-permute-start | bytes 3145736 | tf_op jit(solution)/shard_map/ppermute | solution.py:736
  463.3 51.5 %all-to-all-start.6 = ((bf16[4,128,2048]{2,1,0:T(8,128)(2,1)}), bf16[4,128,2048]{2,1,0:T(8,128)(2,1)S(1)}, u32[]{:S(2)}, u32[]{:S(2)}) async-start(bf16[4,128,2048]{2,1,0:T(8,128)(2,1)} %bitcast.57), calls=%async_computation.6 | async-start | bytes 4194304 | tf_op jit(solution)/shard_map/all_to_all | solution.py:727
  470.3 20.1 %collective-permute-start.42 = (bf16[2816,128]{1,0:T(8,128)(2,1)}, bf16[2816,128]{1,0:T(8,128)(2,1)}, u32[]{:S(2)}, u32[]{:S(2)}) collective-permute-start(bf16[2816,128]{1,0:T(8,128)(2,1)} %get-tuple-element.331.refs_2_), channel_id=1, source_target_pairs={{0,8},{8,0},{16,24},{24,16},{1,9},{9,1},{17,25},{25,17},{2,10},{10... | collective-permute-start | bytes 2162696 | tf_op jit(solution)/shard_map/ppermute | solution.py:783
  473.0 17.4 %collective-permute-start.43 = (bf16[2816,128]{1,0:T(8,128)(2,1)}, bf16[2816,128]{1,0:T(8,128)(2,1)}, u32[]{:S(2)}, u32[]{:S(2)}) collective-permute-start(bf16[2816,128]{1,0:T(8,128)(2,1)} %get-tuple-element.332.refs_2_), channel_id=1, source_target_pairs={{8,16},{16,8},{9,17},{17,9},{10,18},{18,10},{11,19},{19,11},{12,20... | collective-permute-start | bytes 2162696 | tf_op jit(solution)/shard_map/ppermute | solution.py:785
  482.0 23.8 %collective-permute-start.51 = (bf16[2816,128]{1,0:T(8,128)(2,1)}, bf16[2816,128]{1,0:T(8,128)(2,1)S(1)}, u32[]{:S(2)}, u32[]{:S(2)}) collective-permute-start(bf16[2816,128]{1,0:T(8,128)(2,1)} %get-tuple-element.352.refs_4_), channel_id=1, source_target_pairs={{0,8},{8,0},{16,24},{24,16},{1,9},{9,1},{17,25},{25,17},{2,10},{10... | collective-permute-start | bytes 2162696 | tf_op jit(solution)/shard_map/ppermute | solution.py:783
  484.2 21.5 %collective-permute-start.52 = (bf16[2816,128]{1,0:T(8,128)(2,1)}, bf16[2816,128]{1,0:T(8,128)(2,1)}, u32[]{:S(2)}, u32[]{:S(2)}) collective-permute-start(bf16[2816,128]{1,0:T(8,128)(2,1)} %get-tuple-element.353.refs_2_), channel_id=1, source_target_pairs={{8,16},{16,8},{9,17},{17,9},{10,18},{18,10},{11,19},{19,11},{12,20... | collective-permute-start | bytes 2162696 | tf_op jit(solution)/shard_map/ppermute | solution.py:785
  493.8 27.5 %collective-permute-start.44 = (bf16[2816,128]{1,0:T(8,128)(2,1)}, bf16[2816,128]{1,0:T(8,128)(2,1)}, u32[]{:S(2)}, u32[]{:S(2)}) collective-permute-start(bf16[2816,128]{1,0:T(8,128)(2,1)} %get-tuple-element.336.refs_6_), channel_id=1, source_target_pairs={{0,8},{8,0},{16,24},{24,16},{1,9},{9,1},{17,25},{25,17},{2,10},{10... | collective-permute-start | bytes 2162696 | tf_op jit(solution)/shard_map/ppermute | solution.py:783
  497.8 23.5 %collective-permute-start.45 = (bf16[2816,128]{1,0:T(8,128)(2,1)}, bf16[2816,128]{1,0:T(8,128)(2,1)}, u32[]{:S(2)}, u32[]{:S(2)}) collective-permute-start(bf16[2816,128]{1,0:T(8,128)(2,1)} %get-tuple-element.337.refs_2_), channel_id=1, source_target_pairs={{8,16},{16,8},{9,17},{17,9},{10,18},{18,10},{11,19},{19,11},{12,20... | collective-permute-start | bytes 2162696 | tf_op jit(solution)/shard_map/ppermute | solution.py:785
  509.9 26.7 %collective-permute-start.53 = (bf16[2816,128]{1,0:T(8,128)(2,1)}, bf16[2816,128]{1,0:T(8,128)(2,1)S(1)}, u32[]{:S(2)}, u32[]{:S(2)}) collective-permute-start(bf16[2816,128]{1,0:T(8,128)(2,1)} %get-tuple-element.357.refs_0_), channel_id=1, source_target_pairs={{0,8},{8,0},{16,24},{24,16},{1,9},{9,1},{17,25},{25,17},{2,10},{10... | collective-permute-start | bytes 2162696 | tf_op jit(solution)/shard_map/ppermute | solution.py:783
  513.3 23.4 %collective-permute-start.54 = (bf16[2816,128]{1,0:T(8,128)(2,1)}, bf16[2816,128]{1,0:T(8,128)(2,1)}, u32[]{:S(2)}, u32[]{:S(2)}) collective-permute-start(bf16[2816,128]{1,0:T(8,128)(2,1)} %get-tuple-element.358.refs_2_), channel_id=1, source_target_pairs={{8,16},{16,8},{9,17},{17,9},{10,18},{18,10},{11,19},{19,11},{12,20... | collective-permute-start | bytes 2162696 | tf_op jit(solution)/shard_map/ppermute | solution.py:785
  524.6 29.3 %collective-permute-start.46 = (bf16[2816,128]{1,0:T(8,128)(2,1)}, bf16[2816,128]{1,0:T(8,128)(2,1)}, u32[]{:S(2)}, u32[]{:S(2)}) collective-permute-start(bf16[2816,128]{1,0:T(8,128)(2,1)} %get-tuple-element.345.refs_2_), channel_id=1, source_target_pairs={{0,8},{8,0},{16,24},{24,16},{1,9},{9,1},{17,25},{25,17},{2,10},{10... | collective-permute-start | bytes 2162696 | tf_op jit(solution)/shard_map/ppermute | solution.py:783
  528.7 25.2 %collective-permute-start.47 = (bf16[2816,128]{1,0:T(8,128)(2,1)}, bf16[2816,128]{1,0:T(8,128)(2,1)}, u32[]{:S(2)}, u32[]{:S(2)}) collective-permute-start(bf16[2816,128]{1,0:T(8,128)(2,1)} %get-tuple-element.346.refs_2_), channel_id=1, source_target_pairs={{8,16},{16,8},{9,17},{17,9},{10,18},{18,10},{11,19},{19,11},{12,20... | collective-permute-start | bytes 2162696 | tf_op jit(solution)/shard_map/ppermute | solution.py:785
  540.5 31.5 %collective-permute-start.55 = (bf16[2816,128]{1,0:T(8,128)(2,1)}, bf16[2816,128]{1,0:T(8,128)(2,1)}, u32[]{:S(2)}, u32[]{:S(2)}) collective-permute-start(bf16[2816,128]{1,0:T(8,128)(2,1)} %get-tuple-element.362.refs_4_), channel_id=1, source_target_pairs={{0,8},{8,0},{16,24},{24,16},{1,9},{9,1},{17,25},{25,17},{2,10},{10... | collective-permute-start | bytes 2162696 | tf_op jit(solution)/shard_map/ppermute | solution.py:783
  543.8 28.2 %collective-permute-start.56 = (bf16[2048,128]{1,0:T(8,128)(2,1)}, bf16[2048,128]{1,0:T(8,128)(2,1)}, u32[]{:S(2)}, u32[]{:S(2)}) collective-permute-start(bf16[2048,128]{1,0:T(8,128)(2,1)} %get-tuple-element.363.refs_2_), channel_id=1, source_target_pairs={{8,16},{16,8},{9,17},{17,9},{10,18},{18,10},{11,19},{19,11},{12,20... | collective-permute-start | bytes 1572872 | tf_op jit(solution)/shard_map/ppermute | solution.py:785
  554.0 16.0 %collective-permute-start.48 = (f32[2,256]{1,0:T(2,128)S(1)}, f32[2,256]{1,0:T(2,128)S(1)}, u32[]{:S(2)}, u32[]{:S(2)}) collective-permute-start(f32[2,256]{1,0:T(2,128)S(1)} %reduce_sum.20), channel_id=1, source_target_pairs={{0,8},{24,16},{1,9},{25,17},{2,10},{26,18},{3,11},{27,19},{4,12},{... | collective-permute-start | bytes 6152 | tf_op jit(solution)/shard_map/ppermute | solution.py:897
  568.5 21.5 %collective-permute-start.61 = (bf16[2816,128]{1,0:T(8,128)(2,1)}, bf16[2816,128]{1,0:T(8,128)(2,1)}, u32[]{:S(2)}, u32[]{:S(2)}) collective-permute-start(bf16[2816,128]{1,0:T(8,128)(2,1)} %get-tuple-element.377.refs_6_), channel_id=1, source_target_pairs={{0,8},{8,0},{16,24},{24,16},{1,9},{9,1},{17,25},{25,17},{2,10},{10... | collective-permute-start | bytes 2162696 | tf_op jit(solution)/shard_map/ppermute | solution.py:783
  568.5 21.5 %collective-permute-start.62 = (bf16[2048,128]{1,0:T(8,128)(2,1)}, bf16[2048,128]{1,0:T(8,128)(2,1)}, u32[]{:S(2)}, u32[]{:S(2)}) collective-permute-start(bf16[2048,128]{1,0:T(8,128)(2,1)} %get-tuple-element.378.refs_2_), channel_id=1, source_target_pairs={{8,16},{16,8},{9,17},{17,9},{10,18},{18,10},{11,19},{19,11},{12,20... | collective-permute-start | bytes 1572872 | tf_op jit(solution)/shard_map/ppermute | solution.py:785
  574.8 21.3 %collective-permute-start.57 = (bf16[2048,128]{1,0:T(8,128)(2,1)}, bf16[2048,128]{1,0:T(8,128)(2,1)S(1)}, u32[]{:S(2)}, u32[]{:S(2)}) collective-permute-start(bf16[2048,128]{1,0:T(8,128)(2,1)} %get-tuple-element.367.refs_0_), channel_id=1, source_target_pairs={{0,8},{8,0},{16,24},{24,16},{1,9},{9,1},{17,25},{25,17},{2,10},{10... | collective-permute-start | bytes 1572872 | tf_op jit(solution)/shard_map/ppermute | solution.py:783
  592.7 22.6 %collective-permute-start.63 = (bf16[2048,128]{1,0:T(8,128)(2,1)}, bf16[2048,128]{1,0:T(8,128)(2,1)S(1)}, u32[]{:S(2)}, u32[]{:S(2)}) collective-permute-start(bf16[2048,128]{1,0:T(8,128)(2,1)} %get-tuple-element.382.refs_2_), channel_id=1, source_target_pairs={{0,8},{8,0},{16,24},{24,16},{1,9},{9,1},{17,25},{25,17},{2,10},{10... | collective-permute-start | bytes 1572872 | tf_op jit(solution)/shard_map/ppermute | solution.py:783
  (63 other events, 495.1 us)

commit v4 on v3

--- a/solution.py
+++ b/solution.py
@@ -252,7 +252,7 @@
 
 
 def attention_backward(
-    ids, lengths, q, kv_own, kv_other, sums, d_out, cos_table, sin_table, rows, stack=2
+    ids, lengths, q, kv_own, kv_other, sums, d_out, cos_table, sin_table, rows, stack=4
 ):
     own, qw = q.shape
     scale = 1.0 / math.sqrt(HD)
@@ -277,14 +277,18 @@
                 cos, sin = cos_ref[...], sin_ref[...]
                 keys = jnp.concatenate([a_ref[:span, :], b_ref[:span, :]], axis=0)
                 k, v = keys[:, :HD], keys[:, HD:]
-                dk, dv = 0.0, 0.0
-                for g in range(heads // stack):
-                    part = range(g * stack, (g + 1) * stack)
-                    qs = [q_ref[:, h * HD : (h + 1) * HD] for h in part]
-                    qs = jnp.concatenate(qs, axis=0) * jnp.asarray(scale, BF16)
-                    ds = [d_ref[:, h * HD : (h + 1) * HD] * valid for h in part]
+                lane = lax.broadcasted_iota(jnp.int32, (rows, 128), 1)
+
+                def some(g, carry):
+                    at = pl.ds(pl.multiple_of(g * stack * HD, 128), stack * HD)
+                    wide_q = q_ref[:, at] * jnp.asarray(scale, BF16)
+                    wide_d = d_ref[:, at] * valid
+                    qs = [wide_q[:, h * HD : (h + 1) * HD] for h in range(stack)]
+                    qs = jnp.concatenate(qs, axis=0)
+                    ds = [wide_d[:, h * HD : (h + 1) * HD] for h in range(stack)]
                     ds = jnp.concatenate(ds, axis=0)
-                    lse = jnp.stack([l_ref[:, h : h + 1] for h in part])
+                    lse = [jnp.where(lane == g * stack + t, l_ref[...], 0.0) for t in range(stack)]
+                    lse = jnp.stack([jnp.sum(v, axis=-1, keepdims=True) for v in lse])
                     s = dot_nt(qs, k).reshape(stack, rows, 2 * span) + bias[None]
                     p = jnp.exp(s - lse)
                     dp = dot_nt(ds, v).reshape(stack, rows, 2 * span)
@@ -292,16 +296,17 @@
                     grad = (p * (dp - inner)).astype(BF16).reshape(stack * rows, 2 * span)
                     p = p.astype(BF16).reshape(stack * rows, 2 * span)
                     dq = (dot(grad, k) * scale).reshape(stack, rows, HD)
-                    dk = dk + dot_tn(grad, qs)
-                    dv = dv + dot_tn(p, ds)
+                    both = jnp.concatenate([dot_tn(grad, qs), dot_tn(p, ds)], axis=1)
+                    dkv_ref[:span, :] += both[:span]
+                    dkv_ref[own : own + span, :] += both[span:]
                     for t in range(1, stack, 2):
-                        h = g * stack + t
                         w = jnp.concatenate([dq[t - 1], dq[t]], axis=1)
                         w = w * cos - turned(w) * sin
-                        dq_ref[:, (h - 1) * HD : (h + 1) * HD] = w.astype(BF16)
-                both = jnp.concatenate([dk, dv], axis=1)
-                dkv_ref[:span, :] += both[:span]
-                dkv_ref[own : own + span, :] += both[span:]
+                        to = pl.ds(pl.multiple_of((g * stack + t - 1) * HD, 128), 2 * HD)
+                        dq_ref[:, to] = w.astype(BF16)
+                    return carry
+
+                lax.fori_loop(0, heads // stack, some, 0)
 
     blocked = lambda i: (i, 0)
     fixed = pl.BlockSpec((own, 2 * HD), lambda i: (0, 0))
@@ -339,8 +344,9 @@
             for k in range(chips):
                 at = pl.multiple_of((chip ^ k) * rows, rows)
                 z_ref[pl.ds(at, rows), :] = z_refs[k][...]
-
-        def work(cols, first, last):
+            acc_ref[...] = jnp.zeros_like(acc_ref)
+
+        def work(cols, last):
             for m in range(2):
                 for i in range(4):
                     side = core if i < 2 else 1 - core
@@ -359,18 +365,21 @@
             dg_ref[:, :cols] = dg
             du_ref[:, :cols] = du
             back = dot_nt(dg, w_ref[0, :, :cols]) + dot_nt(du, w_ref[1, :, :cols])
-            if not first:
-                back = back + acc_ref[...]
+            back = back + acc_ref[...]
             if last:
                 b_ref[...] = back.astype(BF16)
             else:
                 acc_ref[...] = back
 
-        for n in range(turns):
-
-            @pl.when(turn == n)
-            def _(n=n):
-                work(min(tile, width - n * tile), n == 0, n == turns - 1)
+        if turns > 1:
+
+            @pl.when(turn < turns - 1)
+            def _():
+                work(tile, False)
+
+        @pl.when(turn == turns - 1)
+        def _():
+            work(width - (turns - 1) * tile, True)
 
     joined = pl.BlockSpec((own, model), lambda n, s: (0, 0))
     out_tile = pl.BlockSpec((own, tile), lambda n, s: (0, n))
@@ -786,6 +795,9 @@
         )
         return carry if len(carry) != 1 else carry[0]
 
+    def summed(name, count):
+        return [sums_of[f"{name}{k}"] for k in range(count)]
+
     starts = 2 * rows * jnp.arange(chips, dtype=jnp.int32) + core * rows
     own_pos = (starts[:, None] + jnp.arange(rows, dtype=jnp.int32)[None, :]).reshape(own)
     lane = jnp.arange(128)
@@ -813,18 +825,19 @@
     gate_traded = trade(gate_near)
     kv_far = swap(kv_near)
     attn, sums = attention_forward(ids, doc_lengths, queries, kv_near, kv_far, rows)
-    attn, up_near = tie((attn, up_near))
+    gate_far = swap(gate_near)
+    attn, up_near, gate_far = tie((attn, up_near, gate_far))
     up_traded = trade(up_near)
     *mixed, w_out_c = out_proj(ids, attn, w_out, w_out_far, chips)
     *mixed, cot = tie((*mixed, cot))
     parts = hops(mixed)
     cot_rows = exchange(copies(cot))
-    *parts, gate_traded = tie((*parts, gate_traded))
+    *parts, gate_traded, up_far = tie((*parts, gate_traded, swap(up_near)))
     resid, normed = residual_norm(tokens, parts)
     z_blocks = hops([normed] * chips)
     weights = [
-        [near, far, swap(near), swap(far)]
-        for near, far in ((gate_near, gate_traded), (up_near, up_traded))
+        [gate_near, gate_traded, gate_far, swap(gate_traded)],
+        [up_near, up_traded, up_far, swap(up_traded)],
     ]
     inner, grad_gate, grad_up, normed_two, back = feed_forward(
         ids, z_blocks, cot_rows, weights, w_down_c
@@ -877,38 +890,54 @@
     norms = norms.reshape(2, chips, 2, wrows).transpose(2, 1, 0, 3)
     mine = lax.dynamic_index_in_dim(norms, core, 0, keepdims=False)
     other = lax.dynamic_index_in_dim(norms, 1 - core, 0, keepdims=False)
-    norms = mine + swap(other)
+    mine = mine + swap(other)
     out_part = pair_sum(out_near, out_far)
-    norms, qkv_part, out_part = visit(norms, qkv_part, out_part, new=("up", up_part, 3))
+    if reps == 4:
+        grad_down = beside(ids, summed("down", 4), w_down.shape[0], model // 4)
+        mine, grad_down = tie((mine, grad_down))
+    mine, qkv_part, out_part = visit(mine, qkv_part, out_part, new=("up", up_part, 3))
     parts = exchange(out).reshape(chips, rows, model)
-    visit(new=("out", out_part, 0))
-    parts = visit(parts, new=("out", out_part, 1))
-    norms = jnp.sum(exchange(norms), axis=0)
+    norms = lax.dynamic_index_in_dim(mine, chip, 0, keepdims=False)
+    for k in range(1, chips):
+        norms = norms + hop(lax.dynamic_index_in_dim(mine, chip ^ k, 0, keepdims=False), k)
+    qkv_part = qkv_part.reshape(2, -1, 128)
+    norms = visit(norms, new=("qkv", qkv_part, 0))
+    parts, norms = visit(parts, norms, new=("qkv", qkv_part, 1))
     result = (resid + jnp.sum(parts.astype(F32), axis=0)).astype(BF16)
-    visit(new=("qkv", qkv_part, 0))
-    norms = visit(norms, new=("qkv", qkv_part, 1))
-    for k in range(2, chips):
-        visit(new=("qkv", qkv_part, k))
+    norms = norms.astype(BF16).reshape(-1, 128)
+    norms = jnp.pad(norms, ((0, 256 - norms.shape[0]), (0, 0)))
+    last = jnp.concatenate([out_part[1], norms], axis=0)[None]
+    if reps == 4:
+        grad_gate_out = beside(ids, summed("gate", 4), wrows, width, gain_two)
+        last, grad_gate_out = visit(last, grad_gate_out, new=("out", out_part, 0))
+    else:
+        visit(new=("out", out_part, 0))
+    visit(new=("last", last, 0))
     if reps != 4:
         for k in range(4, chips):
             visit(new=("gate", gate_part, k))
             visit(new=("up", up_part, k))
-    if reps == 4:
-        norms = norms + lax.ppermute(norms, "rep", [(0, 1), (3, 2)])
-        norms = norms + lax.ppermute(norms, "rep", [(1, 2), (2, 1)])
-        norms = jnp.where(ends == 1, lax.ppermute(norms, "rep", [(1, 0), (2, 3)]), norms)
-    else:
-        norms = lax.psum(norms, "rep")
+        grad_gate_out = beside(ids, summed("gate", chips), wrows, width, gain_two)
     while any(line.busy() for line in lines):
         visit()
 
-    def summed(name, count):
-        return [sums_of[f"{name}{k}"] for k in range(count)]
-
-    qkv = summed("qkv", chips)
+    if reps != 4:
+        grad_down = beside(ids, summed("down", 4), w_down.shape[0], model // 4)
+    rows_of = wrows * pl.cdiv(qw + 2 * HD, 128)
+    qkv = [
+        (a[n : n + rows_of], b[n : n + rows_of])
+        for a, b in summed("qkv", 2)
+        for n in range(0, chips // 2 * rows_of, rows_of)
+    ]
+    last = sums_of["last0"]
+    at = out_part.shape[1]
+    norms = jnp.where(ends == 1, last[1], last[0])[at : at + 2 * wrows // 128]
+    norms = norms.astype(F32).reshape(2, wrows)
     grad_query = beside(ids, qkv, wrows, qw, gain_one)
-    at = qw // 128 * wrows
-    kv = [jnp.where(ends == 1, b[at : at + wrows], a[at : at + wrows]) for a, b in qkv]
+    kv_at = qw // 128 * wrows
+    kv = [
+        jnp.where(ends == 1, b[kv_at : kv_at + wrows], a[kv_at : kv_at + wrows]) for a, b in qkv
+    ]
     kv = jnp.stack(kv).astype(F32).reshape(KVH, kv_share, wrows, 2, HD).sum(axis=1)
     kv = kv * gain_one[None, :, :, None]
     grad_key = kv[:, :, 0].transpose(1, 0, 2).reshape(wrows, KVH * HD)
@@ -920,11 +949,11 @@
         grad_query,
         grad_key,
         grad_value,
-        beside(ids, summed("out", 2), wrows, model // 2),
+        beside(ids, [sums_of["out0"], tuple(v[:at] for v in last)], wrows, model // 2),
         norms[1] / gain_two[:, 0],
-        beside(ids, summed("gate", chips), wrows, width, gain_two),
+        grad_gate_out,
         beside(ids, summed("up", chips), wrows, width, gain_two),
-        beside(ids, summed("down", 4), w_down.shape[0], model // 4),
+        grad_down,
     )
 
 

time: 658 us -> 653 us (level)
  waiting for transfers between devices: 203 us -> 223 us
  starting transfers between devices: 147 us -> 135 us
  blocking collectives: 8.63 us -> 0 us
    ppermute x22 -> x20, waiting for transfers between devices: 77.2 us -> 93 us  [visit(): lax.ppermute(ahead, 'rep', outer_pairs)]
    ppermute x22 -> x20, starting transfers between devices: 53.9 us -> 44.5 us  [visit(): lax.ppermute(ahead, 'rep', outer_pairs)]
    all_to_all x1 -> x0, blocking collectives: 8.63 us -> none  [exchange(): return lax.all_to_all(v, 'fsdp', 0, 0, axis_index_groups=sides, tiled=True)]
    ppermute x9 -> x12, starting transfers between devices: 13 us -> 18.8 us  [hop(): return lax.ppermute(v, 'fsdp', [(i, i ^ 2 * k) for i in range(group)])]
    unnamed x97 -> x92, local copies, waits for them, and re-layouts: 20.1 us -> 15.5 us
    pallas_call x20 -> x18, Pallas kernels: 59.4 us -> 56.2 us  [chain_step(): pl.pallas_call(body, grid=(1,), in_specs=[scalars()] + [spec(v) for v in...]
    ppermute x9 -> x12, waiting for transfers between devices: 54.4 us -> 57.1 us  [hop(): return lax.ppermute(v, 'fsdp', [(i, i ^ 2 * k) for i in range(group)])]
    ppermute x18 -> x16, starting transfers between devices: 23.9 us -> 21.2 us  [visit(): lax.ppermute(line.sent[1], 'rep', [(1, 2), (2, 1)])]
  transfers between devices with their start and end apart: 80 -> 76, of which waited for: 25 -> 30; matrix products, arithmetic and copies ran while one was open for 5% -> 6% of each run, Pallas kernels for 30% -> 29%
where the time goes in v4:
time: 653 us; the launch traced here: 645 us
  Pallas kernels  232 us (36%)
  waiting for transfers between devices  223 us (34%)
  starting transfers between devices  135 us (21%)
  local copies, waits for them, and re-layouts  32.4 us (5%)
  matrix products  14.7 us (2%)
  other arithmetic  6.69 us (1%)
    ppermute x20, waiting for transfers between devices, visit(): lax.ppermute(ahead, 'rep', outer_pairs)  93 us
    all_to_all x11, waiting for transfers between devices, exchange(): return lax.all_to_all(v, 'fsdp', 0, 0, axis_index_groups=sides, tiled=True)  62.1 us
    ppermute x12, waiting for transfers between devices, hop(): return lax.ppermute(v, 'fsdp', [(i, i ^ 2 * k) for i in range(group)])  57.1 us
    pallas_call x18, Pallas kernels, chain_step(): pl.pallas_call(body, grid=(1,), in_specs=[scalars()] + [spec(v) for v in...  56.2 us
    all_to_all x11, starting transfers between devices, exchange(): return lax.all_to_all(v, 'fsdp', 0, 0, axis_index_groups=sides, tiled=True)  44.9 us
    ppermute x20, starting transfers between devices, visit(): lax.ppermute(ahead, 'rep', outer_pairs)  44.5 us
    pallas_call x5, Pallas kernels, beside(): pl.pallas_call(body, grid_spec=pltpu.PrefetchScalarGridSpec(num_scalar_pr...  27.9 us
    pallas_call x3, Pallas kernels, weight_grad(): pl.pallas_call(body, grid_spec=pltpu.PrefetchScalarGridSpec(num_scalar_pr...  25.9 us
  transfers between devices with their start and end apart: 76, of which 30 were waited for; matrix products, arithmetic and copies ran while one was open for 6% of the time, Pallas kernels for 29%

profile of v4, /device:TPU:0, one launch (start us, length us, event | category | flops | bytes accessed | tf_op | source)
XLA Modules:
  0.0 644.8 jit_solution(1045917901337006276)
XLA Ops:
  2.6 4.1 pick_qkv.1
  6.7 4.7 all-to-all-start
  16.7 12.6 %all-to-all-done.n_ref = bf16[4,256,640]{2,1,0:T(8,128)(2,1)S(1)} async-done(((bf16[4,256,640]{2,1,0:T(8,128)(2,1)}), bf16[4,256,640]{2,1,0:T(8,128)(2,1)S(1)}, u32[]{:S(2)}, u32[]{:S(2)}) %all-to-all-start) | async-done | bytes 1310752 | tf_op jit(solution)/shard_map/all_to_all | solution.py:736
  31.1 4.9 pick_half.1
  36.0 6.1 join_cores.1.refs_13_
  42.1 9.9 %collective-permute-done.2.refs_3_ = bf16[128,2048]{1,0:T(8,128)(2,1)} collective-permute-done((bf16[128,2048]{1,0:T(8,128)(2,1)S(1)}, bf16[128,2048]{1,0:T(8,128)(2,1)}, u32[]{:S(2)}, u32[]{:S(2)}) %collective-permute-start.2) | collective-permute-done | bytes 524320 | tf_op jit(solution)/shard_map/ppermute | solution.py:739
  52.0 3.6 all-to-all-start.1
  55.6 6.5 %qkv_forward.1 = (bf16[512,2048]{1,0:T(8,128)(2,1)}, bf16[512,512]{1,0:T(8,128)(2,1)}, bf16[512,128]{1,0:T(8,128)(2,1)}, bf16[2048,640]{1,0:T(8,128)(2,1)}) custom-call(s32[5]{0:T(128)} %stack.38.s_ref.c_ref, f32[512,128]{1,0:T(8,128)} %get-tuple-element.200.cos_ref, f32[512,128]{1,0:T(8,128)} %get-tuple-element.201.sin_ref, bf16[4,256,640]{2,1,0:T(8,128)(2,1)} %copy-done.7, ...), custom_call_target="tpu_custom_call" | custom-call | flops 1024 | bytes 1024 | tf_op jit(solution)/shard_map/qkv_forward/pallas_call | solution.py:167
  62.1 11.1 %all-to-all-done.1.refs_5_ = bf16[4,128,1408]{2,1,0:T(8,128)(2,1)S(1)} async-done(((bf16[4,128,1408]{2,1,0:T(8,128)(2,1)}), bf16[4,128,1408]{2,1,0:T(8,128)(2,1)S(1)}, u32[]{:S(2)}, u32[]{:S(2)}) %all-to-all-start.1) | async-done | bytes 1441824 | tf_op jit(solution)/shard_map/all_to_all | solution.py:736
  73.2 4.5 all-to-all-start.2
  81.0 8.9 %attention_forward.1 = (bf16[512,512]{1,0:T(8,128)(2,1)}, f32[512,128]{1,0:T(8,128)}) custom-call(s32[5]{0:T(128)} %stack.38.s_ref.c_ref, s32[4,8]{1,0:T(4,128)} %n_ref.3, bf16[512,512]{1,0:T(8,128)(2,1)} %get-tuple-element.209.q_ref, bf16[512,128]{1,0:T(8,128)(2,1)} %get-tuple-element.210.a_ref, bf16[512,128]{1,0:T(8,128)(2,1)} %collective-permute-done.6.b_ref), custom_call_target="tpu_custom_call" | custom-call | flops 1024 | bytes 1024 | tf_op jit(solution)/shard_map/attention_forward/pallas_call | solution.py:240
  89.9 6.7 %all-to-all-done.2.refs_9_ = bf16[4,128,1408]{2,1,0:T(8,128)(2,1)} async-done(((bf16[4,128,1408]{2,1,0:T(8,128)(2,1)}), bf16[4,128,1408]{2,1,0:T(8,128)(2,1)}, u32[]{:S(2)}, u32[]{:S(2)}) %all-to-all-start.2) | async-done | bytes 1441824 | tf_op jit(solution)/shard_map/all_to_all | solution.py:736
  98.4 4.6 out_proj.1
  105.0 7.3 %collective-permute-done.11.refs_6_ = bf16[4,128,1408]{2,1,0:T(8,128)(2,1)} collective-permute-done((bf16[4,128,1408]{2,1,0:T(8,128)(2,1)S(1)}, bf16[4,128,1408]{2,1,0:T(8,128)(2,1)}, u32[]{:S(2)}, u32[]{:S(2)}) %collective-permute-start.11) | collective-permute-done | bytes 1441824 | tf_op jit(solution)/shard_map/ppermute | solution.py:748
  116.8 3.8 all-to-all-start.3
  120.7 19.9 %collective-permute-done.9.refs_2_ = bf16[128,2048]{1,0:T(8,128)(2,1)} collective-permute-done((bf16[128,2048]{1,0:T(8,128)(2,1)}, bf16[128,2048]{1,0:T(8,128)(2,1)}, u32[]{:S(2)}, u32[]{:S(2)}) %collective-permute-start.9) | collective-permute-done | bytes 524320 | tf_op jit(solution)/shard_map/ppermute | solution.py:739
  152.2 10.9 %collective-permute-done.13.refs_1_ = bf16[128,2048]{1,0:T(8,128)(2,1)} collective-permute-done((bf16[128,2048]{1,0:T(8,128)(2,1)}, bf16[128,2048]{1,0:T(8,128)(2,1)}, u32[]{:S(2)}, u32[]{:S(2)}) %collective-permute-start.13) | collective-permute-done | bytes 524320 | tf_op jit(solution)/shard_map/ppermute | solution.py:739
  163.1 11.6 %collective-permute-done.14.refs_2_ = bf16[128,2048]{1,0:T(8,128)(2,1)} collective-permute-done((bf16[128,2048]{1,0:T(8,128)(2,1)}, bf16[128,2048]{1,0:T(8,128)(2,1)}, u32[]{:S(2)}, u32[]{:S(2)}) %collective-permute-start.14) | collective-permute-done | bytes 524320 | tf_op jit(solution)/shard_map/ppermute | solution.py:739
  175.8 25.7 %feed_forward.1 = (bf16[512,1408]{1,0:T(8,128)(2,1)}, bf16[512,1408]{1,0:T(8,128)(2,1)}, bf16[512,1408]{1,0:T(8,128)(2,1)}, bf16[512,2048]{1,0:T(8,128)(2,1)}, bf16[512,2048]{1,0:T(8,128)(2,1)}) custom-call(s32[5]{0:T(128)} %stack.38.s_ref.c_ref, bf16[128,2048]{1,0:T(8,128)(2,1)} %get-tuple-element.231.refs_0_, ...), custom_call_target="tpu_custom_call" | custom-call | flops 1024 | bytes 1024 | tf_op jit(solution)/shard_map/feed_forward/pallas_call | solution.py:386
  201.5 8.1 %row_grad.2 = (bf16[4,2816,128]{2,1,0:T(8,128)(2,1)}, bf16[4,2816,128]{2,1,0:T(8,128)(2,1)}) custom-call(s32[5]{0:T(128)} %stack.38.s_ref.c_ref, bf16[512,1408]{1,0:T(8,128)(2,1)} %get-tuple-element.256.l_ref, bf16[512,2048]{1,0:T(8,128)(2,1)} %bitcast.81), custom_call_target="tpu_custom_call" | custom-call | flops 1024 | bytes 1024 | tf_op jit(solution)/shard_map/row_grad/pallas_call | solution.py:562
  209.6 10.0 %weight_grad.3 = (bf16[4,2816,128]{2,1,0:T(8,128)(2,1)}, bf16[4,2816,128]{2,1,0:T(8,128)(2,1)}) custom-call(s32[5]{0:T(128)} %stack.38.s_ref.c_ref, bf16[512,2048]{1,0:T(8,128)(2,1)} %get-tuple-element.237.l_ref, bf16[512,1408]{1,0:T(8,128)(2,1)} %get-tuple-element.241.r_ref), custom_call_target="tpu_custom_call" | custom-call | flops 1024 | bytes 1024 | tf_op jit(solution)/shard_map/weight_grad/pallas_call | solution.py:527
  221.3 3.6 all-to-all-start.4
  225.4 4.9 pair_sum.7
  230.3 20.3 %all-to-all-done.4 = bf16[4,128,2048]{2,1,0:T(8,128)(2,1)S(1)} async-done(((bf16[4,128,2048]{2,1,0:T(8,128)(2,1)}), bf16[4,128,2048]{2,1,0:T(8,128)(2,1)S(1)}, u32[]{:S(2)}, u32[]{:S(2)}) %all-to-all-start.4) | async-done | bytes 2097184 | tf_op jit(solution)/shard_map/all_to_all | solution.py:736
  252.0 3.7 all-to-all-start.5
  255.7 4.9 pair_sum.5.refs_0_.refs_2_
  260.6 9.6 %weight_grad.4 = (bf16[4,2816,128]{2,1,0:T(8,128)(2,1)}, bf16[4,2816,128]{2,1,0:T(8,128)(2,1)}) custom-call(s32[5]{0:T(128)} %stack.38.s_ref.c_ref, bf16[512,2048]{1,0:T(8,128)(2,1)} %get-tuple-element.237.l_ref, bf16[512,1408]{1,0:T(8,128)(2,1)} %get-tuple-element.249.r_ref), custom_call_target="tpu_custom_call" | custom-call | flops 1024 | bytes 1024 | tf_op jit(solution)/shard_map/weight_grad/pallas_call | solution.py:527
  272.7 4.6 residual_norm_back.2
  277.2 13.9 %collective-permute-done.20.refs_1_ = bf16[2816,128]{1,0:T(8,128)(2,1)} collective-permute-done((bf16[2816,128]{1,0:T(8,128)(2,1)}, bf16[2816,128]{1,0:T(8,128)(2,1)}, u32[]{:S(2)}, u32[]{:S(2)}) %collective-permute-start.20) | collective-permute-done | bytes 720928 | tf_op jit(solution)/shard_map/ppermute | solution.py:792
  292.8 4.5 all-to-all-start.7
  304.9 7.3 %convolution_convert_fusion.1 = bf16[512,2048]{1,0:T(8,128)(2,1)} fusion(bf16[512,1408]{1,0:T(8,128)(2,1)S(1)} %copy-done.22, bf16[1408,2048]{1,0:T(8,128)(2,1)} %join_cores.1.refs_13_), kind=kOutput, calls=%fused_computation.2 | convolution fusion | flops 2953838592 | bytes 9306112 | tf_op jit(solution)/shard_map/dot_general | solution.py:24
  312.1 4.9 pair_sum.6
  317.5 14.3 %collective-permute-done.24.refs_1_ = bf16[2816,128]{1,0:T(8,128)(2,1)} collective-permute-done((bf16[2816,128]{1,0:T(8,128)(2,1)}, bf16[2816,128]{1,0:T(8,128)(2,1)}, u32[]{:S(2)}, u32[]{:S(2)}) %collective-permute-start.24) | collective-permute-done | bytes 720928 | tf_op jit(solution)/shard_map/ppermute | solution.py:792
  331.8 4.1 all-to-all-start.8
  344.1 3.8 collective-permute-start.28
  349.4 4.9 row_grad.3
  354.3 4.3 convolution_convert_fusion.2.d_ref
  358.6 15.6 %attention_backward.1 = (bf16[512,512]{1,0:T(8,128)(2,1)}, f32[1024,128]{1,0:T(8,128)}) custom-call(s32[5]{0:T(128)} %stack.38.s_ref.c_ref, s32[4,8]{1,0:T(4,128)} %n_ref.3, bf16[512,512]{1,0:T(8,128)(2,1)} %get-tuple-element.209.q_ref, bf16[512,128]{1,0:T(8,128)(2,1)} %get-tuple-element.210.a_ref, bf16[512,128]{1,0:T(8,128)(2,1)} %collective-permute-done.6.b_ref, ...), custom_call_target="tpu_custom_call" | custom-call | flops 1024 | bytes 1024 | tf_op jit(solution)/shard_map/attention_backward/pallas_call | solution.py:315
  379.2 3.7 collective-permute-start.31
  384.6 3.4 chain_step.22
  401.8 4.7 all-to-all-start.9
  406.5 6.3 weight_grad.5
  415.5 3.4 chain_step.23
  418.9 3.9 collective-permute-start.36
  424.6 3.8 pair_sum.8
  428.4 11.5 %collective-permute-done.36.refs_7_.refs_1_ = bf16[2816,128]{1,0:T(8,128)(2,1)S(1)} collective-permute-done((bf16[2816,128]{1,0:T(8,128)(2,1)}, bf16[2816,128]{1,0:T(8,128)(2,1)S(1)}, u32[]{:S(2)}, u32[]{:S(2)}) %collective-permute-start.36) | collective-permute-done | bytes 720928 | tf_op jit(solution)/shard_map/ppermute | solution.py:792
  440.7 4.2 all-to-all-start.10
  452.7 8.7 %all-to-all-done.10 = bf16[4,1280,128]{2,1,0:T(8,128)(2,1)S(1)} async-done(((bf16[4,1280,128]{2,1,0:T(8,128)(2,1)}), bf16[4,1280,128]{2,1,0:T(8,128)(2,1)S(1)}, u32[]{:S(2)}, u32[]{:S(2)}) %all-to-all-start.10) | async-done | bytes 1310752 | tf_op jit(solution)/shard_map/all_to_all | solution.py:736
  462.5 3.6 all-to-all-start.6
  473.7 4.0 residual_norm_back.3
  477.8 3.4 chain_step.26
  488.2 6.6 %beside.5 = f32[704,2048]{1,0:T(8,128)} custom-call(s32[5]{0:T(128)} %stack.38.s_ref.c_ref, f32[704,1]{1,0:T(8,128)} %broadcast_in_dim.39.s_ref, bf16[2816,128]{1,0:T(8,128)(2,1)} %get-tuple-element.287.refs_0_, bf16[2816,128]{1,0:T(8,128)(2,1)} %collective-permute-done.28.refs_1_, bf16[2816,128]{1,0:T(8,128)(2,1)} %get-tuple-element.296.refs_2_, ...), custom_call_target="tpu_custom_call" | custom-call | flops 1024 | bytes 1024 | tf_op jit(solution)/shard_map/beside/pallas_call | solution.py:670
  514.4 3.5 chain_step.29
  521.3 6.6 %beside.6 = f32[256,5632]{1,0:T(8,128)} custom-call(s32[5]{0:T(128)} %stack.38.s_ref.c_ref, f32[256,1]{1,0:T(8,128)} %copy.26.n_ref.s_ref, bf16[2816,128]{1,0:T(8,128)(2,1)} %get-tuple-element.320.refs_0_, bf16[2816,128]{1,0:T(8,128)(2,1)} %collective-permute-done.38.refs_1_, bf16[2816,128]{1,0:T(8,128)(2,1)} %get-tuple-element.331.refs_2_, ...), custom_call_target="tpu_custom_call" | custom-call | flops 1024 | bytes 1024 | tf_op jit(solution)/shard_map/beside/pallas_call | solution.py:670
  528.8 5.5 collective-permute-done.53.refs_1_
  537.5 3.8 collective-permute-start.60
  551.1 7.5 %collective-permute-done.60.refs_1_.refs_5_ = bf16[2816,128]{1,0:T(8,128)(2,1)} collective-permute-done((bf16[2816,128]{1,0:T(8,128)(2,1)}, bf16[2816,128]{1,0:T(8,128)(2,1)}, u32[]{:S(2)}, u32[]{:S(2)}) %collective-permute-start.60) | collective-permute-done | bytes 720928 | tf_op jit(solution)/shard_map/ppermute | solution.py:792
  565.8 8.3 %collective-permute-done.51.refs_1_.refs_3_ = bf16[2816,128]{1,0:T(8,128)(2,1)} collective-permute-done((bf16[2816,128]{1,0:T(8,128)(2,1)}, bf16[2816,128]{1,0:T(8,128)(2,1)}, u32[]{:S(2)}, u32[]{:S(2)}) %collective-permute-start.51) | collective-permute-done | bytes 720928 | tf_op jit(solution)/shard_map/ppermute | solution.py:792
  581.6 6.4 collective-permute-done.62
  593.0 10.4 %collective-permute-done.55.refs_1_.refs_7_ = bf16[2816,128]{1,0:T(8,128)(2,1)S(1)} collective-permute-done((bf16[2816,128]{1,0:T(8,128)(2,1)}, bf16[2816,128]{1,0:T(8,128)(2,1)S(1)}, u32[]{:S(2)}, u32[]{:S(2)}) %collective-permute-start.55) | collective-permute-done | bytes 720928 | tf_op jit(solution)/shard_map/ppermute | solution.py:792
  610.3 6.6 %beside.9 = f32[256,5632]{1,0:T(8,128)} custom-call(s32[5]{0:T(128)} %stack.38.s_ref.c_ref, f32[256,1]{1,0:T(8,128)} %copy.26.n_ref.s_ref, bf16[2816,128]{1,0:T(8,128)(2,1)} %get-tuple-element.358.refs_0_, bf16[2816,128]{1,0:T(8,128)(2,1)} %collective-permute-done.53.refs_1_, bf16[2816,128]{1,0:T(8,128)(2,1)} %get-tuple-element.351.refs_2_, ...), custom_call_target="tpu_custom_call" | custom-call | flops 1024 | bytes 1024 | tf_op jit(solution)/shard_map/beside/pallas_call | solution.py:670
  617.8 7.1 %collective-permute-done.57 = bf16[2560,128]{1,0:T(8,128)(2,1)S(1)} collective-permute-done((bf16[2560,128]{1,0:T(8,128)(2,1)}, bf16[2560,128]{1,0:T(8,128)(2,1)S(1)}, u32[]{:S(2)}, u32[]{:S(2)}) %collective-permute-start.57) | collective-permute-done | bytes 655392 | tf_op jit(solution)/shard_map/ppermute | solution.py:792
  629.9 4.5 beside.7
  640.9 3.7 beside.8
  (274 shorter events, 183.9 us)
Async XLA Ops:
  0.6 28.6 %collective-permute-start.4 = (bf16[704,2048]{1,0:T(8,128)(2,1)}, bf16[704,2048]{1,0:T(8,128)(2,1)}, u32[]{:S(2)}, u32[]{:S(2)}) collective-permute-start(bf16[704,2048]{1,0:T(8,128)(2,1)} %a_ref.3), channel_id=1, source_target_pairs={{0,1},{1,0},{2,3},{3,2},{4,5},{5,4},{6,7},{7,6},{8,9},{9,8},{10,11... | collective-permute-start | bytes 8650760 | tf_op jit(solution)/shard_map/ppermute | solution.py:745
  6.7 22.5 %all-to-all-start = ((bf16[4,256,640]{2,1,0:T(8,128)(2,1)}), bf16[4,256,640]{2,1,0:T(8,128)(2,1)S(1)}, u32[]{:S(2)}, u32[]{:S(2)}) async-start(bf16[4,256,640]{2,1,0:T(8,128)(2,1)} %pick_qkv.1), calls=%async_computation | async-start | bytes 2621440 | tf_op jit(solution)/shard_map/all_to_all | solution.py:736
  11.4 40.6 %collective-permute-start.3 = (bf16[256,2048]{1,0:T(8,128)(2,1)S(1)}, bf16[256,2048]{1,0:T(8,128)(2,1)}, u32[]{:S(2)}, u32[]{:S(2)}) collective-permute-start(bf16[256,2048]{1,0:T(8,128)(2,1)S(1)} %copy-done.25), channel_id=1, source_target_pairs={{0,1},{1,0},{2,3},{3,2},{4,5},{5,4},{6,7},{7,6},{8,9},{9,8},{10,11... | collective-permute-start | bytes 3145736 | tf_op jit(solution)/shard_map/ppermute | solution.py:745
  11.6 30.4 %collective-permute-start = (bf16[128,2048]{1,0:T(8,128)(2,1)S(1)}, bf16[128,2048]{1,0:T(8,128)(2,1)S(1)}, u32[]{:S(2)}, u32[]{:S(2)}) collective-permute-start(bf16[128,2048]{1,0:T(8,128)(2,1)S(1)} %copy-done.8), channel_id=1, source_target_pairs={{0,2},{1,3},{2,0},{3,1},{4,6},{5,7},{6,4},{7,5},{8,10},{9,11},{10,... | collective-permute-start | bytes 1572872 | tf_op jit(solution)/shard_map/ppermute | solution.py:739
  13.5 28.5 %collective-permute-start.1 = (bf16[128,2048]{1,0:T(8,128)(2,1)S(1)}, bf16[128,2048]{1,0:T(8,128)(2,1)}, u32[]{:S(2)}, u32[]{:S(2)}) collective-permute-start(bf16[128,2048]{1,0:T(8,128)(2,1)S(1)} %copy-done.8), channel_id=1, source_target_pairs={{0,4},{1,5},{2,6},{3,7},{4,0},{5,1},{6,2},{7,3},{8,12},{9,13},{10,... | collective-permute-start | bytes 1572872 | tf_op jit(solution)/shard_map/ppermute | solution.py:739
  15.0 37.0 %collective-permute-start.2 = (bf16[128,2048]{1,0:T(8,128)(2,1)S(1)}, bf16[128,2048]{1,0:T(8,128)(2,1)}, u32[]{:S(2)}, u32[]{:S(2)}) collective-permute-start(bf16[128,2048]{1,0:T(8,128)(2,1)S(1)} %copy-done.8), channel_id=1, source_target_pairs={{0,6},{1,7},{2,4},{3,5},{4,2},{5,3},{6,0},{7,1},{8,14},{9,15},{10,... | collective-permute-start | bytes 1572872 | tf_op jit(solution)/shard_map/ppermute | solution.py:739
  29.2 26.3 %collective-permute-start.5 = (bf16[4,256,640]{2,1,0:T(8,128)(2,1)S(1)}, bf16[4,256,640]{2,1,0:T(8,128)(2,1)}, u32[]{:S(2)}, u32[]{:S(2)}) collective-permute-start(bf16[4,256,640]{2,1,0:T(8,128)(2,1)S(1)} %all-to-all-done.n_ref), channel_id=1, source_target_pairs={{0,1},{1,0},{2,3},{3,2},{4,5},{5,4},{6,7},{7,6},{8,9},{9,8},{10,11... | collective-permute-start | bytes 3932168 | tf_op jit(solution)/shard_map/ppermute | solution.py:745
  52.0 21.2 %all-to-all-start.1 = ((bf16[4,128,1408]{2,1,0:T(8,128)(2,1)}), bf16[4,128,1408]{2,1,0:T(8,128)(2,1)S(1)}, u32[]{:S(2)}, u32[]{:S(2)}) async-start(bf16[4,128,1408]{2,1,0:T(8,128)(2,1)} %get-tuple-element.207), calls=%async_computation.1 | async-start | bytes 2883584 | tf_op jit(solution)/shard_map/all_to_all | solution.py:736
  73.2 23.3 %collective-permute-start.7 = (bf16[4,128,1408]{2,1,0:T(8,128)(2,1)S(1)}, bf16[4,128,1408]{2,1,0:T(8,128)(2,1)S(1)}, u32[]{:S(2)}, u32[]{:S(2)}) collective-permute-start(bf16[4,128,1408]{2,1,0:T(8,128)(2,1)S(1)} %all-to-all-done.1.refs_5_), channel_id=1, source_target_pairs={{0,1},{1,0},{2,3},{3,2},{4,5},{5,4},{6,7},{7,6},{8,9},{9,8},{10,11... | collective-permute-start | bytes 4325384 | tf_op jit(solution)/shard_map/ppermute | solution.py:745
  73.2 23.3 %all-to-all-start.2 = ((bf16[4,128,1408]{2,1,0:T(8,128)(2,1)}), bf16[4,128,1408]{2,1,0:T(8,128)(2,1)}, u32[]{:S(2)}, u32[]{:S(2)}) async-start(bf16[4,128,1408]{2,1,0:T(8,128)(2,1)} %get-tuple-element.212), calls=%async_computation.2 | async-start | bytes 2883584 | tf_op jit(solution)/shard_map/all_to_all | solution.py:736
  77.7 34.6 %collective-permute-start.11 = (bf16[4,128,1408]{2,1,0:T(8,128)(2,1)S(1)}, bf16[4,128,1408]{2,1,0:T(8,128)(2,1)}, u32[]{:S(2)}, u32[]{:S(2)}) collective-permute-start(bf16[4,128,1408]{2,1,0:T(8,128)(2,1)S(1)} %all-to-all-done.1.refs_5_), channel_id=1, source_target_pairs={{0,8},{8,0},{16,24},{24,16},{1,9},{9,1},{17,25},{25,17},{2,10},{10... | collective-permute-start | bytes 4325384 | tf_op jit(solution)/shard_map/ppermute | solution.py:748
  96.6 44.8 %collective-permute-start.12 = (bf16[4,128,1408]{2,1,0:T(8,128)(2,1)}, bf16[4,128,1408]{2,1,0:T(8,128)(2,1)}, u32[]{:S(2)}, u32[]{:S(2)}) collective-permute-start(bf16[4,128,1408]{2,1,0:T(8,128)(2,1)} %all-to-all-done.2.refs_9_), channel_id=1, source_target_pairs={{0,1},{1,0},{2,3},{3,2},{4,5},{5,4},{6,7},{7,6},{8,9},{9,8},{10,11... | collective-permute-start | bytes 4325384 | tf_op jit(solution)/shard_map/ppermute | solution.py:745
  96.6 46.2 %collective-permute-start.17 = (bf16[4,128,1408]{2,1,0:T(8,128)(2,1)}, bf16[4,128,1408]{2,1,0:T(8,128)(2,1)}, u32[]{:S(2)}, u32[]{:S(2)}) collective-permute-start(bf16[4,128,1408]{2,1,0:T(8,128)(2,1)} %all-to-all-done.2.refs_9_), channel_id=1, source_target_pairs={{0,8},{8,0},{16,24},{24,16},{1,9},{9,1},{17,25},{25,17},{2,10},{10... | collective-permute-start | bytes 4325384 | tf_op jit(solution)/shard_map/ppermute | solution.py:748
  103.0 17.6 %collective-permute-start.8 = (bf16[128,2048]{1,0:T(8,128)(2,1)}, bf16[128,2048]{1,0:T(8,128)(2,1)}, u32[]{:S(2)}, u32[]{:S(2)}) collective-permute-start(bf16[128,2048]{1,0:T(8,128)(2,1)} %get-tuple-element.222), channel_id=1, source_target_pairs={{0,2},{1,3},{2,0},{3,1},{4,6},{5,7},{6,4},{7,5},{8,10},{9,11},{10,... | collective-permute-start | bytes 1572872 | tf_op jit(solution)/shard_map/ppermute | solution.py:739
  104.5 36.1 %collective-permute-start.9 = (bf16[128,2048]{1,0:T(8,128)(2,1)}, bf16[128,2048]{1,0:T(8,128)(2,1)}, u32[]{:S(2)}, u32[]{:S(2)}) collective-permute-start(bf16[128,2048]{1,0:T(8,128)(2,1)} %get-tuple-element.223), channel_id=1, source_target_pairs={{0,4},{1,5},{2,6},{3,7},{4,0},{5,1},{6,2},{7,3},{8,12},{9,13},{10,... | collective-permute-start | bytes 1572872 | tf_op jit(solution)/shard_map/ppermute | solution.py:739
  112.3 28.3 %collective-permute-start.10 = (bf16[128,2048]{1,0:T(8,128)(2,1)}, bf16[128,2048]{1,0:T(8,128)(2,1)S(1)}, u32[]{:S(2)}, u32[]{:S(2)}) collective-permute-start(bf16[128,2048]{1,0:T(8,128)(2,1)} %get-tuple-element.224), channel_id=1, source_target_pairs={{0,6},{1,7},{2,4},{3,5},{4,2},{5,3},{6,0},{7,1},{8,14},{9,15},{10,... | collective-permute-start | bytes 1572872 | tf_op jit(solution)/shard_map/ppermute | solution.py:739
  116.8 35.4 %all-to-all-start.3 = ((bf16[4,128,2048]{2,1,0:T(8,128)(2,1)}), bf16[4,128,2048]{2,1,0:T(8,128)(2,1)S(1)}, u32[]{:S(2)}, u32[]{:S(2)}) async-start(bf16[4,128,2048]{2,1,0:T(8,128)(2,1)} %broadcast_in_dim.38), calls=%async_computation.3 | async-start | bytes 4194304 | tf_op jit(solution)/shard_map/all_to_all | solution.py:736
  141.4 33.3 %collective-permute-start.16 = (bf16[4,128,1408]{2,1,0:T(8,128)(2,1)}, bf16[4,128,1408]{2,1,0:T(8,128)(2,1)S(1)}, u32[]{:S(2)}, u32[]{:S(2)}) collective-permute-start(bf16[4,128,1408]{2,1,0:T(8,128)(2,1)} %collective-permute-done.11.refs_6_), channel_id=1, source_target_pairs={{0,1},{1,0},{2,3},{3,2},{4,5},{5,4},{6,7},{7,6},{8,9},{9,8},{10,11... | collective-permute-start | bytes 4325384 | tf_op jit(solution)/shard_map/ppermute | solution.py:745
  142.8 31.9 %collective-permute-start.18 = (bf16[4,128,1408]{2,1,0:T(8,128)(2,1)}, bf16[4,128,1408]{2,1,0:T(8,128)(2,1)}, u32[]{:S(2)}, u32[]{:S(2)}) collective-permute-start(bf16[4,128,1408]{2,1,0:T(8,128)(2,1)} %collective-permute-done.17.refs_10_), channel_id=1, source_target_pairs={{0,1},{1,0},{2,3},{3,2},{4,5},{5,4},{6,7},{7,6},{8,9},{9,8},{10,11... | collective-permute-start | bytes 4325384 | tf_op jit(solution)/shard_map/ppermute | solution.py:745
  146.0 17.0 %collective-permute-start.13 = (bf16[128,2048]{1,0:T(8,128)(2,1)}, bf16[128,2048]{1,0:T(8,128)(2,1)}, u32[]{:S(2)}, u32[]{:S(2)}) collective-permute-start(bf16[128,2048]{1,0:T(8,128)(2,1)} %get-tuple-element.231.refs_0_), channel_id=1, source_target_pairs={{0,2},{1,3},{2,0},{3,1},{4,6},{5,7},{6,4},{7,5},{8,10},{9,11},{10,... | collective-permute-start | bytes 1572872 | tf_op jit(solution)/shard_map/ppermute | solution.py:739
  147.8 26.9 %collective-permute-start.14 = (bf16[128,2048]{1,0:T(8,128)(2,1)}, bf16[128,2048]{1,0:T(8,128)(2,1)}, u32[]{:S(2)}, u32[]{:S(2)}) collective-permute-start(bf16[128,2048]{1,0:T(8,128)(2,1)} %get-tuple-element.231.refs_0_), channel_id=1, source_target_pairs={{0,4},{1,5},{2,6},{3,7},{4,0},{5,1},{6,2},{7,3},{8,12},{9,13},{10,... | collective-permute-start | bytes 1572872 | tf_op jit(solution)/shard_map/ppermute | solution.py:739
  149.2 25.4 %collective-permute-start.15 = (bf16[128,2048]{1,0:T(8,128)(2,1)}, bf16[128,2048]{1,0:T(8,128)(2,1)}, u32[]{:S(2)}, u32[]{:S(2)}) collective-permute-start(bf16[128,2048]{1,0:T(8,128)(2,1)} %get-tuple-element.231.refs_0_), channel_id=1, source_target_pairs={{0,6},{1,7},{2,4},{3,5},{4,2},{5,3},{6,0},{7,1},{8,14},{9,15},{10,... | collective-permute-start | bytes 1572872 | tf_op jit(solution)/shard_map/ppermute | solution.py:739
  221.3 29.4 %all-to-all-start.4 = ((bf16[4,128,2048]{2,1,0:T(8,128)(2,1)}), bf16[4,128,2048]{2,1,0:T(8,128)(2,1)S(1)}, u32[]{:S(2)}, u32[]{:S(2)}) async-start(bf16[4,128,2048]{2,1,0:T(8,128)(2,1)} %bitcast.86), calls=%async_computation.4 | async-start | bytes 4194304 | tf_op jit(solution)/shard_map/all_to_all | solution.py:736
  252.0 39.1 %all-to-all-start.5 = ((bf16[4,2816,128]{2,1,0:T(8,128)(2,1)}), bf16[4,2816,128]{2,1,0:T(8,128)(2,1)S(1)}, u32[]{:S(2)}, u32[]{:S(2)}) async-start(bf16[4,2816,128]{2,1,0:T(8,128)(2,1)} %pair_sum.7), calls=%async_computation.5 | async-start | bytes 5767168 | tf_op jit(solution)/shard_map/all_to_all | solution.py:736
  270.2 41.9 %collective-permute-start.21 = (bf16[4,2816,128]{2,1,0:T(8,128)(2,1)}, bf16[4,2816,128]{2,1,0:T(8,128)(2,1)}, u32[]{:S(2)}, u32[]{:S(2)}) collective-permute-start(bf16[4,2816,128]{2,1,0:T(8,128)(2,1)} %get-tuple-element.258), channel_id=1, source_target_pairs={{0,1},{1,0},{2,3},{3,2},{4,5},{5,4},{6,7},{7,6},{8,9},{9,8},{10,11... | collective-permute-start | bytes 8650760 | tf_op jit(solution)/shard_map/ppermute | solution.py:745
  272.2 18.9 %collective-permute-start.20 = (bf16[2816,128]{1,0:T(8,128)(2,1)}, bf16[2816,128]{1,0:T(8,128)(2,1)}, u32[]{:S(2)}, u32[]{:S(2)}) collective-permute-start(bf16[2816,128]{1,0:T(8,128)(2,1)} %slice_bitcast_fusion.1), channel_id=1, source_target_pairs={{0,8},{8,0},{16,24},{24,16},{1,9},{9,1},{17,25},{25,17},{2,10},{10... | collective-permute-start | bytes 2162696 | tf_op jit(solution)/shard_map/ppermute | solution.py:792
  292.8 39.0 %all-to-all-start.7 = ((bf16[4,128,2048]{2,1,0:T(8,128)(2,1)}), bf16[4,128,2048]{2,1,0:T(8,128)(2,1)}, u32[]{:S(2)}, u32[]{:S(2)}) async-start(bf16[4,128,2048]{2,1,0:T(8,128)(2,1)} %bitcast.85), calls=%async_computation.7 | async-start | bytes 4194304 | tf_op jit(solution)/shard_map/all_to_all | solution.py:736
  298.4 19.1 %collective-permute-start.23 = (bf16[2816,128]{1,0:T(8,128)(2,1)S(1)}, bf16[2816,128]{1,0:T(8,128)(2,1)S(1)}, u32[]{:S(2)}, u32[]{:S(2)}) collective-permute-start(bf16[2816,128]{1,0:T(8,128)(2,1)S(1)} %slice_bitcast_fusion), channel_id=1, source_target_pairs={{0,8},{8,0},{16,24},{24,16},{1,9},{9,1},{17,25},{25,17},{2,10},{10... | collective-permute-start | bytes 2162696 | tf_op jit(solution)/shard_map/ppermute | solution.py:792
  301.8 30.0 %collective-permute-start.24 = (bf16[2816,128]{1,0:T(8,128)(2,1)}, bf16[2816,128]{1,0:T(8,128)(2,1)}, u32[]{:S(2)}, u32[]{:S(2)}) collective-permute-start(bf16[2816,128]{1,0:T(8,128)(2,1)} %get-tuple-element.270), channel_id=1, source_target_pairs={{0,8},{8,0},{16,24},{24,16},{1,9},{9,1},{17,25},{25,17},{2,10},{10... | collective-permute-start | bytes 2162696 | tf_op jit(solution)/shard_map/ppermute | solution.py:792
  303.3 28.4 %collective-permute-start.25 = (bf16[2816,128]{1,0:T(8,128)(2,1)}, bf16[2816,128]{1,0:T(8,128)(2,1)}, u32[]{:S(2)}, u32[]{:S(2)}) collective-permute-start(bf16[2816,128]{1,0:T(8,128)(2,1)} %get-tuple-element.271.refs_2_), channel_id=1, source_target_pairs={{8,16},{16,8},{9,17},{17,9},{10,18},{18,10},{11,19},{19,11},{12,20... | collective-permute-start | bytes 2162696 | tf_op jit(solution)/shard_map/ppermute | solution.py:794
  331.8 68.4 %all-to-all-start.8 = ((bf16[4,2816,128]{2,1,0:T(8,128)(2,1)}), bf16[4,2816,128]{2,1,0:T(8,128)(2,1)S(1)}, u32[]{:S(2)}, u32[]{:S(2)}) async-start(bf16[4,2816,128]{2,1,0:T(8,128)(2,1)} %pair_sum.6), calls=%async_computation.8 | async-start | bytes 5767168 | tf_op jit(solution)/shard_map/all_to_all | solution.py:736
  338.9 19.7 %collective-permute-start.26 = (bf16[2816,128]{1,0:T(8,128)(2,1)}, bf16[2816,128]{1,0:T(8,128)(2,1)}, u32[]{:S(2)}, u32[]{:S(2)}) collective-permute-start(bf16[2816,128]{1,0:T(8,128)(2,1)} %get-tuple-element.279), channel_id=1, source_target_pairs={{0,8},{8,0},{16,24},{24,16},{1,9},{9,1},{17,25},{25,17},{2,10},{10... | collective-permute-start | bytes 2162696 | tf_op jit(solution)/shard_map/ppermute | solution.py:792
  339.2 19.4 %collective-permute-start.27 = (bf16[2816,128]{1,0:T(8,128)(2,1)}, bf16[2816,128]{1,0:T(8,128)(2,1)}, u32[]{:S(2)}, u32[]{:S(2)}) collective-permute-start(bf16[2816,128]{1,0:T(8,128)(2,1)} %get-tuple-element.280.refs_2_), channel_id=1, source_target_pairs={{8,16},{16,8},{9,17},{17,9},{10,18},{18,10},{11,19},{19,11},{12,20... | collective-permute-start | bytes 2162696 | tf_op jit(solution)/shard_map/ppermute | solution.py:794
  344.1 30.0 %collective-permute-start.28 = (bf16[2816,128]{1,0:T(8,128)(2,1)}, bf16[2816,128]{1,0:T(8,128)(2,1)}, u32[]{:S(2)}, u32[]{:S(2)}) collective-permute-start(bf16[2816,128]{1,0:T(8,128)(2,1)} %get-tuple-element.287.refs_0_), channel_id=1, source_target_pairs={{0,8},{8,0},{16,24},{24,16},{1,9},{9,1},{17,25},{25,17},{2,10},{10... | collective-permute-start | bytes 2162696 | tf_op jit(solution)/shard_map/ppermute | solution.py:792
  347.9 26.3 %collective-permute-start.29 = (bf16[2816,128]{1,0:T(8,128)(2,1)}, bf16[2816,128]{1,0:T(8,128)(2,1)}, u32[]{:S(2)}, u32[]{:S(2)}) collective-permute-start(bf16[2816,128]{1,0:T(8,128)(2,1)} %get-tuple-element.288.refs_2_), channel_id=1, source_target_pairs={{8,16},{16,8},{9,17},{17,9},{10,18},{18,10},{11,19},{19,11},{12,20... | collective-permute-start | bytes 2162696 | tf_op jit(solution)/shard_map/ppermute | solution.py:794
  375.8 15.9 %collective-permute-start.30 = (bf16[512,128]{1,0:T(8,128)(2,1)}, bf16[512,128]{1,0:T(8,128)(2,1)S(1)}, u32[]{:S(2)}, u32[]{:S(2)}) collective-permute-start(bf16[512,128]{1,0:T(8,128)(2,1)} %slice.187), channel_id=1, source_target_pairs={{0,1},{1,0},{2,3},{3,2},{4,5},{5,4},{6,7},{7,6},{8,9},{9,8},{10,11... | collective-permute-start | bytes 393224 | tf_op jit(solution)/shard_map/ppermute | solution.py:745
  379.2 21.0 %collective-permute-start.31 = (bf16[2816,128]{1,0:T(8,128)(2,1)}, bf16[2816,128]{1,0:T(8,128)(2,1)}, u32[]{:S(2)}, u32[]{:S(2)}) collective-permute-start(bf16[2816,128]{1,0:T(8,128)(2,1)} %get-tuple-element.296.refs_2_), channel_id=1, source_target_pairs={{0,8},{8,0},{16,24},{24,16},{1,9},{9,1},{17,25},{25,17},{2,10},{10... | collective-permute-start | bytes 2162696 | tf_op jit(solution)/shard_map/ppermute | solution.py:792
  382.9 17.3 %collective-permute-start.32 = (bf16[2816,128]{1,0:T(8,128)(2,1)}, bf16[2816,128]{1,0:T(8,128)(2,1)}, u32[]{:S(2)}, u32[]{:S(2)}) collective-permute-start(bf16[2816,128]{1,0:T(8,128)(2,1)} %get-tuple-element.297.refs_2_), channel_id=1, source_target_pairs={{8,16},{16,8},{9,17},{17,9},{10,18},{18,10},{11,19},{19,11},{12,20... | collective-permute-start | bytes 2162696 | tf_op jit(solution)/shard_map/ppermute | solution.py:794
  388.0 27.5 %collective-permute-start.33 = (bf16[2816,128]{1,0:T(8,128)(2,1)}, bf16[2816,128]{1,0:T(8,128)(2,1)}, u32[]{:S(2)}, u32[]{:S(2)}) collective-permute-start(bf16[2816,128]{1,0:T(8,128)(2,1)} %get-tuple-element.304.refs_4_), channel_id=1, source_target_pairs={{0,8},{8,0},{16,24},{24,16},{1,9},{9,1},{17,25},{25,17},{2,10},{10... | collective-permute-start | bytes 2162696 | tf_op jit(solution)/shard_map/ppermute | solution.py:792
  390.1 25.3 %collective-permute-start.34 = (bf16[2816,128]{1,0:T(8,128)(2,1)}, bf16[2816,128]{1,0:T(8,128)(2,1)}, u32[]{:S(2)}, u32[]{:S(2)}) collective-permute-start(bf16[2816,128]{1,0:T(8,128)(2,1)} %get-tuple-element.305.refs_2_), channel_id=1, source_target_pairs={{8,16},{16,8},{9,17},{17,9},{10,18},{18,10},{11,19},{19,11},{12,20... | collective-permute-start | bytes 2162696 | tf_op jit(solution)/shard_map/ppermute | solution.py:794
  401.8 38.1 %all-to-all-start.9 = ((bf16[4,128,2048]{2,1,0:T(8,128)(2,1)}), bf16[4,128,2048]{2,1,0:T(8,128)(2,1)}, u32[]{:S(2)}, u32[]{:S(2)}) async-start(bf16[4,128,2048]{2,1,0:T(8,128)(2,1)} %bitcast.84), calls=%async_computation.9 | async-start | bytes 4194304 | tf_op jit(solution)/shard_map/all_to_all | solution.py:736
  418.9 20.9 %collective-permute-start.36 = (bf16[2816,128]{1,0:T(8,128)(2,1)}, bf16[2816,128]{1,0:T(8,128)(2,1)S(1)}, u32[]{:S(2)}, u32[]{:S(2)}) collective-permute-start(bf16[2816,128]{1,0:T(8,128)(2,1)} %get-tuple-element.313.refs_6_), channel_id=1, source_target_pairs={{0,8},{8,0},{16,24},{24,16},{1,9},{9,1},{17,25},{25,17},{2,10},{10... | collective-permute-start | bytes 2162696 | tf_op jit(solution)/shard_map/ppermute | solution.py:792
  422.8 17.0 %collective-permute-start.37 = (bf16[2816,128]{1,0:T(8,128)(2,1)}, bf16[2816,128]{1,0:T(8,128)(2,1)S(1)}, u32[]{:S(2)}, u32[]{:S(2)}) collective-permute-start(bf16[2816,128]{1,0:T(8,128)(2,1)} %get-tuple-element.314.refs_2_), channel_id=1, source_target_pairs={{8,16},{16,8},{9,17},{17,9},{10,18},{18,10},{11,19},{19,11},{12,20... | collective-permute-start | bytes 2162696 | tf_op jit(solution)/shard_map/ppermute | solution.py:794
  440.7 20.7 %all-to-all-start.10 = ((bf16[4,1280,128]{2,1,0:T(8,128)(2,1)}), bf16[4,1280,128]{2,1,0:T(8,128)(2,1)S(1)}, u32[]{:S(2)}, u32[]{:S(2)}) async-start(bf16[4,1280,128]{2,1,0:T(8,128)(2,1)} %pair_sum.8), calls=%async_computation.10 | async-start | bytes 2621440 | tf_op jit(solution)/shard_map/all_to_all | solution.py:736
  448.3 29.5 %collective-permute-start.38 = (bf16[2816,128]{1,0:T(8,128)(2,1)}, bf16[2816,128]{1,0:T(8,128)(2,1)}, u32[]{:S(2)}, u32[]{:S(2)}) collective-permute-start(bf16[2816,128]{1,0:T(8,128)(2,1)} %get-tuple-element.320.refs_0_), channel_id=1, source_target_pairs={{0,8},{8,0},{16,24},{24,16},{1,9},{9,1},{17,25},{25,17},{2,10},{10... | collective-permute-start | bytes 2162696 | tf_op jit(solution)/shard_map/ppermute | solution.py:792
  451.2 26.6 %collective-permute-start.39 = (bf16[2816,128]{1,0:T(8,128)(2,1)}, bf16[2816,128]{1,0:T(8,128)(2,1)}, u32[]{:S(2)}, u32[]{:S(2)}) collective-permute-start(bf16[2816,128]{1,0:T(8,128)(2,1)} %get-tuple-element.321.refs_2_), channel_id=1, source_target_pairs={{8,16},{16,8},{9,17},{17,9},{10,18},{18,10},{11,19},{19,11},{12,20... | collective-permute-start | bytes 2162696 | tf_op jit(solution)/shard_map/ppermute | solution.py:794
  452.7 32.2 %collective-permute-start.41 = (bf16[2,2048,128]{2,1,0:T(8,128)(2,1)}, bf16[2,2048,128]{2,1,0:T(8,128)(2,1)}, u32[]{:S(2)}, u32[]{:S(2)}) collective-permute-start(bf16[2,2048,128]{2,1,0:T(8,128)(2,1)} %get-tuple-element.328), channel_id=1, source_target_pairs={{0,1},{1,0},{2,3},{3,2},{4,5},{5,4},{6,7},{7,6},{8,9},{9,8},{10,11... | collective-permute-start | bytes 3145736 | tf_op jit(solution)/shard_map/ppermute | solution.py:745
  462.5 58.8 %all-to-all-start.6 = ((bf16[4,128,2048]{2,1,0:T(8,128)(2,1)}), bf16[4,128,2048]{2,1,0:T(8,128)(2,1)S(1)}, u32[]{:S(2)}, u32[]{:S(2)}) async-start(bf16[4,128,2048]{2,1,0:T(8,128)(2,1)} %bitcast.83), calls=%async_computation.6 | async-start | bytes 4194304 | tf_op jit(solution)/shard_map/all_to_all | solution.py:736
  469.5 25.3 %collective-permute-start.42 = (bf16[2816,128]{1,0:T(8,128)(2,1)}, bf16[2816,128]{1,0:T(8,128)(2,1)}, u32[]{:S(2)}, u32[]{:S(2)}) collective-permute-start(bf16[2816,128]{1,0:T(8,128)(2,1)} %get-tuple-element.331.refs_2_), channel_id=1, source_target_pairs={{0,8},{8,0},{16,24},{24,16},{1,9},{9,1},{17,25},{25,17},{2,10},{10... | collective-permute-start | bytes 2162696 | tf_op jit(solution)/shard_map/ppermute | solution.py:792
  472.2 22.6 %collective-permute-start.43 = (bf16[2816,128]{1,0:T(8,128)(2,1)}, bf16[2816,128]{1,0:T(8,128)(2,1)}, u32[]{:S(2)}, u32[]{:S(2)}) collective-permute-start(bf16[2816,128]{1,0:T(8,128)(2,1)} %get-tuple-element.332.refs_2_), channel_id=1, source_target_pairs={{8,16},{16,8},{9,17},{17,9},{10,18},{18,10},{11,19},{19,11},{12,20... | collective-permute-start | bytes 2162696 | tf_op jit(solution)/shard_map/ppermute | solution.py:794
  481.2 32.3 %collective-permute-start.47 = (bf16[2816,128]{1,0:T(8,128)(2,1)}, bf16[2816,128]{1,0:T(8,128)(2,1)S(1)}, u32[]{:S(2)}, u32[]{:S(2)}) collective-permute-start(bf16[2816,128]{1,0:T(8,128)(2,1)} %get-tuple-element.337.refs_4_), channel_id=1, source_target_pairs={{0,8},{8,0},{16,24},{24,16},{1,9},{9,1},{17,25},{25,17},{2,10},{10... | collective-permute-start | bytes 2162696 | tf_op jit(solution)/shard_map/ppermute | solution.py:792
  483.3 30.3 %collective-permute-start.48 = (bf16[2816,128]{1,0:T(8,128)(2,1)}, bf16[2816,128]{1,0:T(8,128)(2,1)}, u32[]{:S(2)}, u32[]{:S(2)}) collective-permute-start(bf16[2816,128]{1,0:T(8,128)(2,1)} %get-tuple-element.338.refs_2_), channel_id=1, source_target_pairs={{8,16},{16,8},{9,17},{17,9},{10,18},{18,10},{11,19},{19,11},{12,20... | collective-permute-start | bytes 2162696 | tf_op jit(solution)/shard_map/ppermute | solution.py:794
  498.2 23.1 %collective-permute-start.49 = (bf16[2816,128]{1,0:T(8,128)(2,1)}, bf16[2816,128]{1,0:T(8,128)(2,1)}, u32[]{:S(2)}, u32[]{:S(2)}) collective-permute-start(bf16[2816,128]{1,0:T(8,128)(2,1)} %get-tuple-element.344.refs_6_), channel_id=1, source_target_pairs={{0,8},{8,0},{16,24},{24,16},{1,9},{9,1},{17,25},{25,17},{2,10},{10... | collective-permute-start | bytes 2162696 | tf_op jit(solution)/shard_map/ppermute | solution.py:792
  500.2 21.1 %collective-permute-start.50 = (bf16[2816,128]{1,0:T(8,128)(2,1)}, bf16[2816,128]{1,0:T(8,128)(2,1)}, u32[]{:S(2)}, u32[]{:S(2)}) collective-permute-start(bf16[2816,128]{1,0:T(8,128)(2,1)} %get-tuple-element.345.refs_2_), channel_id=1, source_target_pairs={{8,16},{16,8},{9,17},{17,9},{10,18},{18,10},{11,19},{19,11},{12,20... | collective-permute-start | bytes 2162696 | tf_op jit(solution)/shard_map/ppermute | solution.py:794
  517.9 16.4 %collective-permute-start.53 = (bf16[2816,128]{1,0:T(8,128)(2,1)}, bf16[2816,128]{1,0:T(8,128)(2,1)}, u32[]{:S(2)}, u32[]{:S(2)}) collective-permute-start(bf16[2816,128]{1,0:T(8,128)(2,1)} %get-tuple-element.358.refs_0_), channel_id=1, source_target_pairs={{0,8},{8,0},{16,24},{24,16},{1,9},{9,1},{17,25},{25,17},{2,10},{10... | collective-permute-start | bytes 2162696 | tf_op jit(solution)/shard_map/ppermute | solution.py:792
  518.9 15.4 %collective-permute-start.54 = (bf16[2816,128]{1,0:T(8,128)(2,1)}, bf16[2816,128]{1,0:T(8,128)(2,1)}, u32[]{:S(2)}, u32[]{:S(2)}) collective-permute-start(bf16[2816,128]{1,0:T(8,128)(2,1)} %get-tuple-element.359.refs_2_), channel_id=1, source_target_pairs={{8,16},{16,8},{9,17},{17,9},{10,18},{18,10},{11,19},{19,11},{12,20... | collective-permute-start | bytes 2162696 | tf_op jit(solution)/shard_map/ppermute | solution.py:794
  537.5 21.1 %collective-permute-start.60 = (bf16[2816,128]{1,0:T(8,128)(2,1)}, bf16[2816,128]{1,0:T(8,128)(2,1)}, u32[]{:S(2)}, u32[]{:S(2)}) collective-permute-start(bf16[2816,128]{1,0:T(8,128)(2,1)} %get-tuple-element.374.refs_4_), channel_id=1, source_target_pairs={{0,8},{8,0},{16,24},{24,16},{1,9},{9,1},{17,25},{25,17},{2,10},{10... | collective-permute-start | bytes 2162696 | tf_op jit(solution)/shard_map/ppermute | solution.py:792
  546.1 27.9 %collective-permute-start.51 = (bf16[2816,128]{1,0:T(8,128)(2,1)}, bf16[2816,128]{1,0:T(8,128)(2,1)}, u32[]{:S(2)}, u32[]{:S(2)}) collective-permute-start(bf16[2816,128]{1,0:T(8,128)(2,1)} %get-tuple-element.351.refs_2_), channel_id=1, source_target_pairs={{0,8},{8,0},{16,24},{24,16},{1,9},{9,1},{17,25},{25,17},{2,10},{10... | collective-permute-start | bytes 2162696 | tf_op jit(solution)/shard_map/ppermute | solution.py:792
  548.2 25.8 %collective-permute-start.52 = (bf16[2816,128]{1,0:T(8,128)(2,1)}, bf16[2816,128]{1,0:T(8,128)(2,1)}, u32[]{:S(2)}, u32[]{:S(2)}) collective-permute-start(bf16[2816,128]{1,0:T(8,128)(2,1)} %get-tuple-element.352.refs_2_), channel_id=1, source_target_pairs={{8,16},{16,8},{9,17},{17,9},{10,18},{18,10},{11,19},{19,11},{12,20... | collective-permute-start | bytes 2162696 | tf_op jit(solution)/shard_map/ppermute | solution.py:794
  561.5 26.5 %collective-permute-start.62 = (bf16[2560,128]{1,0:T(8,128)(2,1)}, bf16[2560,128]{1,0:T(8,128)(2,1)S(1)}, u32[]{:S(2)}, u32[]{:S(2)}) collective-permute-start(bf16[2560,128]{1,0:T(8,128)(2,1)} %get-tuple-element.378), channel_id=1, source_target_pairs={{0,8},{8,0},{16,24},{24,16},{1,9},{9,1},{17,25},{25,17},{2,10},{10... | collective-permute-start | bytes 1966088 | tf_op jit(solution)/shard_map/ppermute | solution.py:792
  564.2 17.5 %collective-permute-start.63 = (bf16[2048,128]{1,0:T(8,128)(2,1)}, bf16[2048,128]{1,0:T(8,128)(2,1)S(1)}, u32[]{:S(2)}, u32[]{:S(2)}) collective-permute-start(bf16[2048,128]{1,0:T(8,128)(2,1)} %get-tuple-element.379.refs_0_), channel_id=1, source_target_pairs={{8,16},{16,8},{9,17},{17,9},{10,18},{18,10},{11,19},{19,11},{12,20... | collective-permute-start | bytes 1572872 | tf_op jit(solution)/shard_map/ppermute | solution.py:794
  577.3 26.2 %collective-permute-start.55 = (bf16[2816,128]{1,0:T(8,128)(2,1)}, bf16[2816,128]{1,0:T(8,128)(2,1)S(1)}, u32[]{:S(2)}, u32[]{:S(2)}) collective-permute-start(bf16[2816,128]{1,0:T(8,128)(2,1)} %get-tuple-element.364.refs_6_), channel_id=1, source_target_pairs={{0,8},{8,0},{16,24},{24,16},{1,9},{9,1},{17,25},{25,17},{2,10},{10... | collective-permute-start | bytes 2162696 | tf_op jit(solution)/shard_map/ppermute | solution.py:792
  590.0 27.8 %collective-permute-start.64 = (bf16[2048,128]{1,0:T(8,128)(2,1)}, bf16[2048,128]{1,0:T(8,128)(2,1)}, u32[]{:S(2)}, u32[]{:S(2)}) collective-permute-start(bf16[2048,128]{1,0:T(8,128)(2,1)} %chain_step.35.refs_0_), channel_id=1, source_target_pairs={{0,8},{8,0},{16,24},{24,16},{1,9},{9,1},{17,25},{25,17},{2,10},{10... | collective-permute-start | bytes 1572872 | tf_op jit(solution)/shard_map/ppermute | solution.py:792
  607.2 17.7 %collective-permute-start.57 = (bf16[2560,128]{1,0:T(8,128)(2,1)}, bf16[2560,128]{1,0:T(8,128)(2,1)S(1)}, u32[]{:S(2)}, u32[]{:S(2)}) collective-permute-start(bf16[2560,128]{1,0:T(8,128)(2,1)} %get-tuple-element.369), channel_id=1, source_target_pairs={{0,8},{8,0},{16,24},{24,16},{1,9},{9,1},{17,25},{25,17},{2,10},{10... | collective-permute-start | bytes 1966088 | tf_op jit(solution)/shard_map/ppermute | solution.py:792
  (55 other events, 442.9 us)

commit v5 on v4

--- a/solution.py
+++ b/solution.py
@@ -500,7 +500,7 @@
     width = right.shape[1]
     rows = model // (2 * chips)
     long = pl.cdiv(width, 128) * rows
-    group = min(4, chips)
+    group = min(2, chips)
     turns = chips // group
 
     def body(c_ref, l_ref, r_ref, near_ref, far_ref):
@@ -552,11 +552,11 @@
 
     def body(c_ref, l_ref, r_ref, near_ref, far_ref, full_ref):
         core = c_ref[1]
-        full_ref[...] = dot_tn(l_ref[...], r_ref[...])
-        near = full_ref[pl.ds(pl.multiple_of(core * rows, 8), rows), :]
-        far = full_ref[pl.ds(pl.multiple_of((1 - core) * rows, 8), rows), :]
-        strips(near.astype(BF16), near_ref, (0,))
-        strips(far.astype(BF16), far_ref, (0,))
+        full_ref[...] = dot_tn(l_ref[...], r_ref[...]).astype(BF16)
+        near = full_ref[pl.ds(pl.multiple_of(core * rows, 16), rows), :]
+        far = full_ref[pl.ds(pl.multiple_of((1 - core) * rows, 16), rows), :]
+        strips(near, near_ref, (0,))
+        strips(far, far_ref, (0,))
 
     out = pl.BlockSpec((1, long, 128), lambda n, c: (n, 0, 0))
     return pl.pallas_call(
@@ -569,7 +569,7 @@
                 pl.BlockSpec((own, width), lambda n, c: (0, n)),
             ],
             out_specs=[out] * 2,
-            scratch_shapes=[pltpu.VMEM((depth, width), F32)],
+            scratch_shapes=[pltpu.VMEM((depth, width), BF16)],
         ),
         out_shape=[jax.ShapeDtypeStruct((cuts, long, 128), BF16)] * 2,
         cost_estimate=tiny(),
@@ -688,10 +688,10 @@
     def body(a_ref, b_ref, out_ref):
         out_ref[...] = a_ref[...] + b_ref[...]
 
-    spec = pl.BlockSpec((1, rows, lanes), lambda k: (k, 0, 0))
-    return pl.pallas_call(
-        body,
-        grid=(count,),
+    spec = pl.BlockSpec((2, rows, lanes), lambda k: (k, 0, 0))
+    return pl.pallas_call(
+        body,
+        grid=(count // 2,),
         in_specs=[spec] * 2,
         out_specs=spec,
         out_shape=jax.ShapeDtypeStruct(near.shape, BF16),

time: 653 us -> 650 us (level)
  no operation moved by 1% of the time
where the time goes in v5:
time: 650 us; the launch traced here: 643 us
  Pallas kernels  228 us (35%)
  waiting for transfers between devices  224 us (34%)
  starting transfers between devices  134 us (21%)
  local copies, waits for them, and re-layouts  32.4 us (5%)
  matrix products  14.7 us (2%)
  other arithmetic  6.69 us (1%)
    ppermute x20, waiting for transfers between devices, visit(): lax.ppermute(ahead, 'rep', outer_pairs)  93.8 us
    all_to_all x11, waiting for transfers between devices, exchange(): return lax.all_to_all(v, 'fsdp', 0, 0, axis_index_groups=sides, tiled=True)  62.9 us
    ppermute x12, waiting for transfers between devices, hop(): return lax.ppermute(v, 'fsdp', [(i, i ^ 2 * k) for i in range(group)])  57.1 us
    pallas_call x18, Pallas kernels, chain_step(): pl.pallas_call(body, grid=(1,), in_specs=[scalars()] + [spec(v) for v in...  56.2 us
    all_to_all x11, starting transfers between devices, exchange(): return lax.all_to_all(v, 'fsdp', 0, 0, axis_index_groups=sides, tiled=True)  44.7 us
    ppermute x20, starting transfers between devices, visit(): lax.ppermute(ahead, 'rep', outer_pairs)  44.5 us
    pallas_call x5, Pallas kernels, beside(): pl.pallas_call(body, grid_spec=pltpu.PrefetchScalarGridSpec(num_scalar_pr...  27.9 us
    pallas_call x1, Pallas kernels, feed_forward(): pl.pallas_call(body, grid_spec=pltpu.PrefetchScalarGridSpec(num_scalar_pr...  25.7 us
  transfers between devices with their start and end apart: 76, of which 30 were waited for; matrix products, arithmetic and copies ran while one was open for 6% of the time, Pallas kernels for 29%

profile of v5, /device:TPU:0, one launch (start us, length us, event | category | flops | bytes accessed | tf_op | source)
XLA Modules:
  0.0 642.5 jit_solution(7809552111864200767)
XLA Ops:
  2.6 4.1 pick_qkv.1
  6.7 4.7 all-to-all-start
  16.7 12.6 %all-to-all-done.n_ref = bf16[4,256,640]{2,1,0:T(8,128)(2,1)S(1)} async-done(((bf16[4,256,640]{2,1,0:T(8,128)(2,1)}), bf16[4,256,640]{2,1,0:T(8,128)(2,1)S(1)}, u32[]{:S(2)}, u32[]{:S(2)}) %all-to-all-start) | async-done | bytes 1310752 | tf_op jit(solution)/shard_map/all_to_all | solution.py:736
  31.1 4.9 pick_half.1
  36.0 6.1 join_cores.1.refs_13_
  42.1 9.9 %collective-permute-done.2.refs_3_ = bf16[128,2048]{1,0:T(8,128)(2,1)} collective-permute-done((bf16[128,2048]{1,0:T(8,128)(2,1)S(1)}, bf16[128,2048]{1,0:T(8,128)(2,1)}, u32[]{:S(2)}, u32[]{:S(2)}) %collective-permute-start.2) | collective-permute-done | bytes 524320 | tf_op jit(solution)/shard_map/ppermute | solution.py:739
  52.0 3.6 all-to-all-start.1
  55.6 6.5 %qkv_forward.1 = (bf16[512,2048]{1,0:T(8,128)(2,1)}, bf16[512,512]{1,0:T(8,128)(2,1)}, bf16[512,128]{1,0:T(8,128)(2,1)}, bf16[2048,640]{1,0:T(8,128)(2,1)}) custom-call(s32[5]{0:T(128)} %stack.38.s_ref.c_ref, f32[512,128]{1,0:T(8,128)} %get-tuple-element.200.cos_ref, f32[512,128]{1,0:T(8,128)} %get-tuple-element.201.sin_ref, bf16[4,256,640]{2,1,0:T(8,128)(2,1)} %copy-done.7, ...), custom_call_target="tpu_custom_call" | custom-call | flops 1024 | bytes 1024 | tf_op jit(solution)/shard_map/qkv_forward/pallas_call | solution.py:167
  62.1 11.1 %all-to-all-done.1.refs_5_ = bf16[4,128,1408]{2,1,0:T(8,128)(2,1)S(1)} async-done(((bf16[4,128,1408]{2,1,0:T(8,128)(2,1)}), bf16[4,128,1408]{2,1,0:T(8,128)(2,1)S(1)}, u32[]{:S(2)}, u32[]{:S(2)}) %all-to-all-start.1) | async-done | bytes 1441824 | tf_op jit(solution)/shard_map/all_to_all | solution.py:736
  73.2 4.5 all-to-all-start.2
  81.0 8.9 %attention_forward.1 = (bf16[512,512]{1,0:T(8,128)(2,1)}, f32[512,128]{1,0:T(8,128)}) custom-call(s32[5]{0:T(128)} %stack.38.s_ref.c_ref, s32[4,8]{1,0:T(4,128)} %n_ref.3, bf16[512,512]{1,0:T(8,128)(2,1)} %get-tuple-element.209.q_ref, bf16[512,128]{1,0:T(8,128)(2,1)} %get-tuple-element.210.a_ref, bf16[512,128]{1,0:T(8,128)(2,1)} %collective-permute-done.6.b_ref), custom_call_target="tpu_custom_call" | custom-call | flops 1024 | bytes 1024 | tf_op jit(solution)/shard_map/attention_forward/pallas_call | solution.py:240
  89.9 6.7 %all-to-all-done.2.refs_9_ = bf16[4,128,1408]{2,1,0:T(8,128)(2,1)} async-done(((bf16[4,128,1408]{2,1,0:T(8,128)(2,1)}), bf16[4,128,1408]{2,1,0:T(8,128)(2,1)}, u32[]{:S(2)}, u32[]{:S(2)}) %all-to-all-start.2) | async-done | bytes 1441824 | tf_op jit(solution)/shard_map/all_to_all | solution.py:736
  98.4 4.6 out_proj.1
  105.0 7.3 %collective-permute-done.11.refs_6_ = bf16[4,128,1408]{2,1,0:T(8,128)(2,1)} collective-permute-done((bf16[4,128,1408]{2,1,0:T(8,128)(2,1)S(1)}, bf16[4,128,1408]{2,1,0:T(8,128)(2,1)}, u32[]{:S(2)}, u32[]{:S(2)}) %collective-permute-start.11) | collective-permute-done | bytes 1441824 | tf_op jit(solution)/shard_map/ppermute | solution.py:748
  116.8 3.8 all-to-all-start.3
  120.7 19.9 %collective-permute-done.9.refs_2_ = bf16[128,2048]{1,0:T(8,128)(2,1)} collective-permute-done((bf16[128,2048]{1,0:T(8,128)(2,1)}, bf16[128,2048]{1,0:T(8,128)(2,1)}, u32[]{:S(2)}, u32[]{:S(2)}) %collective-permute-start.9) | collective-permute-done | bytes 524320 | tf_op jit(solution)/shard_map/ppermute | solution.py:739
  152.2 10.9 %collective-permute-done.13.refs_1_ = bf16[128,2048]{1,0:T(8,128)(2,1)} collective-permute-done((bf16[128,2048]{1,0:T(8,128)(2,1)}, bf16[128,2048]{1,0:T(8,128)(2,1)}, u32[]{:S(2)}, u32[]{:S(2)}) %collective-permute-start.13) | collective-permute-done | bytes 524320 | tf_op jit(solution)/shard_map/ppermute | solution.py:739
  163.1 11.6 %collective-permute-done.14.refs_2_ = bf16[128,2048]{1,0:T(8,128)(2,1)} collective-permute-done((bf16[128,2048]{1,0:T(8,128)(2,1)}, bf16[128,2048]{1,0:T(8,128)(2,1)}, u32[]{:S(2)}, u32[]{:S(2)}) %collective-permute-start.14) | collective-permute-done | bytes 524320 | tf_op jit(solution)/shard_map/ppermute | solution.py:739
  175.8 25.7 %feed_forward.1 = (bf16[512,1408]{1,0:T(8,128)(2,1)}, bf16[512,1408]{1,0:T(8,128)(2,1)}, bf16[512,1408]{1,0:T(8,128)(2,1)}, bf16[512,2048]{1,0:T(8,128)(2,1)}, bf16[512,2048]{1,0:T(8,128)(2,1)}) custom-call(s32[5]{0:T(128)} %stack.38.s_ref.c_ref, bf16[128,2048]{1,0:T(8,128)(2,1)} %get-tuple-element.231.refs_0_, ...), custom_call_target="tpu_custom_call" | custom-call | flops 1024 | bytes 1024 | tf_op jit(solution)/shard_map/feed_forward/pallas_call | solution.py:386
  201.5 8.2 %row_grad.2 = (bf16[4,2816,128]{2,1,0:T(8,128)(2,1)}, bf16[4,2816,128]{2,1,0:T(8,128)(2,1)}) custom-call(s32[5]{0:T(128)} %stack.38.s_ref.c_ref, bf16[512,1408]{1,0:T(8,128)(2,1)} %get-tuple-element.256.l_ref, bf16[512,2048]{1,0:T(8,128)(2,1)} %bitcast.81), custom_call_target="tpu_custom_call" | custom-call | flops 1024 | bytes 1024 | tf_op jit(solution)/shard_map/row_grad/pallas_call | solution.py:562
  209.7 9.5 %weight_grad.3 = (bf16[4,2816,128]{2,1,0:T(8,128)(2,1)}, bf16[4,2816,128]{2,1,0:T(8,128)(2,1)}) custom-call(s32[5]{0:T(128)} %stack.38.s_ref.c_ref, bf16[512,2048]{1,0:T(8,128)(2,1)} %get-tuple-element.237.l_ref, bf16[512,1408]{1,0:T(8,128)(2,1)} %get-tuple-element.241.r_ref), custom_call_target="tpu_custom_call" | custom-call | flops 1024 | bytes 1024 | tf_op jit(solution)/shard_map/weight_grad/pallas_call | solution.py:527
  220.9 3.6 all-to-all-start.4
  225.1 4.1 pair_sum.7
  229.1 21.1 %all-to-all-done.4 = bf16[4,128,2048]{2,1,0:T(8,128)(2,1)S(1)} async-done(((bf16[4,128,2048]{2,1,0:T(8,128)(2,1)}), bf16[4,128,2048]{2,1,0:T(8,128)(2,1)S(1)}, u32[]{:S(2)}, u32[]{:S(2)}) %all-to-all-start.4) | async-done | bytes 2097184 | tf_op jit(solution)/shard_map/all_to_all | solution.py:736
  251.6 3.7 all-to-all-start.5
  255.3 4.1 pair_sum.5.refs_0_.refs_2_
  259.4 9.1 %weight_grad.4 = (bf16[4,2816,128]{2,1,0:T(8,128)(2,1)}, bf16[4,2816,128]{2,1,0:T(8,128)(2,1)}) custom-call(s32[5]{0:T(128)} %stack.38.s_ref.c_ref, bf16[512,2048]{1,0:T(8,128)(2,1)} %get-tuple-element.237.l_ref, bf16[512,1408]{1,0:T(8,128)(2,1)} %get-tuple-element.249.r_ref), custom_call_target="tpu_custom_call" | custom-call | flops 1024 | bytes 1024 | tf_op jit(solution)/shard_map/weight_grad/pallas_call | solution.py:527
  271.0 4.6 residual_norm_back.2
  275.5 13.9 %collective-permute-done.20.refs_1_ = bf16[2816,128]{1,0:T(8,128)(2,1)} collective-permute-done((bf16[2816,128]{1,0:T(8,128)(2,1)}, bf16[2816,128]{1,0:T(8,128)(2,1)}, u32[]{:S(2)}, u32[]{:S(2)}) %collective-permute-start.20) | collective-permute-done | bytes 720928 | tf_op jit(solution)/shard_map/ppermute | solution.py:792
  291.1 4.5 all-to-all-start.7
  303.2 7.3 %convolution_convert_fusion.1 = bf16[512,2048]{1,0:T(8,128)(2,1)} fusion(bf16[512,1408]{1,0:T(8,128)(2,1)S(1)} %copy-done.22, bf16[1408,2048]{1,0:T(8,128)(2,1)} %join_cores.1.refs_13_), kind=kOutput, calls=%fused_computation.2 | convolution fusion | flops 2953838592 | bytes 9306112 | tf_op jit(solution)/shard_map/dot_general | solution.py:24
  310.4 4.1 pair_sum.6
  315.8 14.3 %collective-permute-done.24.refs_1_ = bf16[2816,128]{1,0:T(8,128)(2,1)} collective-permute-done((bf16[2816,128]{1,0:T(8,128)(2,1)}, bf16[2816,128]{1,0:T(8,128)(2,1)}, u32[]{:S(2)}, u32[]{:S(2)}) %collective-permute-start.24) | collective-permute-done | bytes 720928 | tf_op jit(solution)/shard_map/ppermute | solution.py:792
  330.1 4.1 all-to-all-start.8
  342.4 3.7 collective-permute-start.28
  347.7 4.9 row_grad.3
  352.6 4.3 convolution_convert_fusion.2.d_ref
  356.9 15.6 %attention_backward.1 = (bf16[512,512]{1,0:T(8,128)(2,1)}, f32[1024,128]{1,0:T(8,128)}) custom-call(s32[5]{0:T(128)} %stack.38.s_ref.c_ref, s32[4,8]{1,0:T(4,128)} %n_ref.3, bf16[512,512]{1,0:T(8,128)(2,1)} %get-tuple-element.209.q_ref, bf16[512,128]{1,0:T(8,128)(2,1)} %get-tuple-element.210.a_ref, bf16[512,128]{1,0:T(8,128)(2,1)} %collective-permute-done.6.b_ref, ...), custom_call_target="tpu_custom_call" | custom-call | flops 1024 | bytes 1024 | tf_op jit(solution)/shard_map/attention_backward/pallas_call | solution.py:315
  377.5 3.7 collective-permute-start.31
  382.8 3.4 chain_step.22
  400.1 4.5 all-to-all-start.9
  404.5 6.5 %weight_grad.5 = (bf16[4,1280,128]{2,1,0:T(8,128)(2,1)}, bf16[4,1280,128]{2,1,0:T(8,128)(2,1)}) custom-call(s32[5]{0:T(128)} %stack.38.s_ref.c_ref, bf16[512,2048]{1,0:T(8,128)(2,1)} %get-tuple-element.264.l_ref, bf16[512,640]{1,0:T(8,128)(2,1)} %copy-done.17), custom_call_target="tpu_custom_call" | custom-call | flops 1024 | bytes 1024 | tf_op jit(solution)/shard_map/weight_grad/pallas_call | solution.py:527
  413.8 3.4 chain_step.23
  417.2 3.9 collective-permute-start.36
  425.7 12.4 %collective-permute-done.36.refs_7_.refs_1_ = bf16[2816,128]{1,0:T(8,128)(2,1)S(1)} collective-permute-done((bf16[2816,128]{1,0:T(8,128)(2,1)}, bf16[2816,128]{1,0:T(8,128)(2,1)S(1)}, u32[]{:S(2)}, u32[]{:S(2)}) %collective-permute-start.36) | collective-permute-done | bytes 720928 | tf_op jit(solution)/shard_map/ppermute | solution.py:792
  439.0 4.2 all-to-all-start.10
  451.0 8.7 %all-to-all-done.10 = bf16[4,1280,128]{2,1,0:T(8,128)(2,1)S(1)} async-done(((bf16[4,1280,128]{2,1,0:T(8,128)(2,1)}), bf16[4,1280,128]{2,1,0:T(8,128)(2,1)S(1)}, u32[]{:S(2)}, u32[]{:S(2)}) %all-to-all-start.10) | async-done | bytes 1310752 | tf_op jit(solution)/shard_map/all_to_all | solution.py:736
  460.8 3.6 all-to-all-start.6
  472.0 4.0 residual_norm_back.3
  476.1 3.4 chain_step.26
  486.8 6.6 %beside.5 = f32[704,2048]{1,0:T(8,128)} custom-call(s32[5]{0:T(128)} %stack.38.s_ref.c_ref, f32[704,1]{1,0:T(8,128)} %broadcast_in_dim.39.s_ref, bf16[2816,128]{1,0:T(8,128)(2,1)} %get-tuple-element.287.refs_0_, bf16[2816,128]{1,0:T(8,128)(2,1)} %collective-permute-done.28.refs_1_, bf16[2816,128]{1,0:T(8,128)(2,1)} %get-tuple-element.296.refs_2_, ...), custom_call_target="tpu_custom_call" | custom-call | flops 1024 | bytes 1024 | tf_op jit(solution)/shard_map/beside/pallas_call | solution.py:670
  493.4 3.4 chain_step.27
  513.0 3.5 chain_step.29
  519.9 6.6 %beside.6 = f32[256,5632]{1,0:T(8,128)} custom-call(s32[5]{0:T(128)} %stack.38.s_ref.c_ref, f32[256,1]{1,0:T(8,128)} %copy.26.n_ref.s_ref, bf16[2816,128]{1,0:T(8,128)(2,1)} %get-tuple-element.320.refs_0_, bf16[2816,128]{1,0:T(8,128)(2,1)} %collective-permute-done.38.refs_1_, bf16[2816,128]{1,0:T(8,128)(2,1)} %get-tuple-element.331.refs_2_, ...), custom_call_target="tpu_custom_call" | custom-call | flops 1024 | bytes 1024 | tf_op jit(solution)/shard_map/beside/pallas_call | solution.py:670
  527.4 5.2 collective-permute-done.53.refs_1_
  535.8 3.8 collective-permute-start.60
  549.4 7.5 %collective-permute-done.60.refs_1_.refs_5_ = bf16[2816,128]{1,0:T(8,128)(2,1)} collective-permute-done((bf16[2816,128]{1,0:T(8,128)(2,1)}, bf16[2816,128]{1,0:T(8,128)(2,1)}, u32[]{:S(2)}, u32[]{:S(2)}) %collective-permute-start.60) | collective-permute-done | bytes 720928 | tf_op jit(solution)/shard_map/ppermute | solution.py:792
  564.1 8.3 %collective-permute-done.51.refs_1_.refs_3_ = bf16[2816,128]{1,0:T(8,128)(2,1)} collective-permute-done((bf16[2816,128]{1,0:T(8,128)(2,1)}, bf16[2816,128]{1,0:T(8,128)(2,1)}, u32[]{:S(2)}, u32[]{:S(2)}) %collective-permute-start.51) | collective-permute-done | bytes 720928 | tf_op jit(solution)/shard_map/ppermute | solution.py:792
  579.9 6.4 collective-permute-done.62
  591.4 10.4 %collective-permute-done.55.refs_1_.refs_7_ = bf16[2816,128]{1,0:T(8,128)(2,1)S(1)} collective-permute-done((bf16[2816,128]{1,0:T(8,128)(2,1)}, bf16[2816,128]{1,0:T(8,128)(2,1)S(1)}, u32[]{:S(2)}, u32[]{:S(2)}) %collective-permute-start.55) | collective-permute-done | bytes 720928 | tf_op jit(solution)/shard_map/ppermute | solution.py:792
  608.7 6.6 %beside.9 = f32[256,5632]{1,0:T(8,128)} custom-call(s32[5]{0:T(128)} %stack.38.s_ref.c_ref, f32[256,1]{1,0:T(8,128)} %copy.26.n_ref.s_ref, bf16[2816,128]{1,0:T(8,128)(2,1)} %get-tuple-element.358.refs_0_, bf16[2816,128]{1,0:T(8,128)(2,1)} %collective-permute-done.53.refs_1_, bf16[2816,128]{1,0:T(8,128)(2,1)} %get-tuple-element.351.refs_2_, ...), custom_call_target="tpu_custom_call" | custom-call | flops 1024 | bytes 1024 | tf_op jit(solution)/shard_map/beside/pallas_call | solution.py:670
  616.1 6.8 %collective-permute-done.57 = bf16[2560,128]{1,0:T(8,128)(2,1)S(1)} collective-permute-done((bf16[2560,128]{1,0:T(8,128)(2,1)}, bf16[2560,128]{1,0:T(8,128)(2,1)S(1)}, u32[]{:S(2)}, u32[]{:S(2)}) %collective-permute-start.57) | collective-permute-done | bytes 655392 | tf_op jit(solution)/shard_map/ppermute | solution.py:792
  627.9 4.5 beside.7
  638.6 3.7 beside.8
  (274 shorter events, 184.2 us)
Async XLA Ops:
  0.6 28.6 %collective-permute-start.4 = (bf16[704,2048]{1,0:T(8,128)(2,1)}, bf16[704,2048]{1,0:T(8,128)(2,1)}, u32[]{:S(2)}, u32[]{:S(2)}) collective-permute-start(bf16[704,2048]{1,0:T(8,128)(2,1)} %a_ref.3), channel_id=1, source_target_pairs={{0,1},{1,0},{2,3},{3,2},{4,5},{5,4},{6,7},{7,6},{8,9},{9,8},{10,11... | collective-permute-start | bytes 8650760 | tf_op jit(solution)/shard_map/ppermute | solution.py:745
  6.7 22.5 %all-to-all-start = ((bf16[4,256,640]{2,1,0:T(8,128)(2,1)}), bf16[4,256,640]{2,1,0:T(8,128)(2,1)S(1)}, u32[]{:S(2)}, u32[]{:S(2)}) async-start(bf16[4,256,640]{2,1,0:T(8,128)(2,1)} %pick_qkv.1), calls=%async_computation | async-start | bytes 2621440 | tf_op jit(solution)/shard_map/all_to_all | solution.py:736
  11.4 40.6 %collective-permute-start.3 = (bf16[256,2048]{1,0:T(8,128)(2,1)S(1)}, bf16[256,2048]{1,0:T(8,128)(2,1)}, u32[]{:S(2)}, u32[]{:S(2)}) collective-permute-start(bf16[256,2048]{1,0:T(8,128)(2,1)S(1)} %copy-done.25), channel_id=1, source_target_pairs={{0,1},{1,0},{2,3},{3,2},{4,5},{5,4},{6,7},{7,6},{8,9},{9,8},{10,11... | collective-permute-start | bytes 3145736 | tf_op jit(solution)/shard_map/ppermute | solution.py:745
  11.6 30.4 %collective-permute-start = (bf16[128,2048]{1,0:T(8,128)(2,1)S(1)}, bf16[128,2048]{1,0:T(8,128)(2,1)S(1)}, u32[]{:S(2)}, u32[]{:S(2)}) collective-permute-start(bf16[128,2048]{1,0:T(8,128)(2,1)S(1)} %copy-done.8), channel_id=1, source_target_pairs={{0,2},{1,3},{2,0},{3,1},{4,6},{5,7},{6,4},{7,5},{8,10},{9,11},{10,... | collective-permute-start | bytes 1572872 | tf_op jit(solution)/shard_map/ppermute | solution.py:739
  13.5 28.5 %collective-permute-start.1 = (bf16[128,2048]{1,0:T(8,128)(2,1)S(1)}, bf16[128,2048]{1,0:T(8,128)(2,1)}, u32[]{:S(2)}, u32[]{:S(2)}) collective-permute-start(bf16[128,2048]{1,0:T(8,128)(2,1)S(1)} %copy-done.8), channel_id=1, source_target_pairs={{0,4},{1,5},{2,6},{3,7},{4,0},{5,1},{6,2},{7,3},{8,12},{9,13},{10,... | collective-permute-start | bytes 1572872 | tf_op jit(solution)/shard_map/ppermute | solution.py:739
  15.0 37.0 %collective-permute-start.2 = (bf16[128,2048]{1,0:T(8,128)(2,1)S(1)}, bf16[128,2048]{1,0:T(8,128)(2,1)}, u32[]{:S(2)}, u32[]{:S(2)}) collective-permute-start(bf16[128,2048]{1,0:T(8,128)(2,1)S(1)} %copy-done.8), channel_id=1, source_target_pairs={{0,6},{1,7},{2,4},{3,5},{4,2},{5,3},{6,0},{7,1},{8,14},{9,15},{10,... | collective-permute-start | bytes 1572872 | tf_op jit(solution)/shard_map/ppermute | solution.py:739
  29.2 26.3 %collective-permute-start.5 = (bf16[4,256,640]{2,1,0:T(8,128)(2,1)S(1)}, bf16[4,256,640]{2,1,0:T(8,128)(2,1)}, u32[]{:S(2)}, u32[]{:S(2)}) collective-permute-start(bf16[4,256,640]{2,1,0:T(8,128)(2,1)S(1)} %all-to-all-done.n_ref), channel_id=1, source_target_pairs={{0,1},{1,0},{2,3},{3,2},{4,5},{5,4},{6,7},{7,6},{8,9},{9,8},{10,11... | collective-permute-start | bytes 3932168 | tf_op jit(solution)/shard_map/ppermute | solution.py:745
  52.0 21.2 %all-to-all-start.1 = ((bf16[4,128,1408]{2,1,0:T(8,128)(2,1)}), bf16[4,128,1408]{2,1,0:T(8,128)(2,1)S(1)}, u32[]{:S(2)}, u32[]{:S(2)}) async-start(bf16[4,128,1408]{2,1,0:T(8,128)(2,1)} %get-tuple-element.207), calls=%async_computation.1 | async-start | bytes 2883584 | tf_op jit(solution)/shard_map/all_to_all | solution.py:736
  73.2 23.3 %collective-permute-start.7 = (bf16[4,128,1408]{2,1,0:T(8,128)(2,1)S(1)}, bf16[4,128,1408]{2,1,0:T(8,128)(2,1)S(1)}, u32[]{:S(2)}, u32[]{:S(2)}) collective-permute-start(bf16[4,128,1408]{2,1,0:T(8,128)(2,1)S(1)} %all-to-all-done.1.refs_5_), channel_id=1, source_target_pairs={{0,1},{1,0},{2,3},{3,2},{4,5},{5,4},{6,7},{7,6},{8,9},{9,8},{10,11... | collective-permute-start | bytes 4325384 | tf_op jit(solution)/shard_map/ppermute | solution.py:745
  73.2 23.3 %all-to-all-start.2 = ((bf16[4,128,1408]{2,1,0:T(8,128)(2,1)}), bf16[4,128,1408]{2,1,0:T(8,128)(2,1)}, u32[]{:S(2)}, u32[]{:S(2)}) async-start(bf16[4,128,1408]{2,1,0:T(8,128)(2,1)} %get-tuple-element.212), calls=%async_computation.2 | async-start | bytes 2883584 | tf_op jit(solution)/shard_map/all_to_all | solution.py:736
  77.7 34.6 %collective-permute-start.11 = (bf16[4,128,1408]{2,1,0:T(8,128)(2,1)S(1)}, bf16[4,128,1408]{2,1,0:T(8,128)(2,1)}, u32[]{:S(2)}, u32[]{:S(2)}) collective-permute-start(bf16[4,128,1408]{2,1,0:T(8,128)(2,1)S(1)} %all-to-all-done.1.refs_5_), channel_id=1, source_target_pairs={{0,8},{8,0},{16,24},{24,16},{1,9},{9,1},{17,25},{25,17},{2,10},{10... | collective-permute-start | bytes 4325384 | tf_op jit(solution)/shard_map/ppermute | solution.py:748
  96.6 44.8 %collective-permute-start.12 = (bf16[4,128,1408]{2,1,0:T(8,128)(2,1)}, bf16[4,128,1408]{2,1,0:T(8,128)(2,1)}, u32[]{:S(2)}, u32[]{:S(2)}) collective-permute-start(bf16[4,128,1408]{2,1,0:T(8,128)(2,1)} %all-to-all-done.2.refs_9_), channel_id=1, source_target_pairs={{0,1},{1,0},{2,3},{3,2},{4,5},{5,4},{6,7},{7,6},{8,9},{9,8},{10,11... | collective-permute-start | bytes 4325384 | tf_op jit(solution)/shard_map/ppermute | solution.py:745
  96.6 46.2 %collective-permute-start.17 = (bf16[4,128,1408]{2,1,0:T(8,128)(2,1)}, bf16[4,128,1408]{2,1,0:T(8,128)(2,1)}, u32[]{:S(2)}, u32[]{:S(2)}) collective-permute-start(bf16[4,128,1408]{2,1,0:T(8,128)(2,1)} %all-to-all-done.2.refs_9_), channel_id=1, source_target_pairs={{0,8},{8,0},{16,24},{24,16},{1,9},{9,1},{17,25},{25,17},{2,10},{10... | collective-permute-start | bytes 4325384 | tf_op jit(solution)/shard_map/ppermute | solution.py:748
  103.0 17.6 %collective-permute-start.8 = (bf16[128,2048]{1,0:T(8,128)(2,1)}, bf16[128,2048]{1,0:T(8,128)(2,1)}, u32[]{:S(2)}, u32[]{:S(2)}) collective-permute-start(bf16[128,2048]{1,0:T(8,128)(2,1)} %get-tuple-element.222), channel_id=1, source_target_pairs={{0,2},{1,3},{2,0},{3,1},{4,6},{5,7},{6,4},{7,5},{8,10},{9,11},{10,... | collective-permute-start | bytes 1572872 | tf_op jit(solution)/shard_map/ppermute | solution.py:739
  104.5 36.1 %collective-permute-start.9 = (bf16[128,2048]{1,0:T(8,128)(2,1)}, bf16[128,2048]{1,0:T(8,128)(2,1)}, u32[]{:S(2)}, u32[]{:S(2)}) collective-permute-start(bf16[128,2048]{1,0:T(8,128)(2,1)} %get-tuple-element.223), channel_id=1, source_target_pairs={{0,4},{1,5},{2,6},{3,7},{4,0},{5,1},{6,2},{7,3},{8,12},{9,13},{10,... | collective-permute-start | bytes 1572872 | tf_op jit(solution)/shard_map/ppermute | solution.py:739
  112.3 28.3 %collective-permute-start.10 = (bf16[128,2048]{1,0:T(8,128)(2,1)}, bf16[128,2048]{1,0:T(8,128)(2,1)S(1)}, u32[]{:S(2)}, u32[]{:S(2)}) collective-permute-start(bf16[128,2048]{1,0:T(8,128)(2,1)} %get-tuple-element.224), channel_id=1, source_target_pairs={{0,6},{1,7},{2,4},{3,5},{4,2},{5,3},{6,0},{7,1},{8,14},{9,15},{10,... | collective-permute-start | bytes 1572872 | tf_op jit(solution)/shard_map/ppermute | solution.py:739
  116.8 35.4 %all-to-all-start.3 = ((bf16[4,128,2048]{2,1,0:T(8,128)(2,1)}), bf16[4,128,2048]{2,1,0:T(8,128)(2,1)S(1)}, u32[]{:S(2)}, u32[]{:S(2)}) async-start(bf16[4,128,2048]{2,1,0:T(8,128)(2,1)} %broadcast_in_dim.38), calls=%async_computation.3 | async-start | bytes 4194304 | tf_op jit(solution)/shard_map/all_to_all | solution.py:736
  141.4 33.3 %collective-permute-start.16 = (bf16[4,128,1408]{2,1,0:T(8,128)(2,1)}, bf16[4,128,1408]{2,1,0:T(8,128)(2,1)S(1)}, u32[]{:S(2)}, u32[]{:S(2)}) collective-permute-start(bf16[4,128,1408]{2,1,0:T(8,128)(2,1)} %collective-permute-done.11.refs_6_), channel_id=1, source_target_pairs={{0,1},{1,0},{2,3},{3,2},{4,5},{5,4},{6,7},{7,6},{8,9},{9,8},{10,11... | collective-permute-start | bytes 4325384 | tf_op jit(solution)/shard_map/ppermute | solution.py:745
  142.8 31.9 %collective-permute-start.18 = (bf16[4,128,1408]{2,1,0:T(8,128)(2,1)}, bf16[4,128,1408]{2,1,0:T(8,128)(2,1)}, u32[]{:S(2)}, u32[]{:S(2)}) collective-permute-start(bf16[4,128,1408]{2,1,0:T(8,128)(2,1)} %collective-permute-done.17.refs_10_), channel_id=1, source_target_pairs={{0,1},{1,0},{2,3},{3,2},{4,5},{5,4},{6,7},{7,6},{8,9},{9,8},{10,11... | collective-permute-start | bytes 4325384 | tf_op jit(solution)/shard_map/ppermute | solution.py:745
  146.0 17.0 %collective-permute-start.13 = (bf16[128,2048]{1,0:T(8,128)(2,1)}, bf16[128,2048]{1,0:T(8,128)(2,1)}, u32[]{:S(2)}, u32[]{:S(2)}) collective-permute-start(bf16[128,2048]{1,0:T(8,128)(2,1)} %get-tuple-element.231.refs_0_), channel_id=1, source_target_pairs={{0,2},{1,3},{2,0},{3,1},{4,6},{5,7},{6,4},{7,5},{8,10},{9,11},{10,... | collective-permute-start | bytes 1572872 | tf_op jit(solution)/shard_map/ppermute | solution.py:739
  147.8 26.9 %collective-permute-start.14 = (bf16[128,2048]{1,0:T(8,128)(2,1)}, bf16[128,2048]{1,0:T(8,128)(2,1)}, u32[]{:S(2)}, u32[]{:S(2)}) collective-permute-start(bf16[128,2048]{1,0:T(8,128)(2,1)} %get-tuple-element.231.refs_0_), channel_id=1, source_target_pairs={{0,4},{1,5},{2,6},{3,7},{4,0},{5,1},{6,2},{7,3},{8,12},{9,13},{10,... | collective-permute-start | bytes 1572872 | tf_op jit(solution)/shard_map/ppermute | solution.py:739
  149.2 25.4 %collective-permute-start.15 = (bf16[128,2048]{1,0:T(8,128)(2,1)}, bf16[128,2048]{1,0:T(8,128)(2,1)}, u32[]{:S(2)}, u32[]{:S(2)}) collective-permute-start(bf16[128,2048]{1,0:T(8,128)(2,1)} %get-tuple-element.231.refs_0_), channel_id=1, source_target_pairs={{0,6},{1,7},{2,4},{3,5},{4,2},{5,3},{6,0},{7,1},{8,14},{9,15},{10,... | collective-permute-start | bytes 1572872 | tf_op jit(solution)/shard_map/ppermute | solution.py:739
  220.9 29.4 %all-to-all-start.4 = ((bf16[4,128,2048]{2,1,0:T(8,128)(2,1)}), bf16[4,128,2048]{2,1,0:T(8,128)(2,1)S(1)}, u32[]{:S(2)}, u32[]{:S(2)}) async-start(bf16[4,128,2048]{2,1,0:T(8,128)(2,1)} %bitcast.86), calls=%async_computation.4 | async-start | bytes 4194304 | tf_op jit(solution)/shard_map/all_to_all | solution.py:736
  251.6 37.8 %all-to-all-start.5 = ((bf16[4,2816,128]{2,1,0:T(8,128)(2,1)}), bf16[4,2816,128]{2,1,0:T(8,128)(2,1)S(1)}, u32[]{:S(2)}, u32[]{:S(2)}) async-start(bf16[4,2816,128]{2,1,0:T(8,128)(2,1)} %pair_sum.7), calls=%async_computation.5 | async-start | bytes 5767168 | tf_op jit(solution)/shard_map/all_to_all | solution.py:736
  268.5 41.9 %collective-permute-start.21 = (bf16[4,2816,128]{2,1,0:T(8,128)(2,1)}, bf16[4,2816,128]{2,1,0:T(8,128)(2,1)}, u32[]{:S(2)}, u32[]{:S(2)}) collective-permute-start(bf16[4,2816,128]{2,1,0:T(8,128)(2,1)} %get-tuple-element.258), channel_id=1, source_target_pairs={{0,1},{1,0},{2,3},{3,2},{4,5},{5,4},{6,7},{7,6},{8,9},{9,8},{10,11... | collective-permute-start | bytes 8650760 | tf_op jit(solution)/shard_map/ppermute | solution.py:745
  270.5 18.9 %collective-permute-start.20 = (bf16[2816,128]{1,0:T(8,128)(2,1)}, bf16[2816,128]{1,0:T(8,128)(2,1)}, u32[]{:S(2)}, u32[]{:S(2)}) collective-permute-start(bf16[2816,128]{1,0:T(8,128)(2,1)} %slice_bitcast_fusion.1), channel_id=1, source_target_pairs={{0,8},{8,0},{16,24},{24,16},{1,9},{9,1},{17,25},{25,17},{2,10},{10... | collective-permute-start | bytes 2162696 | tf_op jit(solution)/shard_map/ppermute | solution.py:792
  291.1 39.0 %all-to-all-start.7 = ((bf16[4,128,2048]{2,1,0:T(8,128)(2,1)}), bf16[4,128,2048]{2,1,0:T(8,128)(2,1)}, u32[]{:S(2)}, u32[]{:S(2)}) async-start(bf16[4,128,2048]{2,1,0:T(8,128)(2,1)} %bitcast.85), calls=%async_computation.7 | async-start | bytes 4194304 | tf_op jit(solution)/shard_map/all_to_all | solution.py:736
  296.7 19.1 %collective-permute-start.23 = (bf16[2816,128]{1,0:T(8,128)(2,1)S(1)}, bf16[2816,128]{1,0:T(8,128)(2,1)S(1)}, u32[]{:S(2)}, u32[]{:S(2)}) collective-permute-start(bf16[2816,128]{1,0:T(8,128)(2,1)S(1)} %slice_bitcast_fusion), channel_id=1, source_target_pairs={{0,8},{8,0},{16,24},{24,16},{1,9},{9,1},{17,25},{25,17},{2,10},{10... | collective-permute-start | bytes 2162696 | tf_op jit(solution)/shard_map/ppermute | solution.py:792
  300.1 29.9 %collective-permute-start.24 = (bf16[2816,128]{1,0:T(8,128)(2,1)}, bf16[2816,128]{1,0:T(8,128)(2,1)}, u32[]{:S(2)}, u32[]{:S(2)}) collective-permute-start(bf16[2816,128]{1,0:T(8,128)(2,1)} %get-tuple-element.270), channel_id=1, source_target_pairs={{0,8},{8,0},{16,24},{24,16},{1,9},{9,1},{17,25},{25,17},{2,10},{10... | collective-permute-start | bytes 2162696 | tf_op jit(solution)/shard_map/ppermute | solution.py:792
  301.6 28.4 %collective-permute-start.25 = (bf16[2816,128]{1,0:T(8,128)(2,1)}, bf16[2816,128]{1,0:T(8,128)(2,1)}, u32[]{:S(2)}, u32[]{:S(2)}) collective-permute-start(bf16[2816,128]{1,0:T(8,128)(2,1)} %get-tuple-element.271.refs_2_), channel_id=1, source_target_pairs={{8,16},{16,8},{9,17},{17,9},{10,18},{18,10},{11,19},{19,11},{12,20... | collective-permute-start | bytes 2162696 | tf_op jit(solution)/shard_map/ppermute | solution.py:794
  330.1 68.4 %all-to-all-start.8 = ((bf16[4,2816,128]{2,1,0:T(8,128)(2,1)}), bf16[4,2816,128]{2,1,0:T(8,128)(2,1)S(1)}, u32[]{:S(2)}, u32[]{:S(2)}) async-start(bf16[4,2816,128]{2,1,0:T(8,128)(2,1)} %pair_sum.6), calls=%async_computation.8 | async-start | bytes 5767168 | tf_op jit(solution)/shard_map/all_to_all | solution.py:736
  337.2 19.8 %collective-permute-start.26 = (bf16[2816,128]{1,0:T(8,128)(2,1)}, bf16[2816,128]{1,0:T(8,128)(2,1)}, u32[]{:S(2)}, u32[]{:S(2)}) collective-permute-start(bf16[2816,128]{1,0:T(8,128)(2,1)} %get-tuple-element.279), channel_id=1, source_target_pairs={{0,8},{8,0},{16,24},{24,16},{1,9},{9,1},{17,25},{25,17},{2,10},{10... | collective-permute-start | bytes 2162696 | tf_op jit(solution)/shard_map/ppermute | solution.py:792
  337.5 19.4 %collective-permute-start.27 = (bf16[2816,128]{1,0:T(8,128)(2,1)}, bf16[2816,128]{1,0:T(8,128)(2,1)}, u32[]{:S(2)}, u32[]{:S(2)}) collective-permute-start(bf16[2816,128]{1,0:T(8,128)(2,1)} %get-tuple-element.280.refs_2_), channel_id=1, source_target_pairs={{8,16},{16,8},{9,17},{17,9},{10,18},{18,10},{11,19},{19,11},{12,20... | collective-permute-start | bytes 2162696 | tf_op jit(solution)/shard_map/ppermute | solution.py:794
  342.4 30.1 %collective-permute-start.28 = (bf16[2816,128]{1,0:T(8,128)(2,1)}, bf16[2816,128]{1,0:T(8,128)(2,1)}, u32[]{:S(2)}, u32[]{:S(2)}) collective-permute-start(bf16[2816,128]{1,0:T(8,128)(2,1)} %get-tuple-element.287.refs_0_), channel_id=1, source_target_pairs={{0,8},{8,0},{16,24},{24,16},{1,9},{9,1},{17,25},{25,17},{2,10},{10... | collective-permute-start | bytes 2162696 | tf_op jit(solution)/shard_map/ppermute | solution.py:792
  346.2 26.3 %collective-permute-start.29 = (bf16[2816,128]{1,0:T(8,128)(2,1)}, bf16[2816,128]{1,0:T(8,128)(2,1)}, u32[]{:S(2)}, u32[]{:S(2)}) collective-permute-start(bf16[2816,128]{1,0:T(8,128)(2,1)} %get-tuple-element.288.refs_2_), channel_id=1, source_target_pairs={{8,16},{16,8},{9,17},{17,9},{10,18},{18,10},{11,19},{19,11},{12,20... | collective-permute-start | bytes 2162696 | tf_op jit(solution)/shard_map/ppermute | solution.py:794
  374.1 15.8 %collective-permute-start.30 = (bf16[512,128]{1,0:T(8,128)(2,1)}, bf16[512,128]{1,0:T(8,128)(2,1)S(1)}, u32[]{:S(2)}, u32[]{:S(2)}) collective-permute-start(bf16[512,128]{1,0:T(8,128)(2,1)} %slice.187), channel_id=1, source_target_pairs={{0,1},{1,0},{2,3},{3,2},{4,5},{5,4},{6,7},{7,6},{8,9},{9,8},{10,11... | collective-permute-start | bytes 393224 | tf_op jit(solution)/shard_map/ppermute | solution.py:745
  377.5 21.0 %collective-permute-start.31 = (bf16[2816,128]{1,0:T(8,128)(2,1)}, bf16[2816,128]{1,0:T(8,128)(2,1)}, u32[]{:S(2)}, u32[]{:S(2)}) collective-permute-start(bf16[2816,128]{1,0:T(8,128)(2,1)} %get-tuple-element.296.refs_2_), channel_id=1, source_target_pairs={{0,8},{8,0},{16,24},{24,16},{1,9},{9,1},{17,25},{25,17},{2,10},{10... | collective-permute-start | bytes 2162696 | tf_op jit(solution)/shard_map/ppermute | solution.py:792
  381.2 17.3 %collective-permute-start.32 = (bf16[2816,128]{1,0:T(8,128)(2,1)}, bf16[2816,128]{1,0:T(8,128)(2,1)}, u32[]{:S(2)}, u32[]{:S(2)}) collective-permute-start(bf16[2816,128]{1,0:T(8,128)(2,1)} %get-tuple-element.297.refs_2_), channel_id=1, source_target_pairs={{8,16},{16,8},{9,17},{17,9},{10,18},{18,10},{11,19},{19,11},{12,20... | collective-permute-start | bytes 2162696 | tf_op jit(solution)/shard_map/ppermute | solution.py:794
  386.3 27.5 %collective-permute-start.33 = (bf16[2816,128]{1,0:T(8,128)(2,1)}, bf16[2816,128]{1,0:T(8,128)(2,1)}, u32[]{:S(2)}, u32[]{:S(2)}) collective-permute-start(bf16[2816,128]{1,0:T(8,128)(2,1)} %get-tuple-element.304.refs_4_), channel_id=1, source_target_pairs={{0,8},{8,0},{16,24},{24,16},{1,9},{9,1},{17,25},{25,17},{2,10},{10... | collective-permute-start | bytes 2162696 | tf_op jit(solution)/shard_map/ppermute | solution.py:792
  388.4 25.3 %collective-permute-start.34 = (bf16[2816,128]{1,0:T(8,128)(2,1)}, bf16[2816,128]{1,0:T(8,128)(2,1)}, u32[]{:S(2)}, u32[]{:S(2)}) collective-permute-start(bf16[2816,128]{1,0:T(8,128)(2,1)} %get-tuple-element.305.refs_2_), channel_id=1, source_target_pairs={{8,16},{16,8},{9,17},{17,9},{10,18},{18,10},{11,19},{19,11},{12,20... | collective-permute-start | bytes 2162696 | tf_op jit(solution)/shard_map/ppermute | solution.py:794
  400.1 38.1 %all-to-all-start.9 = ((bf16[4,128,2048]{2,1,0:T(8,128)(2,1)}), bf16[4,128,2048]{2,1,0:T(8,128)(2,1)}, u32[]{:S(2)}, u32[]{:S(2)}) async-start(bf16[4,128,2048]{2,1,0:T(8,128)(2,1)} %bitcast.84), calls=%async_computation.9 | async-start | bytes 4194304 | tf_op jit(solution)/shard_map/all_to_all | solution.py:736
  417.2 20.9 %collective-permute-start.36 = (bf16[2816,128]{1,0:T(8,128)(2,1)}, bf16[2816,128]{1,0:T(8,128)(2,1)S(1)}, u32[]{:S(2)}, u32[]{:S(2)}) collective-permute-start(bf16[2816,128]{1,0:T(8,128)(2,1)} %get-tuple-element.313.refs_6_), channel_id=1, source_target_pairs={{0,8},{8,0},{16,24},{24,16},{1,9},{9,1},{17,25},{25,17},{2,10},{10... | collective-permute-start | bytes 2162696 | tf_op jit(solution)/shard_map/ppermute | solution.py:792
  421.1 17.0 %collective-permute-start.37 = (bf16[2816,128]{1,0:T(8,128)(2,1)}, bf16[2816,128]{1,0:T(8,128)(2,1)S(1)}, u32[]{:S(2)}, u32[]{:S(2)}) collective-permute-start(bf16[2816,128]{1,0:T(8,128)(2,1)} %get-tuple-element.314.refs_2_), channel_id=1, source_target_pairs={{8,16},{16,8},{9,17},{17,9},{10,18},{18,10},{11,19},{19,11},{12,20... | collective-permute-start | bytes 2162696 | tf_op jit(solution)/shard_map/ppermute | solution.py:794
  439.0 20.7 %all-to-all-start.10 = ((bf16[4,1280,128]{2,1,0:T(8,128)(2,1)}), bf16[4,1280,128]{2,1,0:T(8,128)(2,1)S(1)}, u32[]{:S(2)}, u32[]{:S(2)}) async-start(bf16[4,1280,128]{2,1,0:T(8,128)(2,1)} %pair_sum.8), calls=%async_computation.10 | async-start | bytes 2621440 | tf_op jit(solution)/shard_map/all_to_all | solution.py:736
  446.6 29.5 %collective-permute-start.38 = (bf16[2816,128]{1,0:T(8,128)(2,1)}, bf16[2816,128]{1,0:T(8,128)(2,1)}, u32[]{:S(2)}, u32[]{:S(2)}) collective-permute-start(bf16[2816,128]{1,0:T(8,128)(2,1)} %get-tuple-element.320.refs_0_), channel_id=1, source_target_pairs={{0,8},{8,0},{16,24},{24,16},{1,9},{9,1},{17,25},{25,17},{2,10},{10... | collective-permute-start | bytes 2162696 | tf_op jit(solution)/shard_map/ppermute | solution.py:792
  449.5 26.6 %collective-permute-start.39 = (bf16[2816,128]{1,0:T(8,128)(2,1)}, bf16[2816,128]{1,0:T(8,128)(2,1)}, u32[]{:S(2)}, u32[]{:S(2)}) collective-permute-start(bf16[2816,128]{1,0:T(8,128)(2,1)} %get-tuple-element.321.refs_2_), channel_id=1, source_target_pairs={{8,16},{16,8},{9,17},{17,9},{10,18},{18,10},{11,19},{19,11},{12,20... | collective-permute-start | bytes 2162696 | tf_op jit(solution)/shard_map/ppermute | solution.py:794
  451.0 32.2 %collective-permute-start.41 = (bf16[2,2048,128]{2,1,0:T(8,128)(2,1)}, bf16[2,2048,128]{2,1,0:T(8,128)(2,1)}, u32[]{:S(2)}, u32[]{:S(2)}) collective-permute-start(bf16[2,2048,128]{2,1,0:T(8,128)(2,1)} %get-tuple-element.328), channel_id=1, source_target_pairs={{0,1},{1,0},{2,3},{3,2},{4,5},{5,4},{6,7},{7,6},{8,9},{9,8},{10,11... | collective-permute-start | bytes 3145736 | tf_op jit(solution)/shard_map/ppermute | solution.py:745
  460.8 59.1 %all-to-all-start.6 = ((bf16[4,128,2048]{2,1,0:T(8,128)(2,1)}), bf16[4,128,2048]{2,1,0:T(8,128)(2,1)S(1)}, u32[]{:S(2)}, u32[]{:S(2)}) async-start(bf16[4,128,2048]{2,1,0:T(8,128)(2,1)} %bitcast.83), calls=%async_computation.6 | async-start | bytes 4194304 | tf_op jit(solution)/shard_map/all_to_all | solution.py:736
  467.8 25.5 %collective-permute-start.42 = (bf16[2816,128]{1,0:T(8,128)(2,1)}, bf16[2816,128]{1,0:T(8,128)(2,1)}, u32[]{:S(2)}, u32[]{:S(2)}) collective-permute-start(bf16[2816,128]{1,0:T(8,128)(2,1)} %get-tuple-element.331.refs_2_), channel_id=1, source_target_pairs={{0,8},{8,0},{16,24},{24,16},{1,9},{9,1},{17,25},{25,17},{2,10},{10... | collective-permute-start | bytes 2162696 | tf_op jit(solution)/shard_map/ppermute | solution.py:792
  470.5 22.9 %collective-permute-start.43 = (bf16[2816,128]{1,0:T(8,128)(2,1)}, bf16[2816,128]{1,0:T(8,128)(2,1)}, u32[]{:S(2)}, u32[]{:S(2)}) collective-permute-start(bf16[2816,128]{1,0:T(8,128)(2,1)} %get-tuple-element.332.refs_2_), channel_id=1, source_target_pairs={{8,16},{16,8},{9,17},{17,9},{10,18},{18,10},{11,19},{19,11},{12,20... | collective-permute-start | bytes 2162696 | tf_op jit(solution)/shard_map/ppermute | solution.py:794
  479.5 32.6 %collective-permute-start.47 = (bf16[2816,128]{1,0:T(8,128)(2,1)}, bf16[2816,128]{1,0:T(8,128)(2,1)S(1)}, u32[]{:S(2)}, u32[]{:S(2)}) collective-permute-start(bf16[2816,128]{1,0:T(8,128)(2,1)} %get-tuple-element.337.refs_4_), channel_id=1, source_target_pairs={{0,8},{8,0},{16,24},{24,16},{1,9},{9,1},{17,25},{25,17},{2,10},{10... | collective-permute-start | bytes 2162696 | tf_op jit(solution)/shard_map/ppermute | solution.py:792
  481.6 30.6 %collective-permute-start.48 = (bf16[2816,128]{1,0:T(8,128)(2,1)}, bf16[2816,128]{1,0:T(8,128)(2,1)}, u32[]{:S(2)}, u32[]{:S(2)}) collective-permute-start(bf16[2816,128]{1,0:T(8,128)(2,1)} %get-tuple-element.338.refs_2_), channel_id=1, source_target_pairs={{8,16},{16,8},{9,17},{17,9},{10,18},{18,10},{11,19},{19,11},{12,20... | collective-permute-start | bytes 2162696 | tf_op jit(solution)/shard_map/ppermute | solution.py:794
  496.8 23.1 %collective-permute-start.49 = (bf16[2816,128]{1,0:T(8,128)(2,1)}, bf16[2816,128]{1,0:T(8,128)(2,1)}, u32[]{:S(2)}, u32[]{:S(2)}) collective-permute-start(bf16[2816,128]{1,0:T(8,128)(2,1)} %get-tuple-element.344.refs_6_), channel_id=1, source_target_pairs={{0,8},{8,0},{16,24},{24,16},{1,9},{9,1},{17,25},{25,17},{2,10},{10... | collective-permute-start | bytes 2162696 | tf_op jit(solution)/shard_map/ppermute | solution.py:792
  498.8 21.1 %collective-permute-start.50 = (bf16[2816,128]{1,0:T(8,128)(2,1)}, bf16[2816,128]{1,0:T(8,128)(2,1)}, u32[]{:S(2)}, u32[]{:S(2)}) collective-permute-start(bf16[2816,128]{1,0:T(8,128)(2,1)} %get-tuple-element.345.refs_2_), channel_id=1, source_target_pairs={{8,16},{16,8},{9,17},{17,9},{10,18},{18,10},{11,19},{19,11},{12,20... | collective-permute-start | bytes 2162696 | tf_op jit(solution)/shard_map/ppermute | solution.py:794
  516.4 16.2 %collective-permute-start.53 = (bf16[2816,128]{1,0:T(8,128)(2,1)}, bf16[2816,128]{1,0:T(8,128)(2,1)}, u32[]{:S(2)}, u32[]{:S(2)}) collective-permute-start(bf16[2816,128]{1,0:T(8,128)(2,1)} %get-tuple-element.358.refs_0_), channel_id=1, source_target_pairs={{0,8},{8,0},{16,24},{24,16},{1,9},{9,1},{17,25},{25,17},{2,10},{10... | collective-permute-start | bytes 2162696 | tf_op jit(solution)/shard_map/ppermute | solution.py:792
  517.5 15.1 %collective-permute-start.54 = (bf16[2816,128]{1,0:T(8,128)(2,1)}, bf16[2816,128]{1,0:T(8,128)(2,1)}, u32[]{:S(2)}, u32[]{:S(2)}) collective-permute-start(bf16[2816,128]{1,0:T(8,128)(2,1)} %get-tuple-element.359.refs_2_), channel_id=1, source_target_pairs={{8,16},{16,8},{9,17},{17,9},{10,18},{18,10},{11,19},{19,11},{12,20... | collective-permute-start | bytes 2162696 | tf_op jit(solution)/shard_map/ppermute | solution.py:794
  535.8 21.2 %collective-permute-start.60 = (bf16[2816,128]{1,0:T(8,128)(2,1)}, bf16[2816,128]{1,0:T(8,128)(2,1)}, u32[]{:S(2)}, u32[]{:S(2)}) collective-permute-start(bf16[2816,128]{1,0:T(8,128)(2,1)} %get-tuple-element.374.refs_4_), channel_id=1, source_target_pairs={{0,8},{8,0},{16,24},{24,16},{1,9},{9,1},{17,25},{25,17},{2,10},{10... | collective-permute-start | bytes 2162696 | tf_op jit(solution)/shard_map/ppermute | solution.py:792
  544.5 27.9 %collective-permute-start.51 = (bf16[2816,128]{1,0:T(8,128)(2,1)}, bf16[2816,128]{1,0:T(8,128)(2,1)}, u32[]{:S(2)}, u32[]{:S(2)}) collective-permute-start(bf16[2816,128]{1,0:T(8,128)(2,1)} %get-tuple-element.351.refs_2_), channel_id=1, source_target_pairs={{0,8},{8,0},{16,24},{24,16},{1,9},{9,1},{17,25},{25,17},{2,10},{10... | collective-permute-start | bytes 2162696 | tf_op jit(solution)/shard_map/ppermute | solution.py:792
  546.5 25.9 %collective-permute-start.52 = (bf16[2816,128]{1,0:T(8,128)(2,1)}, bf16[2816,128]{1,0:T(8,128)(2,1)}, u32[]{:S(2)}, u32[]{:S(2)}) collective-permute-start(bf16[2816,128]{1,0:T(8,128)(2,1)} %get-tuple-element.352.refs_2_), channel_id=1, source_target_pairs={{8,16},{16,8},{9,17},{17,9},{10,18},{18,10},{11,19},{19,11},{12,20... | collective-permute-start | bytes 2162696 | tf_op jit(solution)/shard_map/ppermute | solution.py:794
  559.8 26.5 %collective-permute-start.62 = (bf16[2560,128]{1,0:T(8,128)(2,1)}, bf16[2560,128]{1,0:T(8,128)(2,1)S(1)}, u32[]{:S(2)}, u32[]{:S(2)}) collective-permute-start(bf16[2560,128]{1,0:T(8,128)(2,1)} %get-tuple-element.378), channel_id=1, source_target_pairs={{0,8},{8,0},{16,24},{24,16},{1,9},{9,1},{17,25},{25,17},{2,10},{10... | collective-permute-start | bytes 1966088 | tf_op jit(solution)/shard_map/ppermute | solution.py:792
  562.5 17.5 %collective-permute-start.63 = (bf16[2048,128]{1,0:T(8,128)(2,1)}, bf16[2048,128]{1,0:T(8,128)(2,1)S(1)}, u32[]{:S(2)}, u32[]{:S(2)}) collective-permute-start(bf16[2048,128]{1,0:T(8,128)(2,1)} %get-tuple-element.379.refs_0_), channel_id=1, source_target_pairs={{8,16},{16,8},{9,17},{17,9},{10,18},{18,10},{11,19},{19,11},{12,20... | collective-permute-start | bytes 1572872 | tf_op jit(solution)/shard_map/ppermute | solution.py:794
  575.6 26.2 %collective-permute-start.55 = (bf16[2816,128]{1,0:T(8,128)(2,1)}, bf16[2816,128]{1,0:T(8,128)(2,1)S(1)}, u32[]{:S(2)}, u32[]{:S(2)}) collective-permute-start(bf16[2816,128]{1,0:T(8,128)(2,1)} %get-tuple-element.364.refs_6_), channel_id=1, source_target_pairs={{0,8},{8,0},{16,24},{24,16},{1,9},{9,1},{17,25},{25,17},{2,10},{10... | collective-permute-start | bytes 2162696 | tf_op jit(solution)/shard_map/ppermute | solution.py:792
  588.3 27.8 %collective-permute-start.64 = (bf16[2048,128]{1,0:T(8,128)(2,1)}, bf16[2048,128]{1,0:T(8,128)(2,1)}, u32[]{:S(2)}, u32[]{:S(2)}) collective-permute-start(bf16[2048,128]{1,0:T(8,128)(2,1)} %chain_step.35.refs_0_), channel_id=1, source_target_pairs={{0,8},{8,0},{16,24},{24,16},{1,9},{9,1},{17,25},{25,17},{2,10},{10... | collective-permute-start | bytes 1572872 | tf_op jit(solution)/shard_map/ppermute | solution.py:792
  605.5 17.4 %collective-permute-start.57 = (bf16[2560,128]{1,0:T(8,128)(2,1)}, bf16[2560,128]{1,0:T(8,128)(2,1)S(1)}, u32[]{:S(2)}, u32[]{:S(2)}) collective-permute-start(bf16[2560,128]{1,0:T(8,128)(2,1)} %get-tuple-element.369), channel_id=1, source_target_pairs={{0,8},{8,0},{16,24},{24,16},{1,9},{9,1},{17,25},{25,17},{2,10},{10... | collective-permute-start | bytes 1966088 | tf_op jit(solution)/shard_map/ppermute | solution.py:792
  (55 other events, 441.8 us)

commit v6 on v5

--- a/solution.py
+++ b/solution.py
@@ -335,7 +335,8 @@
 
     def body(s_ref, *refs):
         z_refs, c_ref, w_refs = refs[:chips], refs[chips], refs[chips + 1 : chips + 9]
-        d_ref, m_ref, dg_ref, du_ref, z_ref, b_ref, w_ref, acc_ref = refs[chips + 9 :]
+        d_ref, m_ref, dg_ref, du_ref, z_ref = refs[chips + 9 : chips + 14]
+        b_refs, (w_ref, acc_ref) = refs[chips + 14 : -2], refs[-2:]
         chip, core, half = s_ref[0], s_ref[1], s_ref[2]
         turn = pl.program_id(0)
 
@@ -366,10 +367,11 @@
             du_ref[:, :cols] = du
             back = dot_nt(dg, w_ref[0, :, :cols]) + dot_nt(du, w_ref[1, :, :cols])
             back = back + acc_ref[...]
+            acc_ref[...] = back
             if last:
-                b_ref[...] = back.astype(BF16)
-            else:
-                acc_ref[...] = back
+                for k in range(chips):
+                    at = pl.multiple_of((chip ^ k) * rows, rows)
+                    b_refs[k][...] = acc_ref[pl.ds(at, rows), :].astype(BF16)
 
         if turns > 1:
 
@@ -392,14 +394,17 @@
             + [joined]
             + [pl.BlockSpec((chips, part, tile), lambda n, s: (0, 0, n))] * 8
             + [pl.BlockSpec((tile, model), lambda n, s: (n, 0))],
-            out_specs=[out_tile] * 3 + [joined] * 2,
+            out_specs=[out_tile] * 3
+            + [joined]
+            + [pl.BlockSpec((rows, model), lambda n, s: (0, 0))] * chips,
             scratch_shapes=[
                 pltpu.VMEM((2, model, tile), BF16),
                 pltpu.VMEM((own, model), F32),
             ],
         ),
         out_shape=[jax.ShapeDtypeStruct((own, width), BF16)] * 3
-        + [jax.ShapeDtypeStruct((own, model), BF16)] * 2,
+        + [jax.ShapeDtypeStruct((own, model), BF16)]
+        + [jax.ShapeDtypeStruct((rows, model), BF16)] * chips,
         cost_estimate=tiny(),
         name="feed_forward",
     )(ids, *z_blocks, cot, *weights[0], *weights[1], w_down)
@@ -456,12 +461,14 @@
 
 def residual_norm_back(base, parts, y, copies):
     rows, model = y.shape
-    count = parts.shape[0] // rows
-
-    def body(b_ref, y_ref, p_ref, f_ref, l_ref, n_ref):
-        e = p_ref[:rows, :].astype(F32)
-        for i in range(1, count):
-            e = e + p_ref[i * rows : (i + 1) * rows, :].astype(F32)
+    parts = parts if isinstance(parts, (list, tuple)) else [parts]
+
+    def body(b_ref, y_ref, *refs):
+        p_refs, (f_ref, l_ref, n_ref) = refs[:-3], refs[-3:]
+        e = 0.0
+        for p_ref in p_refs:
+            for i in range(p_ref.shape[0] // rows):
+                e = e + p_ref[i * rows : (i + 1) * rows, :].astype(F32)
         v = y_ref[...].astype(F32)
         inv = lax.rsqrt(jnp.mean(v * v, axis=-1, keepdims=True) + NORM_EPS)
         z = v * inv
@@ -474,7 +481,7 @@
 
     return pl.pallas_call(
         body,
-        in_specs=[whole()] * 3,
+        in_specs=[whole()] * (2 + len(parts)),
         out_specs=[whole()] * 3,
         out_shape=[
             jax.ShapeDtypeStruct((rows, model), F32),
@@ -483,7 +490,7 @@
         ],
         cost_estimate=tiny(),
         name="residual_norm_back",
-    )(base, y, parts)
+    )(base, y, *parts)
 
 
 def strips(value, ref, lead=()):
@@ -839,21 +846,23 @@
         [gate_near, gate_traded, gate_far, swap(gate_traded)],
         [up_near, up_traded, up_far, swap(up_traded)],
     ]
-    inner, grad_gate, grad_up, normed_two, back = feed_forward(
+    inner, grad_gate, grad_up, normed_two, *back = feed_forward(
         ids, z_blocks, cot_rows, weights, w_down_c
     )
 
-    parts = exchange(back)
+    parts = hops(back)
     down_near, down_far = row_grad(ids, inner, cot_rows, 4)
     down_far = swap(down_far)
     grad_gate, down_near = tie((grad_gate, down_near))
     gate_near, gate_far = weight_grad(ids, normed_two, grad_gate, chips)
-    gate_near, gate_far, down_far, grad_up = tie((gate_near, gate_far, down_far, grad_up))
+    gate_near, gate_far, down_far, grad_up, *parts = tie(
+        (gate_near, gate_far, down_far, grad_up, *parts)
+    )
     gate_far = swap(gate_far)
     down = pair_sum(down_near, down_far)
     grad_up = visit(grad_up, new=("down", down, 0))
     up_near, up_far = weight_grad(ids, normed_two, grad_up, chips)
-    up_near, up_far, parts = visit(up_near, up_far, parts, new=("down", down, 1))
+    up_near, up_far, *parts = visit(up_near, up_far, *parts, new=("down", down, 1))
     gate_part = exchange(pair_sum(gate_near, gate_far))
     up_far = swap(up_far)
     grad_resid, da, gain_two_local = residual_norm_back(cotangent, parts, resid, chips)

time: 650 us -> 645 us (level)
    all_to_all x11 -> x10, waiting for transfers between devices: 62.9 us -> 41.9 us  [exchange(): return lax.all_to_all(v, 'fsdp', 0, 0, axis_index_groups=sides, tiled=True)]
    ppermute x12 -> x15, waiting for transfers between devices: 57.1 us -> 70.3 us  [hop(): return lax.ppermute(v, 'fsdp', [(i, i ^ 2 * k) for i in range(group)])]
    ppermute x12 -> x15, starting transfers between devices: 18.8 us -> 22.3 us  [hop(): return lax.ppermute(v, 'fsdp', [(i, i ^ 2 * k) for i in range(group)])]
    all_to_all x11 -> x10, starting transfers between devices: 44.7 us -> 41.3 us  [exchange(): return lax.all_to_all(v, 'fsdp', 0, 0, axis_index_groups=sides, tiled=True)]
  transfers between devices with their start and end apart: 76 -> 78, of which waited for: 30 -> 31; matrix products, arithmetic and copies ran while one was open for 6% -> 6% of each run, Pallas kernels for 29% -> 28%
where the time goes in v6:
time: 645 us; the launch traced here: 638 us
  Pallas kernels  229 us (36%)
  waiting for transfers between devices  221 us (34%)
  starting transfers between devices  135 us (21%)
  local copies, waits for them, and re-layouts  30.1 us (5%)
  matrix products  14.7 us (2%)
  other arithmetic  6.71 us (1%)
    ppermute x20, waiting for transfers between devices, visit(): lax.ppermute(ahead, 'rep', outer_pairs)  92.9 us
    ppermute x15, waiting for transfers between devices, hop(): return lax.ppermute(v, 'fsdp', [(i, i ^ 2 * k) for i in range(group)])  70.3 us
    pallas_call x18, Pallas kernels, chain_step(): pl.pallas_call(body, grid=(1,), in_specs=[scalars()] + [spec(v) for v in...  56.1 us
    ppermute x20, starting transfers between devices, visit(): lax.ppermute(ahead, 'rep', outer_pairs)  45.8 us
    all_to_all x10, waiting for transfers between devices, exchange(): return lax.all_to_all(v, 'fsdp', 0, 0, axis_index_groups=sides, tiled=True)  41.9 us
    all_to_all x10, starting transfers between devices, exchange(): return lax.all_to_all(v, 'fsdp', 0, 0, axis_index_groups=sides, tiled=True)  41.3 us
    pallas_call x5, Pallas kernels, beside(): pl.pallas_call(body, grid_spec=pltpu.PrefetchScalarGridSpec(num_scalar_pr...  27.9 us
    pallas_call x1, Pallas kernels, feed_forward(): pl.pallas_call(body, grid_spec=pltpu.PrefetchScalarGridSpec(num_scalar_pr...  26.2 us
  transfers between devices with their start and end apart: 78, of which 31 were waited for; matrix products, arithmetic and copies ran while one was open for 6% of the time, Pallas kernels for 28%

profile of v6, /device:TPU:0, one launch (start us, length us, event | category | flops | bytes accessed | tf_op | source)
XLA Modules:
  0.0 637.7 jit_solution(15709515093123505127)
XLA Ops:
  2.6 4.1 pick_qkv.1
  6.7 4.7 all-to-all-start
  16.7 12.6 %all-to-all-done.n_ref = bf16[4,256,640]{2,1,0:T(8,128)(2,1)S(1)} async-done(((bf16[4,256,640]{2,1,0:T(8,128)(2,1)}), bf16[4,256,640]{2,1,0:T(8,128)(2,1)S(1)}, u32[]{:S(2)}, u32[]{:S(2)}) %all-to-all-start) | async-done | bytes 1310752 | tf_op jit(solution)/shard_map/all_to_all | solution.py:743
  31.1 4.9 pick_half.1
  36.0 6.1 join_cores.1.refs_13_
  42.1 9.9 %collective-permute-done.2.refs_3_ = bf16[128,2048]{1,0:T(8,128)(2,1)} collective-permute-done((bf16[128,2048]{1,0:T(8,128)(2,1)S(1)}, bf16[128,2048]{1,0:T(8,128)(2,1)}, u32[]{:S(2)}, u32[]{:S(2)}) %collective-permute-start.2) | collective-permute-done | bytes 524320 | tf_op jit(solution)/shard_map/ppermute | solution.py:746
  52.0 3.6 all-to-all-start.1
  55.6 6.5 %qkv_forward.1 = (bf16[512,2048]{1,0:T(8,128)(2,1)}, bf16[512,512]{1,0:T(8,128)(2,1)}, bf16[512,128]{1,0:T(8,128)(2,1)}, bf16[2048,640]{1,0:T(8,128)(2,1)}) custom-call(s32[5]{0:T(128)} %stack.38.s_ref.c_ref, f32[512,128]{1,0:T(8,128)} %get-tuple-element.210.cos_ref, f32[512,128]{1,0:T(8,128)} %get-tuple-element.211.sin_ref, bf16[4,256,640]{2,1,0:T(8,128)(2,1)} %copy-done.6, ...), custom_call_target="tpu_custom_call" | custom-call | flops 1024 | bytes 1024 | tf_op jit(solution)/shard_map/qkv_forward/pallas_call | solution.py:167
  62.1 11.1 %all-to-all-done.1.refs_5_ = bf16[4,128,1408]{2,1,0:T(8,128)(2,1)S(1)} async-done(((bf16[4,128,1408]{2,1,0:T(8,128)(2,1)}), bf16[4,128,1408]{2,1,0:T(8,128)(2,1)S(1)}, u32[]{:S(2)}, u32[]{:S(2)}) %all-to-all-start.1) | async-done | bytes 1441824 | tf_op jit(solution)/shard_map/all_to_all | solution.py:743
  73.2 4.5 all-to-all-start.2
  81.0 8.9 %attention_forward.1 = (bf16[512,512]{1,0:T(8,128)(2,1)}, f32[512,128]{1,0:T(8,128)}) custom-call(s32[5]{0:T(128)} %stack.38.s_ref.c_ref, s32[4,8]{1,0:T(4,128)} %n_ref.3, bf16[512,512]{1,0:T(8,128)(2,1)} %get-tuple-element.219.q_ref, bf16[512,128]{1,0:T(8,128)(2,1)} %get-tuple-element.220.a_ref, bf16[512,128]{1,0:T(8,128)(2,1)} %collective-permute-done.6.b_ref), custom_call_target="tpu_custom_call" | custom-call | flops 1024 | bytes 1024 | tf_op jit(solution)/shard_map/attention_forward/pallas_call | solution.py:240
  89.9 6.7 %all-to-all-done.2.refs_9_ = bf16[4,128,1408]{2,1,0:T(8,128)(2,1)} async-done(((bf16[4,128,1408]{2,1,0:T(8,128)(2,1)}), bf16[4,128,1408]{2,1,0:T(8,128)(2,1)}, u32[]{:S(2)}, u32[]{:S(2)}) %all-to-all-start.2) | async-done | bytes 1441824 | tf_op jit(solution)/shard_map/all_to_all | solution.py:743
  98.4 4.6 out_proj.1
  105.0 7.3 %collective-permute-done.11.refs_6_ = bf16[4,128,1408]{2,1,0:T(8,128)(2,1)} collective-permute-done((bf16[4,128,1408]{2,1,0:T(8,128)(2,1)S(1)}, bf16[4,128,1408]{2,1,0:T(8,128)(2,1)}, u32[]{:S(2)}, u32[]{:S(2)}) %collective-permute-start.11) | collective-permute-done | bytes 1441824 | tf_op jit(solution)/shard_map/ppermute | solution.py:755
  116.8 3.8 all-to-all-start.3
  120.7 19.9 %collective-permute-done.9.refs_2_ = bf16[128,2048]{1,0:T(8,128)(2,1)} collective-permute-done((bf16[128,2048]{1,0:T(8,128)(2,1)}, bf16[128,2048]{1,0:T(8,128)(2,1)}, u32[]{:S(2)}, u32[]{:S(2)}) %collective-permute-start.9) | collective-permute-done | bytes 524320 | tf_op jit(solution)/shard_map/ppermute | solution.py:746
  152.2 10.9 %collective-permute-done.13.refs_1_ = bf16[128,2048]{1,0:T(8,128)(2,1)} collective-permute-done((bf16[128,2048]{1,0:T(8,128)(2,1)}, bf16[128,2048]{1,0:T(8,128)(2,1)}, u32[]{:S(2)}, u32[]{:S(2)}) %collective-permute-start.13) | collective-permute-done | bytes 524320 | tf_op jit(solution)/shard_map/ppermute | solution.py:746
  163.1 11.6 %collective-permute-done.14.refs_2_ = bf16[128,2048]{1,0:T(8,128)(2,1)} collective-permute-done((bf16[128,2048]{1,0:T(8,128)(2,1)}, bf16[128,2048]{1,0:T(8,128)(2,1)}, u32[]{:S(2)}, u32[]{:S(2)}) %collective-permute-start.14) | collective-permute-done | bytes 524320 | tf_op jit(solution)/shard_map/ppermute | solution.py:746
  175.8 26.2 %feed_forward.1 = (bf16[512,1408]{1,0:T(8,128)(2,1)}, bf16[512,1408]{1,0:T(8,128)(2,1)}, bf16[512,1408]{1,0:T(8,128)(2,1)}, bf16[512,2048]{1,0:T(8,128)(2,1)}, b...) custom-call(s32[5]{0:T(128)} %stack.38.s_ref.c_ref, ...), custom_call_target="tpu_custom_call" | custom-call | flops 1024 | bytes 1024 | tf_op jit(solution)/shard_map/feed_forward/pallas_call | solution.py:388
  202.0 8.2 %row_grad.2 = (bf16[4,2816,128]{2,1,0:T(8,128)(2,1)}, bf16[4,2816,128]{2,1,0:T(8,128)(2,1)}) custom-call(s32[5]{0:T(128)} %stack.38.s_ref.c_ref, bf16[512,1408]{1,0:T(8,128)(2,1)} %get-tuple-element.276.l_ref, bf16[512,2048]{1,0:T(8,128)(2,1)} %bitcast.79), custom_call_target="tpu_custom_call" | custom-call | flops 1024 | bytes 1024 | tf_op jit(solution)/shard_map/row_grad/pallas_call | solution.py:569
  213.7 9.5 %weight_grad.3 = (bf16[4,2816,128]{2,1,0:T(8,128)(2,1)}, bf16[4,2816,128]{2,1,0:T(8,128)(2,1)}) custom-call(s32[5]{0:T(128)} %stack.38.s_ref.c_ref, bf16[512,2048]{1,0:T(8,128)(2,1)} %get-tuple-element.247.l_ref, bf16[512,1408]{1,0:T(8,128)(2,1)} %get-tuple-element.251.r_ref), custom_call_target="tpu_custom_call" | custom-call | flops 1024 | bytes 1024 | tf_op jit(solution)/shard_map/weight_grad/pallas_call | solution.py:534
  225.2 11.2 %collective-permute-done.21.refs_2_ = bf16[128,2048]{1,0:T(8,128)(2,1)} collective-permute-done((bf16[128,2048]{1,0:T(8,128)(2,1)}, bf16[128,2048]{1,0:T(8,128)(2,1)}, u32[]{:S(2)}, u32[]{:S(2)}) %collective-permute-start.21) | collective-permute-done | bytes 524320 | tf_op jit(solution)/shard_map/ppermute | solution.py:746
  236.5 5.6 collective-permute-done.25.b_ref
  242.1 4.1 pair_sum.7
  246.2 3.7 all-to-all-start.4
  249.9 4.1 pair_sum.5.refs_0_.refs_2_
  254.0 9.1 %weight_grad.4 = (bf16[4,2816,128]{2,1,0:T(8,128)(2,1)}, bf16[4,2816,128]{2,1,0:T(8,128)(2,1)}) custom-call(s32[5]{0:T(128)} %stack.38.s_ref.c_ref, bf16[512,2048]{1,0:T(8,128)(2,1)} %get-tuple-element.247.l_ref, bf16[512,1408]{1,0:T(8,128)(2,1)} %get-tuple-element.263.r_ref), custom_call_target="tpu_custom_call" | custom-call | flops 1024 | bytes 1024 | tf_op jit(solution)/shard_map/weight_grad/pallas_call | solution.py:534
  266.2 4.4 residual_norm_back.2
  270.6 13.4 %collective-permute-done.23.refs_1_ = bf16[2816,128]{1,0:T(8,128)(2,1)} collective-permute-done((bf16[2816,128]{1,0:T(8,128)(2,1)}, bf16[2816,128]{1,0:T(8,128)(2,1)}, u32[]{:S(2)}, u32[]{:S(2)}) %collective-permute-start.23) | collective-permute-done | bytes 720928 | tf_op jit(solution)/shard_map/ppermute | solution.py:799
  285.7 4.4 all-to-all-start.6
  297.8 7.3 %convolution_convert_fusion.1 = bf16[512,2048]{1,0:T(8,128)(2,1)} fusion(bf16[512,1408]{1,0:T(8,128)(2,1)S(1)} %copy-done.21, bf16[1408,2048]{1,0:T(8,128)(2,1)} %join_cores.1.refs_13_), kind=kOutput, calls=%fused_computation.2 | convolution fusion | flops 2953838592 | bytes 9306112 | tf_op jit(solution)/shard_map/dot_general | solution.py:24
  305.1 4.1 pair_sum.6
  310.4 14.1 %collective-permute-done.27.refs_1_ = bf16[2816,128]{1,0:T(8,128)(2,1)} collective-permute-done((bf16[2816,128]{1,0:T(8,128)(2,1)}, bf16[2816,128]{1,0:T(8,128)(2,1)}, u32[]{:S(2)}, u32[]{:S(2)}) %collective-permute-start.27) | collective-permute-done | bytes 720928 | tf_op jit(solution)/shard_map/ppermute | solution.py:799
  324.5 4.3 all-to-all-start.7
  337.5 3.7 collective-permute-start.31
  342.7 4.9 row_grad.3
  347.6 4.3 convolution_convert_fusion.2.d_ref
  351.9 15.6 %attention_backward.1 = (bf16[512,512]{1,0:T(8,128)(2,1)}, f32[1024,128]{1,0:T(8,128)}) custom-call(s32[5]{0:T(128)} %stack.38.s_ref.c_ref, s32[4,8]{1,0:T(4,128)} %n_ref.3, bf16[512,512]{1,0:T(8,128)(2,1)} %get-tuple-element.219.q_ref, bf16[512,128]{1,0:T(8,128)(2,1)} %get-tuple-element.220.a_ref, bf16[512,128]{1,0:T(8,128)(2,1)} %collective-permute-done.6.b_ref, ...), custom_call_target="tpu_custom_call" | custom-call | flops 1024 | bytes 1024 | tf_op jit(solution)/shard_map/attention_backward/pallas_call | solution.py:315
  394.7 4.5 all-to-all-start.8
  399.1 6.5 %weight_grad.5 = (bf16[4,1280,128]{2,1,0:T(8,128)(2,1)}, bf16[4,1280,128]{2,1,0:T(8,128)(2,1)}) custom-call(s32[5]{0:T(128)} %stack.38.s_ref.c_ref, bf16[512,2048]{1,0:T(8,128)(2,1)} %get-tuple-element.284.l_ref, bf16[512,640]{1,0:T(8,128)(2,1)} %copy-done.16), custom_call_target="tpu_custom_call" | custom-call | flops 1024 | bytes 1024 | tf_op jit(solution)/shard_map/weight_grad/pallas_call | solution.py:534
  408.3 3.4 chain_step.23
  411.8 4.2 collective-permute-start.39
  420.6 12.4 %collective-permute-done.39.refs_7_.refs_1_ = bf16[2816,128]{1,0:T(8,128)(2,1)S(1)} collective-permute-done((bf16[2816,128]{1,0:T(8,128)(2,1)}, bf16[2816,128]{1,0:T(8,128)(2,1)S(1)}, u32[]{:S(2)}, u32[]{:S(2)}) %collective-permute-start.39) | collective-permute-done | bytes 720928 | tf_op jit(solution)/shard_map/ppermute | solution.py:799
  433.9 4.2 all-to-all-start.9
  438.1 3.4 chain_step.24
  445.8 8.8 %all-to-all-done.9 = bf16[4,1280,128]{2,1,0:T(8,128)(2,1)S(1)} async-done(((bf16[4,1280,128]{2,1,0:T(8,128)(2,1)}), bf16[4,1280,128]{2,1,0:T(8,128)(2,1)S(1)}, u32[]{:S(2)}, u32[]{:S(2)}) %all-to-all-start.9) | async-done | bytes 1310752 | tf_op jit(solution)/shard_map/all_to_all | solution.py:743
  455.6 3.6 all-to-all-start.5
  459.3 3.4 chain_step.25
  466.9 4.0 residual_norm_back.3
  470.9 3.4 chain_step.26
  481.8 6.6 %beside.5 = f32[704,2048]{1,0:T(8,128)} custom-call(s32[5]{0:T(128)} %stack.38.s_ref.c_ref, f32[704,1]{1,0:T(8,128)} %broadcast_in_dim.39.s_ref, bf16[2816,128]{1,0:T(8,128)(2,1)} %get-tuple-element.307.refs_0_, bf16[2816,128]{1,0:T(8,128)(2,1)} %collective-permute-done.31.refs_1_, bf16[2816,128]{1,0:T(8,128)(2,1)} %get-tuple-element.316.refs_2_, ...), custom_call_target="tpu_custom_call" | custom-call | flops 1024 | bytes 1024 | tf_op jit(solution)/shard_map/beside/pallas_call | solution.py:677
  488.4 3.4 chain_step.27
  508.0 3.5 chain_step.29
  514.9 6.6 %beside.6 = f32[256,5632]{1,0:T(8,128)} custom-call(s32[5]{0:T(128)} %stack.38.s_ref.c_ref, f32[256,1]{1,0:T(8,128)} %copy.26.n_ref.s_ref, bf16[2816,128]{1,0:T(8,128)(2,1)} %get-tuple-element.340.refs_0_, bf16[2816,128]{1,0:T(8,128)(2,1)} %collective-permute-done.41.refs_1_, bf16[2816,128]{1,0:T(8,128)(2,1)} %get-tuple-element.351.refs_2_, ...), custom_call_target="tpu_custom_call" | custom-call | flops 1024 | bytes 1024 | tf_op jit(solution)/shard_map/beside/pallas_call | solution.py:677
  522.3 5.2 collective-permute-done.56.refs_1_
  530.8 3.8 collective-permute-start.63
  544.4 7.5 %collective-permute-done.63.refs_1_.refs_5_ = bf16[2816,128]{1,0:T(8,128)(2,1)} collective-permute-done((bf16[2816,128]{1,0:T(8,128)(2,1)}, bf16[2816,128]{1,0:T(8,128)(2,1)}, u32[]{:S(2)}, u32[]{:S(2)}) %collective-permute-start.63) | collective-permute-done | bytes 720928 | tf_op jit(solution)/shard_map/ppermute | solution.py:799
  559.1 8.3 %collective-permute-done.54.refs_1_.refs_3_ = bf16[2816,128]{1,0:T(8,128)(2,1)} collective-permute-done((bf16[2816,128]{1,0:T(8,128)(2,1)}, bf16[2816,128]{1,0:T(8,128)(2,1)}, u32[]{:S(2)}, u32[]{:S(2)}) %collective-permute-start.54) | collective-permute-done | bytes 720928 | tf_op jit(solution)/shard_map/ppermute | solution.py:799
  575.0 6.4 %collective-permute-done.65 = bf16[2560,128]{1,0:T(8,128)(2,1)S(1)} collective-permute-done((bf16[2560,128]{1,0:T(8,128)(2,1)}, bf16[2560,128]{1,0:T(8,128)(2,1)S(1)}, u32[]{:S(2)}, u32[]{:S(2)}) %collective-permute-start.65) | collective-permute-done | bytes 655392 | tf_op jit(solution)/shard_map/ppermute | solution.py:799
  586.5 10.3 %collective-permute-done.58.refs_1_.refs_7_ = bf16[2816,128]{1,0:T(8,128)(2,1)S(1)} collective-permute-done((bf16[2816,128]{1,0:T(8,128)(2,1)}, bf16[2816,128]{1,0:T(8,128)(2,1)S(1)}, u32[]{:S(2)}, u32[]{:S(2)}) %collective-permute-start.58) | collective-permute-done | bytes 720928 | tf_op jit(solution)/shard_map/ppermute | solution.py:799
  603.7 6.6 %beside.9 = f32[256,5632]{1,0:T(8,128)} custom-call(s32[5]{0:T(128)} %stack.38.s_ref.c_ref, f32[256,1]{1,0:T(8,128)} %copy.26.n_ref.s_ref, bf16[2816,128]{1,0:T(8,128)(2,1)} %get-tuple-element.378.refs_0_, bf16[2816,128]{1,0:T(8,128)(2,1)} %collective-permute-done.56.refs_1_, bf16[2816,128]{1,0:T(8,128)(2,1)} %get-tuple-element.371.refs_2_, ...), custom_call_target="tpu_custom_call" | custom-call | flops 1024 | bytes 1024 | tf_op jit(solution)/shard_map/beside/pallas_call | solution.py:677
  611.2 6.8 %collective-permute-done.60 = bf16[2560,128]{1,0:T(8,128)(2,1)S(1)} collective-permute-done((bf16[2560,128]{1,0:T(8,128)(2,1)}, bf16[2560,128]{1,0:T(8,128)(2,1)S(1)}, u32[]{:S(2)}, u32[]{:S(2)}) %collective-permute-start.60) | collective-permute-done | bytes 655392 | tf_op jit(solution)/shard_map/ppermute | solution.py:799
  623.0 4.5 beside.7
  633.7 3.7 beside.8
  (278 shorter events, 187.3 us)
Async XLA Ops:
  0.6 28.6 %collective-permute-start.4 = (bf16[704,2048]{1,0:T(8,128)(2,1)}, bf16[704,2048]{1,0:T(8,128)(2,1)}, u32[]{:S(2)}, u32[]{:S(2)}) collective-permute-start(bf16[704,2048]{1,0:T(8,128)(2,1)} %a_ref.3), channel_id=1, source_target_pairs={{0,1},{1,0},{2,3},{3,2},{4,5},{5,4},{6,7},{7,6},{8,9},{9,8},{10,11... | collective-permute-start | bytes 8650760 | tf_op jit(solution)/shard_map/ppermute | solution.py:752
  6.7 22.5 %all-to-all-start = ((bf16[4,256,640]{2,1,0:T(8,128)(2,1)}), bf16[4,256,640]{2,1,0:T(8,128)(2,1)S(1)}, u32[]{:S(2)}, u32[]{:S(2)}) async-start(bf16[4,256,640]{2,1,0:T(8,128)(2,1)} %pick_qkv.1), calls=%async_computation | async-start | bytes 2621440 | tf_op jit(solution)/shard_map/all_to_all | solution.py:743
  11.4 40.6 %collective-permute-start.3 = (bf16[256,2048]{1,0:T(8,128)(2,1)S(1)}, bf16[256,2048]{1,0:T(8,128)(2,1)}, u32[]{:S(2)}, u32[]{:S(2)}) collective-permute-start(bf16[256,2048]{1,0:T(8,128)(2,1)S(1)} %copy-done.24), channel_id=1, source_target_pairs={{0,1},{1,0},{2,3},{3,2},{4,5},{5,4},{6,7},{7,6},{8,9},{9,8},{10,11... | collective-permute-start | bytes 3145736 | tf_op jit(solution)/shard_map/ppermute | solution.py:752
  11.6 30.4 %collective-permute-start = (bf16[128,2048]{1,0:T(8,128)(2,1)S(1)}, bf16[128,2048]{1,0:T(8,128)(2,1)S(1)}, u32[]{:S(2)}, u32[]{:S(2)}) collective-permute-start(bf16[128,2048]{1,0:T(8,128)(2,1)S(1)} %copy-done.7), channel_id=1, source_target_pairs={{0,2},{1,3},{2,0},{3,1},{4,6},{5,7},{6,4},{7,5},{8,10},{9,11},{10,... | collective-permute-start | bytes 1572872 | tf_op jit(solution)/shard_map/ppermute | solution.py:746
  13.5 28.5 %collective-permute-start.1 = (bf16[128,2048]{1,0:T(8,128)(2,1)S(1)}, bf16[128,2048]{1,0:T(8,128)(2,1)}, u32[]{:S(2)}, u32[]{:S(2)}) collective-permute-start(bf16[128,2048]{1,0:T(8,128)(2,1)S(1)} %copy-done.7), channel_id=1, source_target_pairs={{0,4},{1,5},{2,6},{3,7},{4,0},{5,1},{6,2},{7,3},{8,12},{9,13},{10,... | collective-permute-start | bytes 1572872 | tf_op jit(solution)/shard_map/ppermute | solution.py:746
  15.0 37.0 %collective-permute-start.2 = (bf16[128,2048]{1,0:T(8,128)(2,1)S(1)}, bf16[128,2048]{1,0:T(8,128)(2,1)}, u32[]{:S(2)}, u32[]{:S(2)}) collective-permute-start(bf16[128,2048]{1,0:T(8,128)(2,1)S(1)} %copy-done.7), channel_id=1, source_target_pairs={{0,6},{1,7},{2,4},{3,5},{4,2},{5,3},{6,0},{7,1},{8,14},{9,15},{10,... | collective-permute-start | bytes 1572872 | tf_op jit(solution)/shard_map/ppermute | solution.py:746
  29.2 26.3 %collective-permute-start.5 = (bf16[4,256,640]{2,1,0:T(8,128)(2,1)S(1)}, bf16[4,256,640]{2,1,0:T(8,128)(2,1)}, u32[]{:S(2)}, u32[]{:S(2)}) collective-permute-start(bf16[4,256,640]{2,1,0:T(8,128)(2,1)S(1)} %all-to-all-done.n_ref), channel_id=1, source_target_pairs={{0,1},{1,0},{2,3},{3,2},{4,5},{5,4},{6,7},{7,6},{8,9},{9,8},{10,11... | collective-permute-start | bytes 3932168 | tf_op jit(solution)/shard_map/ppermute | solution.py:752
  52.0 21.2 %all-to-all-start.1 = ((bf16[4,128,1408]{2,1,0:T(8,128)(2,1)}), bf16[4,128,1408]{2,1,0:T(8,128)(2,1)S(1)}, u32[]{:S(2)}, u32[]{:S(2)}) async-start(bf16[4,128,1408]{2,1,0:T(8,128)(2,1)} %get-tuple-element.217), calls=%async_computation.1 | async-start | bytes 2883584 | tf_op jit(solution)/shard_map/all_to_all | solution.py:743
  73.2 23.4 %collective-permute-start.7 = (bf16[4,128,1408]{2,1,0:T(8,128)(2,1)S(1)}, bf16[4,128,1408]{2,1,0:T(8,128)(2,1)S(1)}, u32[]{:S(2)}, u32[]{:S(2)}) collective-permute-start(bf16[4,128,1408]{2,1,0:T(8,128)(2,1)S(1)} %all-to-all-done.1.refs_5_), channel_id=1, source_target_pairs={{0,1},{1,0},{2,3},{3,2},{4,5},{5,4},{6,7},{7,6},{8,9},{9,8},{10,11... | collective-permute-start | bytes 4325384 | tf_op jit(solution)/shard_map/ppermute | solution.py:752
  73.2 23.3 %all-to-all-start.2 = ((bf16[4,128,1408]{2,1,0:T(8,128)(2,1)}), bf16[4,128,1408]{2,1,0:T(8,128)(2,1)}, u32[]{:S(2)}, u32[]{:S(2)}) async-start(bf16[4,128,1408]{2,1,0:T(8,128)(2,1)} %get-tuple-element.222), calls=%async_computation.2 | async-start | bytes 2883584 | tf_op jit(solution)/shard_map/all_to_all | solution.py:743
  77.7 34.6 %collective-permute-start.11 = (bf16[4,128,1408]{2,1,0:T(8,128)(2,1)S(1)}, bf16[4,128,1408]{2,1,0:T(8,128)(2,1)}, u32[]{:S(2)}, u32[]{:S(2)}) collective-permute-start(bf16[4,128,1408]{2,1,0:T(8,128)(2,1)S(1)} %all-to-all-done.1.refs_5_), channel_id=1, source_target_pairs={{0,8},{8,0},{16,24},{24,16},{1,9},{9,1},{17,25},{25,17},{2,10},{10... | collective-permute-start | bytes 4325384 | tf_op jit(solution)/shard_map/ppermute | solution.py:755
  96.6 44.8 %collective-permute-start.12 = (bf16[4,128,1408]{2,1,0:T(8,128)(2,1)}, bf16[4,128,1408]{2,1,0:T(8,128)(2,1)}, u32[]{:S(2)}, u32[]{:S(2)}) collective-permute-start(bf16[4,128,1408]{2,1,0:T(8,128)(2,1)} %all-to-all-done.2.refs_9_), channel_id=1, source_target_pairs={{0,1},{1,0},{2,3},{3,2},{4,5},{5,4},{6,7},{7,6},{8,9},{9,8},{10,11... | collective-permute-start | bytes 4325384 | tf_op jit(solution)/shard_map/ppermute | solution.py:752
  96.6 46.2 %collective-permute-start.17 = (bf16[4,128,1408]{2,1,0:T(8,128)(2,1)}, bf16[4,128,1408]{2,1,0:T(8,128)(2,1)}, u32[]{:S(2)}, u32[]{:S(2)}) collective-permute-start(bf16[4,128,1408]{2,1,0:T(8,128)(2,1)} %all-to-all-done.2.refs_9_), channel_id=1, source_target_pairs={{0,8},{8,0},{16,24},{24,16},{1,9},{9,1},{17,25},{25,17},{2,10},{10... | collective-permute-start | bytes 4325384 | tf_op jit(solution)/shard_map/ppermute | solution.py:755
  103.0 17.7 %collective-permute-start.8 = (bf16[128,2048]{1,0:T(8,128)(2,1)}, bf16[128,2048]{1,0:T(8,128)(2,1)}, u32[]{:S(2)}, u32[]{:S(2)}) collective-permute-start(bf16[128,2048]{1,0:T(8,128)(2,1)} %get-tuple-element.232), channel_id=1, source_target_pairs={{0,2},{1,3},{2,0},{3,1},{4,6},{5,7},{6,4},{7,5},{8,10},{9,11},{10,... | collective-permute-start | bytes 1572872 | tf_op jit(solution)/shard_map/ppermute | solution.py:746
  104.4 36.1 %collective-permute-start.9 = (bf16[128,2048]{1,0:T(8,128)(2,1)}, bf16[128,2048]{1,0:T(8,128)(2,1)}, u32[]{:S(2)}, u32[]{:S(2)}) collective-permute-start(bf16[128,2048]{1,0:T(8,128)(2,1)} %get-tuple-element.233), channel_id=1, source_target_pairs={{0,4},{1,5},{2,6},{3,7},{4,0},{5,1},{6,2},{7,3},{8,12},{9,13},{10,... | collective-permute-start | bytes 1572872 | tf_op jit(solution)/shard_map/ppermute | solution.py:746
  112.3 28.3 %collective-permute-start.10 = (bf16[128,2048]{1,0:T(8,128)(2,1)}, bf16[128,2048]{1,0:T(8,128)(2,1)S(1)}, u32[]{:S(2)}, u32[]{:S(2)}) collective-permute-start(bf16[128,2048]{1,0:T(8,128)(2,1)} %get-tuple-element.234), channel_id=1, source_target_pairs={{0,6},{1,7},{2,4},{3,5},{4,2},{5,3},{6,0},{7,1},{8,14},{9,15},{10,... | collective-permute-start | bytes 1572872 | tf_op jit(solution)/shard_map/ppermute | solution.py:746
  116.8 35.4 %all-to-all-start.3 = ((bf16[4,128,2048]{2,1,0:T(8,128)(2,1)}), bf16[4,128,2048]{2,1,0:T(8,128)(2,1)S(1)}, u32[]{:S(2)}, u32[]{:S(2)}) async-start(bf16[4,128,2048]{2,1,0:T(8,128)(2,1)} %broadcast_in_dim.38), calls=%async_computation.3 | async-start | bytes 4194304 | tf_op jit(solution)/shard_map/all_to_all | solution.py:743
  141.3 33.3 %collective-permute-start.16 = (bf16[4,128,1408]{2,1,0:T(8,128)(2,1)}, bf16[4,128,1408]{2,1,0:T(8,128)(2,1)S(1)}, u32[]{:S(2)}, u32[]{:S(2)}) collective-permute-start(bf16[4,128,1408]{2,1,0:T(8,128)(2,1)} %collective-permute-done.11.refs_6_), channel_id=1, source_target_pairs={{0,1},{1,0},{2,3},{3,2},{4,5},{5,4},{6,7},{7,6},{8,9},{9,8},{10,11... | collective-permute-start | bytes 4325384 | tf_op jit(solution)/shard_map/ppermute | solution.py:752
  142.8 31.9 %collective-permute-start.18 = (bf16[4,128,1408]{2,1,0:T(8,128)(2,1)}, bf16[4,128,1408]{2,1,0:T(8,128)(2,1)}, u32[]{:S(2)}, u32[]{:S(2)}) collective-permute-start(bf16[4,128,1408]{2,1,0:T(8,128)(2,1)} %collective-permute-done.17.refs_10_), channel_id=1, source_target_pairs={{0,1},{1,0},{2,3},{3,2},{4,5},{5,4},{6,7},{7,6},{8,9},{9,8},{10,11... | collective-permute-start | bytes 4325384 | tf_op jit(solution)/shard_map/ppermute | solution.py:752
  146.0 17.1 %collective-permute-start.13 = (bf16[128,2048]{1,0:T(8,128)(2,1)}, bf16[128,2048]{1,0:T(8,128)(2,1)}, u32[]{:S(2)}, u32[]{:S(2)}) collective-permute-start(bf16[128,2048]{1,0:T(8,128)(2,1)} %get-tuple-element.241.refs_0_), channel_id=1, source_target_pairs={{0,2},{1,3},{2,0},{3,1},{4,6},{5,7},{6,4},{7,5},{8,10},{9,11},{10,... | collective-permute-start | bytes 1572872 | tf_op jit(solution)/shard_map/ppermute | solution.py:746
  147.7 27.0 %collective-permute-start.14 = (bf16[128,2048]{1,0:T(8,128)(2,1)}, bf16[128,2048]{1,0:T(8,128)(2,1)}, u32[]{:S(2)}, u32[]{:S(2)}) collective-permute-start(bf16[128,2048]{1,0:T(8,128)(2,1)} %get-tuple-element.241.refs_0_), channel_id=1, source_target_pairs={{0,4},{1,5},{2,6},{3,7},{4,0},{5,1},{6,2},{7,3},{8,12},{9,13},{10,... | collective-permute-start | bytes 1572872 | tf_op jit(solution)/shard_map/ppermute | solution.py:746
  149.1 25.5 %collective-permute-start.15 = (bf16[128,2048]{1,0:T(8,128)(2,1)}, bf16[128,2048]{1,0:T(8,128)(2,1)}, u32[]{:S(2)}, u32[]{:S(2)}) collective-permute-start(bf16[128,2048]{1,0:T(8,128)(2,1)} %get-tuple-element.241.refs_0_), channel_id=1, source_target_pairs={{0,6},{1,7},{2,4},{3,5},{4,2},{5,3},{6,0},{7,1},{8,14},{9,15},{10,... | collective-permute-start | bytes 1572872 | tf_op jit(solution)/shard_map/ppermute | solution.py:746
  210.2 26.2 %collective-permute-start.19 = (bf16[4,2816,128]{2,1,0:T(8,128)(2,1)}, bf16[4,2816,128]{2,1,0:T(8,128)(2,1)S(1)}, u32[]{:S(2)}, u32[]{:S(2)}) collective-permute-start(bf16[4,2816,128]{2,1,0:T(8,128)(2,1)} %get-tuple-element.254), channel_id=1, source_target_pairs={{0,1},{1,0},{2,3},{3,2},{4,5},{5,4},{6,7},{7,6},{8,9},{9,8},{10,11... | collective-permute-start | bytes 8650760 | tf_op jit(solution)/shard_map/ppermute | solution.py:752
  210.8 25.6 %collective-permute-start.21 = (bf16[128,2048]{1,0:T(8,128)(2,1)}, bf16[128,2048]{1,0:T(8,128)(2,1)}, u32[]{:S(2)}, u32[]{:S(2)}) collective-permute-start(bf16[128,2048]{1,0:T(8,128)(2,1)} %get-tuple-element.258), channel_id=1, source_target_pairs={{0,4},{1,5},{2,6},{3,7},{4,0},{5,1},{6,2},{7,3},{8,12},{9,13},{10,... | collective-permute-start | bytes 1572872 | tf_op jit(solution)/shard_map/ppermute | solution.py:746
  212.3 24.1 %collective-permute-start.22 = (bf16[128,2048]{1,0:T(8,128)(2,1)}, bf16[128,2048]{1,0:T(8,128)(2,1)}, u32[]{:S(2)}, u32[]{:S(2)}) collective-permute-start(bf16[128,2048]{1,0:T(8,128)(2,1)} %get-tuple-element.259), channel_id=1, source_target_pairs={{0,6},{1,7},{2,4},{3,5},{4,2},{5,3},{6,0},{7,1},{8,14},{9,15},{10,... | collective-permute-start | bytes 1572872 | tf_op jit(solution)/shard_map/ppermute | solution.py:746
  246.2 37.8 %all-to-all-start.4 = ((bf16[4,2816,128]{2,1,0:T(8,128)(2,1)}), bf16[4,2816,128]{2,1,0:T(8,128)(2,1)S(1)}, u32[]{:S(2)}, u32[]{:S(2)}) async-start(bf16[4,2816,128]{2,1,0:T(8,128)(2,1)} %pair_sum.7), calls=%async_computation.4 | async-start | bytes 5767168 | tf_op jit(solution)/shard_map/all_to_all | solution.py:743
  263.1 41.9 %collective-permute-start.24 = (bf16[4,2816,128]{2,1,0:T(8,128)(2,1)}, bf16[4,2816,128]{2,1,0:T(8,128)(2,1)}, u32[]{:S(2)}, u32[]{:S(2)}) collective-permute-start(bf16[4,2816,128]{2,1,0:T(8,128)(2,1)} %get-tuple-element.278), channel_id=1, source_target_pairs={{0,1},{1,0},{2,3},{3,2},{4,5},{5,4},{6,7},{7,6},{8,9},{9,8},{10,11... | collective-permute-start | bytes 8650760 | tf_op jit(solution)/shard_map/ppermute | solution.py:752
  265.3 18.7 %collective-permute-start.23 = (bf16[2816,128]{1,0:T(8,128)(2,1)}, bf16[2816,128]{1,0:T(8,128)(2,1)}, u32[]{:S(2)}, u32[]{:S(2)}) collective-permute-start(bf16[2816,128]{1,0:T(8,128)(2,1)} %slice_bitcast_fusion.1), channel_id=1, source_target_pairs={{0,8},{8,0},{16,24},{24,16},{1,9},{9,1},{17,25},{25,17},{2,10},{10... | collective-permute-start | bytes 2162696 | tf_op jit(solution)/shard_map/ppermute | solution.py:799
  285.7 38.9 %all-to-all-start.6 = ((bf16[4,128,2048]{2,1,0:T(8,128)(2,1)}), bf16[4,128,2048]{2,1,0:T(8,128)(2,1)}, u32[]{:S(2)}, u32[]{:S(2)}) async-start(bf16[4,128,2048]{2,1,0:T(8,128)(2,1)} %bitcast.82), calls=%async_computation.6 | async-start | bytes 4194304 | tf_op jit(solution)/shard_map/all_to_all | solution.py:743
  291.3 19.1 %collective-permute-start.26 = (bf16[2816,128]{1,0:T(8,128)(2,1)S(1)}, bf16[2816,128]{1,0:T(8,128)(2,1)S(1)}, u32[]{:S(2)}, u32[]{:S(2)}) collective-permute-start(bf16[2816,128]{1,0:T(8,128)(2,1)S(1)} %slice_bitcast_fusion), channel_id=1, source_target_pairs={{0,8},{8,0},{16,24},{24,16},{1,9},{9,1},{17,25},{25,17},{2,10},{10... | collective-permute-start | bytes 2162696 | tf_op jit(solution)/shard_map/ppermute | solution.py:799
  295.2 29.3 %collective-permute-start.27 = (bf16[2816,128]{1,0:T(8,128)(2,1)}, bf16[2816,128]{1,0:T(8,128)(2,1)}, u32[]{:S(2)}, u32[]{:S(2)}) collective-permute-start(bf16[2816,128]{1,0:T(8,128)(2,1)} %get-tuple-element.290), channel_id=1, source_target_pairs={{0,8},{8,0},{16,24},{24,16},{1,9},{9,1},{17,25},{25,17},{2,10},{10... | collective-permute-start | bytes 2162696 | tf_op jit(solution)/shard_map/ppermute | solution.py:799
  296.3 28.2 %collective-permute-start.28 = (bf16[2816,128]{1,0:T(8,128)(2,1)}, bf16[2816,128]{1,0:T(8,128)(2,1)}, u32[]{:S(2)}, u32[]{:S(2)}) collective-permute-start(bf16[2816,128]{1,0:T(8,128)(2,1)} %get-tuple-element.291.refs_2_), channel_id=1, source_target_pairs={{8,16},{16,8},{9,17},{17,9},{10,18},{18,10},{11,19},{19,11},{12,20... | collective-permute-start | bytes 2162696 | tf_op jit(solution)/shard_map/ppermute | solution.py:801
  324.5 68.5 %all-to-all-start.7 = ((bf16[4,2816,128]{2,1,0:T(8,128)(2,1)}), bf16[4,2816,128]{2,1,0:T(8,128)(2,1)S(1)}, u32[]{:S(2)}, u32[]{:S(2)}) async-start(bf16[4,2816,128]{2,1,0:T(8,128)(2,1)} %pair_sum.6), calls=%async_computation.7 | async-start | bytes 5767168 | tf_op jit(solution)/shard_map/all_to_all | solution.py:743
  331.7 20.2 %collective-permute-start.29 = (bf16[2816,128]{1,0:T(8,128)(2,1)}, bf16[2816,128]{1,0:T(8,128)(2,1)}, u32[]{:S(2)}, u32[]{:S(2)}) collective-permute-start(bf16[2816,128]{1,0:T(8,128)(2,1)} %get-tuple-element.299), channel_id=1, source_target_pairs={{0,8},{8,0},{16,24},{24,16},{1,9},{9,1},{17,25},{25,17},{2,10},{10... | collective-permute-start | bytes 2162696 | tf_op jit(solution)/shard_map/ppermute | solution.py:799
  332.6 19.4 %collective-permute-start.30 = (bf16[2816,128]{1,0:T(8,128)(2,1)}, bf16[2816,128]{1,0:T(8,128)(2,1)}, u32[]{:S(2)}, u32[]{:S(2)}) collective-permute-start(bf16[2816,128]{1,0:T(8,128)(2,1)} %get-tuple-element.300.refs_2_), channel_id=1, source_target_pairs={{8,16},{16,8},{9,17},{17,9},{10,18},{18,10},{11,19},{19,11},{12,20... | collective-permute-start | bytes 2162696 | tf_op jit(solution)/shard_map/ppermute | solution.py:801
  337.5 30.0 %collective-permute-start.31 = (bf16[2816,128]{1,0:T(8,128)(2,1)}, bf16[2816,128]{1,0:T(8,128)(2,1)}, u32[]{:S(2)}, u32[]{:S(2)}) collective-permute-start(bf16[2816,128]{1,0:T(8,128)(2,1)} %get-tuple-element.307.refs_0_), channel_id=1, source_target_pairs={{0,8},{8,0},{16,24},{24,16},{1,9},{9,1},{17,25},{25,17},{2,10},{10... | collective-permute-start | bytes 2162696 | tf_op jit(solution)/shard_map/ppermute | solution.py:799
  341.2 26.3 %collective-permute-start.32 = (bf16[2816,128]{1,0:T(8,128)(2,1)}, bf16[2816,128]{1,0:T(8,128)(2,1)}, u32[]{:S(2)}, u32[]{:S(2)}) collective-permute-start(bf16[2816,128]{1,0:T(8,128)(2,1)} %get-tuple-element.308.refs_2_), channel_id=1, source_target_pairs={{8,16},{16,8},{9,17},{17,9},{10,18},{18,10},{11,19},{19,11},{12,20... | collective-permute-start | bytes 2162696 | tf_op jit(solution)/shard_map/ppermute | solution.py:801
  372.5 20.5 %collective-permute-start.34 = (bf16[2816,128]{1,0:T(8,128)(2,1)}, bf16[2816,128]{1,0:T(8,128)(2,1)}, u32[]{:S(2)}, u32[]{:S(2)}) collective-permute-start(bf16[2816,128]{1,0:T(8,128)(2,1)} %get-tuple-element.316.refs_2_), channel_id=1, source_target_pairs={{0,8},{8,0},{16,24},{24,16},{1,9},{9,1},{17,25},{25,17},{2,10},{10... | collective-permute-start | bytes 2162696 | tf_op jit(solution)/shard_map/ppermute | solution.py:799
  375.8 17.3 %collective-permute-start.35 = (bf16[2816,128]{1,0:T(8,128)(2,1)}, bf16[2816,128]{1,0:T(8,128)(2,1)}, u32[]{:S(2)}, u32[]{:S(2)}) collective-permute-start(bf16[2816,128]{1,0:T(8,128)(2,1)} %get-tuple-element.317.refs_2_), channel_id=1, source_target_pairs={{8,16},{16,8},{9,17},{17,9},{10,18},{18,10},{11,19},{19,11},{12,20... | collective-permute-start | bytes 2162696 | tf_op jit(solution)/shard_map/ppermute | solution.py:801
  380.8 27.5 %collective-permute-start.36 = (bf16[2816,128]{1,0:T(8,128)(2,1)}, bf16[2816,128]{1,0:T(8,128)(2,1)}, u32[]{:S(2)}, u32[]{:S(2)}) collective-permute-start(bf16[2816,128]{1,0:T(8,128)(2,1)} %get-tuple-element.324.refs_4_), channel_id=1, source_target_pairs={{0,8},{8,0},{16,24},{24,16},{1,9},{9,1},{17,25},{25,17},{2,10},{10... | collective-permute-start | bytes 2162696 | tf_op jit(solution)/shard_map/ppermute | solution.py:799
  383.4 25.0 %collective-permute-start.37 = (bf16[2816,128]{1,0:T(8,128)(2,1)}, bf16[2816,128]{1,0:T(8,128)(2,1)}, u32[]{:S(2)}, u32[]{:S(2)}) collective-permute-start(bf16[2816,128]{1,0:T(8,128)(2,1)} %get-tuple-element.325.refs_2_), channel_id=1, source_target_pairs={{8,16},{16,8},{9,17},{17,9},{10,18},{18,10},{11,19},{19,11},{12,20... | collective-permute-start | bytes 2162696 | tf_op jit(solution)/shard_map/ppermute | solution.py:801
  394.7 38.3 %all-to-all-start.8 = ((bf16[4,128,2048]{2,1,0:T(8,128)(2,1)}), bf16[4,128,2048]{2,1,0:T(8,128)(2,1)}, u32[]{:S(2)}, u32[]{:S(2)}) async-start(bf16[4,128,2048]{2,1,0:T(8,128)(2,1)} %bitcast.81), calls=%async_computation.8 | async-start | bytes 4194304 | tf_op jit(solution)/shard_map/all_to_all | solution.py:743
  411.8 21.2 %collective-permute-start.39 = (bf16[2816,128]{1,0:T(8,128)(2,1)}, bf16[2816,128]{1,0:T(8,128)(2,1)S(1)}, u32[]{:S(2)}, u32[]{:S(2)}) collective-permute-start(bf16[2816,128]{1,0:T(8,128)(2,1)} %get-tuple-element.333.refs_6_), channel_id=1, source_target_pairs={{0,8},{8,0},{16,24},{24,16},{1,9},{9,1},{17,25},{25,17},{2,10},{10... | collective-permute-start | bytes 2162696 | tf_op jit(solution)/shard_map/ppermute | solution.py:799
  415.9 17.0 %collective-permute-start.40 = (bf16[2816,128]{1,0:T(8,128)(2,1)}, bf16[2816,128]{1,0:T(8,128)(2,1)S(1)}, u32[]{:S(2)}, u32[]{:S(2)}) collective-permute-start(bf16[2816,128]{1,0:T(8,128)(2,1)} %get-tuple-element.334.refs_2_), channel_id=1, source_target_pairs={{8,16},{16,8},{9,17},{17,9},{10,18},{18,10},{11,19},{19,11},{12,20... | collective-permute-start | bytes 2162696 | tf_op jit(solution)/shard_map/ppermute | solution.py:801
  433.9 20.7 %all-to-all-start.9 = ((bf16[4,1280,128]{2,1,0:T(8,128)(2,1)}), bf16[4,1280,128]{2,1,0:T(8,128)(2,1)S(1)}, u32[]{:S(2)}, u32[]{:S(2)}) async-start(bf16[4,1280,128]{2,1,0:T(8,128)(2,1)} %pair_sum.8), calls=%async_computation.9 | async-start | bytes 2621440 | tf_op jit(solution)/shard_map/all_to_all | solution.py:743
  441.4 29.4 %collective-permute-start.41 = (bf16[2816,128]{1,0:T(8,128)(2,1)}, bf16[2816,128]{1,0:T(8,128)(2,1)}, u32[]{:S(2)}, u32[]{:S(2)}) collective-permute-start(bf16[2816,128]{1,0:T(8,128)(2,1)} %get-tuple-element.340.refs_0_), channel_id=1, source_target_pairs={{0,8},{8,0},{16,24},{24,16},{1,9},{9,1},{17,25},{25,17},{2,10},{10... | collective-permute-start | bytes 2162696 | tf_op jit(solution)/shard_map/ppermute | solution.py:799
  444.3 26.6 %collective-permute-start.42 = (bf16[2816,128]{1,0:T(8,128)(2,1)}, bf16[2816,128]{1,0:T(8,128)(2,1)}, u32[]{:S(2)}, u32[]{:S(2)}) collective-permute-start(bf16[2816,128]{1,0:T(8,128)(2,1)} %get-tuple-element.341.refs_2_), channel_id=1, source_target_pairs={{8,16},{16,8},{9,17},{17,9},{10,18},{18,10},{11,19},{19,11},{12,20... | collective-permute-start | bytes 2162696 | tf_op jit(solution)/shard_map/ppermute | solution.py:801
  445.8 32.4 %collective-permute-start.44 = (bf16[2,2048,128]{2,1,0:T(8,128)(2,1)}, bf16[2,2048,128]{2,1,0:T(8,128)(2,1)}, u32[]{:S(2)}, u32[]{:S(2)}) collective-permute-start(bf16[2,2048,128]{2,1,0:T(8,128)(2,1)} %get-tuple-element.348), channel_id=1, source_target_pairs={{0,1},{1,0},{2,3},{3,2},{4,5},{5,4},{6,7},{7,6},{8,9},{9,8},{10,11... | collective-permute-start | bytes 3145736 | tf_op jit(solution)/shard_map/ppermute | solution.py:752
  455.6 59.2 %all-to-all-start.5 = ((bf16[4,128,2048]{2,1,0:T(8,128)(2,1)}), bf16[4,128,2048]{2,1,0:T(8,128)(2,1)S(1)}, u32[]{:S(2)}, u32[]{:S(2)}) async-start(bf16[4,128,2048]{2,1,0:T(8,128)(2,1)} %bitcast.80), calls=%async_computation.5 | async-start | bytes 4194304 | tf_op jit(solution)/shard_map/all_to_all | solution.py:743
  462.7 25.7 %collective-permute-start.45 = (bf16[2816,128]{1,0:T(8,128)(2,1)}, bf16[2816,128]{1,0:T(8,128)(2,1)}, u32[]{:S(2)}, u32[]{:S(2)}) collective-permute-start(bf16[2816,128]{1,0:T(8,128)(2,1)} %get-tuple-element.351.refs_2_), channel_id=1, source_target_pairs={{0,8},{8,0},{16,24},{24,16},{1,9},{9,1},{17,25},{25,17},{2,10},{10... | collective-permute-start | bytes 2162696 | tf_op jit(solution)/shard_map/ppermute | solution.py:799
  465.3 23.0 %collective-permute-start.46 = (bf16[2816,128]{1,0:T(8,128)(2,1)}, bf16[2816,128]{1,0:T(8,128)(2,1)}, u32[]{:S(2)}, u32[]{:S(2)}) collective-permute-start(bf16[2816,128]{1,0:T(8,128)(2,1)} %get-tuple-element.352.refs_2_), channel_id=1, source_target_pairs={{8,16},{16,8},{9,17},{17,9},{10,18},{18,10},{11,19},{19,11},{12,20... | collective-permute-start | bytes 2162696 | tf_op jit(solution)/shard_map/ppermute | solution.py:801
  474.3 32.8 %collective-permute-start.50 = (bf16[2816,128]{1,0:T(8,128)(2,1)}, bf16[2816,128]{1,0:T(8,128)(2,1)S(1)}, u32[]{:S(2)}, u32[]{:S(2)}) collective-permute-start(bf16[2816,128]{1,0:T(8,128)(2,1)} %get-tuple-element.357.refs_4_), channel_id=1, source_target_pairs={{0,8},{8,0},{16,24},{24,16},{1,9},{9,1},{17,25},{25,17},{2,10},{10... | collective-permute-start | bytes 2162696 | tf_op jit(solution)/shard_map/ppermute | solution.py:799
  476.6 30.6 %collective-permute-start.51 = (bf16[2816,128]{1,0:T(8,128)(2,1)}, bf16[2816,128]{1,0:T(8,128)(2,1)}, u32[]{:S(2)}, u32[]{:S(2)}) collective-permute-start(bf16[2816,128]{1,0:T(8,128)(2,1)} %get-tuple-element.358.refs_2_), channel_id=1, source_target_pairs={{8,16},{16,8},{9,17},{17,9},{10,18},{18,10},{11,19},{19,11},{12,20... | collective-permute-start | bytes 2162696 | tf_op jit(solution)/shard_map/ppermute | solution.py:801
  491.8 23.1 %collective-permute-start.52 = (bf16[2816,128]{1,0:T(8,128)(2,1)}, bf16[2816,128]{1,0:T(8,128)(2,1)}, u32[]{:S(2)}, u32[]{:S(2)}) collective-permute-start(bf16[2816,128]{1,0:T(8,128)(2,1)} %get-tuple-element.364.refs_6_), channel_id=1, source_target_pairs={{0,8},{8,0},{16,24},{24,16},{1,9},{9,1},{17,25},{25,17},{2,10},{10... | collective-permute-start | bytes 2162696 | tf_op jit(solution)/shard_map/ppermute | solution.py:799
  493.8 21.0 %collective-permute-start.53 = (bf16[2816,128]{1,0:T(8,128)(2,1)}, bf16[2816,128]{1,0:T(8,128)(2,1)}, u32[]{:S(2)}, u32[]{:S(2)}) collective-permute-start(bf16[2816,128]{1,0:T(8,128)(2,1)} %get-tuple-element.365.refs_2_), channel_id=1, source_target_pairs={{8,16},{16,8},{9,17},{17,9},{10,18},{18,10},{11,19},{19,11},{12,20... | collective-permute-start | bytes 2162696 | tf_op jit(solution)/shard_map/ppermute | solution.py:801
  511.4 16.2 %collective-permute-start.56 = (bf16[2816,128]{1,0:T(8,128)(2,1)}, bf16[2816,128]{1,0:T(8,128)(2,1)}, u32[]{:S(2)}, u32[]{:S(2)}) collective-permute-start(bf16[2816,128]{1,0:T(8,128)(2,1)} %get-tuple-element.378.refs_0_), channel_id=1, source_target_pairs={{0,8},{8,0},{16,24},{24,16},{1,9},{9,1},{17,25},{25,17},{2,10},{10... | collective-permute-start | bytes 2162696 | tf_op jit(solution)/shard_map/ppermute | solution.py:799
  530.8 21.2 %collective-permute-start.63 = (bf16[2816,128]{1,0:T(8,128)(2,1)}, bf16[2816,128]{1,0:T(8,128)(2,1)}, u32[]{:S(2)}, u32[]{:S(2)}) collective-permute-start(bf16[2816,128]{1,0:T(8,128)(2,1)} %get-tuple-element.394.refs_4_), channel_id=1, source_target_pairs={{0,8},{8,0},{16,24},{24,16},{1,9},{9,1},{17,25},{25,17},{2,10},{10... | collective-permute-start | bytes 2162696 | tf_op jit(solution)/shard_map/ppermute | solution.py:799
  539.5 28.0 %collective-permute-start.54 = (bf16[2816,128]{1,0:T(8,128)(2,1)}, bf16[2816,128]{1,0:T(8,128)(2,1)}, u32[]{:S(2)}, u32[]{:S(2)}) collective-permute-start(bf16[2816,128]{1,0:T(8,128)(2,1)} %get-tuple-element.371.refs_2_), channel_id=1, source_target_pairs={{0,8},{8,0},{16,24},{24,16},{1,9},{9,1},{17,25},{25,17},{2,10},{10... | collective-permute-start | bytes 2162696 | tf_op jit(solution)/shard_map/ppermute | solution.py:799
  541.6 25.9 %collective-permute-start.55 = (bf16[2816,128]{1,0:T(8,128)(2,1)}, bf16[2816,128]{1,0:T(8,128)(2,1)}, u32[]{:S(2)}, u32[]{:S(2)}) collective-permute-start(bf16[2816,128]{1,0:T(8,128)(2,1)} %get-tuple-element.372.refs_2_), channel_id=1, source_target_pairs={{8,16},{16,8},{9,17},{17,9},{10,18},{18,10},{11,19},{19,11},{12,20... | collective-permute-start | bytes 2162696 | tf_op jit(solution)/shard_map/ppermute | solution.py:801
  554.8 26.6 %collective-permute-start.65 = (bf16[2560,128]{1,0:T(8,128)(2,1)}, bf16[2560,128]{1,0:T(8,128)(2,1)S(1)}, u32[]{:S(2)}, u32[]{:S(2)}) collective-permute-start(bf16[2560,128]{1,0:T(8,128)(2,1)} %get-tuple-element.398), channel_id=1, source_target_pairs={{0,8},{8,0},{16,24},{24,16},{1,9},{9,1},{17,25},{25,17},{2,10},{10... | collective-permute-start | bytes 1966088 | tf_op jit(solution)/shard_map/ppermute | solution.py:799
  557.5 17.5 %collective-permute-start.66 = (bf16[2048,128]{1,0:T(8,128)(2,1)}, bf16[2048,128]{1,0:T(8,128)(2,1)S(1)}, u32[]{:S(2)}, u32[]{:S(2)}) collective-permute-start(bf16[2048,128]{1,0:T(8,128)(2,1)} %get-tuple-element.399.refs_0_), channel_id=1, source_target_pairs={{8,16},{16,8},{9,17},{17,9},{10,18},{18,10},{11,19},{19,11},{12,20... | collective-permute-start | bytes 1572872 | tf_op jit(solution)/shard_map/ppermute | solution.py:801
  570.7 26.2 %collective-permute-start.58 = (bf16[2816,128]{1,0:T(8,128)(2,1)}, bf16[2816,128]{1,0:T(8,128)(2,1)S(1)}, u32[]{:S(2)}, u32[]{:S(2)}) collective-permute-start(bf16[2816,128]{1,0:T(8,128)(2,1)} %get-tuple-element.384.refs_6_), channel_id=1, source_target_pairs={{0,8},{8,0},{16,24},{24,16},{1,9},{9,1},{17,25},{25,17},{2,10},{10... | collective-permute-start | bytes 2162696 | tf_op jit(solution)/shard_map/ppermute | solution.py:799
  583.4 27.8 %collective-permute-start.67 = (bf16[2048,128]{1,0:T(8,128)(2,1)}, bf16[2048,128]{1,0:T(8,128)(2,1)}, u32[]{:S(2)}, u32[]{:S(2)}) collective-permute-start(bf16[2048,128]{1,0:T(8,128)(2,1)} %chain_step.35.refs_0_), channel_id=1, source_target_pairs={{0,8},{8,0},{16,24},{24,16},{1,9},{9,1},{17,25},{25,17},{2,10},{10... | collective-permute-start | bytes 1572872 | tf_op jit(solution)/shard_map/ppermute | solution.py:799
  600.6 17.4 %collective-permute-start.60 = (bf16[2560,128]{1,0:T(8,128)(2,1)}, bf16[2560,128]{1,0:T(8,128)(2,1)S(1)}, u32[]{:S(2)}, u32[]{:S(2)}) collective-permute-start(bf16[2560,128]{1,0:T(8,128)(2,1)} %get-tuple-element.389), channel_id=1, source_target_pairs={{0,8},{8,0},{16,24},{24,16},{1,9},{9,1},{17,25},{25,17},{2,10},{10... | collective-permute-start | bytes 1966088 | tf_op jit(solution)/shard_map/ppermute | solution.py:799
  (57 other events, 507.9 us)

commit v7 on v6

--- a/solution.py
+++ b/solution.py
@@ -859,13 +859,14 @@
         (gate_near, gate_far, down_far, grad_up, *parts)
     )
     gate_far = swap(gate_far)
+    grad_resid, da, gain_two_local = residual_norm_back(cotangent, parts, resid, chips)
+    da, gate_near, down_near = tie((da, gate_near, down_near))
     down = pair_sum(down_near, down_far)
     grad_up = visit(grad_up, new=("down", down, 0))
     up_near, up_far = weight_grad(ids, normed_two, grad_up, chips)
-    up_near, up_far, *parts = visit(up_near, up_far, *parts, new=("down", down, 1))
+    up_near, up_far, da = visit(up_near, up_far, da, new=("down", down, 1))
     gate_part = exchange(pair_sum(gate_near, gate_far))
     up_far = swap(up_far)
-    grad_resid, da, gain_two_local = residual_norm_back(cotangent, parts, resid, chips)
     da, inner = visit(da, inner, new=("down", down, 2))
     out = dot(inner, w_down_c).astype(BF16)
     up_part = pair_sum(up_near, up_far)

time: 645 us -> 644 us (level)
  transfers between devices with their start and end apart: 78 -> 78, of which waited for: 31 -> 32; matrix products, arithmetic and copies ran while one was open for 6% -> 6% of each run, Pallas kernels for 28% -> 29%
where the time goes in v7:
time: 644 us; the launch traced here: 637 us
  Pallas kernels  229 us (36%)
  waiting for transfers between devices  220 us (34%)
  starting transfers between devices  135 us (21%)
  local copies, waits for them, and re-layouts  29.2 us (5%)
  matrix products  14.7 us (2%)
  other arithmetic  6.71 us (1%)
    ppermute x20, waiting for transfers between devices, visit(): lax.ppermute(ahead, 'rep', outer_pairs)  97 us
    ppermute x15, waiting for transfers between devices, hop(): return lax.ppermute(v, 'fsdp', [(i, i ^ 2 * k) for i in range(group)])  70.3 us
    pallas_call x18, Pallas kernels, chain_step(): pl.pallas_call(body, grid=(1,), in_specs=[scalars()] + [spec(v) for v in...  56.1 us
    ppermute x20, starting transfers between devices, visit(): lax.ppermute(ahead, 'rep', outer_pairs)  46.1 us
    all_to_all x10, waiting for transfers between devices, exchange(): return lax.all_to_all(v, 'fsdp', 0, 0, axis_index_groups=sides, tiled=True)  42.6 us
    all_to_all x10, starting transfers between devices, exchange(): return lax.all_to_all(v, 'fsdp', 0, 0, axis_index_groups=sides, tiled=True)  40.8 us
    pallas_call x5, Pallas kernels, beside(): pl.pallas_call(body, grid_spec=pltpu.PrefetchScalarGridSpec(num_scalar_pr...  27.9 us
    pallas_call x1, Pallas kernels, feed_forward(): pl.pallas_call(body, grid_spec=pltpu.PrefetchScalarGridSpec(num_scalar_pr...  26 us
  transfers between devices with their start and end apart: 78, of which 32 were waited for; matrix products, arithmetic and copies ran while one was open for 6% of the time, Pallas kernels for 29%

profile of v7, /device:TPU:0, one launch (start us, length us, event | category | flops | bytes accessed | tf_op | source)
XLA Modules:
  0.0 636.8 jit_solution(5746531307624499256)
XLA Ops:
  2.6 4.1 pick_qkv.1
  6.7 4.7 all-to-all-start
  16.7 12.6 %all-to-all-done.n_ref = bf16[4,256,640]{2,1,0:T(8,128)(2,1)S(1)} async-done(((bf16[4,256,640]{2,1,0:T(8,128)(2,1)}), bf16[4,256,640]{2,1,0:T(8,128)(2,1)S(1)}, u32[]{:S(2)}, u32[]{:S(2)}) %all-to-all-start) | async-done | bytes 1310752 | tf_op jit(solution)/shard_map/all_to_all | solution.py:743
  31.1 4.9 pick_half.1
  36.0 6.1 join_cores.1.refs_13_
  42.1 9.9 %collective-permute-done.2.refs_3_ = bf16[128,2048]{1,0:T(8,128)(2,1)} collective-permute-done((bf16[128,2048]{1,0:T(8,128)(2,1)S(1)}, bf16[128,2048]{1,0:T(8,128)(2,1)}, u32[]{:S(2)}, u32[]{:S(2)}) %collective-permute-start.2) | collective-permute-done | bytes 524320 | tf_op jit(solution)/shard_map/ppermute | solution.py:746
  52.0 3.6 all-to-all-start.1
  55.6 6.5 %qkv_forward.1 = (bf16[512,2048]{1,0:T(8,128)(2,1)}, bf16[512,512]{1,0:T(8,128)(2,1)}, bf16[512,128]{1,0:T(8,128)(2,1)}, bf16[2048,640]{1,0:T(8,128)(2,1)}) custom-call(s32[5]{0:T(128)} %stack.38.s_ref.c_ref, f32[512,128]{1,0:T(8,128)} %get-tuple-element.210.cos_ref, f32[512,128]{1,0:T(8,128)} %get-tuple-element.211.sin_ref, bf16[4,256,640]{2,1,0:T(8,128)(2,1)} %copy-done.6, ...), custom_call_target="tpu_custom_call" | custom-call | flops 1024 | bytes 1024 | tf_op jit(solution)/shard_map/qkv_forward/pallas_call | solution.py:167
  62.1 11.1 %all-to-all-done.1.refs_5_ = bf16[4,128,1408]{2,1,0:T(8,128)(2,1)S(1)} async-done(((bf16[4,128,1408]{2,1,0:T(8,128)(2,1)}), bf16[4,128,1408]{2,1,0:T(8,128)(2,1)S(1)}, u32[]{:S(2)}, u32[]{:S(2)}) %all-to-all-start.1) | async-done | bytes 1441824 | tf_op jit(solution)/shard_map/all_to_all | solution.py:743
  73.2 4.5 all-to-all-start.2
  81.0 8.9 %attention_forward.1 = (bf16[512,512]{1,0:T(8,128)(2,1)}, f32[512,128]{1,0:T(8,128)}) custom-call(s32[5]{0:T(128)} %stack.38.s_ref.c_ref, s32[4,8]{1,0:T(4,128)} %n_ref.3, bf16[512,512]{1,0:T(8,128)(2,1)} %get-tuple-element.219.q_ref, bf16[512,128]{1,0:T(8,128)(2,1)} %get-tuple-element.220.a_ref, bf16[512,128]{1,0:T(8,128)(2,1)} %collective-permute-done.6.b_ref), custom_call_target="tpu_custom_call" | custom-call | flops 1024 | bytes 1024 | tf_op jit(solution)/shard_map/attention_forward/pallas_call | solution.py:240
  89.9 6.7 %all-to-all-done.2.refs_9_ = bf16[4,128,1408]{2,1,0:T(8,128)(2,1)} async-done(((bf16[4,128,1408]{2,1,0:T(8,128)(2,1)}), bf16[4,128,1408]{2,1,0:T(8,128)(2,1)}, u32[]{:S(2)}, u32[]{:S(2)}) %all-to-all-start.2) | async-done | bytes 1441824 | tf_op jit(solution)/shard_map/all_to_all | solution.py:743
  98.4 4.6 out_proj.1
  105.0 7.3 %collective-permute-done.11.refs_6_ = bf16[4,128,1408]{2,1,0:T(8,128)(2,1)} collective-permute-done((bf16[4,128,1408]{2,1,0:T(8,128)(2,1)S(1)}, bf16[4,128,1408]{2,1,0:T(8,128)(2,1)}, u32[]{:S(2)}, u32[]{:S(2)}) %collective-permute-start.11) | collective-permute-done | bytes 1441824 | tf_op jit(solution)/shard_map/ppermute | solution.py:755
  116.8 3.8 all-to-all-start.3
  120.7 19.9 %collective-permute-done.9.refs_2_ = bf16[128,2048]{1,0:T(8,128)(2,1)} collective-permute-done((bf16[128,2048]{1,0:T(8,128)(2,1)}, bf16[128,2048]{1,0:T(8,128)(2,1)}, u32[]{:S(2)}, u32[]{:S(2)}) %collective-permute-start.9) | collective-permute-done | bytes 524320 | tf_op jit(solution)/shard_map/ppermute | solution.py:746
  152.2 10.9 %collective-permute-done.13.refs_1_ = bf16[128,2048]{1,0:T(8,128)(2,1)} collective-permute-done((bf16[128,2048]{1,0:T(8,128)(2,1)}, bf16[128,2048]{1,0:T(8,128)(2,1)}, u32[]{:S(2)}, u32[]{:S(2)}) %collective-permute-start.13) | collective-permute-done | bytes 524320 | tf_op jit(solution)/shard_map/ppermute | solution.py:746
  163.1 11.6 %collective-permute-done.14.refs_2_ = bf16[128,2048]{1,0:T(8,128)(2,1)} collective-permute-done((bf16[128,2048]{1,0:T(8,128)(2,1)}, bf16[128,2048]{1,0:T(8,128)(2,1)}, u32[]{:S(2)}, u32[]{:S(2)}) %collective-permute-start.14) | collective-permute-done | bytes 524320 | tf_op jit(solution)/shard_map/ppermute | solution.py:746
  175.8 26.0 %feed_forward.1 = (bf16[512,1408]{1,0:T(8,128)(2,1)}, bf16[512,1408]{1,0:T(8,128)(2,1)}, bf16[512,1408]{1,0:T(8,128)(2,1)}, bf16[512,2048]{1,0:T(8,128)(2,1)}, b...) custom-call(s32[5]{0:T(128)} %stack.38.s_ref.c_ref, ...), custom_call_target="tpu_custom_call" | custom-call | flops 1024 | bytes 1024 | tf_op jit(solution)/shard_map/feed_forward/pallas_call | solution.py:388
  201.8 8.2 %row_grad.2 = (bf16[4,2816,128]{2,1,0:T(8,128)(2,1)}, bf16[4,2816,128]{2,1,0:T(8,128)(2,1)}) custom-call(s32[5]{0:T(128)} %stack.38.s_ref.c_ref, bf16[512,1408]{1,0:T(8,128)(2,1)} %get-tuple-element.276.l_ref, bf16[512,2048]{1,0:T(8,128)(2,1)} %bitcast.79), custom_call_target="tpu_custom_call" | custom-call | flops 1024 | bytes 1024 | tf_op jit(solution)/shard_map/row_grad/pallas_call | solution.py:569
  213.5 9.5 %weight_grad.3 = (bf16[4,2816,128]{2,1,0:T(8,128)(2,1)}, bf16[4,2816,128]{2,1,0:T(8,128)(2,1)}) custom-call(s32[5]{0:T(128)} %stack.38.s_ref.c_ref, bf16[512,2048]{1,0:T(8,128)(2,1)} %get-tuple-element.247.l_ref, bf16[512,1408]{1,0:T(8,128)(2,1)} %get-tuple-element.251.r_ref), custom_call_target="tpu_custom_call" | custom-call | flops 1024 | bytes 1024 | tf_op jit(solution)/shard_map/weight_grad/pallas_call | solution.py:534
  225.0 11.2 %collective-permute-done.21.refs_2_ = bf16[128,2048]{1,0:T(8,128)(2,1)} collective-permute-done((bf16[128,2048]{1,0:T(8,128)(2,1)}, bf16[128,2048]{1,0:T(8,128)(2,1)}, u32[]{:S(2)}, u32[]{:S(2)}) %collective-permute-start.21) | collective-permute-done | bytes 524320 | tf_op jit(solution)/shard_map/ppermute | solution.py:746
  236.3 5.5 residual_norm_back.2
  241.9 4.1 pair_sum.7
  246.0 3.7 all-to-all-start.4
  249.7 4.2 pair_sum.5.refs_0_.refs_2_
  253.9 9.1 %weight_grad.4 = (bf16[4,2816,128]{2,1,0:T(8,128)(2,1)}, bf16[4,2816,128]{2,1,0:T(8,128)(2,1)}) custom-call(s32[5]{0:T(128)} %stack.38.s_ref.c_ref, bf16[512,2048]{1,0:T(8,128)(2,1)} %get-tuple-element.247.l_ref, bf16[512,1408]{1,0:T(8,128)(2,1)} %get-tuple-element.270.r_ref), custom_call_target="tpu_custom_call" | custom-call | flops 1024 | bytes 1024 | tf_op jit(solution)/shard_map/weight_grad/pallas_call | solution.py:534
  265.2 17.6 %collective-permute-done.23.refs_1_ = bf16[2816,128]{1,0:T(8,128)(2,1)} collective-permute-done((bf16[2816,128]{1,0:T(8,128)(2,1)S(1)}, bf16[2816,128]{1,0:T(8,128)(2,1)}, u32[]{:S(2)}, u32[]{:S(2)}) %collective-permute-start.23) | collective-permute-done | bytes 720928 | tf_op jit(solution)/shard_map/ppermute | solution.py:799
  285.2 4.4 all-to-all-start.6
  297.3 7.3 %convolution_convert_fusion.1 = bf16[512,2048]{1,0:T(8,128)(2,1)} fusion(bf16[512,1408]{1,0:T(8,128)(2,1)S(1)} %copy-done.21, bf16[1408,2048]{1,0:T(8,128)(2,1)} %join_cores.1.refs_13_), kind=kOutput, calls=%fused_computation.2 | convolution fusion | flops 2953838592 | bytes 9306112 | tf_op jit(solution)/shard_map/dot_general | solution.py:24
  304.6 4.1 pair_sum.6
  310.0 13.9 %collective-permute-done.27.refs_1_ = bf16[2816,128]{1,0:T(8,128)(2,1)} collective-permute-done((bf16[2816,128]{1,0:T(8,128)(2,1)}, bf16[2816,128]{1,0:T(8,128)(2,1)}, u32[]{:S(2)}, u32[]{:S(2)}) %collective-permute-start.27) | collective-permute-done | bytes 720928 | tf_op jit(solution)/shard_map/ppermute | solution.py:799
  323.9 3.9 all-to-all-start.7
  336.4 3.7 collective-permute-start.31
  341.7 4.9 row_grad.3
  346.6 4.3 convolution_convert_fusion.2.d_ref
  350.9 15.6 %attention_backward.1 = (bf16[512,512]{1,0:T(8,128)(2,1)}, f32[1024,128]{1,0:T(8,128)}) custom-call(s32[5]{0:T(128)} %stack.38.s_ref.c_ref, s32[4,8]{1,0:T(4,128)} %n_ref.3, bf16[512,512]{1,0:T(8,128)(2,1)} %get-tuple-element.219.q_ref, bf16[512,128]{1,0:T(8,128)(2,1)} %get-tuple-element.220.a_ref, bf16[512,128]{1,0:T(8,128)(2,1)} %collective-permute-done.6.b_ref, ...), custom_call_target="tpu_custom_call" | custom-call | flops 1024 | bytes 1024 | tf_op jit(solution)/shard_map/attention_backward/pallas_call | solution.py:315
  368.1 3.4 chain_step.21
  376.4 3.4 chain_step.22
  393.6 4.5 all-to-all-start.8
  398.1 6.5 %weight_grad.5 = (bf16[4,1280,128]{2,1,0:T(8,128)(2,1)}, bf16[4,1280,128]{2,1,0:T(8,128)(2,1)}) custom-call(s32[5]{0:T(128)} %stack.38.s_ref.c_ref, bf16[512,2048]{1,0:T(8,128)(2,1)} %get-tuple-element.284.l_ref, bf16[512,640]{1,0:T(8,128)(2,1)} %copy-done.16), custom_call_target="tpu_custom_call" | custom-call | flops 1024 | bytes 1024 | tf_op jit(solution)/shard_map/weight_grad/pallas_call | solution.py:534
  407.3 3.4 chain_step.23
  410.7 4.2 collective-permute-start.39
  419.5 12.4 %collective-permute-done.39.refs_7_.refs_1_ = bf16[2816,128]{1,0:T(8,128)(2,1)S(1)} collective-permute-done((bf16[2816,128]{1,0:T(8,128)(2,1)}, bf16[2816,128]{1,0:T(8,128)(2,1)S(1)}, u32[]{:S(2)}, u32[]{:S(2)}) %collective-permute-start.39) | collective-permute-done | bytes 720928 | tf_op jit(solution)/shard_map/ppermute | solution.py:799
  432.8 4.2 all-to-all-start.9
  444.8 8.7 %all-to-all-done.9 = bf16[4,1280,128]{2,1,0:T(8,128)(2,1)S(1)} async-done(((bf16[4,1280,128]{2,1,0:T(8,128)(2,1)}), bf16[4,1280,128]{2,1,0:T(8,128)(2,1)S(1)}, u32[]{:S(2)}, u32[]{:S(2)}) %all-to-all-start.9) | async-done | bytes 1310752 | tf_op jit(solution)/shard_map/all_to_all | solution.py:743
  454.6 3.6 all-to-all-start.5
  458.2 3.4 chain_step.25
  465.8 4.0 residual_norm_back.3
  469.8 3.4 chain_step.26
  480.7 6.6 %beside.5 = f32[704,2048]{1,0:T(8,128)} custom-call(s32[5]{0:T(128)} %stack.38.s_ref.c_ref, f32[704,1]{1,0:T(8,128)} %broadcast_in_dim.39.s_ref, bf16[2816,128]{1,0:T(8,128)(2,1)} %get-tuple-element.307.refs_0_, bf16[2816,128]{1,0:T(8,128)(2,1)} %collective-permute-done.31.refs_1_, bf16[2816,128]{1,0:T(8,128)(2,1)} %get-tuple-element.316.refs_2_, ...), custom_call_target="tpu_custom_call" | custom-call | flops 1024 | bytes 1024 | tf_op jit(solution)/shard_map/beside/pallas_call | solution.py:677
  487.3 3.4 chain_step.27
  506.9 3.4 chain_step.29
  513.7 6.6 %beside.6 = f32[256,5632]{1,0:T(8,128)} custom-call(s32[5]{0:T(128)} %stack.38.s_ref.c_ref, f32[256,1]{1,0:T(8,128)} %copy.26.n_ref.s_ref, bf16[2816,128]{1,0:T(8,128)(2,1)} %get-tuple-element.340.refs_0_, bf16[2816,128]{1,0:T(8,128)(2,1)} %collective-permute-done.41.refs_1_, bf16[2816,128]{1,0:T(8,128)(2,1)} %get-tuple-element.351.refs_2_, ...), custom_call_target="tpu_custom_call" | custom-call | flops 1024 | bytes 1024 | tf_op jit(solution)/shard_map/beside/pallas_call | solution.py:677
  521.2 5.2 collective-permute-done.56.refs_1_
  529.7 3.8 collective-permute-start.63
  543.3 7.5 %collective-permute-done.63.refs_1_.refs_5_ = bf16[2816,128]{1,0:T(8,128)(2,1)} collective-permute-done((bf16[2816,128]{1,0:T(8,128)(2,1)}, bf16[2816,128]{1,0:T(8,128)(2,1)}, u32[]{:S(2)}, u32[]{:S(2)}) %collective-permute-start.63) | collective-permute-done | bytes 720928 | tf_op jit(solution)/shard_map/ppermute | solution.py:799
  557.9 8.3 %collective-permute-done.54.refs_1_.refs_3_ = bf16[2816,128]{1,0:T(8,128)(2,1)} collective-permute-done((bf16[2816,128]{1,0:T(8,128)(2,1)}, bf16[2816,128]{1,0:T(8,128)(2,1)}, u32[]{:S(2)}, u32[]{:S(2)}) %collective-permute-start.54) | collective-permute-done | bytes 720928 | tf_op jit(solution)/shard_map/ppermute | solution.py:799
  573.8 6.4 %collective-permute-done.65 = bf16[2560,128]{1,0:T(8,128)(2,1)S(1)} collective-permute-done((bf16[2560,128]{1,0:T(8,128)(2,1)}, bf16[2560,128]{1,0:T(8,128)(2,1)S(1)}, u32[]{:S(2)}, u32[]{:S(2)}) %collective-permute-start.65) | collective-permute-done | bytes 655392 | tf_op jit(solution)/shard_map/ppermute | solution.py:799
  585.3 10.3 %collective-permute-done.58.refs_1_.refs_7_ = bf16[2816,128]{1,0:T(8,128)(2,1)S(1)} collective-permute-done((bf16[2816,128]{1,0:T(8,128)(2,1)}, bf16[2816,128]{1,0:T(8,128)(2,1)S(1)}, u32[]{:S(2)}, u32[]{:S(2)}) %collective-permute-start.58) | collective-permute-done | bytes 720928 | tf_op jit(solution)/shard_map/ppermute | solution.py:799
  602.6 6.6 %beside.9 = f32[256,5632]{1,0:T(8,128)} custom-call(s32[5]{0:T(128)} %stack.38.s_ref.c_ref, f32[256,1]{1,0:T(8,128)} %copy.26.n_ref.s_ref, bf16[2816,128]{1,0:T(8,128)(2,1)} %get-tuple-element.378.refs_0_, bf16[2816,128]{1,0:T(8,128)(2,1)} %collective-permute-done.56.refs_1_, bf16[2816,128]{1,0:T(8,128)(2,1)} %get-tuple-element.371.refs_2_, ...), custom_call_target="tpu_custom_call" | custom-call | flops 1024 | bytes 1024 | tf_op jit(solution)/shard_map/beside/pallas_call | solution.py:677
  610.0 7.0 %collective-permute-done.60 = bf16[2560,128]{1,0:T(8,128)(2,1)S(1)} collective-permute-done((bf16[2560,128]{1,0:T(8,128)(2,1)}, bf16[2560,128]{1,0:T(8,128)(2,1)S(1)}, u32[]{:S(2)}, u32[]{:S(2)}) %collective-permute-start.60) | collective-permute-done | bytes 655392 | tf_op jit(solution)/shard_map/ppermute | solution.py:799
  621.9 4.5 beside.7
  632.8 3.7 beside.8
  (278 shorter events, 184.2 us)
Async XLA Ops:
  0.6 28.6 %collective-permute-start.4 = (bf16[704,2048]{1,0:T(8,128)(2,1)}, bf16[704,2048]{1,0:T(8,128)(2,1)}, u32[]{:S(2)}, u32[]{:S(2)}) collective-permute-start(bf16[704,2048]{1,0:T(8,128)(2,1)} %a_ref.3), channel_id=1, source_target_pairs={{0,1},{1,0},{2,3},{3,2},{4,5},{5,4},{6,7},{7,6},{8,9},{9,8},{10,11... | collective-permute-start | bytes 8650760 | tf_op jit(solution)/shard_map/ppermute | solution.py:752
  6.7 22.5 %all-to-all-start = ((bf16[4,256,640]{2,1,0:T(8,128)(2,1)}), bf16[4,256,640]{2,1,0:T(8,128)(2,1)S(1)}, u32[]{:S(2)}, u32[]{:S(2)}) async-start(bf16[4,256,640]{2,1,0:T(8,128)(2,1)} %pick_qkv.1), calls=%async_computation | async-start | bytes 2621440 | tf_op jit(solution)/shard_map/all_to_all | solution.py:743
  11.4 40.6 %collective-permute-start.3 = (bf16[256,2048]{1,0:T(8,128)(2,1)S(1)}, bf16[256,2048]{1,0:T(8,128)(2,1)}, u32[]{:S(2)}, u32[]{:S(2)}) collective-permute-start(bf16[256,2048]{1,0:T(8,128)(2,1)S(1)} %copy-done.24), channel_id=1, source_target_pairs={{0,1},{1,0},{2,3},{3,2},{4,5},{5,4},{6,7},{7,6},{8,9},{9,8},{10,11... | collective-permute-start | bytes 3145736 | tf_op jit(solution)/shard_map/ppermute | solution.py:752
  11.6 30.4 %collective-permute-start = (bf16[128,2048]{1,0:T(8,128)(2,1)S(1)}, bf16[128,2048]{1,0:T(8,128)(2,1)S(1)}, u32[]{:S(2)}, u32[]{:S(2)}) collective-permute-start(bf16[128,2048]{1,0:T(8,128)(2,1)S(1)} %copy-done.7), channel_id=1, source_target_pairs={{0,2},{1,3},{2,0},{3,1},{4,6},{5,7},{6,4},{7,5},{8,10},{9,11},{10,... | collective-permute-start | bytes 1572872 | tf_op jit(solution)/shard_map/ppermute | solution.py:746
  13.5 28.5 %collective-permute-start.1 = (bf16[128,2048]{1,0:T(8,128)(2,1)S(1)}, bf16[128,2048]{1,0:T(8,128)(2,1)}, u32[]{:S(2)}, u32[]{:S(2)}) collective-permute-start(bf16[128,2048]{1,0:T(8,128)(2,1)S(1)} %copy-done.7), channel_id=1, source_target_pairs={{0,4},{1,5},{2,6},{3,7},{4,0},{5,1},{6,2},{7,3},{8,12},{9,13},{10,... | collective-permute-start | bytes 1572872 | tf_op jit(solution)/shard_map/ppermute | solution.py:746
  15.0 37.0 %collective-permute-start.2 = (bf16[128,2048]{1,0:T(8,128)(2,1)S(1)}, bf16[128,2048]{1,0:T(8,128)(2,1)}, u32[]{:S(2)}, u32[]{:S(2)}) collective-permute-start(bf16[128,2048]{1,0:T(8,128)(2,1)S(1)} %copy-done.7), channel_id=1, source_target_pairs={{0,6},{1,7},{2,4},{3,5},{4,2},{5,3},{6,0},{7,1},{8,14},{9,15},{10,... | collective-permute-start | bytes 1572872 | tf_op jit(solution)/shard_map/ppermute | solution.py:746
  29.2 26.3 %collective-permute-start.5 = (bf16[4,256,640]{2,1,0:T(8,128)(2,1)S(1)}, bf16[4,256,640]{2,1,0:T(8,128)(2,1)}, u32[]{:S(2)}, u32[]{:S(2)}) collective-permute-start(bf16[4,256,640]{2,1,0:T(8,128)(2,1)S(1)} %all-to-all-done.n_ref), channel_id=1, source_target_pairs={{0,1},{1,0},{2,3},{3,2},{4,5},{5,4},{6,7},{7,6},{8,9},{9,8},{10,11... | collective-permute-start | bytes 3932168 | tf_op jit(solution)/shard_map/ppermute | solution.py:752
  52.0 21.2 %all-to-all-start.1 = ((bf16[4,128,1408]{2,1,0:T(8,128)(2,1)}), bf16[4,128,1408]{2,1,0:T(8,128)(2,1)S(1)}, u32[]{:S(2)}, u32[]{:S(2)}) async-start(bf16[4,128,1408]{2,1,0:T(8,128)(2,1)} %get-tuple-element.217), calls=%async_computation.1 | async-start | bytes 2883584 | tf_op jit(solution)/shard_map/all_to_all | solution.py:743
  73.2 23.4 %collective-permute-start.7 = (bf16[4,128,1408]{2,1,0:T(8,128)(2,1)S(1)}, bf16[4,128,1408]{2,1,0:T(8,128)(2,1)S(1)}, u32[]{:S(2)}, u32[]{:S(2)}) collective-permute-start(bf16[4,128,1408]{2,1,0:T(8,128)(2,1)S(1)} %all-to-all-done.1.refs_5_), channel_id=1, source_target_pairs={{0,1},{1,0},{2,3},{3,2},{4,5},{5,4},{6,7},{7,6},{8,9},{9,8},{10,11... | collective-permute-start | bytes 4325384 | tf_op jit(solution)/shard_map/ppermute | solution.py:752
  73.2 23.3 %all-to-all-start.2 = ((bf16[4,128,1408]{2,1,0:T(8,128)(2,1)}), bf16[4,128,1408]{2,1,0:T(8,128)(2,1)}, u32[]{:S(2)}, u32[]{:S(2)}) async-start(bf16[4,128,1408]{2,1,0:T(8,128)(2,1)} %get-tuple-element.222), calls=%async_computation.2 | async-start | bytes 2883584 | tf_op jit(solution)/shard_map/all_to_all | solution.py:743
  77.7 34.6 %collective-permute-start.11 = (bf16[4,128,1408]{2,1,0:T(8,128)(2,1)S(1)}, bf16[4,128,1408]{2,1,0:T(8,128)(2,1)}, u32[]{:S(2)}, u32[]{:S(2)}) collective-permute-start(bf16[4,128,1408]{2,1,0:T(8,128)(2,1)S(1)} %all-to-all-done.1.refs_5_), channel_id=1, source_target_pairs={{0,8},{8,0},{16,24},{24,16},{1,9},{9,1},{17,25},{25,17},{2,10},{10... | collective-permute-start | bytes 4325384 | tf_op jit(solution)/shard_map/ppermute | solution.py:755
  96.6 44.8 %collective-permute-start.12 = (bf16[4,128,1408]{2,1,0:T(8,128)(2,1)}, bf16[4,128,1408]{2,1,0:T(8,128)(2,1)}, u32[]{:S(2)}, u32[]{:S(2)}) collective-permute-start(bf16[4,128,1408]{2,1,0:T(8,128)(2,1)} %all-to-all-done.2.refs_9_), channel_id=1, source_target_pairs={{0,1},{1,0},{2,3},{3,2},{4,5},{5,4},{6,7},{7,6},{8,9},{9,8},{10,11... | collective-permute-start | bytes 4325384 | tf_op jit(solution)/shard_map/ppermute | solution.py:752
  96.6 46.2 %collective-permute-start.17 = (bf16[4,128,1408]{2,1,0:T(8,128)(2,1)}, bf16[4,128,1408]{2,1,0:T(8,128)(2,1)}, u32[]{:S(2)}, u32[]{:S(2)}) collective-permute-start(bf16[4,128,1408]{2,1,0:T(8,128)(2,1)} %all-to-all-done.2.refs_9_), channel_id=1, source_target_pairs={{0,8},{8,0},{16,24},{24,16},{1,9},{9,1},{17,25},{25,17},{2,10},{10... | collective-permute-start | bytes 4325384 | tf_op jit(solution)/shard_map/ppermute | solution.py:755
  103.0 17.7 %collective-permute-start.8 = (bf16[128,2048]{1,0:T(8,128)(2,1)}, bf16[128,2048]{1,0:T(8,128)(2,1)}, u32[]{:S(2)}, u32[]{:S(2)}) collective-permute-start(bf16[128,2048]{1,0:T(8,128)(2,1)} %get-tuple-element.232), channel_id=1, source_target_pairs={{0,2},{1,3},{2,0},{3,1},{4,6},{5,7},{6,4},{7,5},{8,10},{9,11},{10,... | collective-permute-start | bytes 1572872 | tf_op jit(solution)/shard_map/ppermute | solution.py:746
  104.4 36.1 %collective-permute-start.9 = (bf16[128,2048]{1,0:T(8,128)(2,1)}, bf16[128,2048]{1,0:T(8,128)(2,1)}, u32[]{:S(2)}, u32[]{:S(2)}) collective-permute-start(bf16[128,2048]{1,0:T(8,128)(2,1)} %get-tuple-element.233), channel_id=1, source_target_pairs={{0,4},{1,5},{2,6},{3,7},{4,0},{5,1},{6,2},{7,3},{8,12},{9,13},{10,... | collective-permute-start | bytes 1572872 | tf_op jit(solution)/shard_map/ppermute | solution.py:746
  112.3 28.3 %collective-permute-start.10 = (bf16[128,2048]{1,0:T(8,128)(2,1)}, bf16[128,2048]{1,0:T(8,128)(2,1)S(1)}, u32[]{:S(2)}, u32[]{:S(2)}) collective-permute-start(bf16[128,2048]{1,0:T(8,128)(2,1)} %get-tuple-element.234), channel_id=1, source_target_pairs={{0,6},{1,7},{2,4},{3,5},{4,2},{5,3},{6,0},{7,1},{8,14},{9,15},{10,... | collective-permute-start | bytes 1572872 | tf_op jit(solution)/shard_map/ppermute | solution.py:746
  116.8 35.4 %all-to-all-start.3 = ((bf16[4,128,2048]{2,1,0:T(8,128)(2,1)}), bf16[4,128,2048]{2,1,0:T(8,128)(2,1)S(1)}, u32[]{:S(2)}, u32[]{:S(2)}) async-start(bf16[4,128,2048]{2,1,0:T(8,128)(2,1)} %broadcast_in_dim.38), calls=%async_computation.3 | async-start | bytes 4194304 | tf_op jit(solution)/shard_map/all_to_all | solution.py:743
  141.3 33.3 %collective-permute-start.16 = (bf16[4,128,1408]{2,1,0:T(8,128)(2,1)}, bf16[4,128,1408]{2,1,0:T(8,128)(2,1)S(1)}, u32[]{:S(2)}, u32[]{:S(2)}) collective-permute-start(bf16[4,128,1408]{2,1,0:T(8,128)(2,1)} %collective-permute-done.11.refs_6_), channel_id=1, source_target_pairs={{0,1},{1,0},{2,3},{3,2},{4,5},{5,4},{6,7},{7,6},{8,9},{9,8},{10,11... | collective-permute-start | bytes 4325384 | tf_op jit(solution)/shard_map/ppermute | solution.py:752
  142.8 31.9 %collective-permute-start.18 = (bf16[4,128,1408]{2,1,0:T(8,128)(2,1)}, bf16[4,128,1408]{2,1,0:T(8,128)(2,1)}, u32[]{:S(2)}, u32[]{:S(2)}) collective-permute-start(bf16[4,128,1408]{2,1,0:T(8,128)(2,1)} %collective-permute-done.17.refs_10_), channel_id=1, source_target_pairs={{0,1},{1,0},{2,3},{3,2},{4,5},{5,4},{6,7},{7,6},{8,9},{9,8},{10,11... | collective-permute-start | bytes 4325384 | tf_op jit(solution)/shard_map/ppermute | solution.py:752
  146.0 17.1 %collective-permute-start.13 = (bf16[128,2048]{1,0:T(8,128)(2,1)}, bf16[128,2048]{1,0:T(8,128)(2,1)}, u32[]{:S(2)}, u32[]{:S(2)}) collective-permute-start(bf16[128,2048]{1,0:T(8,128)(2,1)} %get-tuple-element.241.refs_0_), channel_id=1, source_target_pairs={{0,2},{1,3},{2,0},{3,1},{4,6},{5,7},{6,4},{7,5},{8,10},{9,11},{10,... | collective-permute-start | bytes 1572872 | tf_op jit(solution)/shard_map/ppermute | solution.py:746
  147.7 27.0 %collective-permute-start.14 = (bf16[128,2048]{1,0:T(8,128)(2,1)}, bf16[128,2048]{1,0:T(8,128)(2,1)}, u32[]{:S(2)}, u32[]{:S(2)}) collective-permute-start(bf16[128,2048]{1,0:T(8,128)(2,1)} %get-tuple-element.241.refs_0_), channel_id=1, source_target_pairs={{0,4},{1,5},{2,6},{3,7},{4,0},{5,1},{6,2},{7,3},{8,12},{9,13},{10,... | collective-permute-start | bytes 1572872 | tf_op jit(solution)/shard_map/ppermute | solution.py:746
  149.1 25.5 %collective-permute-start.15 = (bf16[128,2048]{1,0:T(8,128)(2,1)}, bf16[128,2048]{1,0:T(8,128)(2,1)}, u32[]{:S(2)}, u32[]{:S(2)}) collective-permute-start(bf16[128,2048]{1,0:T(8,128)(2,1)} %get-tuple-element.241.refs_0_), channel_id=1, source_target_pairs={{0,6},{1,7},{2,4},{3,5},{4,2},{5,3},{6,0},{7,1},{8,14},{9,15},{10,... | collective-permute-start | bytes 1572872 | tf_op jit(solution)/shard_map/ppermute | solution.py:746
  210.0 26.2 %collective-permute-start.19 = (bf16[4,2816,128]{2,1,0:T(8,128)(2,1)}, bf16[4,2816,128]{2,1,0:T(8,128)(2,1)S(1)}, u32[]{:S(2)}, u32[]{:S(2)}) collective-permute-start(bf16[4,2816,128]{2,1,0:T(8,128)(2,1)} %get-tuple-element.254), channel_id=1, source_target_pairs={{0,1},{1,0},{2,3},{3,2},{4,5},{5,4},{6,7},{7,6},{8,9},{9,8},{10,11... | collective-permute-start | bytes 8650760 | tf_op jit(solution)/shard_map/ppermute | solution.py:752
  210.6 25.6 %collective-permute-start.21 = (bf16[128,2048]{1,0:T(8,128)(2,1)}, bf16[128,2048]{1,0:T(8,128)(2,1)}, u32[]{:S(2)}, u32[]{:S(2)}) collective-permute-start(bf16[128,2048]{1,0:T(8,128)(2,1)} %get-tuple-element.258), channel_id=1, source_target_pairs={{0,4},{1,5},{2,6},{3,7},{4,0},{5,1},{6,2},{7,3},{8,12},{9,13},{10,... | collective-permute-start | bytes 1572872 | tf_op jit(solution)/shard_map/ppermute | solution.py:746
  212.1 24.1 %collective-permute-start.22 = (bf16[128,2048]{1,0:T(8,128)(2,1)}, bf16[128,2048]{1,0:T(8,128)(2,1)}, u32[]{:S(2)}, u32[]{:S(2)}) collective-permute-start(bf16[128,2048]{1,0:T(8,128)(2,1)} %get-tuple-element.259), channel_id=1, source_target_pairs={{0,6},{1,7},{2,4},{3,5},{4,2},{5,3},{6,0},{7,1},{8,14},{9,15},{10,... | collective-permute-start | bytes 1572872 | tf_op jit(solution)/shard_map/ppermute | solution.py:746
  246.0 37.5 %all-to-all-start.4 = ((bf16[4,2816,128]{2,1,0:T(8,128)(2,1)}), bf16[4,2816,128]{2,1,0:T(8,128)(2,1)S(1)}, u32[]{:S(2)}, u32[]{:S(2)}) async-start(bf16[4,2816,128]{2,1,0:T(8,128)(2,1)} %pair_sum.7), calls=%async_computation.4 | async-start | bytes 5767168 | tf_op jit(solution)/shard_map/all_to_all | solution.py:743
  262.9 41.7 %collective-permute-start.24 = (bf16[4,2816,128]{2,1,0:T(8,128)(2,1)}, bf16[4,2816,128]{2,1,0:T(8,128)(2,1)}, u32[]{:S(2)}, u32[]{:S(2)}) collective-permute-start(bf16[4,2816,128]{2,1,0:T(8,128)(2,1)} %get-tuple-element.278), channel_id=1, source_target_pairs={{0,1},{1,0},{2,3},{3,2},{4,5},{5,4},{6,7},{7,6},{8,9},{9,8},{10,11... | collective-permute-start | bytes 8650760 | tf_op jit(solution)/shard_map/ppermute | solution.py:752
  264.2 18.6 %collective-permute-start.23 = (bf16[2816,128]{1,0:T(8,128)(2,1)S(1)}, bf16[2816,128]{1,0:T(8,128)(2,1)}, u32[]{:S(2)}, u32[]{:S(2)}) collective-permute-start(bf16[2816,128]{1,0:T(8,128)(2,1)S(1)} %slice_bitcast_fusion.1), channel_id=1, source_target_pairs={{0,8},{8,0},{16,24},{24,16},{1,9},{9,1},{17,25},{25,17},{2,10},{10... | collective-permute-start | bytes 2162696 | tf_op jit(solution)/shard_map/ppermute | solution.py:799
  285.2 38.7 %all-to-all-start.6 = ((bf16[4,128,2048]{2,1,0:T(8,128)(2,1)}), bf16[4,128,2048]{2,1,0:T(8,128)(2,1)}, u32[]{:S(2)}, u32[]{:S(2)}) async-start(bf16[4,128,2048]{2,1,0:T(8,128)(2,1)} %bitcast.81), calls=%async_computation.6 | async-start | bytes 4194304 | tf_op jit(solution)/shard_map/all_to_all | solution.py:743
  290.8 19.1 %collective-permute-start.26 = (bf16[2816,128]{1,0:T(8,128)(2,1)S(1)}, bf16[2816,128]{1,0:T(8,128)(2,1)S(1)}, u32[]{:S(2)}, u32[]{:S(2)}) collective-permute-start(bf16[2816,128]{1,0:T(8,128)(2,1)S(1)} %slice_bitcast_fusion), channel_id=1, source_target_pairs={{0,8},{8,0},{16,24},{24,16},{1,9},{9,1},{17,25},{25,17},{2,10},{10... | collective-permute-start | bytes 2162696 | tf_op jit(solution)/shard_map/ppermute | solution.py:799
  294.7 29.1 %collective-permute-start.27 = (bf16[2816,128]{1,0:T(8,128)(2,1)}, bf16[2816,128]{1,0:T(8,128)(2,1)}, u32[]{:S(2)}, u32[]{:S(2)}) collective-permute-start(bf16[2816,128]{1,0:T(8,128)(2,1)} %get-tuple-element.290), channel_id=1, source_target_pairs={{0,8},{8,0},{16,24},{24,16},{1,9},{9,1},{17,25},{25,17},{2,10},{10... | collective-permute-start | bytes 2162696 | tf_op jit(solution)/shard_map/ppermute | solution.py:799
  295.8 28.1 %collective-permute-start.28 = (bf16[2816,128]{1,0:T(8,128)(2,1)}, bf16[2816,128]{1,0:T(8,128)(2,1)}, u32[]{:S(2)}, u32[]{:S(2)}) collective-permute-start(bf16[2816,128]{1,0:T(8,128)(2,1)} %get-tuple-element.291.refs_2_), channel_id=1, source_target_pairs={{8,16},{16,8},{9,17},{17,9},{10,18},{18,10},{11,19},{19,11},{12,20... | collective-permute-start | bytes 2162696 | tf_op jit(solution)/shard_map/ppermute | solution.py:801
  323.9 68.2 %all-to-all-start.7 = ((bf16[4,2816,128]{2,1,0:T(8,128)(2,1)}), bf16[4,2816,128]{2,1,0:T(8,128)(2,1)S(1)}, u32[]{:S(2)}, u32[]{:S(2)}) async-start(bf16[4,2816,128]{2,1,0:T(8,128)(2,1)} %pair_sum.6), calls=%async_computation.7 | async-start | bytes 5767168 | tf_op jit(solution)/shard_map/all_to_all | solution.py:743
  330.7 20.2 %collective-permute-start.29 = (bf16[2816,128]{1,0:T(8,128)(2,1)}, bf16[2816,128]{1,0:T(8,128)(2,1)}, u32[]{:S(2)}, u32[]{:S(2)}) collective-permute-start(bf16[2816,128]{1,0:T(8,128)(2,1)} %get-tuple-element.299), channel_id=1, source_target_pairs={{0,8},{8,0},{16,24},{24,16},{1,9},{9,1},{17,25},{25,17},{2,10},{10... | collective-permute-start | bytes 2162696 | tf_op jit(solution)/shard_map/ppermute | solution.py:799
  331.5 19.4 %collective-permute-start.30 = (bf16[2816,128]{1,0:T(8,128)(2,1)}, bf16[2816,128]{1,0:T(8,128)(2,1)}, u32[]{:S(2)}, u32[]{:S(2)}) collective-permute-start(bf16[2816,128]{1,0:T(8,128)(2,1)} %get-tuple-element.300.refs_2_), channel_id=1, source_target_pairs={{8,16},{16,8},{9,17},{17,9},{10,18},{18,10},{11,19},{19,11},{12,20... | collective-permute-start | bytes 2162696 | tf_op jit(solution)/shard_map/ppermute | solution.py:801
  336.4 30.0 %collective-permute-start.31 = (bf16[2816,128]{1,0:T(8,128)(2,1)}, bf16[2816,128]{1,0:T(8,128)(2,1)}, u32[]{:S(2)}, u32[]{:S(2)}) collective-permute-start(bf16[2816,128]{1,0:T(8,128)(2,1)} %get-tuple-element.307.refs_0_), channel_id=1, source_target_pairs={{0,8},{8,0},{16,24},{24,16},{1,9},{9,1},{17,25},{25,17},{2,10},{10... | collective-permute-start | bytes 2162696 | tf_op jit(solution)/shard_map/ppermute | solution.py:799
  340.2 26.3 %collective-permute-start.32 = (bf16[2816,128]{1,0:T(8,128)(2,1)}, bf16[2816,128]{1,0:T(8,128)(2,1)}, u32[]{:S(2)}, u32[]{:S(2)}) collective-permute-start(bf16[2816,128]{1,0:T(8,128)(2,1)} %get-tuple-element.308.refs_2_), channel_id=1, source_target_pairs={{8,16},{16,8},{9,17},{17,9},{10,18},{18,10},{11,19},{19,11},{12,20... | collective-permute-start | bytes 2162696 | tf_op jit(solution)/shard_map/ppermute | solution.py:801
  371.5 20.5 %collective-permute-start.34 = (bf16[2816,128]{1,0:T(8,128)(2,1)}, bf16[2816,128]{1,0:T(8,128)(2,1)}, u32[]{:S(2)}, u32[]{:S(2)}) collective-permute-start(bf16[2816,128]{1,0:T(8,128)(2,1)} %get-tuple-element.316.refs_2_), channel_id=1, source_target_pairs={{0,8},{8,0},{16,24},{24,16},{1,9},{9,1},{17,25},{25,17},{2,10},{10... | collective-permute-start | bytes 2162696 | tf_op jit(solution)/shard_map/ppermute | solution.py:799
  374.7 17.3 %collective-permute-start.35 = (bf16[2816,128]{1,0:T(8,128)(2,1)}, bf16[2816,128]{1,0:T(8,128)(2,1)}, u32[]{:S(2)}, u32[]{:S(2)}) collective-permute-start(bf16[2816,128]{1,0:T(8,128)(2,1)} %get-tuple-element.317.refs_2_), channel_id=1, source_target_pairs={{8,16},{16,8},{9,17},{17,9},{10,18},{18,10},{11,19},{19,11},{12,20... | collective-permute-start | bytes 2162696 | tf_op jit(solution)/shard_map/ppermute | solution.py:801
  379.8 27.5 %collective-permute-start.36 = (bf16[2816,128]{1,0:T(8,128)(2,1)}, bf16[2816,128]{1,0:T(8,128)(2,1)}, u32[]{:S(2)}, u32[]{:S(2)}) collective-permute-start(bf16[2816,128]{1,0:T(8,128)(2,1)} %get-tuple-element.324.refs_4_), channel_id=1, source_target_pairs={{0,8},{8,0},{16,24},{24,16},{1,9},{9,1},{17,25},{25,17},{2,10},{10... | collective-permute-start | bytes 2162696 | tf_op jit(solution)/shard_map/ppermute | solution.py:799
  382.4 24.9 %collective-permute-start.37 = (bf16[2816,128]{1,0:T(8,128)(2,1)}, bf16[2816,128]{1,0:T(8,128)(2,1)}, u32[]{:S(2)}, u32[]{:S(2)}) collective-permute-start(bf16[2816,128]{1,0:T(8,128)(2,1)} %get-tuple-element.325.refs_2_), channel_id=1, source_target_pairs={{8,16},{16,8},{9,17},{17,9},{10,18},{18,10},{11,19},{19,11},{12,20... | collective-permute-start | bytes 2162696 | tf_op jit(solution)/shard_map/ppermute | solution.py:801
  393.6 38.3 %all-to-all-start.8 = ((bf16[4,128,2048]{2,1,0:T(8,128)(2,1)}), bf16[4,128,2048]{2,1,0:T(8,128)(2,1)}, u32[]{:S(2)}, u32[]{:S(2)}) async-start(bf16[4,128,2048]{2,1,0:T(8,128)(2,1)} %bitcast.82), calls=%async_computation.8 | async-start | bytes 4194304 | tf_op jit(solution)/shard_map/all_to_all | solution.py:743
  410.7 21.2 %collective-permute-start.39 = (bf16[2816,128]{1,0:T(8,128)(2,1)}, bf16[2816,128]{1,0:T(8,128)(2,1)S(1)}, u32[]{:S(2)}, u32[]{:S(2)}) collective-permute-start(bf16[2816,128]{1,0:T(8,128)(2,1)} %get-tuple-element.333.refs_6_), channel_id=1, source_target_pairs={{0,8},{8,0},{16,24},{24,16},{1,9},{9,1},{17,25},{25,17},{2,10},{10... | collective-permute-start | bytes 2162696 | tf_op jit(solution)/shard_map/ppermute | solution.py:799
  414.9 17.0 %collective-permute-start.40 = (bf16[2816,128]{1,0:T(8,128)(2,1)}, bf16[2816,128]{1,0:T(8,128)(2,1)S(1)}, u32[]{:S(2)}, u32[]{:S(2)}) collective-permute-start(bf16[2816,128]{1,0:T(8,128)(2,1)} %get-tuple-element.334.refs_2_), channel_id=1, source_target_pairs={{8,16},{16,8},{9,17},{17,9},{10,18},{18,10},{11,19},{19,11},{12,20... | collective-permute-start | bytes 2162696 | tf_op jit(solution)/shard_map/ppermute | solution.py:801
  432.8 20.7 %all-to-all-start.9 = ((bf16[4,1280,128]{2,1,0:T(8,128)(2,1)}), bf16[4,1280,128]{2,1,0:T(8,128)(2,1)S(1)}, u32[]{:S(2)}, u32[]{:S(2)}) async-start(bf16[4,1280,128]{2,1,0:T(8,128)(2,1)} %pair_sum.8), calls=%async_computation.9 | async-start | bytes 2621440 | tf_op jit(solution)/shard_map/all_to_all | solution.py:743
  440.3 29.5 %collective-permute-start.41 = (bf16[2816,128]{1,0:T(8,128)(2,1)}, bf16[2816,128]{1,0:T(8,128)(2,1)}, u32[]{:S(2)}, u32[]{:S(2)}) collective-permute-start(bf16[2816,128]{1,0:T(8,128)(2,1)} %get-tuple-element.340.refs_0_), channel_id=1, source_target_pairs={{0,8},{8,0},{16,24},{24,16},{1,9},{9,1},{17,25},{25,17},{2,10},{10... | collective-permute-start | bytes 2162696 | tf_op jit(solution)/shard_map/ppermute | solution.py:799
  443.2 26.6 %collective-permute-start.42 = (bf16[2816,128]{1,0:T(8,128)(2,1)}, bf16[2816,128]{1,0:T(8,128)(2,1)}, u32[]{:S(2)}, u32[]{:S(2)}) collective-permute-start(bf16[2816,128]{1,0:T(8,128)(2,1)} %get-tuple-element.341.refs_2_), channel_id=1, source_target_pairs={{8,16},{16,8},{9,17},{17,9},{10,18},{18,10},{11,19},{19,11},{12,20... | collective-permute-start | bytes 2162696 | tf_op jit(solution)/shard_map/ppermute | solution.py:801
  444.8 32.4 %collective-permute-start.44 = (bf16[2,2048,128]{2,1,0:T(8,128)(2,1)}, bf16[2,2048,128]{2,1,0:T(8,128)(2,1)}, u32[]{:S(2)}, u32[]{:S(2)}) collective-permute-start(bf16[2,2048,128]{2,1,0:T(8,128)(2,1)} %get-tuple-element.348), channel_id=1, source_target_pairs={{0,1},{1,0},{2,3},{3,2},{4,5},{5,4},{6,7},{7,6},{8,9},{9,8},{10,11... | collective-permute-start | bytes 3145736 | tf_op jit(solution)/shard_map/ppermute | solution.py:752
  454.6 59.2 %all-to-all-start.5 = ((bf16[4,128,2048]{2,1,0:T(8,128)(2,1)}), bf16[4,128,2048]{2,1,0:T(8,128)(2,1)S(1)}, u32[]{:S(2)}, u32[]{:S(2)}) async-start(bf16[4,128,2048]{2,1,0:T(8,128)(2,1)} %bitcast.80), calls=%async_computation.5 | async-start | bytes 4194304 | tf_op jit(solution)/shard_map/all_to_all | solution.py:743
  461.6 25.7 %collective-permute-start.45 = (bf16[2816,128]{1,0:T(8,128)(2,1)}, bf16[2816,128]{1,0:T(8,128)(2,1)}, u32[]{:S(2)}, u32[]{:S(2)}) collective-permute-start(bf16[2816,128]{1,0:T(8,128)(2,1)} %get-tuple-element.351.refs_2_), channel_id=1, source_target_pairs={{0,8},{8,0},{16,24},{24,16},{1,9},{9,1},{17,25},{25,17},{2,10},{10... | collective-permute-start | bytes 2162696 | tf_op jit(solution)/shard_map/ppermute | solution.py:799
  464.3 23.0 %collective-permute-start.46 = (bf16[2816,128]{1,0:T(8,128)(2,1)}, bf16[2816,128]{1,0:T(8,128)(2,1)}, u32[]{:S(2)}, u32[]{:S(2)}) collective-permute-start(bf16[2816,128]{1,0:T(8,128)(2,1)} %get-tuple-element.352.refs_2_), channel_id=1, source_target_pairs={{8,16},{16,8},{9,17},{17,9},{10,18},{18,10},{11,19},{19,11},{12,20... | collective-permute-start | bytes 2162696 | tf_op jit(solution)/shard_map/ppermute | solution.py:801
  473.2 32.8 %collective-permute-start.50 = (bf16[2816,128]{1,0:T(8,128)(2,1)}, bf16[2816,128]{1,0:T(8,128)(2,1)S(1)}, u32[]{:S(2)}, u32[]{:S(2)}) collective-permute-start(bf16[2816,128]{1,0:T(8,128)(2,1)} %get-tuple-element.357.refs_4_), channel_id=1, source_target_pairs={{0,8},{8,0},{16,24},{24,16},{1,9},{9,1},{17,25},{25,17},{2,10},{10... | collective-permute-start | bytes 2162696 | tf_op jit(solution)/shard_map/ppermute | solution.py:799
  475.5 30.5 %collective-permute-start.51 = (bf16[2816,128]{1,0:T(8,128)(2,1)}, bf16[2816,128]{1,0:T(8,128)(2,1)}, u32[]{:S(2)}, u32[]{:S(2)}) collective-permute-start(bf16[2816,128]{1,0:T(8,128)(2,1)} %get-tuple-element.358.refs_2_), channel_id=1, source_target_pairs={{8,16},{16,8},{9,17},{17,9},{10,18},{18,10},{11,19},{19,11},{12,20... | collective-permute-start | bytes 2162696 | tf_op jit(solution)/shard_map/ppermute | solution.py:801
  490.7 23.0 %collective-permute-start.52 = (bf16[2816,128]{1,0:T(8,128)(2,1)}, bf16[2816,128]{1,0:T(8,128)(2,1)}, u32[]{:S(2)}, u32[]{:S(2)}) collective-permute-start(bf16[2816,128]{1,0:T(8,128)(2,1)} %get-tuple-element.364.refs_6_), channel_id=1, source_target_pairs={{0,8},{8,0},{16,24},{24,16},{1,9},{9,1},{17,25},{25,17},{2,10},{10... | collective-permute-start | bytes 2162696 | tf_op jit(solution)/shard_map/ppermute | solution.py:799
  492.7 21.0 %collective-permute-start.53 = (bf16[2816,128]{1,0:T(8,128)(2,1)}, bf16[2816,128]{1,0:T(8,128)(2,1)}, u32[]{:S(2)}, u32[]{:S(2)}) collective-permute-start(bf16[2816,128]{1,0:T(8,128)(2,1)} %get-tuple-element.365.refs_2_), channel_id=1, source_target_pairs={{8,16},{16,8},{9,17},{17,9},{10,18},{18,10},{11,19},{19,11},{12,20... | collective-permute-start | bytes 2162696 | tf_op jit(solution)/shard_map/ppermute | solution.py:801
  510.3 16.2 %collective-permute-start.56 = (bf16[2816,128]{1,0:T(8,128)(2,1)}, bf16[2816,128]{1,0:T(8,128)(2,1)}, u32[]{:S(2)}, u32[]{:S(2)}) collective-permute-start(bf16[2816,128]{1,0:T(8,128)(2,1)} %get-tuple-element.378.refs_0_), channel_id=1, source_target_pairs={{0,8},{8,0},{16,24},{24,16},{1,9},{9,1},{17,25},{25,17},{2,10},{10... | collective-permute-start | bytes 2162696 | tf_op jit(solution)/shard_map/ppermute | solution.py:799
  529.7 21.2 %collective-permute-start.63 = (bf16[2816,128]{1,0:T(8,128)(2,1)}, bf16[2816,128]{1,0:T(8,128)(2,1)}, u32[]{:S(2)}, u32[]{:S(2)}) collective-permute-start(bf16[2816,128]{1,0:T(8,128)(2,1)} %get-tuple-element.394.refs_4_), channel_id=1, source_target_pairs={{0,8},{8,0},{16,24},{24,16},{1,9},{9,1},{17,25},{25,17},{2,10},{10... | collective-permute-start | bytes 2162696 | tf_op jit(solution)/shard_map/ppermute | solution.py:799
  538.3 28.0 %collective-permute-start.54 = (bf16[2816,128]{1,0:T(8,128)(2,1)}, bf16[2816,128]{1,0:T(8,128)(2,1)}, u32[]{:S(2)}, u32[]{:S(2)}) collective-permute-start(bf16[2816,128]{1,0:T(8,128)(2,1)} %get-tuple-element.371.refs_2_), channel_id=1, source_target_pairs={{0,8},{8,0},{16,24},{24,16},{1,9},{9,1},{17,25},{25,17},{2,10},{10... | collective-permute-start | bytes 2162696 | tf_op jit(solution)/shard_map/ppermute | solution.py:799
  540.5 25.8 %collective-permute-start.55 = (bf16[2816,128]{1,0:T(8,128)(2,1)}, bf16[2816,128]{1,0:T(8,128)(2,1)}, u32[]{:S(2)}, u32[]{:S(2)}) collective-permute-start(bf16[2816,128]{1,0:T(8,128)(2,1)} %get-tuple-element.372.refs_2_), channel_id=1, source_target_pairs={{8,16},{16,8},{9,17},{17,9},{10,18},{18,10},{11,19},{19,11},{12,20... | collective-permute-start | bytes 2162696 | tf_op jit(solution)/shard_map/ppermute | solution.py:801
  553.6 26.6 %collective-permute-start.65 = (bf16[2560,128]{1,0:T(8,128)(2,1)}, bf16[2560,128]{1,0:T(8,128)(2,1)S(1)}, u32[]{:S(2)}, u32[]{:S(2)}) collective-permute-start(bf16[2560,128]{1,0:T(8,128)(2,1)} %get-tuple-element.398), channel_id=1, source_target_pairs={{0,8},{8,0},{16,24},{24,16},{1,9},{9,1},{17,25},{25,17},{2,10},{10... | collective-permute-start | bytes 1966088 | tf_op jit(solution)/shard_map/ppermute | solution.py:799
  556.3 17.5 %collective-permute-start.66 = (bf16[2048,128]{1,0:T(8,128)(2,1)}, bf16[2048,128]{1,0:T(8,128)(2,1)S(1)}, u32[]{:S(2)}, u32[]{:S(2)}) collective-permute-start(bf16[2048,128]{1,0:T(8,128)(2,1)} %get-tuple-element.399.refs_0_), channel_id=1, source_target_pairs={{8,16},{16,8},{9,17},{17,9},{10,18},{18,10},{11,19},{19,11},{12,20... | collective-permute-start | bytes 1572872 | tf_op jit(solution)/shard_map/ppermute | solution.py:801
  569.5 26.2 %collective-permute-start.58 = (bf16[2816,128]{1,0:T(8,128)(2,1)}, bf16[2816,128]{1,0:T(8,128)(2,1)S(1)}, u32[]{:S(2)}, u32[]{:S(2)}) collective-permute-start(bf16[2816,128]{1,0:T(8,128)(2,1)} %get-tuple-element.384.refs_6_), channel_id=1, source_target_pairs={{0,8},{8,0},{16,24},{24,16},{1,9},{9,1},{17,25},{25,17},{2,10},{10... | collective-permute-start | bytes 2162696 | tf_op jit(solution)/shard_map/ppermute | solution.py:799
  582.2 27.8 %collective-permute-start.67 = (bf16[2048,128]{1,0:T(8,128)(2,1)}, bf16[2048,128]{1,0:T(8,128)(2,1)}, u32[]{:S(2)}, u32[]{:S(2)}) collective-permute-start(bf16[2048,128]{1,0:T(8,128)(2,1)} %chain_step.35.refs_0_), channel_id=1, source_target_pairs={{0,8},{8,0},{16,24},{24,16},{1,9},{9,1},{17,25},{25,17},{2,10},{10... | collective-permute-start | bytes 1572872 | tf_op jit(solution)/shard_map/ppermute | solution.py:799
  599.4 17.6 %collective-permute-start.60 = (bf16[2560,128]{1,0:T(8,128)(2,1)}, bf16[2560,128]{1,0:T(8,128)(2,1)S(1)}, u32[]{:S(2)}, u32[]{:S(2)}) collective-permute-start(bf16[2560,128]{1,0:T(8,128)(2,1)} %get-tuple-element.389), channel_id=1, source_target_pairs={{0,8},{8,0},{16,24},{24,16},{1,9},{9,1},{17,25},{25,17},{2,10},{10... | collective-permute-start | bytes 1966088 | tf_op jit(solution)/shard_map/ppermute | solution.py:799
  (57 other events, 498.4 us)
